TPU v7x, 32 devices: a whole 2x2x4 slice. The times are simulated.
32 devices in a mesh: req: 4 (over z), row: 4 (over y, core), col: 2 (over x).
Axes of the slice: x: 2, y: 2, z: 4, core: 2. Of those that a mesh axis runs over, the one named last changes fastest.
Arguments:
- hidden: bfloat16 [1024, 2048], P(('req', 'row')), may hold values from -6 to 6
- latent_cache: bfloat16 [16, 384, 576], P('req'), may hold values from -144 to 144
- lengths: int32 [16], P('req'), may hold values from 96 to 384
- parents: int32 [16, 64], P('req'), may hold values from -1 to 62, as said below
- routes: int32 [1024, 6], P(('req', 'row')), may hold values from 0 to 15, all different within a row; in each aligned block of 64 rows (0 to 63, 64 to 127, ...) at most 48 rows name the same one
- accepted: int32 [16], P(('req', 'row')), may hold values from 0 to 63
- input_gain: float32 [2048], replicated, may hold values from 0.25 to 1.75
- query_weight: bfloat16 [2048, 3072], P(None, ('row', 'col')), may hold values from -0.125 to 0.125
- latent_weight: bfloat16 [2048, 576], replicated, may hold values from -0.125 to 0.125
- latent_gain: float32 [512], replicated, may hold values from 0.25 to 1.75
- key_absorb: bfloat16 [16, 128, 512], P(('row', 'col')), may hold values from -0.5 to 0.5
- value_absorb: bfloat16 [16, 512, 128], P(('row', 'col')), may hold values from -0.25 to 0.25
- output_weight: bfloat16 [2048, 2048], P(('row', 'col')), may hold values from -0.125 to 0.125
- post_gain: float32 [2048], replicated, may hold values from 0.25 to 1.75
- router_weight: bfloat16 [2048, 16], replicated, may hold values from -0.046875 to 0.046875
- shared_gate_up: bfloat16 [2, 2048, 2816], P(None, None, ('row', 'col')), may hold values from -0.125 to 0.125
- shared_down: bfloat16 [2816, 2048], P(('row', 'col')), may hold values from -0.109375 to 0.109375
- expert_gate_up: bfloat16 [16, 2, 2048, 1408], P(('req', 'row'), None, None, 'col'), may hold values from -0.125 to 0.125
- expert_down: bfloat16 [16, 1408, 2048], P(('req', 'row'), 'col'), may hold values from -1.5 to 1.5
Outputs:
- layer_output: bfloat16 [1024, 2048], P(('req', 'row'))
- accepted_latents: bfloat16 [16, 64, 576], P(('req', 'row'))
Inputs may be any that keep to these rules, and one draw needn't show every extreme that they name: parents[r, 0] is -1 and parents[r, i] lies in 0 to i - 1 for i >= 1. `routes`: the 6 experts of a token differ; within the 64 rows of one index of req and row no expert is named by more than 48 rows.
All inputs are finite; a program needn't handle non-finite values.
Results may differ from a plain program's by a relative error of at most 0.009.
The roundings to bfloat16 on the way count: a program that leaves them out, or rounds other values in their place, can miss the bound.
Values may be sent and summed in bfloat16 or wider, within the bound.
No kernel may reach another device: no remote copies, remote signals or barrier semaphores. Data moves between devices by JAX's collectives and lax.ppermute only.
A program may use at most 128 MiB of HBM per device.

v0:
```python
import math

import jax
import jax.numpy as jnp
from jax import lax
from jax.sharding import PartitionSpec as P

NOPE = 128
ROPE = 64
LAT = 512
VDIM = 128
CACHE = 384
WINDOW = 160
SINK = 4


EPSILON = 1e-06


def rms_scale(values, gain_row):
    mean_square = jnp.mean(values * values, axis=-1, keepdims=True)
    return values * lax.rsqrt(mean_square + EPSILON) * gain_row


def rope_tables(positions, rope_width):
    half_width = rope_width // 2
    frequency = jnp.exp(
        jnp.arange(half_width, dtype=jnp.float32) * (-2.0 * math.log(10000.0) / rope_width)
    )
    angles = positions[..., None] * frequency
    return (jnp.cos(angles), jnp.sin(angles))


def rotate(values, cosine, sine_part):
    half_width = values.shape[-1] // 2
    first_half = values[..., :half_width]
    second_half = values[..., half_width:]
    return jnp.concatenate(
        [
            first_half * cosine - second_half * sine_part,
            second_half * cosine + first_half * sine_part,
        ],
        axis=-1,
    )


def ancestry(parents):
    tree_size = parents.shape[-1]
    node_ids = jnp.arange(tree_size, dtype=jnp.int32)
    links = (parents[..., :, None] == node_ids[None, :]).astype(jnp.float32)
    closure = links + jnp.eye(tree_size, dtype=jnp.float32)
    for repeat in range(max(1, (tree_size - 1).bit_length())):
        closure = jnp.minimum(
            jnp.einsum("...ij,...jk->...ik", closure, closure, precision=lax.Precision.HIGHEST), 1.0
        )
    depths = jnp.sum(closure, axis=-1) - 1.0
    return (closure, depths)


def gather_rows(values):
    return lax.all_gather(values, "row", axis=0, tiled=True)


def project_down(values, weight):
    return lax.psum_scatter(
        jnp.dot(values, weight, preferred_element_type=jnp.float32),
        "row",
        scatter_dimension=0,
        tiled=True,
    )


def col_total(values):
    return lax.psum(values, "col")


def body(
    hidden,
    latent_cache,
    lengths,
    parents,
    routes,
    accepted,
    input_gain,
    query_weight,
    latent_weight,
    latent_gain,
    key_absorb,
    value_absorb,
    output_weight,
    post_gain,
    router_weight,
    shared_gate_up,
    shared_down,
    expert_gate_up,
    expert_down,
):
    tok_rows = hidden.shape[0]
    model_width = hidden.shape[1]
    group_reqs, tree_size = parents.shape
    head_count = key_absorb.shape[0]
    scale_factor = 1.0 / math.sqrt(NOPE + ROPE)
    normed = rms_scale(hidden.astype(jnp.float32), input_gain).astype(jnp.bfloat16)
    group_rows = gather_rows(normed)
    closure, depths = ancestry(parents)
    queries = jnp.dot(group_rows, query_weight, preferred_element_type=jnp.float32).astype(
        jnp.bfloat16
    )
    queries = queries.reshape(group_reqs, tree_size, head_count, NOPE + ROPE)
    projected = jnp.dot(group_rows, latent_weight, preferred_element_type=jnp.float32).reshape(
        group_reqs, tree_size, LAT + ROPE
    )
    positions = lengths.astype(jnp.float32)[:, None] + depths
    cosine, sine_part = rope_tables(positions, ROPE)
    content = rms_scale(projected[..., :LAT], latent_gain)
    key_rope = rotate(projected[..., LAT:], cosine, sine_part)
    fresh_latents = jnp.concatenate([content, key_rope], axis=-1).astype(jnp.bfloat16)
    query_latent = jnp.einsum(
        "rthn,hnl->rthl", queries[..., :NOPE], key_absorb, preferred_element_type=jnp.float32
    ).astype(jnp.bfloat16)
    query_rope = rotate(
        queries[..., NOPE:].astype(jnp.float32), cosine[:, :, None, :], sine_part[:, :, None, :]
    ).astype(jnp.bfloat16)
    query_full = jnp.concatenate([query_latent, query_rope], axis=-1)
    key_rows = jnp.concatenate([latent_cache, fresh_latents], axis=1)
    scores = (
        jnp.einsum("rthc,rkc->rhtk", query_full, key_rows, preferred_element_type=jnp.float32)
        * scale_factor
    )
    cache_spots = jnp.arange(CACHE, dtype=jnp.int32)[None, :]
    length_col = lengths[:, None]
    cache_allowed = (cache_spots < length_col) & (
        (cache_spots < SINK) | (cache_spots >= length_col - WINDOW)
    )
    allowed = jnp.concatenate(
        [
            jnp.broadcast_to(cache_allowed[:, None, :], (group_reqs, tree_size, CACHE)),
            closure > 0.5,
        ],
        axis=-1,
    )
    scores = jnp.where(allowed[:, None], scores, -1e30)
    row_peak = jnp.max(scores, axis=-1, keepdims=True)
    weights = jnp.exp(scores - row_peak)
    attention_weights = (weights / jnp.sum(weights, axis=-1, keepdims=True)).astype(jnp.bfloat16)
    out_latent = jnp.einsum(
        "rhtk,rkl->rthl", attention_weights, key_rows[..., :LAT], preferred_element_type=jnp.float32
    ).astype(jnp.bfloat16)
    head_output = jnp.einsum(
        "rthl,hlv->rthv", out_latent, value_absorb, preferred_element_type=jnp.float32
    ).astype(jnp.bfloat16)
    head_rows = head_output.reshape(group_reqs * tree_size, head_count * VDIM)
    attention_part = project_down(head_rows, output_weight)
    residual = hidden.astype(jnp.float32) + col_total(attention_part)
    post_normed = rms_scale(residual, post_gain).astype(jnp.bfloat16)
    router = jax.nn.softmax(
        jnp.dot(post_normed, router_weight, preferred_element_type=jnp.float32), axis=-1
    )
    experts = router_weight.shape[1]
    top_count = routes.shape[1]
    capacity = min(tok_rows, max(2, 2 * tok_rows * top_count // experts))
    labels = jnp.arange(experts, dtype=jnp.int32)
    chosen = jnp.sum((routes[:, :, None] == labels[None, None, :]).astype(jnp.float32), axis=1)
    row_order = jnp.arange(tok_rows, dtype=jnp.int32)
    earlier = (row_order[None, :] < row_order[:, None]).astype(jnp.float32)
    slot_rank = jnp.dot(earlier, chosen, precision=lax.Precision.HIGHEST)
    slot_ids = jnp.arange(capacity, dtype=jnp.float32)
    placing = (chosen.T[:, None, :] > 0.5) & (slot_rank.T[:, None, :] == slot_ids[None, :, None])
    outbound = jnp.einsum(
        "est,td->esd", placing.astype(jnp.bfloat16), post_normed, preferred_element_type=jnp.float32
    ).astype(jnp.bfloat16)
    inbound = lax.all_to_all(outbound, ("req", "row"), split_axis=0, concat_axis=0, tiled=True)
    group_post = gather_rows(post_normed)
    shared_gate = jnp.dot(group_post, shared_gate_up[0], preferred_element_type=jnp.float32)
    shared_upper = jnp.dot(group_post, shared_gate_up[1], preferred_element_type=jnp.float32)
    shared_hidden = (jax.nn.silu(shared_gate) * shared_upper).astype(jnp.bfloat16)
    shared_part = project_down(shared_hidden, shared_down)
    sources = inbound.shape[0]
    slot_rows = inbound.reshape(sources * capacity, model_width)
    expert_gate = jnp.dot(slot_rows, expert_gate_up[0, 0], preferred_element_type=jnp.float32)
    expert_upper = jnp.dot(slot_rows, expert_gate_up[0, 1], preferred_element_type=jnp.float32)
    expert_hidden = (jax.nn.silu(expert_gate) * expert_upper).astype(jnp.bfloat16)
    expert_result = jnp.dot(
        expert_hidden, expert_down[0], preferred_element_type=jnp.float32
    ).reshape(sources, capacity, model_width)
    returned = lax.all_to_all(
        expert_result.astype(jnp.bfloat16), ("req", "row"), split_axis=0, concat_axis=0, tiled=True
    ).astype(expert_result.dtype)
    weighting = placing.astype(jnp.float32) * router.T[:, None, :]
    routed = jnp.einsum("est,esd->td", weighting, returned, precision=lax.Precision.HIGHEST)
    summed_parts = col_total(shared_part + routed)
    layer_output = (residual + summed_parts).astype(jnp.bfloat16)
    own_count = accepted.shape[0]
    own_start = lax.axis_index("row") * own_count
    own_closure = lax.dynamic_slice_in_dim(closure, own_start, own_count, 0)
    own_depths = lax.dynamic_slice_in_dim(depths, own_start, own_count, 0)
    own_fresh = lax.dynamic_slice_in_dim(fresh_latents, own_start, own_count, 0)
    chooser = (jnp.arange(tree_size, dtype=jnp.int32)[None, :] == accepted[:, None]).astype(
        jnp.float32
    )
    path_mask = jnp.einsum("qi,qij->qj", chooser, own_closure, precision=lax.Precision.HIGHEST)
    levels = jnp.arange(tree_size, dtype=jnp.float32)
    path_places = path_mask[:, None, :] * (own_depths[:, None, :] == levels[None, :, None]).astype(
        jnp.float32
    )
    accepted_latents = jnp.einsum(
        "qkj,qjc->qkc",
        path_places.astype(jnp.bfloat16),
        own_fresh,
        preferred_element_type=jnp.float32,
    ).astype(jnp.bfloat16)
    return (layer_output, accepted_latents)


def solution(mesh):
    placed = (
        P(("req", "row"), None),
        P("req", None, None),
        P("req"),
        P("req", None),
        P(("req", "row"), None),
        P(("req", "row")),
        P(),
        P(None, ("row", "col")),
        P(),
        P(),
        P(("row", "col"), None, None),
        P(("row", "col"), None, None),
        P(("row", "col"), None),
        P(),
        P(),
        P(None, None, ("row", "col")),
        P(("row", "col"), None),
        P(("req", "row"), None, None, "col"),
        P(("req", "row"), "col", None),
    )
    return jax.shard_map(
        body,
        mesh=mesh,
        in_specs=placed,
        out_specs=(P(("req", "row"), None), P(("req", "row"), None, None)),
        check_vma=False,
    )
```

profile of v0, /device:TPU:0, one launch (start us, length us, event | category | flops | bytes accessed | tf_op | source)
XLA Modules:
  0.0 329.5 jit_solution(12373238078999165010)
XLA Ops:
  7.2 0.0 all-gather.3.cloned.1.call-start
  7.2 1.3 fusion.52
  8.5 1.8 fusion.54
  10.3 0.0 all-gather.3.cloned.1.call-update
  10.3 0.0 reduce-scatter.3.cloned.1.call-start
  10.4 0.7 broadcast_add_fusion.2
  11.1 1.1 convolution_minimum_fusion.5
  12.2 0.3 convolution_minimum_fusion.4
  12.5 3.9 %copy.34 = bf16[4,384,576]{2,1,0:T(8,128)(2,1)} copy(bf16[4,384,576]{1,2,0:T(8,128)(2,1)} %param.20) | data formatting | bytes 3538944 | tf_op args[1]
  16.4 0.1 fusion.96
  16.5 0.3 convolution_minimum_fusion.3
  16.8 0.3 convolution_minimum_fusion.2
  17.0 0.3 convolution_minimum_fusion.1
  17.3 0.4 fusion.110
  17.7 0.7 pad_add_fusion
  18.4 0.6 broadcast_add_fusion
  19.0 11.0 %all-gather.3.cloned.1.call-done = bf16[256,2048]{1,0:T(8,128)(2,1)} async-done(((bf16[64,2048]{1,0:T(8,128)(2,1)}), bf16[256,2048]{1,0:T(8,128)(2,1)}) %all-gather.3.cloned.1.call-update) | async-done | bytes 1048592 | tf_op jit(solution)/shard_map/all_gather | solution.py:61
  30.0 2.4 convolution_convert_fusion.3
  32.4 0.2 reshape.209
  32.6 0.1 slice.56
  32.7 3.0 fusion.117
  35.8 0.1 multiply_reduce_fusion.1
  36.0 0.1 multiply_convert_fusion.2
  36.1 0.6 multiply_cosine_fusion
  36.7 0.0 copy-done.10
  36.7 0.8 slice-done
  37.5 1.1 fusion.32
  38.5 0.8 subtract_convert_fusion
  39.3 1.7 maximum_maximum_fusion
  41.0 3.8 %fusion.111 = (f32[4,2,64]{2,1,0:T(2,128)S(1)}, f32[4,2,64,448]{3,2,1,0:T(8,128)}) fusion(bf16[4,448,576]{2,1,0:T(8,128)(2,1)} %maximum_maximum_fusion, bf16[4,64,2,32]{3,1,2,0:T(8,128)(2,1)} %get-tuple-element.5, bf16[4,64,2,32]{3,1,2,0:T(8,128)(2,1)S(1)} %get-tuple-element.4, bf16[4,64,2,512]{3,1,2,0:T(8,128)(2,1)} %fusion.32, ...), kind=kOutput, calls=%fused_computation.152 | convolution fusion | flops 266928576 | bytes 3688448 | tf_op jit(solution)/shard_map/sub | solution.py:144
  44.8 2.5 fusion.45
  47.3 0.1 copy.38
  47.5 3.1 fusion.76
  50.5 0.0 all-reduce.3.cloned.1.call-start
  50.6 31.5 %reduce-scatter.3.cloned.1.call-done = f32[64,2048]{1,0:T(8,128)} async-done(((f32[256,2048]{1,0:T(8,128)}), f32[64,2048]{1,0:T(8,128)}) %reduce-scatter.3.cloned.1.call-update) | async-done | bytes 524304 | tf_op jit(solution)/shard_map/reduce_scatter | solution.py:65
  82.1 0.0 all-reduce.3.cloned.1.call-update
  82.2 0.1 fusion.91
  82.3 30.8 %all-reduce.3.cloned.1.call-done = f32[64,2048]{1,0:T(8,128)} async-done(((f32[64,2048]{1,0:T(8,128)}), f32[64,2048]{1,0:T(8,128)}) %all-reduce.3.cloned.1.call-update) | async-done | bytes 524304 | tf_op jit(solution)/shard_map/psum | solution.py:74
  113.1 1.2 multiply_reduce_fusion
  114.3 1.2 multiply_convert_fusion.1
  115.5 2.7 convolution_convert_fusion.1
  118.2 5.7 %all-to-all-start = ((bf16[16,48,2048]{2,1,0:T(8,128)(2,1)}), bf16[16,48,2048]{2,1,0:T(8,128)(2,1)}, u32[]{:S(2)}, u32[]{:S(2)}) async-start(bf16[16,48,2048]{2,1,0:T(8,128)(2,1)} %convolution_convert_fusion.1), calls=%async_computation.2 | async-start | bytes 6291456 | tf_op jit(solution)/shard_map/all_to_all | solution.py:172
  123.9 0.2 all-gather.5.cloned.1.call-start
  124.1 0.3 all-gather.5.cloned.1.call-update
  124.5 58.9 %all-to-all-done = bf16[16,48,2048]{2,1,0:T(8,128)(2,1)} async-done(((bf16[16,48,2048]{2,1,0:T(8,128)(2,1)}), bf16[16,48,2048]{2,1,0:T(8,128)(2,1)}, u32[]{:S(2)}, u32[]{:S(2)}) %all-to-all-start) | async-done | bytes 3145760 | tf_op jit(solution)/shard_map/all_to_all | solution.py:172
  183.3 5.2 %fusion.4 = f32[768,704]{0,1:T(8,128)S(1)} fusion(bf16[768,2048]{1,0:T(8,128)(2,1)} %bitcast.16, bf16[1,2,2048,704]{2,3,1,0:T(8,128)(2,1)} %param.36), kind=kOutput, calls=%fused_computation.6 | convolution fusion | flops 2214592512 | bytes 8192000 | tf_op jit(solution)/shard_map/dot_general | solution.py:180
  188.6 6.3 %multiply_convert_fusion = bf16[768,704]{0,1:T(8,128)(2,1)} fusion(f32[768,704]{0,1:T(8,128)S(1)} %fusion.4, bf16[768,2048]{1,0:T(8,128)(2,1)} %bitcast.16, bf16[1,2,2048,704]{2,3,1,0:T(8,128)(2,1)} %param.36), kind=kOutput, calls=%fused_computation.15 | convolution fusion | flops 2217836544 | bytes 9273344 | tf_op jit(solution)/shard_map/dot_general | solution.py:181
  194.9 2.4 copy.39
  197.3 5.3 %convolution_convert_fusion = bf16[16,48,2048]{2,1,0:T(8,128)(2,1)} fusion(bf16[16,48,704]{2,1,0:T(8,128)(2,1)} %bitcast.141, bf16[1,704,2048]{2,1,0:T(8,128)(2,1)S(1)} %copy-done), kind=kOutput, calls=%fused_computation.1 | convolution fusion | flops 2216165376 | bytes 7110656 | tf_op jit(solution)/shard_map/dot_general | solution.py:183
  202.6 15.5 %all-to-all-start.1 = ((bf16[16,48,2048]{2,1,0:T(8,128)(2,1)}), bf16[16,48,2048]{2,1,0:T(8,128)(2,1)}, u32[]{:S(2)}, u32[]{:S(2)}) async-start(bf16[16,48,2048]{2,1,0:T(8,128)(2,1)} %convolution_convert_fusion), calls=%async_computation.3 | async-start | bytes 6291456 | tf_op jit(solution)/shard_map/all_to_all | solution.py:186
  218.1 0.0 reduce-scatter.5.cloned.1.call-start
  218.1 0.0 all-gather.5.cloned.1.call-done
  218.2 3.0 fusion.17
  221.2 5.7 %fusion.43 = f32[256,2048]{1,0:T(8,128)} fusion(bf16[352,2048]{1,0:T(8,128)(2,1)} %param.35, bf16[256,2048]{1,0:T(8,128)(2,1)} %all-gather.5.cloned.1.call-done, bf16[2,2048,352]{1,2,0:T(8,128)(2,1)} %param.34, f32[256,352]{0,1:T(8,128)} %fusion.17), kind=kOutput, calls=%fused_computation.38 | convolution fusion | flops 738738176 | bytes 6389760 | tf_op jit(solution)/shard_map/dot_general | solution.py:66
  226.9 0.0 all-reduce.5.cloned.1.call-start
  226.9 1.0 fusion.112
  228.0 38.3 %reduce-scatter.5.cloned.1.call-done = f32[64,2048]{1,0:T(8,128)} async-done(((f32[256,2048]{1,0:T(8,128)}), f32[64,2048]{1,0:T(8,128)}) %reduce-scatter.5.cloned.1.call-update) | async-done | bytes 524304 | tf_op jit(solution)/shard_map/reduce_scatter | solution.py:65
  266.3 11.3 %all-to-all-done.1 = bf16[16,48,2048]{2,1,0:T(8,128)(2,1)} async-done(((bf16[16,48,2048]{2,1,0:T(8,128)(2,1)}), bf16[16,48,2048]{2,1,0:T(8,128)(2,1)}, u32[]{:S(2)}, u32[]{:S(2)}) %all-to-all-start.1) | async-done | bytes 3145760 | tf_op jit(solution)/shard_map/all_to_all | solution.py:186
  277.6 4.6 %fusion.8 = f32[64,2048]{1,0:T(8,128)} fusion(f32[64,2048]{1,0:T(8,128)} %reduce-scatter.5.cloned.1.call-done, bf16[16,48,2048]{2,1,0:T(8,128)(2,1)} %all-to-all-done.1, f32[16,64]{1,0:T(8,128)S(1)} %divide_bitcast_fusion, f32[16,64]{1,0:T(8,128)S(1)} %fusion.91, pred[16,64]{1,0:T(8,128)(4,1)} %copy-done.12), kind=kOutput, calls=%fused_computation.11 | convolution fusion | flops 1208238080 | bytes 4203520 | tf_op jit(solution)/shard_map/est,esd->td/dot_general | solution.py:190
  282.9 0.1 convolution_bitcast_fusion.1
  283.0 0.7 fusion.102
  283.7 1.6 fusion.46
  285.3 35.4 %all-reduce.5.cloned.1.call-done = f32[64,2048]{1,0:T(8,128)} async-done(((f32[64,2048]{1,0:T(8,128)}), f32[64,2048]{1,0:T(8,128)}) %all-reduce.5.cloned.1.call-update) | async-done | bytes 524304 | tf_op jit(solution)/shard_map/psum | solution.py:74
  320.7 2.0 add_convert_fusion
  (48 shorter events, 0.3 us)
Async XLA Ops:
  7.2 190.1 %copy-start = (bf16[1,704,2048]{2,1,0:T(8,128)(2,1)S(1)}, bf16[1,704,2048]{2,1,0:T(8,128)(2,1)}, u32[]{:S(2)}) copy-start(bf16[1,704,2048]{2,1,0:T(8,128)(2,1)} %param.37) | copy-start | bytes 8650756
  7.2 22.8 %all-gather.3.cloned.1.call-start = ((), (), s32[]{:S(2)}) async-start(), calls=%async_computation.4 | async-start | bytes 1310720 | tf_op jit(solution)/shard_map/all_gather | solution.py:61
  10.3 6.1 %copy-start.15 = (s32[4]{0:T(128)S(1)}, s32[4]{0:T(128)}, u32[]{:S(2)}) copy-start(s32[4]{0:T(128)} %param.21) | copy-start | bytes 52
  10.3 71.8 %reduce-scatter.3.cloned.1.call-start = ((), (), s32[]{:S(2)}) async-start(), calls=%async_computation.5 | async-start | bytes 2621440 | tf_op jit(solution)/shard_map/reduce_scatter | solution.py:65
  32.6 3.1 copy-start.7
  32.7 3.2 copy-start.14
  35.7 1.0 copy-start.10
  35.8 3.6 %copy-start.1 = (bf16[4,384,576]{2,1,0:T(8,128)(2,1)S(1)}, bf16[4,384,576]{2,1,0:T(8,128)(2,1)}, u32[]{:S(2)}) copy-start(bf16[4,384,576]{2,1,0:T(8,128)(2,1)} %copy.34) | copy-start | bytes 5308420
  35.8 1.7 slice-start
  36.1 4.9 %copy-start.5 = (bf16[4,64,512]{2,1,0:T(8,128)(2,1)}, bf16[4,64,512]{2,1,0:T(8,128)(2,1)S(1)}, u32[]{:S(2)}) copy-start(bf16[4,64,512]{2,1,0:T(8,128)(2,1)S(1)} %multiply_convert_fusion.2) | copy-start | bytes 786436
  37.5 3.5 %copy-start.8 = (bf16[4,64,32]{2,1,0:T(8,128)(2,1)}, bf16[4,64,32]{2,1,0:T(8,128)(2,1)S(1)}, u32[]{:S(2)}) copy-start(bf16[4,64,32]{2,1,0:T(8,128)(2,1)S(1)} %get-tuple-element.8) | copy-start | bytes 49156
  37.5 3.5 %copy-start.9 = (bf16[4,64,32]{2,1,0:T(8,128)(2,1)}, bf16[4,64,32]{2,1,0:T(8,128)(2,1)S(1)}, u32[]{:S(2)}) copy-start(bf16[4,64,32]{2,1,0:T(8,128)(2,1)S(1)} %get-tuple-element.9) | copy-start | bytes 49156
  39.3 1.7 copy-start.11
  47.4 34.7 %copy-start.13 = (s32[64,6]{0,1:T(8,128)S(1)}, s32[64,6]{0,1:T(8,128)}, u32[]{:S(2)}) copy-start(s32[64,6]{0,1:T(8,128)} %param.23) | copy-start | bytes 4612
  47.4 65.7 %copy-start.2 = (bf16[64,2048]{1,0:T(8,128)(2,1)S(1)}, bf16[64,2048]{1,0:T(8,128)(2,1)}, u32[]{:S(2)}) copy-start(bf16[64,2048]{1,0:T(8,128)(2,1)} %param.19) | copy-start | bytes 786436
  50.5 62.6 %all-reduce.3.cloned.1.call-start = ((), (), s32[]{:S(2)}) async-start(), calls=%async_computation.6 | async-start | bytes 1048576 | tf_op jit(solution)/shard_map/psum | solution.py:74
  82.1 36.1 %copy-start.12 = (pred[16,64]{1,0:T(8,128)(4,1)}, pred[16,64]{1,0:T(8,128)(4,1)S(1)}, u32[]{:S(2)}) copy-start(pred[16,64]{1,0:T(8,128)(4,1)S(1)} %compare_bitcast_fusion) | copy-start | bytes 3076
  115.5 2.7 copy-start.3
  118.2 65.1 %all-to-all-start = ((bf16[16,48,2048]{2,1,0:T(8,128)(2,1)}), bf16[16,48,2048]{2,1,0:T(8,128)(2,1)}, u32[]{:S(2)}, u32[]{:S(2)}) async-start(bf16[16,48,2048]{2,1,0:T(8,128)(2,1)} %convolution_convert_fusion.1), calls=%async_computation.2 | async-start | bytes 6291456 | tf_op jit(solution)/shard_map/all_to_all | solution.py:172
  123.9 94.3 %all-gather.5.cloned.1.call-start = ((), (), s32[]{:S(2)}) async-start(), calls=%async_computation.7 | async-start | bytes 1310720 | tf_op jit(solution)/shard_map/all_gather | solution.py:61
  202.6 75.0 %all-to-all-start.1 = ((bf16[16,48,2048]{2,1,0:T(8,128)(2,1)}), bf16[16,48,2048]{2,1,0:T(8,128)(2,1)}, u32[]{:S(2)}, u32[]{:S(2)}) async-start(bf16[16,48,2048]{2,1,0:T(8,128)(2,1)} %convolution_convert_fusion), calls=%async_computation.3 | async-start | bytes 6291456 | tf_op jit(solution)/shard_map/all_to_all | solution.py:186
  218.1 48.3 %reduce-scatter.5.cloned.1.call-start = ((), (), s32[]{:S(2)}) async-start(), calls=%async_computation.8 | async-start | bytes 2621440 | tf_op jit(solution)/shard_map/reduce_scatter | solution.py:65
  221.2 5.7 %copy-start.4 = (bf16[64,2048]{1,0:T(8,128)(2,1)S(1)}, bf16[64,2048]{1,0:T(8,128)(2,1)}, u32[]{:S(2)}) copy-start(bf16[64,2048]{1,0:T(8,128)(2,1)} %copy-done.3) | copy-start | bytes 786436
  226.9 93.9 %all-reduce.5.cloned.1.call-start = ((), (), s32[]{:S(2)}) async-start(), calls=%async_computation.9 | async-start | bytes 1048576 | tf_op jit(solution)/shard_map/psum | solution.py:74
  228.0 55.7 %copy-start.6 = (bf16[4,64,512]{2,1,0:T(8,128)(2,1)S(1)}, bf16[4,64,512]{2,1,0:T(8,128)(2,1)}, u32[]{:S(2)}) copy-start(bf16[4,64,512]{2,1,0:T(8,128)(2,1)} %copy-done.5) | copy-start | bytes 786436
Sparse Core Ops, SparseCore 0:
  10.4 19.5 all-gather.2
  50.7 31.3 reduce-scatter.2
  84.5 28.5 all-reduce.2
  126.5 30.3 all-gather.4
  227.0 39.3 reduce-scatter.4
  282.4 38.2 all-reduce.4
where the time goes:
time: 330 us
  waiting for transfers between devices  218 us (66%)
  matrix products  54 us (16%)
  starting transfers between devices  21.6 us (7%)
  between operations  15.1 us (5%)
  other arithmetic  12.9 us (4%)
  local copies, waits for them, and re-layouts  8.26 us (3%)
    reduce_scatter x2, waiting for transfers between devices, project_down(): lax.psum_scatter(jnp.dot(values, weight, preferred_element_type=jnp.float...  69.8 us
    psum x2, waiting for transfers between devices, col_total(): return lax.psum(values, 'col')  66.2 us
    all_to_all x1, waiting for transfers between devices, body(): lax.all_to_all(outbound, ('req', 'row'), split_axis=0, concat_axis=0, til...  58.9 us
    all_to_all x1, starting transfers between devices, body(): lax.all_to_all(expert_result.astype(jnp.bfloat16), ('req', 'row'), split_...  15.5 us
    all_to_all x1, waiting for transfers between devices, body(): lax.all_to_all(expert_result.astype(jnp.bfloat16), ('req', 'row'), split_...  11.3 us
    all_gather x2, waiting for transfers between devices, gather_rows(): return lax.all_gather(values, 'row', axis=0, tiled=True)  11 us
    dot_general x2, matrix products, project_down(): jnp.dot(values, weight, preferred_element_type=jnp.float32)  8.71 us
  transfers between devices with their start and end apart: 8, of which 7 were waited for; matrix products, arithmetic and copies ran while one was open for 12% of the time, Pallas kernels for 0%

commit v1 on v0

v1 whole, which is shorter than its diff:
```python
import functools
import math

import jax
import jax.numpy as jnp
from jax import lax
from jax.sharding import PartitionSpec as P

NOPE = 128
ROPE = 64
LAT = 512
VDIM = 128
CACHE = 384
WINDOW = 160
SINK = 4


EPSILON = 1e-06


def rms_scale(values, gain_row):
    mean_square = jnp.mean(values * values, axis=-1, keepdims=True)
    return values * lax.rsqrt(mean_square + EPSILON) * gain_row


def rope_tables(positions, rope_width):
    half_width = rope_width // 2
    frequency = jnp.exp(
        jnp.arange(half_width, dtype=jnp.float32) * (-2.0 * math.log(10000.0) / rope_width)
    )
    angles = positions[..., None] * frequency
    return (jnp.cos(angles), jnp.sin(angles))


def rotate(values, cosine, sine_part):
    half_width = values.shape[-1] // 2
    first_half = values[..., :half_width]
    second_half = values[..., half_width:]
    return jnp.concatenate(
        [
            first_half * cosine - second_half * sine_part,
            second_half * cosine + first_half * sine_part,
        ],
        axis=-1,
    )


def ancestry(parents):
    tree_size = parents.shape[-1]
    node_ids = jnp.arange(tree_size, dtype=jnp.int32)
    links = (parents[..., :, None] == node_ids[None, :]).astype(jnp.float32)
    closure = links + jnp.eye(tree_size, dtype=jnp.float32)
    for repeat in range(max(1, (tree_size - 1).bit_length())):
        closure = jnp.minimum(
            jnp.einsum("...ij,...jk->...ik", closure, closure, precision=lax.Precision.HIGHEST), 1.0
        )
    depths = jnp.sum(closure, axis=-1) - 1.0
    return (closure, depths)


def swap(values, axis, size, bits):
    return lax.ppermute(values, axis, [(i, i ^ bits) for i in range(size)])


def body(
    sizes,
    hidden,
    latent_cache,
    lengths,
    parents,
    routes,
    accepted,
    input_gain,
    query_weight,
    latent_weight,
    latent_gain,
    key_absorb,
    value_absorb,
    output_weight,
    post_gain,
    router_weight,
    shared_gate_up,
    shared_down,
    expert_gate_up,
    expert_down,
):
    n_req, n_row, n_col = sizes
    tok_rows, model_width = hidden.shape
    group_reqs, tree_size = parents.shape
    head_count = key_absorb.shape[0]
    scale_factor = 1.0 / math.sqrt(NOPE + ROPE)
    req_index = lax.axis_index("req")
    row_index = lax.axis_index("row")
    half = n_row // 2
    bf16 = jnp.bfloat16

    all_routes = lax.all_gather(routes, ("req", "row"), axis=0, tiled=False)

    normed = rms_scale(hidden.astype(jnp.float32), input_gain).astype(bf16)
    far = swap(normed, "row", n_row, 2)
    near = swap(normed, "row", n_row, 1)
    far_near = swap(far, "row", n_row, 1)
    group_rows = jnp.concatenate([normed, near, far, far_near], axis=0)

    order = jnp.arange(group_reqs, dtype=jnp.int32) ^ row_index
    cache = jnp.take(latent_cache, order, axis=0)
    lengths = jnp.take(lengths, order, axis=0)
    parents = jnp.take(parents, order, axis=0)
    closure, depths = ancestry(parents)
    queries = jnp.dot(group_rows, query_weight, preferred_element_type=jnp.float32).astype(bf16)
    queries = queries.reshape(group_reqs, tree_size, head_count, NOPE + ROPE)
    projected = jnp.dot(group_rows, latent_weight, preferred_element_type=jnp.float32).reshape(
        group_reqs, tree_size, LAT + ROPE
    )
    positions = lengths.astype(jnp.float32)[:, None] + depths
    cosine, sine_part = rope_tables(positions, ROPE)
    content = rms_scale(projected[..., :LAT], latent_gain)
    key_rope = rotate(projected[..., LAT:], cosine, sine_part)
    fresh_latents = jnp.concatenate([content, key_rope], axis=-1).astype(bf16)
    query_latent = jnp.einsum(
        "rthn,hnl->rthl", queries[..., :NOPE], key_absorb, preferred_element_type=jnp.float32
    ).astype(bf16)
    query_rope = rotate(
        queries[..., NOPE:].astype(jnp.float32), cosine[:, :, None, :], sine_part[:, :, None, :]
    ).astype(bf16)
    query_full = jnp.concatenate([query_latent, query_rope], axis=-1)
    key_rows = jnp.concatenate([cache, fresh_latents], axis=1)
    scores = (
        jnp.einsum("rthc,rkc->rhtk", query_full, key_rows, preferred_element_type=jnp.float32)
        * scale_factor
    )
    cache_spots = jnp.arange(CACHE, dtype=jnp.int32)[None, :]
    length_col = lengths[:, None]
    cache_allowed = (cache_spots < length_col) & (
        (cache_spots < SINK) | (cache_spots >= length_col - WINDOW)
    )
    allowed = jnp.concatenate(
        [
            jnp.broadcast_to(cache_allowed[:, None, :], (group_reqs, tree_size, CACHE)),
            closure > 0.5,
        ],
        axis=-1,
    )
    scores = jnp.where(allowed[:, None], scores, -1e30)
    row_peak = jnp.max(scores, axis=-1, keepdims=True)
    weights = jnp.exp(scores - row_peak)
    attention_weights = (weights / jnp.sum(weights, axis=-1, keepdims=True)).astype(bf16)
    out_latent = jnp.einsum(
        "rhtk,rkl->rthl", attention_weights, key_rows[..., :LAT], preferred_element_type=jnp.float32
    ).astype(bf16)
    head_output = jnp.einsum(
        "rthl,hlv->rthv", out_latent, value_absorb, preferred_element_type=jnp.float32
    ).astype(bf16)
    head_rows = head_output.reshape(group_reqs * tree_size, head_count * VDIM)
    partial = jnp.dot(head_rows, output_weight, preferred_element_type=jnp.float32)
    partial = partial.reshape(half, 2, tok_rows, model_width)
    partial = partial[:, 0] + swap(partial[:, 1].astype(bf16), "row", n_row, 1).astype(jnp.float32)
    partial = partial[0] + swap(partial[1].astype(bf16), "row", n_row, 2).astype(jnp.float32)
    partial = col_sum(partial, n_col)
    residual = hidden.astype(jnp.float32) + partial
    post_normed = rms_scale(residual, post_gain).astype(bf16)

    far_own = swap(post_normed, "row", n_row, 2)
    across = [swap(post_normed, "req", n_req, s) for s in range(1, n_req)]
    across = jnp.concatenate(across, axis=0)
    near_own = swap(jnp.concatenate([post_normed, far_own], axis=0), "row", n_row, 1)
    own_group = jnp.concatenate([post_normed, far_own, near_own], axis=0)
    near_across = swap(across, "row", n_row, 1)
    far_across = swap(across, "row", n_row, 2)
    near_far = swap(far_across, "row", n_row, 1)

    expert_id = req_index * n_row + row_index
    named = jnp.any(all_routes == expert_id, axis=-1).astype(jnp.float32).reshape(n_req, n_row, tok_rows)
    named = jnp.take(named, jnp.arange(n_req, dtype=jnp.int32) ^ req_index, axis=0)
    named = jnp.take(named, jnp.arange(n_row, dtype=jnp.int32) ^ row_index, axis=1)

    def expert_part(rows, marks):
        router = jax.nn.softmax(
            jnp.dot(rows, router_weight, preferred_element_type=jnp.float32), axis=-1
        )
        share = lax.dynamic_slice_in_dim(router, expert_id, 1, axis=1) * marks.reshape(-1, 1)
        gate = jnp.dot(rows, expert_gate_up[0, 0], preferred_element_type=jnp.float32)
        upper = jnp.dot(rows, expert_gate_up[0, 1], preferred_element_type=jnp.float32)
        inner = (jax.nn.silu(gate) * upper).astype(bf16)
        return share * jnp.dot(inner, expert_down[0], preferred_element_type=jnp.float32)

    gate = jnp.dot(own_group, shared_gate_up[0], preferred_element_type=jnp.float32)
    upper = jnp.dot(own_group, shared_gate_up[1], preferred_element_type=jnp.float32)
    inner = (jax.nn.silu(gate) * upper).astype(bf16)
    own_part = jnp.dot(inner, shared_down, preferred_element_type=jnp.float32)
    own_part = own_part + expert_part(own_group, jnp.stack([named[0, 0], named[0, 2], named[0, 1], named[0, 3]]))
    own_part = own_part.reshape(2, 2, tok_rows, model_width)
    lane_part = expert_part(
        jnp.concatenate([across, near_across], axis=0), jnp.stack([named[1:, 0], named[1:, 1]])
    ).reshape(2, n_req - 1, tok_rows, model_width)
    far_part = expert_part(
        jnp.concatenate([far_across, near_far], axis=0), jnp.stack([named[1:, 2], named[1:, 3]])
    ).reshape(2, n_req - 1, tok_rows, model_width)

    def fold(keep, send, bits):
        return keep + swap(send.astype(bf16), "row", n_row, bits).astype(jnp.float32)

    own_part = fold(own_part[0], own_part[1], 1)
    lane_part = fold(lane_part[0], lane_part[1], 1)
    far_part = fold(far_part[0], far_part[1], 1)
    own_sum = fold(own_part[0], own_part[1], 2)
    lane_sum = fold(lane_part, far_part, 2).astype(bf16)
    for s in range(1, n_req):
        own_sum = own_sum + swap(lane_sum[s - 1], "req", n_req, s).astype(jnp.float32)
    summed_parts = col_sum(own_sum, n_col)
    layer_output = (residual + summed_parts).astype(bf16)

    chooser = (jnp.arange(tree_size, dtype=jnp.int32)[None, :] == accepted[:, None]).astype(
        jnp.float32
    )
    path_mask = jnp.einsum("qi,qij->qj", chooser, closure[:1], precision=lax.Precision.HIGHEST)
    levels = jnp.arange(tree_size, dtype=jnp.float32)
    path_places = path_mask[:, None, :] * (depths[:1, None, :] == levels[None, :, None]).astype(
        jnp.float32
    )
    accepted_latents = jnp.einsum(
        "qkj,qjc->qkc",
        path_places.astype(bf16),
        fresh_latents[:1],
        preferred_element_type=jnp.float32,
    ).astype(bf16)
    return (layer_output, accepted_latents)


def col_sum(values, n_col):
    bits = 1
    while bits < n_col:
        sent = values.astype(jnp.bfloat16)
        values = sent.astype(jnp.float32) + swap(sent, "col", n_col, bits).astype(jnp.float32)
        bits *= 2
    return values


def solution(mesh):
    placed = (
        P(("req", "row"), None),
        P("req", None, None),
        P("req"),
        P("req", None),
        P(("req", "row"), None),
        P(("req", "row")),
        P(),
        P(None, ("row", "col")),
        P(),
        P(),
        P(("row", "col"), None, None),
        P(("row", "col"), None, None),
        P(("row", "col"), None),
        P(),
        P(),
        P(None, None, ("row", "col")),
        P(("row", "col"), None),
        P(("req", "row"), None, None, "col"),
        P(("req", "row"), "col", None),
    )
    sizes = (mesh.shape["req"], mesh.shape["row"], mesh.shape["col"])
    return jax.shard_map(
        functools.partial(body, sizes),
        mesh=mesh,
        in_specs=placed,
        out_specs=(P(("req", "row"), None), P(("req", "row"), None, None)),
        check_vma=False,
    )
```

time: 330 us -> 233 us (0.71)
  waiting for transfers between devices: 218 us -> 64.1 us
  local copies, waits for them, and re-layouts: 8.26 us -> 32.1 us
  blocking collectives: 0 us -> 21 us
  between operations: 15.1 us -> 1.94 us
  other arithmetic: 12.9 us -> 25.5 us
  matrix products: 54 us -> 62.9 us
    all_to_all x2 -> x0, waiting for transfers between devices: 70.1 us -> none  [the longest x1 58.9 us: body(): lax.all_to_all(outbound, ('req', 'row'), split_axis=0, concat_axis=0, til...]
    reduce_scatter x2 -> x0, waiting for transfers between devices: 69.8 us -> none  [project_down(): lax.psum_scatter(jnp.dot(values, weight, preferred_element_type=jnp.float...]
    psum x2 -> x0, waiting for transfers between devices: 66.2 us -> none  [col_total(): return lax.psum(values, 'col')]
    ppermute x0 -> x23, waiting for transfers between devices: none -> 64.1 us  [swap(): return lax.ppermute(values, axis, [(i, i ^ bits) for i in range(size)])]
    ppermute x0 -> x23, starting transfers between devices: none -> 23.2 us  [swap(): return lax.ppermute(values, axis, [(i, i ^ bits) for i in range(size)])]
    all_to_all x2 -> x0, starting transfers between devices: 21.2 us -> none  [the longest x1 15.5 us: body(): lax.all_to_all(expert_result.astype(jnp.bfloat16), ('req', 'row'), split_...]
    all_gather x0 -> x1, blocking collectives: none -> 21 us  [body(): all_routes = lax.all_gather(routes, ('req', 'row'), axis=0, tiled=False)]
    all_gather x2 -> x0, waiting for transfers between devices: 11 us -> none  [gather_rows(): return lax.all_gather(values, 'row', axis=0, tiled=True)]
  transfers between devices with their start and end apart: 8 -> 23, of which waited for: 7 -> 10; matrix products, arithmetic and copies ran while one was open for 12% -> 39% of each run, Pallas kernels for 0% -> 0%
where the time goes in v1:
time: 233 us; the launch traced here: 231 us
  waiting for transfers between devices  64.1 us (28%)
  matrix products  62.9 us (27%)
  local copies, waits for them, and re-layouts  32.1 us (14%)
  other arithmetic  25.5 us (11%)
  starting transfers between devices  23.2 us (10%)
  blocking collectives  21 us (9%)
    ppermute x23, waiting for transfers between devices, swap(): return lax.ppermute(values, axis, [(i, i ^ bits) for i in range(size)])  64.1 us
    ppermute x23, starting transfers between devices, swap(): return lax.ppermute(values, axis, [(i, i ^ bits) for i in range(size)])  23.2 us
    dot_general x3, matrix products, expert_part(): jnp.dot(inner, expert_down[0], preferred_element_type=jnp.float32)  22.4 us
    all_gather x1, blocking collectives, body(): all_routes = lax.all_gather(routes, ('req', 'row'), axis=0, tiled=False)  21 us
    dot_general x3, matrix products, expert_part(): jnp.dot(rows, expert_gate_up[0, 1], preferred_element_type=jnp.float32)  11.7 us
    unnamed x70, local copies, waits for them, and re-layouts  8.35 us
    gather x2, local copies, waits for them, and re-layouts, body(): cache = jnp.take(latent_cache, order, axis=0)  7.38 us
    dot_general x1, matrix products, body(): own_part = jnp.dot(inner, shared_down, preferred_element_type=jnp.float32)  5.69 us
  transfers between devices with their start and end apart: 23, of which 10 were waited for; matrix products, arithmetic and copies ran while one was open for 39% of the time, Pallas kernels for 0%

profile of v1, /device:TPU:0, one launch (start us, length us, event | category | flops | bytes accessed | tf_op | source)
XLA Modules:
  0.0 230.7 jit_solution(6614831954283284783)
XLA Ops:
  0.7 1.3 fusion.74
  1.9 1.1 fusion.76
  3.0 3.0 %collective-permute-start.1 = (bf16[64,2048]{1,0:T(8,128)(2,1)S(1)}, bf16[64,2048]{1,0:T(8,128)(2,1)}, u32[]{:S(2)}, u32[]{:S(2)}) collective-permute-start(bf16[64,2048]{1,0:T(8,128)(2,1)S(1)} %fusion.76), channel_id=1, source_target_pairs={{0,4},{2,6},{4,0},{6,2},{1,5},{3,7},{5,1},{7,3},{8,12},{10,14},{12... | collective-permute-start | bytes 786440 | tf_op jit(solution)/shard_map/ppermute | solution.py:62
  6.1 1.2 gather_fusion.2
  9.9 3.5 %gather_fusion = bf16[4,384,576]{1,2,0:T(8,128)(2,1)} fusion(bf16[4,384,576]{1,2,0:T(8,128)(2,1)} %param.20, s32[1024]{0:T(1024)S(1)} %pad_clamp_fusion.1), kind=kCustom, calls=%fused_computation | custom fusion | bytes 3538960 | tf_op jit(solution)/shard_map/jit(_take)/gather | solution.py:106
  13.4 3.9 %copy.45 = bf16[4,384,576]{2,1,0:T(8,128)(2,1)} copy(bf16[4,384,576]{1,2,0:T(8,128)(2,1)} %gather_fusion) | data formatting | bytes 3538944 | tf_op jit(solution)/shard_map/jit(_take)/gather | solution.py:106
  18.1 3.1 %broadcast_select_fusion = bf16[4,384,576]{2,1,0:T(8,128)(2,1)} fusion(bf16[4,384,576]{2,1,0:T(8,128)(2,1)} %copy.45, pred[4]{0:T(512)(128)(4,1)S(1)} %compare_and_fusion.1), kind=kLoop, calls=%fused_computation.35 | loop fusion | flops 884736 | bytes 3538948 | tf_op jit(solution)/shard_map/jit(_take)/select_n | solution.py:106
  22.4 0.8 collective-permute-done.2
  23.9 1.8 convolution_convert_fusion.1
  25.9 3.0 %fusion.102 = f32[256,576]{1,0:T(8,128)S(1)} fusion(bf16[2048,576]{0,1:T(8,128)(2,1)} %param.27, bf16[64,2048]{1,0:T(8,128)(2,1)} %copy-done.30, bf16[64,2048]{1,0:T(8,128)(2,1)} %collective-permute-done.1, bf16[64,2048]{1,0:T(8,128)(2,1)} %collective-permute-done, bf16[64,2048]{1,0:T(8,128)(2,1)} %copy-done.19), kind=kOutput, calls=%fused_computation.131 | convolution fusion | flops 608174080 | bytes 3997696 | tf_op jit(solution)/shard_map/dot_general | solution.py:112
  30.5 1.1 fusion.50
  31.6 0.8 subtract_convert_fusion
  32.4 1.7 maximum_maximum_fusion
  34.1 3.7 %fusion.139 = (f32[4,2,64]{2,1,0:T(2,128)S(1)}, f32[4,2,64,448]{3,2,1,0:T(8,128)}) fusion(bf16[4,448,576]{2,1,0:T(8,128)(2,1)} %maximum_maximum_fusion, bf16[4,64,2,32]{3,1,2,0:T(8,128)(2,1)} %get-tuple-element.16, bf16[4,64,2,32]{3,1,2,0:T(8,128)(2,1)S(1)} %get-tuple-element.15, bf16[4,64,2,512]{3,1,2,0:T(8,128)(2,1)} %fusion.50, ...), kind=kOutput, calls=%fused_computation.228 | convolution fusion | flops 266928576 | bytes 3688448 | tf_op jit(solution)/shard_map/sub | solution.py:146
  37.8 2.5 %fusion.54 = bf16[4,64,2,128]{3,1,0,2:T(8,128)(2,1)S(1)} fusion(bf16[4,448,576]{2,1,0:T(8,128)(2,1)} %maximum_maximum_fusion, bf16[2,512,128]{2,1,0:T(8,128)(2,1)} %param.30, f32[4,2,64,448]{3,2,1,0:T(8,128)} %get-tuple-element.40, f32[4,2,64]{2,1,0:T(2,128)S(1)} %get-tuple-element.39), kind=kOutput, calls=%fused_computation.60 | convolution fusion | flops 302776320 | bytes 3278848 | tf_op jit(solution)/shard_map/rthl,hlv->rthv/dot_general | solution.py:151
  40.6 1.7 fusion.57
  42.3 1.4 copy-done.4
  43.6 0.8 fusion.77
  44.9 21.0 %all-gather.1 = s32[16,64,6]{1,2,0:T(8,128)S(1)} all-gather(s32[1,64,6]{1,2,0:T(8,128)S(1)} %bitcast.221), channel_id=2, replica_groups=mesh['req'=4,'row'=4,'col'=2] {'req','row'}, dimensions={0}, use_global_device_ids=true | all-gather | bytes 26112 | tf_op jit(solution)/shard_map/all_gather | solution.py:97
  66.5 1.5 fusion.56
  68.0 1.0 copy-done.6
  71.7 6.0 %collective-permute-done.4 = bf16[64,2048]{1,0:T(8,128)(2,1)} collective-permute-done((bf16[64,2048]{1,0:T(8,128)(2,1)S(1)}, bf16[64,2048]{1,0:T(8,128)(2,1)}, u32[]{:S(2)}, u32[]{:S(2)}) %collective-permute-start.4) | collective-permute-done | bytes 262176 | tf_op jit(solution)/shard_map/ppermute | solution.py:62
  77.7 1.2 fusion.84
  78.9 1.6 collective-permute-start.5
  81.1 5.6 %collective-permute-done.5 = bf16[64,2048]{1,0:T(8,128)(2,1)S(1)} collective-permute-done((bf16[64,2048]{1,0:T(8,128)(2,1)S(1)}, bf16[64,2048]{1,0:T(8,128)(2,1)S(1)}, u32[]{:S(2)}, u32[]{:S(2)}) %collective-permute-start.5) | collective-permute-done | bytes 262176 | tf_op jit(solution)/shard_map/ppermute | solution.py:62
  87.4 1.5 multiply_convert_fusion.5
  91.6 4.4 %collective-permute-start.12 = (bf16[64,2048]{1,0:T(8,128)(2,1)}, bf16[64,2048]{1,0:T(8,128)(2,1)S(1)}, u32[]{:S(2)}, u32[]{:S(2)}) collective-permute-start(bf16[64,2048]{1,0:T(8,128)(2,1)} %multiply_convert_fusion.5), channel_id=1, source_target_pairs={{0,24},{8,16},{16,8},{24,0},{1,25},{9,17},{17,9},{25,1},{2,26},{10... | collective-permute-start | bytes 786440 | tf_op jit(solution)/shard_map/ppermute | solution.py:62
  96.1 1.1 pad_maximum_fusion.2
  97.2 0.8 collective-permute-done.10
  98.1 1.8 constant_dynamic-update-slice_fusion.6
  99.9 12.3 %collective-permute-done.11 = bf16[64,2048]{1,0:T(8,128)(2,1)S(1)} collective-permute-done((bf16[64,2048]{1,0:T(8,128)(2,1)}, bf16[64,2048]{1,0:T(8,128)(2,1)S(1)}, u32[]{:S(2)}, u32[]{:S(2)}) %collective-permute-start.11) | collective-permute-done | bytes 262176 | tf_op jit(solution)/shard_map/ppermute | solution.py:62
  112.2 0.8 constant_dynamic-update-slice_fusion.5
  113.0 0.8 constant_dynamic-update-slice_fusion.4
  113.9 1.1 collective-permute-start.15
  114.9 1.6 fusion.140
  117.2 3.9 %fusion.9 = f32[256,704]{0,1:T(8,128)} fusion(bf16[1,2,2048,704]{2,3,1,0:T(8,128)(2,1)} %param.36, bf16[128,2048]{1,0:T(8,128)(2,1)S(1)} %collective-permute-done.7, bf16[64,2048]{1,0:T(8,128)(2,1)} %collective-permute-done.6, bf16[64,2048]{1,0:T(8,128)(2,1)} %multiply_convert_fusion.5), kind=kOutput, calls=%fused_computation.16 | convolution fusion | flops 741343232 | bytes 4653056 | tf_op jit(solution)/shard_map/dot_general | solution.py:183
  121.1 2.3 %fusion.33 = f32[256,352]{0,1:T(8,128)} fusion(bf16[2,2048,352]{1,2,0:T(8,128)(2,1)S(1)} %copy-done.27, bf16[128,2048]{1,0:T(8,128)(2,1)S(1)} %collective-permute-done.7, bf16[64,2048]{1,0:T(8,128)(2,1)} %collective-permute-done.6, bf16[64,2048]{1,0:T(8,128)(2,1)} %multiply_convert_fusion.5), kind=kOutput, calls=%fused_computation.43 | convolution fusion | flops 372244480 | bytes 2850816 | tf_op jit(solution)/shard_map/dot_general | solution.py:188
  123.5 5.7 %fusion.96 = f32[256,2048]{1,0:T(8,128)} fusion(bf16[352,2048]{1,0:T(8,128)(2,1)} %param.35, f32[256,352]{0,1:T(8,128)} %fusion.33, bf16[2,2048,352]{1,2,0:T(8,128)(2,1)} %param.34, bf16[128,2048]{1,0:T(8,128)(2,1)} %copy-done.29, bf16[64,2048]{1,0:T(8,128)(2,1)} %collective-permute-done.6, bf16[64,2048]{1,0:T(8,128)(2,1)} %multiply_convert_fusion.5), kind=kOutput, calls=%fused_computation.129 | convolution fusion | flops 741883904 | bytes 6389760 | tf_op jit(solution)/shard_map/dot_general | solution.py:190
  129.2 1.3 divide_multiply_fusion.2
  130.4 7.6 %fusion.20 = f32[256,2048]{1,0:T(8,128)} fusion(f32[256,2048]{1,0:T(8,128)} %fusion.96, bf16[1,704,2048]{2,1,0:T(8,128)(2,1)S(1)} %copy-done, f32[256]{0:T(256)} %bitcast.222, f32[256,704]{0,1:T(8,128)} %fusion.9, bf16[1,2,2048,704]{2,3,1,0:T(8,128)(2,1)} %param.36, bf16[128,2048]{1,0:T(8,128)(2,1)} %copy-done.29, ...), kind=kOutput, calls=%fused_computation.25 | convolution fusion | flops 1481670656 | bytes 11731968 | tf_op jit(solution)/shard_map/dot_general | solution.py:185
  138.1 2.1 slice.330
  140.7 1.2 constant_dynamic-update-slice_fusion.8
  141.9 2.1 constant_dynamic-update-slice_fusion.3
  144.0 2.1 fusion.142
  146.1 5.1 %fusion.7 = f32[384,704]{0,1:T(8,128)} fusion(bf16[384,2048]{1,0:T(8,128)(2,1)} %constant_dynamic-update-slice_fusion.3, bf16[1,2,2048,704]{2,3,1,0:T(8,128)(2,1)} %param.36), kind=kOutput, calls=%fused_computation.14 | convolution fusion | flops 1107296256 | bytes 5537792 | tf_op jit(solution)/shard_map/dot_general | solution.py:183
  151.9 2.7 %fusion.5 = f32[384,704]{0,1:T(8,128)} fusion(bf16[384,2048]{1,0:T(8,128)(2,1)S(1)} %constant_dynamic-update-slice_fusion.7, bf16[1,2,2048,704]{2,3,1,0:T(8,128)(2,1)S(1)} %bitcast.224), kind=kOutput, calls=%fused_computation.12 | convolution fusion | flops 1107296256 | bytes 5537792 | tf_op jit(solution)/shard_map/dot_general | solution.py:183
  155.2 7.5 %convolution_multiply_fusion = f32[384,2048]{1,0:T(8,128)} fusion(bf16[1,704,2048]{2,1,0:T(8,128)(2,1)S(1)} %copy-done, f32[384]{0:T(512)S(1)} %fusion.120, f32[384,704]{0,1:T(8,128)} %fusion.5, bf16[384,2048]{1,0:T(8,128)(2,1)} %copy-done.5, bf16[1,2,2048,704]{2,3,1,0:T(8,128)(2,1)} %param.36), kind=kOutput, calls=%fused_computation.6 | convolution fusion | flops 2217000960 | bytes 11568640 | tf_op jit(solution)/shard_map/dot_general | solution.py:185
  162.7 2.4 %slice.328 = bf16[192,2048]{1,0:T(8,128)(2,1)} slice(f32[384,2048]{1,0:T(8,128)} %convolution_multiply_fusion), slice={[192:384], [0:2048]} | slice | bytes 1572864 | tf_op jit(solution)/shard_map/slice | solution.py:205
  165.6 0.7 fusion.119
  166.3 7.3 %convolution_multiply_fusion.1 = f32[384,2048]{1,0:T(8,128)} fusion(bf16[1,704,2048]{2,1,0:T(8,128)(2,1)S(1)} %copy-done, f32[384]{0:T(512)S(1)} %fusion.119, f32[384,704]{0,1:T(8,128)} %fusion.7, bf16[384,2048]{1,0:T(8,128)(2,1)} %constant_dynamic-update-slice_fusion.3, bf16[1,2,2048,704]{2,3,1,0:T(8,128)(2,1)} %param.36), kind=kOutput, calls=%fused_computation.7 | convolution fusion | flops 2217000960 | bytes 11568640 | tf_op jit(solution)/shard_map/dot_general | solution.py:185
  173.6 1.7 slice.329
  175.5 1.3 add_convert_fusion.1
  176.9 1.1 collective-permute-start.18
  177.9 1.2 convert_add_fusion
  179.1 1.1 collective-permute-start.9
  180.3 17.0 %collective-permute-done.18 = bf16[3,64,2048]{2,1,0:T(8,128)(2,1)S(1)} collective-permute-done((bf16[3,64,2048]{2,1,0:T(8,128)(2,1)S(1)}, bf16[3,64,2048]{2,1,0:T(8,128)(2,1)S(1)}, u32[]{:S(2)}, u32[]{:S(2)}) %collective-permute-start.18) | collective-permute-done | bytes 786464 | tf_op jit(solution)/shard_map/ppermute | solution.py:62
  197.8 4.1 %collective-permute-start.19 = (bf16[64,2048]{1,0:T(8,128)(2,1)S(1)}, bf16[64,2048]{1,0:T(8,128)(2,1)S(1)}, u32[]{:S(2)}, u32[]{:S(2)}) collective-permute-start(bf16[64,2048]{1,0:T(8,128)(2,1)S(1)} %get-tuple-element.10), channel_id=1, source_target_pairs={{0,8},{8,0},{16,24},{24,16},{1,9},{9,1},{17,25},{25,17},{2,10},{10... | collective-permute-start | bytes 786440 | tf_op jit(solution)/shard_map/ppermute | solution.py:62
  201.9 2.4 %collective-permute-start.21 = (bf16[64,2048]{1,0:T(8,128)(2,1)S(1)}, bf16[64,2048]{1,0:T(8,128)(2,1)S(1)}, u32[]{:S(2)}, u32[]{:S(2)}) collective-permute-start(bf16[64,2048]{1,0:T(8,128)(2,1)S(1)} %get-tuple-element.11), channel_id=1, source_target_pairs={{0,24},{8,16},{16,8},{24,0},{1,25},{9,17},{17,9},{25,1},{2,26},{10... | collective-permute-start | bytes 786440 | tf_op jit(solution)/shard_map/ppermute | solution.py:62
  204.3 6.9 %collective-permute-done.19 = bf16[64,2048]{1,0:T(8,128)(2,1)S(1)} collective-permute-done((bf16[64,2048]{1,0:T(8,128)(2,1)S(1)}, bf16[64,2048]{1,0:T(8,128)(2,1)S(1)}, u32[]{:S(2)}, u32[]{:S(2)}) %collective-permute-start.19) | collective-permute-done | bytes 262176 | tf_op jit(solution)/shard_map/ppermute | solution.py:62
  211.2 12.0 %collective-permute-done.20 = bf16[64,2048]{1,0:T(8,128)(2,1)S(1)} collective-permute-done((bf16[64,2048]{1,0:T(8,128)(2,1)S(1)}, bf16[64,2048]{1,0:T(8,128)(2,1)S(1)}, u32[]{:S(2)}, u32[]{:S(2)}) %collective-permute-start.20) | collective-permute-done | bytes 262176 | tf_op jit(solution)/shard_map/ppermute | solution.py:62
  223.4 1.6 collective-permute-start.22
  226.5 0.8 fusion.55
  227.3 2.6 %collective-permute-done.22 = bf16[64,2048]{1,0:T(8,128)(2,1)S(1)} collective-permute-done((bf16[64,2048]{1,0:T(8,128)(2,1)S(1)}, bf16[64,2048]{1,0:T(8,128)(2,1)S(1)}, u32[]{:S(2)}, u32[]{:S(2)}) %collective-permute-start.22) | collective-permute-done | bytes 262176 | tf_op jit(solution)/shard_map/ppermute | solution.py:62
  229.9 0.9 add_convert_fusion.2
  (163 shorter events, 19.8 us)
Async XLA Ops:
  0.6 129.8 %copy-start = (bf16[1,704,2048]{2,1,0:T(8,128)(2,1)S(1)}, bf16[1,704,2048]{2,1,0:T(8,128)(2,1)}, u32[]{:S(2)}) copy-start(bf16[1,704,2048]{2,1,0:T(8,128)(2,1)} %param.37) | copy-start | bytes 8650756
  0.6 8.6 %copy-start.1 = (s32[4]{0:T(128)S(1)}, s32[4]{0:T(128)}, u32[]{:S(2)}) copy-start(s32[4]{0:T(128)} %param.21) | copy-start | bytes 52
  3.0 20.1 %copy-start.19 = (bf16[64,2048]{1,0:T(8,128)(2,1)}, bf16[64,2048]{1,0:T(8,128)(2,1)S(1)}, u32[]{:S(2)}) copy-start(bf16[64,2048]{1,0:T(8,128)(2,1)S(1)} %fusion.76) | copy-start | bytes 786436
  3.0 18.2 %collective-permute-start.1 = (bf16[64,2048]{1,0:T(8,128)(2,1)S(1)}, bf16[64,2048]{1,0:T(8,128)(2,1)}, u32[]{:S(2)}, u32[]{:S(2)}) collective-permute-start(bf16[64,2048]{1,0:T(8,128)(2,1)S(1)} %fusion.76), channel_id=1, source_target_pairs={{0,4},{2,6},{4,0},{6,2},{1,5},{3,7},{5,1},{7,3},{8,12},{10,14},{12... | collective-permute-start | bytes 786440 | tf_op jit(solution)/shard_map/ppermute | solution.py:62
  6.1 16.3 %collective-permute-start = (bf16[64,2048]{1,0:T(8,128)(2,1)S(1)}, bf16[64,2048]{1,0:T(8,128)(2,1)}, u32[]{:S(2)}, u32[]{:S(2)}) collective-permute-start(bf16[64,2048]{1,0:T(8,128)(2,1)S(1)} %fusion.76), channel_id=1, source_target_pairs={{0,2},{2,0},{4,6},{6,4},{1,3},{3,1},{5,7},{7,5},{8,10},{10,8},{12,... | collective-permute-start | bytes 786440 | tf_op jit(solution)/shard_map/ppermute | solution.py:62
  6.1 12.1 %copy-start.24 = (pred[4]{0:T(512)(128)(4,1)}, pred[4]{0:T(512)(128)(4,1)S(1)}, u32[]{:S(2)}) copy-start(pred[4]{0:T(512)(128)(4,1)S(1)} %compare_and_fusion.1) | copy-start | bytes 16
  6.1 7.3 %copy-start.21 = (s32[1024]{0:T(1024)}, s32[1024]{0:T(1024)S(1)}, u32[]{:S(2)}) copy-start(s32[1024]{0:T(1024)S(1)} %pad_clamp_fusion.1) | copy-start | bytes 12292
  17.4 6.4 %copy-start.28 = (bf16[2048,384]{1,0:T(8,128)(2,1)S(1)}, bf16[2048,384]{1,0:T(8,128)(2,1)}, u32[]{:S(2)}) copy-start(bf16[2048,384]{1,0:T(8,128)(2,1)} %param.26) | copy-start | bytes 4718596
  21.3 1.9 collective-permute-start.2
  23.2 0.7 copy-start.30
  25.8 3.2 %copy-start.11 = (bf16[4,64,2,192]{3,2,1,0:T(2,128)(2,1)}, bf16[4,64,2,192]{3,2,1,0:T(2,128)(2,1)S(1)}, u32[]{:S(2)}) copy-start(bf16[4,64,2,192]{3,2,1,0:T(2,128)(2,1)S(1)} %reshape.312) | copy-start | bytes 589828
  25.9 3.8 %copy-start.26 = (f32[512]{0:T(512)S(1)}, f32[512]{0:T(512)}, u32[]{:S(2)}) copy-start(f32[512]{0:T(512)} %param.28) | copy-start | bytes 6148
  28.9 1.0 copy-start.16
  29.0 1.6 slice-start.3
  29.0 3.4 %copy-start.2 = (bf16[4,384,576]{2,1,0:T(8,128)(2,1)S(1)}, bf16[4,384,576]{2,1,0:T(8,128)(2,1)}, u32[]{:S(2)}) copy-start(bf16[4,384,576]{2,1,0:T(8,128)(2,1)} %broadcast_select_fusion) | copy-start | bytes 5308420
  29.7 4.3 %copy-start.12 = (bf16[4,64,32]{2,1,0:T(8,128)(2,1)}, bf16[4,64,32]{2,1,0:T(8,128)(2,1)S(1)}, u32[]{:S(2)}) copy-start(bf16[4,64,32]{2,1,0:T(8,128)(2,1)S(1)} %get-tuple-element.33) | copy-start | bytes 49156
  29.7 4.3 %copy-start.14 = (bf16[4,64,32]{2,1,0:T(8,128)(2,1)}, bf16[4,64,32]{2,1,0:T(8,128)(2,1)S(1)}, u32[]{:S(2)}) copy-start(bf16[4,64,32]{2,1,0:T(8,128)(2,1)S(1)} %get-tuple-element.34) | copy-start | bytes 49156
  30.5 3.6 %copy-start.7 = (bf16[4,64,512]{2,1,0:T(8,128)(2,1)}, bf16[4,64,512]{2,1,0:T(8,128)(2,1)S(1)}, u32[]{:S(2)}) copy-start(bf16[4,64,512]{2,1,0:T(8,128)(2,1)S(1)} %multiply_convert_fusion.6) | copy-start | bytes 786436
  32.4 1.7 copy-start.20
  40.6 4.3 %copy-start.25 = (s32[64,6]{0,1:T(8,128)S(1)}, s32[64,6]{0,1:T(8,128)}, u32[]{:S(2)}) copy-start(s32[64,6]{0,1:T(8,128)} %param.23) | copy-start | bytes 4612
  42.3 1.4 copy-start.4
  44.5 22.0 %collective-permute-start.3 = (bf16[2,64,2048]{2,1,0:T(8,128)(2,1)}, bf16[2,64,2048]{2,1,0:T(8,128)(2,1)}, u32[]{:S(2)}, u32[]{:S(2)}) collective-permute-start(bf16[2,64,2048]{2,1,0:T(8,128)(2,1)} %fusion.77), channel_id=1, source_target_pairs={{0,2},{2,0},{4,6},{6,4},{1,3},{3,1},{5,7},{7,5},{8,10},{10,8},{12,... | collective-permute-start | bytes 1572872 | tf_op jit(solution)/shard_map/ppermute | solution.py:62
  66.5 20.2 %copy-start.3 = (bf16[64,2048]{1,0:T(8,128)(2,1)S(1)}, bf16[64,2048]{1,0:T(8,128)(2,1)}, u32[]{:S(2)}) copy-start(bf16[64,2048]{1,0:T(8,128)(2,1)} %param.19) | copy-start | bytes 786436
  68.0 1.0 copy-start.6
  69.0 8.7 %collective-permute-start.4 = (bf16[64,2048]{1,0:T(8,128)(2,1)S(1)}, bf16[64,2048]{1,0:T(8,128)(2,1)}, u32[]{:S(2)}, u32[]{:S(2)}) collective-permute-start(bf16[64,2048]{1,0:T(8,128)(2,1)S(1)} %fusion.92), channel_id=1, source_target_pairs={{0,4},{2,6},{4,0},{6,2},{1,5},{3,7},{5,1},{7,3},{8,12},{10,14},{12... | collective-permute-start | bytes 786440 | tf_op jit(solution)/shard_map/ppermute | solution.py:62
  78.9 7.8 %collective-permute-start.5 = (bf16[64,2048]{1,0:T(8,128)(2,1)S(1)}, bf16[64,2048]{1,0:T(8,128)(2,1)S(1)}, u32[]{:S(2)}, u32[]{:S(2)}) collective-permute-start(bf16[64,2048]{1,0:T(8,128)(2,1)S(1)} %fusion.84), channel_id=1, source_target_pairs={{0,1},{1,0},{2,3},{3,2},{4,5},{5,4},{6,7},{7,6},{8,9},{9,8},{10,11... | collective-permute-start | bytes 786440 | tf_op jit(solution)/shard_map/ppermute | solution.py:62
  86.7 0.7 copy-start.9
  88.9 7.2 %collective-permute-start.6 = (bf16[64,2048]{1,0:T(8,128)(2,1)}, bf16[64,2048]{1,0:T(8,128)(2,1)}, u32[]{:S(2)}, u32[]{:S(2)}) collective-permute-start(bf16[64,2048]{1,0:T(8,128)(2,1)} %multiply_convert_fusion.5), channel_id=1, source_target_pairs={{0,4},{2,6},{4,0},{6,2},{1,5},{3,7},{5,1},{7,3},{8,12},{10,14},{12... | collective-permute-start | bytes 786440 | tf_op jit(solution)/shard_map/ppermute | solution.py:62
  89.6 8.5 %collective-permute-start.10 = (bf16[64,2048]{1,0:T(8,128)(2,1)}, bf16[64,2048]{1,0:T(8,128)(2,1)}, u32[]{:S(2)}, u32[]{:S(2)}) collective-permute-start(bf16[64,2048]{1,0:T(8,128)(2,1)} %multiply_convert_fusion.5), channel_id=1, source_target_pairs={{0,8},{8,0},{16,24},{24,16},{1,9},{9,1},{17,25},{25,17},{2,10},{10... | collective-permute-start | bytes 786440 | tf_op jit(solution)/shard_map/ppermute | solution.py:62
  91.6 23.4 %copy-start.17 = (bf16[2048,16]{0,1:T(8,128)(2,1)S(1)}, bf16[2048,16]{0,1:T(8,128)(2,1)}, u32[]{:S(2)}) copy-start(bf16[2048,16]{0,1:T(8,128)(2,1)} %param.33) | copy-start | bytes 196612
  91.6 20.6 %collective-permute-start.11 = (bf16[64,2048]{1,0:T(8,128)(2,1)}, bf16[64,2048]{1,0:T(8,128)(2,1)S(1)}, u32[]{:S(2)}, u32[]{:S(2)}) collective-permute-start(bf16[64,2048]{1,0:T(8,128)(2,1)} %multiply_convert_fusion.5), channel_id=1, source_target_pairs={{0,16},{8,24},{16,0},{24,8},{1,17},{9,25},{17,1},{25,9},{2,18},{10... | collective-permute-start | bytes 786440 | tf_op jit(solution)/shard_map/ppermute | solution.py:62
  91.6 21.4 %collective-permute-start.12 = (bf16[64,2048]{1,0:T(8,128)(2,1)}, bf16[64,2048]{1,0:T(8,128)(2,1)S(1)}, u32[]{:S(2)}, u32[]{:S(2)}) collective-permute-start(bf16[64,2048]{1,0:T(8,128)(2,1)} %multiply_convert_fusion.5), channel_id=1, source_target_pairs={{0,24},{8,16},{16,8},{24,0},{1,25},{9,17},{17,9},{25,1},{2,26},{10... | collective-permute-start | bytes 786440 | tf_op jit(solution)/shard_map/ppermute | solution.py:62
  97.2 17.8 %collective-permute-start.7 = (bf16[128,2048]{1,0:T(8,128)(2,1)S(1)}, bf16[128,2048]{1,0:T(8,128)(2,1)S(1)}, u32[]{:S(2)}, u32[]{:S(2)}) collective-permute-start(bf16[128,2048]{1,0:T(8,128)(2,1)S(1)} %pad_maximum_fusion.2), channel_id=1, source_target_pairs={{0,2},{2,0},{4,6},{6,4},{1,3},{3,1},{5,7},{7,5},{8,10},{10,8},{12,... | collective-permute-start | bytes 1572872 | tf_op jit(solution)/shard_map/ppermute | solution.py:62
  113.9 26.8 %collective-permute-start.15 = (bf16[192,2048]{1,0:T(8,128)(2,1)}, bf16[192,2048]{1,0:T(8,128)(2,1)}, u32[]{:S(2)}, u32[]{:S(2)}) collective-permute-start(bf16[192,2048]{1,0:T(8,128)(2,1)} %get-tuple-element.18), channel_id=1, source_target_pairs={{0,4},{2,6},{4,0},{6,2},{1,5},{3,7},{5,1},{7,3},{8,12},{10,14},{12... | collective-permute-start | bytes 2359304 | tf_op jit(solution)/shard_map/ppermute | solution.py:62
  114.9 27.0 %collective-permute-start.13 = (bf16[192,2048]{1,0:T(8,128)(2,1)}, bf16[192,2048]{1,0:T(8,128)(2,1)}, u32[]{:S(2)}, u32[]{:S(2)}) collective-permute-start(bf16[192,2048]{1,0:T(8,128)(2,1)} %get-tuple-element.18), channel_id=1, source_target_pairs={{0,2},{2,0},{4,6},{6,4},{1,3},{3,1},{5,7},{7,5},{8,10},{10,8},{12,... | collective-permute-start | bytes 2359304 | tf_op jit(solution)/shard_map/ppermute | solution.py:62
  114.9 6.2 %copy-start.29 = (bf16[128,2048]{1,0:T(8,128)(2,1)}, bf16[128,2048]{1,0:T(8,128)(2,1)S(1)}, u32[]{:S(2)}) copy-start(bf16[128,2048]{1,0:T(8,128)(2,1)S(1)} %collective-permute-done.7) | copy-start | bytes 1572868
  117.2 3.9 %copy-start.27 = (bf16[2,2048,352]{1,2,0:T(8,128)(2,1)S(1)}, bf16[2,2048,352]{1,2,0:T(8,128)(2,1)}, u32[]{:S(2)}) copy-start(bf16[2,2048,352]{1,2,0:T(8,128)(2,1)} %param.34) | copy-start | bytes 8650756
  140.2 3.9 %copy-start.18 = (bf16[2048,16]{0,1:T(8,128)(2,1)S(1)}, bf16[2048,16]{0,1:T(8,128)(2,1)}, u32[]{:S(2)}) copy-start(bf16[2048,16]{0,1:T(8,128)(2,1)} %param.33) | copy-start | bytes 196612
  140.2 37.7 %collective-permute-start.8 = (bf16[2,64,2048]{2,1,0:T(8,128)(2,1)}, bf16[2,64,2048]{2,1,0:T(8,128)(2,1)}, u32[]{:S(2)}, u32[]{:S(2)}) collective-permute-start(bf16[2,64,2048]{2,1,0:T(8,128)(2,1)} %bitcast.33), channel_id=1, source_target_pairs={{0,2},{2,0},{4,6},{6,4},{1,3},{3,1},{5,7},{7,5},{8,10},{10,8},{12,... | collective-permute-start | bytes 1572872 | tf_op jit(solution)/shard_map/ppermute | solution.py:62
  140.7 10.5 %collective-permute-start.16 = (bf16[192,2048]{1,0:T(8,128)(2,1)}, bf16[192,2048]{1,0:T(8,128)(2,1)S(1)}, u32[]{:S(2)}, u32[]{:S(2)}) collective-permute-start(bf16[192,2048]{1,0:T(8,128)(2,1)} %collective-permute-done.15), channel_id=1, source_target_pairs={{0,2},{2,0},{4,6},{6,4},{1,3},{3,1},{5,7},{7,5},{8,10},{10,8},{12,... | collective-permute-start | bytes 2359304 | tf_op jit(solution)/shard_map/ppermute | solution.py:62
  144.0 7.8 %slice-start.4 = ((s8[5767168]{0:T(1024)(128)(4,1)}), s8[4194304]{0:T(1024)(128)(4,1)S(1)}, s32[]{:S(2)}) async-start(s8[5767168]{0:T(1024)(128)(4,1)} %bitcast.223), calls=%async_computation.4 | async-start | bytes 8388608
  146.1 5.7 %slice-start.5 = ((s8[5767168]{0:T(1024)(128)(4,1)}), s8[1572864]{0:T(1024)(128)(4,1)S(1)}, s32[]{:S(2)}) async-start(s8[5767168]{0:T(1024)(128)(4,1)} %bitcast.223), calls=%async_computation.5 | async-start | bytes 3145728
  151.3 3.3 %copy-start.5 = (bf16[384,2048]{1,0:T(8,128)(2,1)}, bf16[384,2048]{1,0:T(8,128)(2,1)S(1)}, u32[]{:S(2)}) copy-start(bf16[384,2048]{1,0:T(8,128)(2,1)S(1)} %constant_dynamic-update-slice_fusion.7) | copy-start | bytes 4718596
  151.9 3.3 %copy-start.23 = (f32[384,1]{0,1:T(1,128)S(1)}, f32[384,1]{0,1:T(1,128)}, u32[]{:S(2)}) copy-start(f32[384,1]{0,1:T(1,128)} %reshape.315) | copy-start | bytes 4612
  162.7 2.9 %copy-start.22 = (f32[384,1]{0,1:T(1,128)S(1)}, f32[384,1]{0,1:T(1,128)}, u32[]{:S(2)}) copy-start(f32[384,1]{0,1:T(1,128)} %reshape.314) | copy-start | bytes 4612
  165.1 10.3 %collective-permute-start.17 = (bf16[3,64,2048]{2,1,0:T(8,128)(2,1)}, bf16[3,64,2048]{2,1,0:T(8,128)(2,1)}, u32[]{:S(2)}, u32[]{:S(2)}) collective-permute-start(bf16[3,64,2048]{2,1,0:T(8,128)(2,1)} %bitcast.43), channel_id=1, source_target_pairs={{0,2},{2,0},{4,6},{6,4},{1,3},{3,1},{5,7},{7,5},{8,10},{10,8},{12,... | collective-permute-start | bytes 2359304 | tf_op jit(solution)/shard_map/ppermute | solution.py:62
  173.6 1.9 slice-start
  173.6 4.3 %slice-start.2 = ((f32[256,2048]{1,0:T(8,128)}), f32[128,2048]{1,0:T(8,128)S(1)}, s32[]{:S(2)}) async-start(f32[256,2048]{1,0:T(8,128)} %fusion.20), calls=%async_computation.2 | async-start | bytes 2097152 | tf_op jit(solution)/shard_map/slice | solution.py:203
  175.3 5.0 %collective-permute-start.14 = (bf16[3,64,2048]{2,1,0:T(8,128)(2,1)S(1)}, bf16[3,64,2048]{2,1,0:T(8,128)(2,1)S(1)}, u32[]{:S(2)}, u32[]{:S(2)}) collective-permute-start(bf16[3,64,2048]{2,1,0:T(8,128)(2,1)S(1)} %bitcast.219), channel_id=1, source_target_pairs={{0,2},{2,0},{4,6},{6,4},{1,3},{3,1},{5,7},{7,5},{8,10},{10,8},{12,... | collective-permute-start | bytes 2359304 | tf_op jit(solution)/shard_map/ppermute | solution.py:62
  176.9 20.4 %collective-permute-start.18 = (bf16[3,64,2048]{2,1,0:T(8,128)(2,1)S(1)}, bf16[3,64,2048]{2,1,0:T(8,128)(2,1)S(1)}, u32[]{:S(2)}, u32[]{:S(2)}) collective-permute-start(bf16[3,64,2048]{2,1,0:T(8,128)(2,1)S(1)} %add_convert_fusion.1), channel_id=1, source_target_pairs={{0,4},{2,6},{4,0},{6,2},{1,5},{3,7},{5,1},{7,3},{8,12},{10,14},{12... | collective-permute-start | bytes 2359304 | tf_op jit(solution)/shard_map/ppermute | solution.py:62
  179.1 18.2 %slice-start.1 = ((f32[384,2048]{1,0:T(8,128)}), f32[192,2048]{1,0:T(8,128)S(1)}, s32[]{:S(2)}) async-start(f32[384,2048]{1,0:T(8,128)} %convolution_multiply_fusion.1), calls=%async_computation.1 | async-start | bytes 3145728 | tf_op jit(solution)/shard_map/slice | solution.py:204
  179.1 25.2 %collective-permute-start.9 = (bf16[64,2048]{1,0:T(8,128)(2,1)S(1)}, bf16[64,2048]{1,0:T(8,128)(2,1)S(1)}, u32[]{:S(2)}, u32[]{:S(2)}) collective-permute-start(bf16[64,2048]{1,0:T(8,128)(2,1)S(1)} %fusion.93), channel_id=1, source_target_pairs={{0,4},{2,6},{4,0},{6,2},{1,5},{3,7},{5,1},{7,3},{8,12},{10,14},{12... | collective-permute-start | bytes 786440 | tf_op jit(solution)/shard_map/ppermute | solution.py:62
  197.6 28.8 %copy-start.8 = (bf16[4,64,512]{2,1,0:T(8,128)(2,1)S(1)}, bf16[4,64,512]{2,1,0:T(8,128)(2,1)}, u32[]{:S(2)}) copy-start(bf16[4,64,512]{2,1,0:T(8,128)(2,1)} %copy-done.7) | copy-start | bytes 786436
  197.7 28.8 %copy-start.13 = (bf16[4,64,32]{2,1,0:T(8,128)(2,1)S(1)}, bf16[4,64,32]{2,1,0:T(8,128)(2,1)}, u32[]{:S(2)}) copy-start(bf16[4,64,32]{2,1,0:T(8,128)(2,1)} %copy-done.12) | copy-start | bytes 49156
  197.7 28.8 %copy-start.15 = (bf16[4,64,32]{2,1,0:T(8,128)(2,1)S(1)}, bf16[4,64,32]{2,1,0:T(8,128)(2,1)}, u32[]{:S(2)}) copy-start(bf16[4,64,32]{2,1,0:T(8,128)(2,1)} %copy-done.14) | copy-start | bytes 49156
  197.7 32.2 %copy-start.10 = (bf16[64,2048]{1,0:T(8,128)(2,1)S(1)}, bf16[64,2048]{1,0:T(8,128)(2,1)}, u32[]{:S(2)}) copy-start(bf16[64,2048]{1,0:T(8,128)(2,1)} %copy-done.9) | copy-start | bytes 786436
  197.8 13.5 %collective-permute-start.19 = (bf16[64,2048]{1,0:T(8,128)(2,1)S(1)}, bf16[64,2048]{1,0:T(8,128)(2,1)S(1)}, u32[]{:S(2)}, u32[]{:S(2)}) collective-permute-start(bf16[64,2048]{1,0:T(8,128)(2,1)S(1)} %get-tuple-element.10), channel_id=1, source_target_pairs={{0,8},{8,0},{16,24},{24,16},{1,9},{9,1},{17,25},{25,17},{2,10},{10... | collective-permute-start | bytes 786440 | tf_op jit(solution)/shard_map/ppermute | solution.py:62
  201.9 21.4 %collective-permute-start.20 = (bf16[64,2048]{1,0:T(8,128)(2,1)S(1)}, bf16[64,2048]{1,0:T(8,128)(2,1)S(1)}, u32[]{:S(2)}, u32[]{:S(2)}) collective-permute-start(bf16[64,2048]{1,0:T(8,128)(2,1)S(1)} %get-tuple-element.12), channel_id=1, source_target_pairs={{0,16},{8,24},{16,0},{24,8},{1,17},{9,25},{17,1},{25,9},{2,18},{10... | collective-permute-start | bytes 786440 | tf_op jit(solution)/shard_map/ppermute | solution.py:62
  201.9 21.4 %collective-permute-start.21 = (bf16[64,2048]{1,0:T(8,128)(2,1)S(1)}, bf16[64,2048]{1,0:T(8,128)(2,1)S(1)}, u32[]{:S(2)}, u32[]{:S(2)}) collective-permute-start(bf16[64,2048]{1,0:T(8,128)(2,1)S(1)} %get-tuple-element.11), channel_id=1, source_target_pairs={{0,24},{8,16},{16,8},{24,0},{1,25},{9,17},{17,9},{25,1},{2,26},{10... | collective-permute-start | bytes 786440 | tf_op jit(solution)/shard_map/ppermute | solution.py:62
  223.4 6.4 %collective-permute-start.22 = (bf16[64,2048]{1,0:T(8,128)(2,1)S(1)}, bf16[64,2048]{1,0:T(8,128)(2,1)S(1)}, u32[]{:S(2)}, u32[]{:S(2)}) collective-permute-start(bf16[64,2048]{1,0:T(8,128)(2,1)S(1)} %fusion.82), channel_id=1, source_target_pairs={{0,1},{1,0},{2,3},{3,2},{4,5},{5,4},{6,7},{7,6},{8,9},{9,8},{10,11... | collective-permute-start | bytes 786440 | tf_op jit(solution)/shard_map/ppermute | solution.py:62

commit v2 on v1

--- a/solution.py
+++ b/solution.py
@@ -4,6 +4,8 @@
 import jax
 import jax.numpy as jnp
 from jax import lax
+from jax.experimental import pallas as pl
+from jax.experimental.pallas import tpu as pltpu
 from jax.sharding import PartitionSpec as P
 
 NOPE = 128
@@ -56,6 +58,134 @@
         )
     depths = jnp.sum(closure, axis=-1) - 1.0
     return (closure, depths)
+
+
+STEPS = 4
+ROUTE_COLUMNS = 512
+
+
+def transposed_dot(values, weight):
+    return lax.dot_general(
+        values, weight, (((1,), (1,)), ((), ())), preferred_element_type=jnp.float32
+    )
+
+
+def expert_kernel(shared, *refs):
+    rows, refs = refs[:4], refs[4:]
+    marks_ref, router_ref, gate_up_ref, down_ref = refs[:4]
+    refs = refs[4:]
+    if shared:
+        shared_gate_up_ref, shared_down_ref = refs[:2]
+        refs = refs[2:]
+    keep_ref, send_ref, logits, gate, upper, inner, share = refs[:7]
+    if shared:
+        shared_gate, shared_upper, shared_inner = refs[7:]
+    step = pl.program_id(0)
+
+    @pl.when(step < STEPS)
+    def _():
+        tile = jnp.concatenate([ref[...] for ref in rows], axis=0)
+        first = step == 0
+
+        def add(total, term):
+            total[...] = jnp.where(first, 0.0, total[...]) + term
+
+        add(logits, transposed_dot(tile, router_ref[...]))
+        add(gate, transposed_dot(tile, gate_up_ref[0]))
+        add(upper, transposed_dot(tile, gate_up_ref[1]))
+        if shared:
+            add(shared_gate, transposed_dot(tile, shared_gate_up_ref[0]))
+            add(shared_upper, transposed_dot(tile, shared_gate_up_ref[1]))
+
+    @pl.when(step == STEPS - 1)
+    def _():
+        raised = jnp.exp(logits[...] - jnp.max(logits[...], axis=-1, keepdims=True))
+        router = raised / jnp.sum(raised, axis=-1, keepdims=True)
+        share[...] = jnp.sum(router * marks_ref[...], axis=-1, keepdims=True)
+        inner[...] = (jax.nn.silu(gate[...]) * upper[...]).astype(jnp.bfloat16)
+        if shared:
+            shared_inner[...] = (jax.nn.silu(shared_gate[...]) * shared_upper[...]).astype(
+                jnp.bfloat16
+            )
+
+    @pl.when(step >= STEPS)
+    def _():
+        result = share[...] * jnp.dot(
+            inner[...], down_ref[...], preferred_element_type=jnp.float32
+        )
+        if shared:
+            result = result + jnp.dot(
+                shared_inner[...], shared_down_ref[...], preferred_element_type=jnp.float32
+            )
+        kept = keep_ref.shape[0] * keep_ref.shape[1]
+        keep_ref[...] = result[:kept].reshape(keep_ref.shape)
+        send_ref[...] = result[kept:].astype(jnp.bfloat16).reshape(send_ref.shape)
+
+
+def expert_part(blocks, marks, router, gate_up, down, shared_gate_up=None, shared_down=None):
+    shared = shared_gate_up is not None
+    tok_rows, width = blocks[0].shape
+    total_rows = 4 * tok_rows
+    tile = width // STEPS
+    hidden_units = gate_up.shape[1]
+    experts = router.shape[0]
+
+    def early(step):
+        return jnp.minimum(step, STEPS - 1)
+
+    def late(step):
+        return jnp.maximum(step - STEPS, 0)
+
+    in_specs = [pl.BlockSpec((tok_rows, tile), lambda i: (0, early(i)))] * 4 + [
+        pl.BlockSpec((total_rows, experts), lambda i: (0, 0)),
+        pl.BlockSpec((experts, tile), lambda i: (0, early(i))),
+        pl.BlockSpec((2, hidden_units, tile), lambda i: (0, 0, early(i))),
+        pl.BlockSpec((hidden_units, tile), lambda i: (0, late(i))),
+    ]
+    operands = [*blocks, marks, router, gate_up, down]
+    scratch = [
+        pltpu.VMEM((total_rows, experts), jnp.float32),
+        pltpu.VMEM((total_rows, hidden_units), jnp.float32),
+        pltpu.VMEM((total_rows, hidden_units), jnp.float32),
+        pltpu.VMEM((total_rows, hidden_units), jnp.bfloat16),
+        pltpu.VMEM((total_rows, 1), jnp.float32),
+    ]
+    units = hidden_units
+    if shared:
+        shared_units = shared_gate_up.shape[1]
+        units += shared_units
+        in_specs += [
+            pl.BlockSpec((2, shared_units, tile), lambda i: (0, 0, early(i))),
+            pl.BlockSpec((shared_units, tile), lambda i: (0, late(i))),
+        ]
+        operands += [shared_gate_up, shared_down]
+        scratch += [
+            pltpu.VMEM((total_rows, shared_units), jnp.float32),
+            pltpu.VMEM((total_rows, shared_units), jnp.float32),
+            pltpu.VMEM((total_rows, shared_units), jnp.bfloat16),
+        ]
+    out_block = (2, tok_rows, tile)
+    return pl.pallas_call(
+        functools.partial(expert_kernel, shared),
+        out_shape=(
+            jax.ShapeDtypeStruct((2, tok_rows, width), jnp.float32),
+            jax.ShapeDtypeStruct((2, tok_rows, width), jnp.bfloat16),
+        ),
+        grid=(2 * STEPS,),
+        in_specs=in_specs,
+        out_specs=(
+            pl.BlockSpec(out_block, lambda i: (0, 0, late(i))),
+            pl.BlockSpec(out_block, lambda i: (0, 0, late(i))),
+        ),
+        scratch_shapes=scratch,
+        compiler_params=pltpu.CompilerParams(vmem_limit_bytes=24 << 20),
+        cost_estimate=pl.CostEstimate(
+            flops=6 * total_rows * width * units,
+            bytes_accessed=6 * width * units + 8 * total_rows * width,
+            transcendentals=total_rows * units,
+        ),
+        name="experts",
+    )(*operands)
 
 
 def swap(values, axis, size, bits):
@@ -94,7 +224,10 @@
     half = n_row // 2
     bf16 = jnp.bfloat16
 
-    all_routes = lax.all_gather(routes, ("req", "row"), axis=0, tiled=False)
+    experts = router_weight.shape[1]
+    named = (routes[:, :, None] == jnp.arange(experts, dtype=jnp.int32)).any(axis=1).astype(bf16)
+    named = jnp.tile(named, (1, ROUTE_COLUMNS // experts))
+    named = lax.all_gather(named, ("req", "row"), axis=0, tiled=True)[:, :experts]
 
     normed = rms_scale(hidden.astype(jnp.float32), input_gain).astype(bf16)
     far = swap(normed, "row", n_row, 2)
@@ -160,54 +293,38 @@
     residual = hidden.astype(jnp.float32) + partial
     post_normed = rms_scale(residual, post_gain).astype(bf16)
 
-    far_own = swap(post_normed, "row", n_row, 2)
-    across = [swap(post_normed, "req", n_req, s) for s in range(1, n_req)]
-    across = jnp.concatenate(across, axis=0)
-    near_own = swap(jnp.concatenate([post_normed, far_own], axis=0), "row", n_row, 1)
-    own_group = jnp.concatenate([post_normed, far_own, near_own], axis=0)
-    near_across = swap(across, "row", n_row, 1)
-    far_across = swap(across, "row", n_row, 2)
-    near_far = swap(far_across, "row", n_row, 1)
-
-    expert_id = req_index * n_row + row_index
-    named = jnp.any(all_routes == expert_id, axis=-1).astype(jnp.float32).reshape(n_req, n_row, tok_rows)
-    named = jnp.take(named, jnp.arange(n_req, dtype=jnp.int32) ^ req_index, axis=0)
-    named = jnp.take(named, jnp.arange(n_row, dtype=jnp.int32) ^ row_index, axis=1)
-
-    def expert_part(rows, marks):
-        router = jax.nn.softmax(
-            jnp.dot(rows, router_weight, preferred_element_type=jnp.float32), axis=-1
+    own_expert = jnp.arange(experts, dtype=jnp.int32) == req_index * n_row + row_index
+    marks = jnp.where(own_expert, named.astype(jnp.float32), 0.0)
+    marks = marks.reshape(n_req, n_row, tok_rows, experts)
+    marks = jnp.take(marks, jnp.arange(n_req, dtype=jnp.int32) ^ req_index, axis=0)
+    marks = jnp.take(marks, jnp.array([0, 2, 1, 3], jnp.int32) ^ row_index, axis=1)
+    marks = marks.reshape(n_req, n_row * tok_rows, experts)
+    router = router_weight.T
+    gate_up = jnp.swapaxes(expert_gate_up[0], 1, 2)
+    shared_weights = (jnp.swapaxes(shared_gate_up, 1, 2), shared_down)
+
+    distances = [*range(n_req - 1, 0, -1), 0]
+    arrived = {s: swap(post_normed, "req", n_req, s) if s else post_normed for s in distances}
+    total = None
+    for s in [0, *distances[:-1]]:
+        far = swap(arrived[s], "row", n_row, 2)
+        near = swap(arrived[s], "row", n_row, 1)
+        far_near = swap(far, "row", n_row, 1)
+        keep, send = expert_part(
+            (arrived[s], far, near, far_near),
+            marks[s],
+            router,
+            gate_up,
+            expert_down[0],
+            *(() if s else shared_weights),
         )
-        share = lax.dynamic_slice_in_dim(router, expert_id, 1, axis=1) * marks.reshape(-1, 1)
-        gate = jnp.dot(rows, expert_gate_up[0, 0], preferred_element_type=jnp.float32)
-        upper = jnp.dot(rows, expert_gate_up[0, 1], preferred_element_type=jnp.float32)
-        inner = (jax.nn.silu(gate) * upper).astype(bf16)
-        return share * jnp.dot(inner, expert_down[0], preferred_element_type=jnp.float32)
-
-    gate = jnp.dot(own_group, shared_gate_up[0], preferred_element_type=jnp.float32)
-    upper = jnp.dot(own_group, shared_gate_up[1], preferred_element_type=jnp.float32)
-    inner = (jax.nn.silu(gate) * upper).astype(bf16)
-    own_part = jnp.dot(inner, shared_down, preferred_element_type=jnp.float32)
-    own_part = own_part + expert_part(own_group, jnp.stack([named[0, 0], named[0, 2], named[0, 1], named[0, 3]]))
-    own_part = own_part.reshape(2, 2, tok_rows, model_width)
-    lane_part = expert_part(
-        jnp.concatenate([across, near_across], axis=0), jnp.stack([named[1:, 0], named[1:, 1]])
-    ).reshape(2, n_req - 1, tok_rows, model_width)
-    far_part = expert_part(
-        jnp.concatenate([far_across, near_far], axis=0), jnp.stack([named[1:, 2], named[1:, 3]])
-    ).reshape(2, n_req - 1, tok_rows, model_width)
-
-    def fold(keep, send, bits):
-        return keep + swap(send.astype(bf16), "row", n_row, bits).astype(jnp.float32)
-
-    own_part = fold(own_part[0], own_part[1], 1)
-    lane_part = fold(lane_part[0], lane_part[1], 1)
-    far_part = fold(far_part[0], far_part[1], 1)
-    own_sum = fold(own_part[0], own_part[1], 2)
-    lane_sum = fold(lane_part, far_part, 2).astype(bf16)
-    for s in range(1, n_req):
-        own_sum = own_sum + swap(lane_sum[s - 1], "req", n_req, s).astype(jnp.float32)
-    summed_parts = col_sum(own_sum, n_col)
+        from_near = swap(send, "row", n_row, 1).astype(jnp.float32)
+        from_far = swap((keep[1] + from_near[1]).astype(bf16), "row", n_row, 2)
+        part = keep[0] + from_near[0] + from_far.astype(jnp.float32)
+        if s:
+            part = swap(part.astype(bf16), "req", n_req, s).astype(jnp.float32)
+        total = part if total is None else total + part
+    summed_parts = col_sum(total, n_col)
     layer_output = (residual + summed_parts).astype(bf16)
 
     chooser = (jnp.arange(tree_size, dtype=jnp.int32)[None, :] == accepted[:, None]).astype(

time: 233 us -> 210 us (0.901)
  the two profiles are of different devices: /device:TPU:0 before, /device:TPU:8 now
where the time goes in v2:
time: 210 us; the launch traced here: 209 us
  waiting for transfers between devices  74.8 us (36%)
  local copies, waits for them, and re-layouts  30.3 us (14%)
  starting transfers between devices  30.1 us (14%)
  Pallas kernels  27.2 us (13%)
  other arithmetic  15.7 us (7%)
  matrix products  15.6 us (7%)
  between operations  15.4 us (7%)
    ppermute x33, waiting for transfers between devices, swap(): return lax.ppermute(values, axis, [(i, i ^ bits) for i in range(size)])  71.5 us
    ppermute x33, starting transfers between devices, swap(): return lax.ppermute(values, axis, [(i, i ^ bits) for i in range(size)])  30.1 us
    pallas_call x4, Pallas kernels, expert_part(): pl.pallas_call(functools.partial(expert_kernel, shared), out_shape=(jax.S...  27.2 us
    unnamed x64, local copies, waits for them, and re-layouts  12.4 us
    gather x2, local copies, waits for them, and re-layouts, body(): cache = jnp.take(latent_cache, order, axis=0)  7.38 us
  transfers between devices with their start and end apart: 34, of which 14 were waited for; matrix products, arithmetic and copies ran while one was open for 13% of the time, Pallas kernels for 13%

profile of v2, /device:TPU:8, one launch (start us, length us, event | category | flops | bytes accessed | tf_op | source)
XLA Modules:
  0.0 209.2 jit_solution(10739205794057887138)
XLA Ops:
  7.2 1.3 fusion.30
  8.5 1.1 fusion.32
  9.6 1.6 collective-permute-start.1
  11.3 1.2 gather_fusion.2
  14.4 0.6 gather_fusion.1
  15.0 3.5 %gather_fusion = bf16[4,384,576]{1,2,0:T(8,128)(2,1)} fusion(bf16[4,384,576]{1,2,0:T(8,128)(2,1)} %param.21, s32[1024]{0:T(1024)S(1)} %pad_clamp_fusion.2), kind=kCustom, calls=%fused_computation | custom fusion | bytes 3538960 | tf_op jit(solution)/shard_map/jit(_take)/gather | solution.py:239
  18.5 3.9 %copy.71 = bf16[4,384,576]{2,1,0:T(8,128)(2,1)} copy(bf16[4,384,576]{1,2,0:T(8,128)(2,1)} %gather_fusion) | data formatting | bytes 3538944 | tf_op jit(solution)/shard_map/jit(_take)/gather | solution.py:239
  22.6 0.7 pad_add_fusion
  23.3 3.1 %broadcast_select_fusion = bf16[4,384,576]{2,1,0:T(8,128)(2,1)} fusion(bf16[4,384,576]{2,1,0:T(8,128)(2,1)} %copy.71, pred[4]{0:T(512)(128)(4,1)S(1)} %compare_and_fusion.2), kind=kLoop, calls=%fused_computation.9 | loop fusion | flops 884736 | bytes 3538948 | tf_op jit(solution)/shard_map/jit(_take)/select_n | solution.py:239
  27.0 1.1 collective-permute-done.2
  28.0 0.7 copy-done.31
  28.7 1.7 convolution_convert_fusion.1
  30.7 2.0 fusion.64
  34.5 1.6 maximum_maximum_fusion
  36.1 3.6 %fusion.94 = (f32[4,2,64]{2,1,0:T(2,128)S(1)}, f32[4,2,64,448]{3,2,1,0:T(8,128)}) fusion(bf16[4,448,576]{2,1,0:T(8,128)(2,1)} %maximum_maximum_fusion, bf16[4,64,2,32]{3,1,2,0:T(8,128)(2,1)S(1)} %get-tuple-element.25, bf16[4,64,2,32]{3,1,2,0:T(8,128)(2,1)S(1)} %get-tuple-element.24, bf16[4,64,2,512]{3,1,2,0:T(8,128)(2,1)S(1)} %fusion.16, ...), kind=kOutput, calls=%fused_computation.171 | convolution fusion | flops 266928576 | bytes 3688448 | tf_op jit(solution)/shard_map/sub | solution.py:279
  39.8 3.2 %fusion.20 = bf16[4,64,2,128]{3,1,0,2:T(8,128)(2,1)} fusion(bf16[4,448,576]{2,1,0:T(8,128)(2,1)} %maximum_maximum_fusion, bf16[2,512,128]{2,1,0:T(8,128)(2,1)} %param.31, f32[4,2,64,448]{3,2,1,0:T(8,128)} %get-tuple-element.39, f32[4,2,64]{2,1,0:T(2,128)S(1)} %get-tuple-element.38), kind=kOutput, calls=%fused_computation.24 | convolution fusion | flops 302776320 | bytes 3278848 | tf_op jit(solution)/shard_map/rthl,hlv->rthv/dot_general | solution.py:284
  43.0 1.7 copy.76
  44.7 1.6 dot_general.59
  46.3 1.3 fusion.23
  48.2 1.5 collective-permute-done.3
  49.9 1.0 copy-done.14
  50.9 0.6 collective-permute-start.4
  51.6 0.7 copy.79
  52.3 7.2 %collective-permute-done.4 = bf16[64,2048]{1,0:T(8,128)(2,1)S(1)} collective-permute-done((bf16[64,2048]{1,0:T(8,128)(2,1)S(1)}, bf16[64,2048]{1,0:T(8,128)(2,1)S(1)}, u32[]{:S(2)}, u32[]{:S(2)}) %collective-permute-start.4) | collective-permute-done | bytes 262176 | tf_op jit(solution)/shard_map/ppermute | solution.py:192
  59.6 1.1 fusion.54
  60.7 1.6 collective-permute-start.5
  62.8 5.7 %collective-permute-done.5 = bf16[64,2048]{1,0:T(8,128)(2,1)S(1)} collective-permute-done((bf16[64,2048]{1,0:T(8,128)(2,1)S(1)}, bf16[64,2048]{1,0:T(8,128)(2,1)S(1)}, u32[]{:S(2)}, u32[]{:S(2)}) %collective-permute-start.5) | collective-permute-done | bytes 262176 | tf_op jit(solution)/shard_map/ppermute | solution.py:192
  69.9 2.6 %collective-permute-start.18 = (bf16[64,2048]{1,0:T(8,128)(2,1)S(1)}, bf16[64,2048]{1,0:T(8,128)(2,1)}, u32[]{:S(2)}, u32[]{:S(2)}) collective-permute-start(bf16[64,2048]{1,0:T(8,128)(2,1)S(1)} %multiply_convert_fusion.refs_0_), channel_id=1, source_target_pairs={{0,16},{8,24},{16,0},{24,8},{1,17},{9,25},{17,1},{25,9},{2,18},{10... | collective-permute-start | bytes 786440 | tf_op jit(solution)/shard_map/ppermute | solution.py:192
  73.1 2.7 %collective-permute-done.6.refs_1_ = bf16[64,2048]{1,0:T(8,128)(2,1)S(1)} collective-permute-done((bf16[64,2048]{1,0:T(8,128)(2,1)S(1)}, bf16[64,2048]{1,0:T(8,128)(2,1)S(1)}, u32[]{:S(2)}, u32[]{:S(2)}) %collective-permute-start.6) | collective-permute-done | bytes 262176 | tf_op jit(solution)/shard_map/ppermute | solution.py:192
  75.8 3.7 %collective-permute-done.25.refs_0_ = bf16[64,2048]{1,0:T(8,128)(2,1)} collective-permute-done((bf16[64,2048]{1,0:T(8,128)(2,1)S(1)}, bf16[64,2048]{1,0:T(8,128)(2,1)}, u32[]{:S(2)}, u32[]{:S(2)}) %collective-permute-start.25) | collective-permute-done | bytes 262176 | tf_op jit(solution)/shard_map/ppermute | solution.py:192
  79.5 1.3 collective-permute-start.26
  80.8 12.5 %collective-permute-done.18.refs_0_ = bf16[64,2048]{1,0:T(8,128)(2,1)} collective-permute-done((bf16[64,2048]{1,0:T(8,128)(2,1)S(1)}, bf16[64,2048]{1,0:T(8,128)(2,1)}, u32[]{:S(2)}, u32[]{:S(2)}) %collective-permute-start.18) | collective-permute-done | bytes 262176 | tf_op jit(solution)/shard_map/ppermute | solution.py:192
  93.2 1.4 collective-permute-start.19
  94.6 3.3 %all-gather.2.cloned.1.call-done = bf16[1024,512]{1,0:T(8,128)(2,1)} async-done(((bf16[64,512]{1,0:T(8,128)(2,1)}), bf16[1024,512]{1,0:T(8,128)(2,1)}) %all-gather.2.cloned.1.call-update) | async-done | bytes 1048592 | tf_op jit(solution)/shard_map/all_gather | solution.py:230
  97.9 1.8 convert_select_fusion
  99.7 1.3 copy.81
  101.5 0.7 broadcast_select_fusion.1
  102.9 0.6 fusion.92
  103.8 0.9 copy.83
  105.3 1.6 collective-permute-start.12
  107.4 2.6 %copy-done.1 = bf16[1,2,2048,704]{2,3,1,0:T(8,128)(2,1)S(1)} copy-done((bf16[1,2,2048,704]{2,3,1,0:T(8,128)(2,1)S(1)}, bf16[1,2,2048,704]{2,3,1,0:T(8,128)(2,1)}, u32[]{:S(2)}) %copy-start.1) | copy-done | bytes 5767192
  110.0 1.8 copy-done.3
  111.8 1.8 copy-done.5
  113.6 1.4 copy-done.6
  115.0 8.4 %experts.4 = (f32[2,64,2048]{2,1,0:T(8,128)S(1)}, bf16[2,64,2048]{2,1,0:T(8,128)(2,1)S(1)}) custom-call(bf16[64,2048]{1,0:T(8,128)(2,1)S(1)} %multiply_convert_fusion.refs_0_, bf16[64,2048]{1,0:T(8,128)(2,1)S(1)} %collective-permute-done.6.refs_1_, bf16[64,2048]{1,0:T(8,128)(2,1)} %collective-permute-done.7.refs_2_, ...), custom_call_target="tpu_custom_call" | custom-call | flops 3321888768 | bytes 17170432 | tf_op jit(solution)/shard_map/experts/pallas_call | solution.py:168
  124.1 2.6 %copy-done.2 = bf16[1,2,2048,704]{2,3,1,0:T(8,128)(2,1)S(1)} copy-done((bf16[1,2,2048,704]{2,3,1,0:T(8,128)(2,1)S(1)}, bf16[1,2,2048,704]{2,3,1,0:T(8,128)(2,1)}, u32[]{:S(2)}) %copy-start.2) | copy-done | bytes 5767192
  126.7 6.3 %experts.7 = (f32[2,64,2048]{2,1,0:T(8,128)S(1)}, bf16[2,64,2048]{2,1,0:T(8,128)(2,1)S(1)}) custom-call(bf16[64,2048]{1,0:T(8,128)(2,1)} %collective-permute-done.25.refs_0_, bf16[64,2048]{1,0:T(8,128)(2,1)} %collective-permute-done.26.refs_1_, bf16[64,2048]{1,0:T(8,128)(2,1)S(1)} %collective-permute-done.27.refs_2_, ...), custom_call_target="tpu_custom_call" | custom-call | flops 2214592512 | bytes 12845056 | tf_op jit(solution)/shard_map/experts/pallas_call | solution.py:168
  133.5 6.3 %experts.6 = (f32[2,64,2048]{2,1,0:T(8,128)S(1)}, bf16[2,64,2048]{2,1,0:T(8,128)(2,1)S(1)}) custom-call(bf16[64,2048]{1,0:T(8,128)(2,1)} %collective-permute-done.18.refs_0_, bf16[64,2048]{1,0:T(8,128)(2,1)} %collective-permute-done.19.refs_1_, bf16[64,2048]{1,0:T(8,128)(2,1)S(1)} %collective-permute-done.20.refs_2_, ...), custom_call_target="tpu_custom_call" | custom-call | flops 2214592512 | bytes 12845056 | tf_op jit(solution)/shard_map/experts/pallas_call | solution.py:168
  140.1 6.2 %experts.5 = (f32[2,64,2048]{2,1,0:T(8,128)S(1)}, bf16[2,64,2048]{2,1,0:T(8,128)(2,1)S(1)}) custom-call(bf16[64,2048]{1,0:T(8,128)(2,1)} %collective-permute-done.11.refs_0_, bf16[64,2048]{1,0:T(8,128)(2,1)S(1)} %collective-permute-done.12.refs_1_, bf16[64,2048]{1,0:T(8,128)(2,1)S(1)} %collective-permute-done.13.refs_2_, ...), custom_call_target="tpu_custom_call" | custom-call | flops 2214592512 | bytes 12845056 | tf_op jit(solution)/shard_map/experts/pallas_call | solution.py:168
  147.5 1.7 collective-permute-start.30
  150.0 1.7 collective-permute-start.16
  151.7 10.0 %collective-permute-done.30 = bf16[64,2048]{1,0:T(8,128)(2,1)S(1)} collective-permute-done((bf16[64,2048]{1,0:T(8,128)(2,1)S(1)}, bf16[64,2048]{1,0:T(8,128)(2,1)S(1)}, u32[]{:S(2)}, u32[]{:S(2)}) %collective-permute-start.30) | collective-permute-done | bytes 262176 | tf_op jit(solution)/shard_map/ppermute | solution.py:192
  161.8 3.4 %collective-permute-start.31 = (bf16[64,2048]{1,0:T(8,128)(2,1)S(1)}, bf16[64,2048]{1,0:T(8,128)(2,1)S(1)}, u32[]{:S(2)}, u32[]{:S(2)}) collective-permute-start(bf16[64,2048]{1,0:T(8,128)(2,1)S(1)} %fusion.37), channel_id=1, source_target_pairs={{0,8},{8,0},{16,24},{24,16},{1,9},{9,1},{17,25},{25,17},{2,10},{10... | collective-permute-start | bytes 786440 | tf_op jit(solution)/shard_map/ppermute | solution.py:192
  165.1 2.2 %collective-permute-done.23 = bf16[64,2048]{1,0:T(8,128)(2,1)S(1)} collective-permute-done((bf16[64,2048]{1,0:T(8,128)(2,1)S(1)}, bf16[64,2048]{1,0:T(8,128)(2,1)S(1)}, u32[]{:S(2)}, u32[]{:S(2)}) %collective-permute-start.23) | collective-permute-done | bytes 262176 | tf_op jit(solution)/shard_map/ppermute | solution.py:192
  167.5 3.5 %collective-permute-start.24 = (bf16[64,2048]{1,0:T(8,128)(2,1)S(1)}, bf16[64,2048]{1,0:T(8,128)(2,1)S(1)}, u32[]{:S(2)}, u32[]{:S(2)}) collective-permute-start(bf16[64,2048]{1,0:T(8,128)(2,1)S(1)} %fusion.41), channel_id=1, source_target_pairs={{0,16},{8,24},{16,0},{24,8},{1,17},{9,25},{17,1},{25,9},{2,18},{10... | collective-permute-start | bytes 786440 | tf_op jit(solution)/shard_map/ppermute | solution.py:192
  171.0 1.3 collective-permute-done.16
  172.3 1.3 collective-permute-start.17
  173.6 12.6 %collective-permute-done.24 = bf16[64,2048]{1,0:T(8,128)(2,1)S(1)} collective-permute-done((bf16[64,2048]{1,0:T(8,128)(2,1)S(1)}, bf16[64,2048]{1,0:T(8,128)(2,1)S(1)}, u32[]{:S(2)}, u32[]{:S(2)}) %collective-permute-start.24) | collective-permute-done | bytes 262176 | tf_op jit(solution)/shard_map/ppermute | solution.py:192
  186.3 6.7 %collective-permute-done.17 = bf16[64,2048]{1,0:T(8,128)(2,1)S(1)} collective-permute-done((bf16[64,2048]{1,0:T(8,128)(2,1)S(1)}, bf16[64,2048]{1,0:T(8,128)(2,1)S(1)}, u32[]{:S(2)}, u32[]{:S(2)}) %collective-permute-start.17) | collective-permute-done | bytes 262176 | tf_op jit(solution)/shard_map/ppermute | solution.py:192
  193.1 1.5 collective-permute-start.32
  195.3 0.9 convolution_bitcast_fusion
  196.2 0.8 fusion.21
  197.1 4.4 %collective-permute-done.32 = bf16[64,2048]{1,0:T(8,128)(2,1)S(1)} collective-permute-done((bf16[64,2048]{1,0:T(8,128)(2,1)S(1)}, bf16[64,2048]{1,0:T(8,128)(2,1)S(1)}, u32[]{:S(2)}, u32[]{:S(2)}) %collective-permute-start.32) | collective-permute-done | bytes 262176 | tf_op jit(solution)/shard_map/ppermute | solution.py:192
  201.4 0.9 add_convert_fusion
  (164 shorter events, 14.3 us)
Async XLA Ops:
  7.2 23.5 %copy-start = (bf16[2048,576]{0,1:T(8,128)(2,1)S(1)}, bf16[2048,576]{0,1:T(8,128)(2,1)}, u32[]{:S(2)}) copy-start(bf16[2048,576]{0,1:T(8,128)(2,1)} %param.28) | copy-start | bytes 7077892
  7.2 7.2 %copy-start.8 = (s32[4]{0:T(128)S(1)}, s32[4]{0:T(128)}, u32[]{:S(2)}) copy-start(s32[4]{0:T(128)} %param.22) | copy-start | bytes 52
  7.2 90.7 %all-gather.2.cloned.1.call-start = ((), (), s32[]{:S(2)}) async-start(), calls=%async_computation | async-start | bytes 1114112 | tf_op jit(solution)/shard_map/all_gather | solution.py:230
  9.6 16.8 %collective-permute-start.1 = (bf16[64,2048]{1,0:T(8,128)(2,1)S(1)}, bf16[64,2048]{1,0:T(8,128)(2,1)S(1)}, u32[]{:S(2)}, u32[]{:S(2)}) collective-permute-start(bf16[64,2048]{1,0:T(8,128)(2,1)S(1)} %fusion.32), channel_id=1, source_target_pairs={{0,4},{2,6},{4,0},{6,2},{1,5},{3,7},{5,1},{7,3},{8,12},{10,14},{12... | collective-permute-start | bytes 786440 | tf_op jit(solution)/shard_map/ppermute | solution.py:192
  11.2 15.8 %collective-permute-start = (bf16[64,2048]{1,0:T(8,128)(2,1)S(1)}, bf16[64,2048]{1,0:T(8,128)(2,1)}, u32[]{:S(2)}, u32[]{:S(2)}) collective-permute-start(bf16[64,2048]{1,0:T(8,128)(2,1)S(1)} %fusion.32), channel_id=1, source_target_pairs={{0,2},{2,0},{4,6},{6,4},{1,3},{3,1},{5,7},{7,5},{8,10},{10,8},{12,... | collective-permute-start | bytes 786440 | tf_op jit(solution)/shard_map/ppermute | solution.py:192
  14.4 8.0 %copy-start.21 = (f32[4,64,64]{2,1,0:T(8,128)}, f32[4,64,64]{2,1,0:T(8,128)S(1)}, u32[]{:S(2)}) copy-start(f32[4,64,64]{2,1,0:T(8,128)S(1)} %get-tuple-element.37) | copy-start | bytes 196612
  22.5 6.2 %copy-start.30 = (bf16[2048,384]{1,0:T(8,128)(2,1)S(1)}, bf16[2048,384]{1,0:T(8,128)(2,1)}, u32[]{:S(2)}) copy-start(bf16[2048,384]{1,0:T(8,128)(2,1)} %param.27) | copy-start | bytes 4718596
  26.4 1.7 collective-permute-start.2
  30.6 2.2 %copy-start.20 = (bf16[4,64,2,192]{3,2,1,0:T(2,128)(2,1)}, bf16[4,64,2,192]{3,2,1,0:T(2,128)(2,1)S(1)}, u32[]{:S(2)}) copy-start(bf16[4,64,2,192]{3,2,1,0:T(2,128)(2,1)S(1)} %reshape.310) | copy-start | bytes 589828
  30.7 2.9 %copy-start.28 = (f32[512]{0:T(512)S(1)}, f32[512]{0:T(512)}, u32[]{:S(2)}) copy-start(f32[512]{0:T(512)} %param.29) | copy-start | bytes 6148
  32.8 1.7 copy-start.9
  33.6 2.6 %copy-start.22 = (bf16[4,64,32]{2,1,0:T(8,128)(2,1)}, bf16[4,64,32]{2,1,0:T(8,128)(2,1)S(1)}, u32[]{:S(2)}) copy-start(bf16[4,64,32]{2,1,0:T(8,128)(2,1)S(1)} %get-tuple-element.33) | copy-start | bytes 49156
  33.8 2.4 %copy-start.15 = (bf16[4,64,512]{2,1,0:T(8,128)(2,1)}, bf16[4,64,512]{2,1,0:T(8,128)(2,1)S(1)}, u32[]{:S(2)}) copy-start(bf16[4,64,512]{2,1,0:T(8,128)(2,1)S(1)} %multiply_convert_fusion.1) | copy-start | bytes 786436
  34.5 1.6 copy-start.25
  39.7 6.6 %copy-start.19 = (bf16[256,2048]{1,0:T(8,128)(2,1)S(1)}, bf16[256,2048]{1,0:T(8,128)(2,1)}, u32[]{:S(2)}) copy-start(bf16[256,2048]{1,0:T(8,128)(2,1)} %param.32) | copy-start | bytes 3145732
  47.7 3.8 %copy-start.27 = (s32[64,6]{0,1:T(8,128)S(1)}, s32[64,6]{0,1:T(8,128)}, u32[]{:S(2)}) copy-start(s32[64,6]{0,1:T(8,128)} %param.24) | copy-start | bytes 4612
  47.8 15.0 %copy-start.29 = (s32[4]{0:T(128)S(1)}, s32[4]{0:T(128)}, u32[]{:S(2)}) copy-start(s32[4]{0:T(128)} %constant.112.clone) | copy-start | bytes 52
  47.8 20.7 %copy-start.10 = (bf16[64,2048]{1,0:T(8,128)(2,1)S(1)}, bf16[64,2048]{1,0:T(8,128)(2,1)}, u32[]{:S(2)}) copy-start(bf16[64,2048]{1,0:T(8,128)(2,1)} %param.20) | copy-start | bytes 786436
  47.8 20.9 %copy-start.26 = (f32[2048]{0:T(1024)S(1)}, f32[2048]{0:T(1024)}, u32[]{:S(2)}) copy-start(f32[2048]{0:T(1024)} %param.33) | copy-start | bytes 24580
  47.8 2.0 collective-permute-start.3
  49.9 1.0 copy-start.14
  50.9 8.6 %collective-permute-start.4 = (bf16[64,2048]{1,0:T(8,128)(2,1)S(1)}, bf16[64,2048]{1,0:T(8,128)(2,1)S(1)}, u32[]{:S(2)}, u32[]{:S(2)}) collective-permute-start(bf16[64,2048]{1,0:T(8,128)(2,1)S(1)} %fusion.57), channel_id=1, source_target_pairs={{0,4},{2,6},{4,0},{6,2},{1,5},{3,7},{5,1},{7,3},{8,12},{10,14},{12... | collective-permute-start | bytes 786440 | tf_op jit(solution)/shard_map/ppermute | solution.py:192
  60.7 40.8 %copy-start.12 = (bf16[64,2048]{1,0:T(8,128)(2,1)}, bf16[64,2048]{1,0:T(8,128)(2,1)S(1)}, u32[]{:S(2)}) copy-start(bf16[64,2048]{1,0:T(8,128)(2,1)S(1)} %fusion.54) | copy-start | bytes 786436
  60.7 7.8 %collective-permute-start.5 = (bf16[64,2048]{1,0:T(8,128)(2,1)S(1)}, bf16[64,2048]{1,0:T(8,128)(2,1)S(1)}, u32[]{:S(2)}, u32[]{:S(2)}) collective-permute-start(bf16[64,2048]{1,0:T(8,128)(2,1)S(1)} %fusion.54), channel_id=1, source_target_pairs={{0,1},{1,0},{2,3},{3,2},{4,5},{5,4},{6,7},{7,6},{8,9},{9,8},{10,11... | collective-permute-start | bytes 786440 | tf_op jit(solution)/shard_map/ppermute | solution.py:192
  68.5 31.2 %copy-start.17 = (bf16[64,2048]{1,0:T(8,128)(2,1)}, bf16[64,2048]{1,0:T(8,128)(2,1)S(1)}, u32[]{:S(2)}) copy-start(bf16[64,2048]{1,0:T(8,128)(2,1)S(1)} %collective-permute-done.5) | copy-start | bytes 786436
  68.9 6.9 %collective-permute-start.6 = (bf16[64,2048]{1,0:T(8,128)(2,1)S(1)}, bf16[64,2048]{1,0:T(8,128)(2,1)S(1)}, u32[]{:S(2)}, u32[]{:S(2)}) collective-permute-start(bf16[64,2048]{1,0:T(8,128)(2,1)S(1)} %multiply_convert_fusion.refs_0_), channel_id=1, source_target_pairs={{0,4},{2,6},{4,0},{6,2},{1,5},{3,7},{5,1},{7,3},{8,12},{10,14},{12... | collective-permute-start | bytes 786440 | tf_op jit(solution)/shard_map/ppermute | solution.py:192
  69.5 10.0 %collective-permute-start.25 = (bf16[64,2048]{1,0:T(8,128)(2,1)S(1)}, bf16[64,2048]{1,0:T(8,128)(2,1)}, u32[]{:S(2)}, u32[]{:S(2)}) collective-permute-start(bf16[64,2048]{1,0:T(8,128)(2,1)S(1)} %multiply_convert_fusion.refs_0_), channel_id=1, source_target_pairs={{0,8},{8,0},{16,24},{24,16},{1,9},{9,1},{17,25},{25,17},{2,10},{10... | collective-permute-start | bytes 786440 | tf_op jit(solution)/shard_map/ppermute | solution.py:192
  69.9 23.3 %collective-permute-start.18 = (bf16[64,2048]{1,0:T(8,128)(2,1)S(1)}, bf16[64,2048]{1,0:T(8,128)(2,1)}, u32[]{:S(2)}, u32[]{:S(2)}) collective-permute-start(bf16[64,2048]{1,0:T(8,128)(2,1)S(1)} %multiply_convert_fusion.refs_0_), channel_id=1, source_target_pairs={{0,16},{8,24},{16,0},{24,8},{1,17},{9,25},{17,1},{25,9},{2,18},{10... | collective-permute-start | bytes 786440 | tf_op jit(solution)/shard_map/ppermute | solution.py:192
  72.5 32.1 %collective-permute-start.7 = (bf16[64,2048]{1,0:T(8,128)(2,1)S(1)}, bf16[64,2048]{1,0:T(8,128)(2,1)}, u32[]{:S(2)}, u32[]{:S(2)}) collective-permute-start(bf16[64,2048]{1,0:T(8,128)(2,1)S(1)} %multiply_convert_fusion.refs_0_), channel_id=1, source_target_pairs={{0,2},{2,0},{4,6},{6,4},{1,3},{3,1},{5,7},{7,5},{8,10},{10,8},{12,... | collective-permute-start | bytes 786440 | tf_op jit(solution)/shard_map/ppermute | solution.py:192
  72.6 32.4 %collective-permute-start.11 = (bf16[64,2048]{1,0:T(8,128)(2,1)S(1)}, bf16[64,2048]{1,0:T(8,128)(2,1)}, u32[]{:S(2)}, u32[]{:S(2)}) collective-permute-start(bf16[64,2048]{1,0:T(8,128)(2,1)S(1)} %multiply_convert_fusion.refs_0_), channel_id=1, source_target_pairs={{0,24},{8,16},{16,8},{24,0},{1,25},{9,17},{17,9},{25,1},{2,26},{10... | collective-permute-start | bytes 786440 | tf_op jit(solution)/shard_map/ppermute | solution.py:192
  75.8 29.4 %collective-permute-start.8 = (bf16[64,2048]{1,0:T(8,128)(2,1)S(1)}, bf16[64,2048]{1,0:T(8,128)(2,1)}, u32[]{:S(2)}, u32[]{:S(2)}) collective-permute-start(bf16[64,2048]{1,0:T(8,128)(2,1)S(1)} %collective-permute-done.6.refs_1_), channel_id=1, source_target_pairs={{0,2},{2,0},{4,6},{6,4},{1,3},{3,1},{5,7},{7,5},{8,10},{10,8},{12,... | collective-permute-start | bytes 786440 | tf_op jit(solution)/shard_map/ppermute | solution.py:192
  79.5 27.4 %collective-permute-start.26 = (bf16[64,2048]{1,0:T(8,128)(2,1)}, bf16[64,2048]{1,0:T(8,128)(2,1)}, u32[]{:S(2)}, u32[]{:S(2)}) collective-permute-start(bf16[64,2048]{1,0:T(8,128)(2,1)} %collective-permute-done.25.refs_0_), channel_id=1, source_target_pairs={{0,4},{2,6},{4,0},{6,2},{1,5},{3,7},{5,1},{7,3},{8,12},{10,14},{12... | collective-permute-start | bytes 786440 | tf_op jit(solution)/shard_map/ppermute | solution.py:192
  93.2 13.6 %collective-permute-start.19 = (bf16[64,2048]{1,0:T(8,128)(2,1)}, bf16[64,2048]{1,0:T(8,128)(2,1)}, u32[]{:S(2)}, u32[]{:S(2)}) collective-permute-start(bf16[64,2048]{1,0:T(8,128)(2,1)} %collective-permute-done.18.refs_0_), channel_id=1, source_target_pairs={{0,4},{2,6},{4,0},{6,2},{1,5},{3,7},{5,1},{7,3},{8,12},{10,14},{12... | collective-permute-start | bytes 786440 | tf_op jit(solution)/shard_map/ppermute | solution.py:192
  99.7 7.7 %copy-start.7 = (bf16[2048,16]{0,1:T(8,128)(2,1)S(1)}, bf16[2048,16]{0,1:T(8,128)(2,1)}, u32[]{:S(2)}) copy-start(bf16[2048,16]{0,1:T(8,128)(2,1)} %param.34) | copy-start | bytes 196612
  104.7 18.7 %collective-permute-start.27 = (bf16[64,2048]{1,0:T(8,128)(2,1)}, bf16[64,2048]{1,0:T(8,128)(2,1)S(1)}, u32[]{:S(2)}, u32[]{:S(2)}) collective-permute-start(bf16[64,2048]{1,0:T(8,128)(2,1)} %collective-permute-done.25.refs_0_), channel_id=1, source_target_pairs={{0,2},{2,0},{4,6},{6,4},{1,3},{3,1},{5,7},{7,5},{8,10},{10,8},{12,... | collective-permute-start | bytes 786440 | tf_op jit(solution)/shard_map/ppermute | solution.py:192
  105.0 28.0 %collective-permute-start.20 = (bf16[64,2048]{1,0:T(8,128)(2,1)}, bf16[64,2048]{1,0:T(8,128)(2,1)S(1)}, u32[]{:S(2)}, u32[]{:S(2)}) collective-permute-start(bf16[64,2048]{1,0:T(8,128)(2,1)} %collective-permute-done.18.refs_0_), channel_id=1, source_target_pairs={{0,2},{2,0},{4,6},{6,4},{1,3},{3,1},{5,7},{7,5},{8,10},{10,8},{12,... | collective-permute-start | bytes 786440 | tf_op jit(solution)/shard_map/ppermute | solution.py:192
  105.3 18.3 %collective-permute-start.12 = (bf16[64,2048]{1,0:T(8,128)(2,1)}, bf16[64,2048]{1,0:T(8,128)(2,1)S(1)}, u32[]{:S(2)}, u32[]{:S(2)}) collective-permute-start(bf16[64,2048]{1,0:T(8,128)(2,1)} %collective-permute-done.11.refs_0_), channel_id=1, source_target_pairs={{0,4},{2,6},{4,0},{6,2},{1,5},{3,7},{5,1},{7,3},{8,12},{10,14},{12... | collective-permute-start | bytes 786440 | tf_op jit(solution)/shard_map/ppermute | solution.py:192
  106.9 17.1 %collective-permute-start.28 = (bf16[64,2048]{1,0:T(8,128)(2,1)}, bf16[64,2048]{1,0:T(8,128)(2,1)S(1)}, u32[]{:S(2)}, u32[]{:S(2)}) collective-permute-start(bf16[64,2048]{1,0:T(8,128)(2,1)} %collective-permute-done.26.refs_1_), channel_id=1, source_target_pairs={{0,2},{2,0},{4,6},{6,4},{1,3},{3,1},{5,7},{7,5},{8,10},{10,8},{12,... | collective-permute-start | bytes 786440 | tf_op jit(solution)/shard_map/ppermute | solution.py:192
  106.9 26.6 %collective-permute-start.21 = (bf16[64,2048]{1,0:T(8,128)(2,1)}, bf16[64,2048]{1,0:T(8,128)(2,1)S(1)}, u32[]{:S(2)}, u32[]{:S(2)}) collective-permute-start(bf16[64,2048]{1,0:T(8,128)(2,1)} %collective-permute-done.19.refs_1_), channel_id=1, source_target_pairs={{0,2},{2,0},{4,6},{6,4},{1,3},{3,1},{5,7},{7,5},{8,10},{10,8},{12,... | collective-permute-start | bytes 786440 | tf_op jit(solution)/shard_map/ppermute | solution.py:192
  107.4 2.6 %copy-start.1 = (bf16[1,2,2048,704]{2,3,1,0:T(8,128)(2,1)S(1)}, bf16[1,2,2048,704]{2,3,1,0:T(8,128)(2,1)}, u32[]{:S(2)}) copy-start(bf16[1,2,2048,704]{2,3,1,0:T(8,128)(2,1)} %param.37) | copy-start | bytes 17301508
  110.0 1.8 copy-start.3
  111.8 1.8 copy-start.5
  113.6 1.4 copy-start.6
  115.0 9.1 %copy-start.4 = (bf16[1,704,2048]{2,1,0:T(8,128)(2,1)S(1)}, bf16[1,704,2048]{2,1,0:T(8,128)(2,1)}, u32[]{:S(2)}) copy-start(bf16[1,704,2048]{2,1,0:T(8,128)(2,1)} %param.38) | copy-start | bytes 8650756
  123.4 16.7 %collective-permute-start.13 = (bf16[64,2048]{1,0:T(8,128)(2,1)}, bf16[64,2048]{1,0:T(8,128)(2,1)S(1)}, u32[]{:S(2)}, u32[]{:S(2)}) collective-permute-start(bf16[64,2048]{1,0:T(8,128)(2,1)} %collective-permute-done.11.refs_0_), channel_id=1, source_target_pairs={{0,2},{2,0},{4,6},{6,4},{1,3},{3,1},{5,7},{7,5},{8,10},{10,8},{12,... | collective-permute-start | bytes 786440 | tf_op jit(solution)/shard_map/ppermute | solution.py:192
  123.5 23.2 %collective-permute-start.9 = (bf16[2,64,2048]{2,1,0:T(8,128)(2,1)S(1)}, bf16[2,64,2048]{2,1,0:T(8,128)(2,1)S(1)}, u32[]{:S(2)}, u32[]{:S(2)}) collective-permute-start(bf16[2,64,2048]{2,1,0:T(8,128)(2,1)S(1)} %get-tuple-element.11), channel_id=1, source_target_pairs={{0,2},{2,0},{4,6},{6,4},{1,3},{3,1},{5,7},{7,5},{8,10},{10,8},{12,... | collective-permute-start | bytes 1572872 | tf_op jit(solution)/shard_map/ppermute | solution.py:192
  124.0 16.1 %collective-permute-start.14 = (bf16[64,2048]{1,0:T(8,128)(2,1)S(1)}, bf16[64,2048]{1,0:T(8,128)(2,1)S(1)}, u32[]{:S(2)}, u32[]{:S(2)}) collective-permute-start(bf16[64,2048]{1,0:T(8,128)(2,1)S(1)} %collective-permute-done.12.refs_1_), channel_id=1, source_target_pairs={{0,2},{2,0},{4,6},{6,4},{1,3},{3,1},{5,7},{7,5},{8,10},{10,8},{12,... | collective-permute-start | bytes 786440 | tf_op jit(solution)/shard_map/ppermute | solution.py:192
  124.1 2.6 %copy-start.2 = (bf16[1,2,2048,704]{2,3,1,0:T(8,128)(2,1)S(1)}, bf16[1,2,2048,704]{2,3,1,0:T(8,128)(2,1)}, u32[]{:S(2)}) copy-start(bf16[1,2,2048,704]{2,3,1,0:T(8,128)(2,1)} %param.37) | copy-start | bytes 17301508
  133.0 14.4 %collective-permute-start.29 = (bf16[2,64,2048]{2,1,0:T(8,128)(2,1)S(1)}, bf16[2,64,2048]{2,1,0:T(8,128)(2,1)S(1)}, u32[]{:S(2)}, u32[]{:S(2)}) collective-permute-start(bf16[2,64,2048]{2,1,0:T(8,128)(2,1)S(1)} %get-tuple-element.17), channel_id=1, source_target_pairs={{0,2},{2,0},{4,6},{6,4},{1,3},{3,1},{5,7},{7,5},{8,10},{10,8},{12,... | collective-permute-start | bytes 1572872 | tf_op jit(solution)/shard_map/ppermute | solution.py:192
  139.8 9.4 %collective-permute-start.22 = (bf16[2,64,2048]{2,1,0:T(8,128)(2,1)S(1)}, bf16[2,64,2048]{2,1,0:T(8,128)(2,1)S(1)}, u32[]{:S(2)}, u32[]{:S(2)}) collective-permute-start(bf16[2,64,2048]{2,1,0:T(8,128)(2,1)S(1)} %get-tuple-element.15), channel_id=1, source_target_pairs={{0,2},{2,0},{4,6},{6,4},{1,3},{3,1},{5,7},{7,5},{8,10},{10,8},{12,... | collective-permute-start | bytes 1572872 | tf_op jit(solution)/shard_map/ppermute | solution.py:192
  146.4 3.5 %collective-permute-start.15 = (bf16[2,64,2048]{2,1,0:T(8,128)(2,1)S(1)}, bf16[2,64,2048]{2,1,0:T(8,128)(2,1)S(1)}, u32[]{:S(2)}, u32[]{:S(2)}) collective-permute-start(bf16[2,64,2048]{2,1,0:T(8,128)(2,1)S(1)} %get-tuple-element.13), channel_id=1, source_target_pairs={{0,2},{2,0},{4,6},{6,4},{1,3},{3,1},{5,7},{7,5},{8,10},{10,8},{12,... | collective-permute-start | bytes 1572872 | tf_op jit(solution)/shard_map/ppermute | solution.py:192
  146.9 26.7 %collective-permute-start.10 = (bf16[64,2048]{1,0:T(8,128)(2,1)S(1)}, bf16[64,2048]{1,0:T(8,128)(2,1)S(1)}, u32[]{:S(2)}, u32[]{:S(2)}) collective-permute-start(bf16[64,2048]{1,0:T(8,128)(2,1)S(1)} %fusion.58), channel_id=1, source_target_pairs={{0,4},{2,6},{4,0},{6,2},{1,5},{3,7},{5,1},{7,3},{8,12},{10,14},{12... | collective-permute-start | bytes 786440 | tf_op jit(solution)/shard_map/ppermute | solution.py:192
  147.5 14.2 %collective-permute-start.30 = (bf16[64,2048]{1,0:T(8,128)(2,1)S(1)}, bf16[64,2048]{1,0:T(8,128)(2,1)S(1)}, u32[]{:S(2)}, u32[]{:S(2)}) collective-permute-start(bf16[64,2048]{1,0:T(8,128)(2,1)S(1)} %fusion.61), channel_id=1, source_target_pairs={{0,4},{2,6},{4,0},{6,2},{1,5},{3,7},{5,1},{7,3},{8,12},{10,14},{12... | collective-permute-start | bytes 786440 | tf_op jit(solution)/shard_map/ppermute | solution.py:192
  149.4 17.9 %collective-permute-start.23 = (bf16[64,2048]{1,0:T(8,128)(2,1)S(1)}, bf16[64,2048]{1,0:T(8,128)(2,1)S(1)}, u32[]{:S(2)}, u32[]{:S(2)}) collective-permute-start(bf16[64,2048]{1,0:T(8,128)(2,1)S(1)} %fusion.60), channel_id=1, source_target_pairs={{0,4},{2,6},{4,0},{6,2},{1,5},{3,7},{5,1},{7,3},{8,12},{10,14},{12... | collective-permute-start | bytes 786440 | tf_op jit(solution)/shard_map/ppermute | solution.py:192
  150.0 22.2 %collective-permute-start.16 = (bf16[64,2048]{1,0:T(8,128)(2,1)S(1)}, bf16[64,2048]{1,0:T(8,128)(2,1)S(1)}, u32[]{:S(2)}, u32[]{:S(2)}) collective-permute-start(bf16[64,2048]{1,0:T(8,128)(2,1)S(1)} %fusion.59), channel_id=1, source_target_pairs={{0,4},{2,6},{4,0},{6,2},{1,5},{3,7},{5,1},{7,3},{8,12},{10,14},{12... | collective-permute-start | bytes 786440 | tf_op jit(solution)/shard_map/ppermute | solution.py:192
  161.8 11.8 %collective-permute-start.31 = (bf16[64,2048]{1,0:T(8,128)(2,1)S(1)}, bf16[64,2048]{1,0:T(8,128)(2,1)S(1)}, u32[]{:S(2)}, u32[]{:S(2)}) collective-permute-start(bf16[64,2048]{1,0:T(8,128)(2,1)S(1)} %fusion.37), channel_id=1, source_target_pairs={{0,8},{8,0},{16,24},{24,16},{1,9},{9,1},{17,25},{25,17},{2,10},{10... | collective-permute-start | bytes 786440 | tf_op jit(solution)/shard_map/ppermute | solution.py:192
  167.4 28.8 %copy-start.16 = (bf16[4,64,512]{2,1,0:T(8,128)(2,1)S(1)}, bf16[4,64,512]{2,1,0:T(8,128)(2,1)}, u32[]{:S(2)}) copy-start(bf16[4,64,512]{2,1,0:T(8,128)(2,1)} %copy-done.15) | copy-start | bytes 786436
  167.4 28.8 %copy-start.23 = (bf16[4,64,32]{2,1,0:T(8,128)(2,1)S(1)}, bf16[4,64,32]{2,1,0:T(8,128)(2,1)}, u32[]{:S(2)}) copy-start(bf16[4,64,32]{2,1,0:T(8,128)(2,1)} %copy-done.22) | copy-start | bytes 49156
  167.4 34.0 %copy-start.11 = (bf16[64,2048]{1,0:T(8,128)(2,1)S(1)}, bf16[64,2048]{1,0:T(8,128)(2,1)}, u32[]{:S(2)}) copy-start(bf16[64,2048]{1,0:T(8,128)(2,1)} %param.20) | copy-start | bytes 786436
  167.4 34.0 %copy-start.13 = (bf16[64,2048]{1,0:T(8,128)(2,1)S(1)}, bf16[64,2048]{1,0:T(8,128)(2,1)}, u32[]{:S(2)}) copy-start(bf16[64,2048]{1,0:T(8,128)(2,1)} %copy-done.12) | copy-start | bytes 786436
  167.4 34.0 %copy-start.18 = (bf16[64,2048]{1,0:T(8,128)(2,1)S(1)}, bf16[64,2048]{1,0:T(8,128)(2,1)}, u32[]{:S(2)}) copy-start(bf16[64,2048]{1,0:T(8,128)(2,1)} %copy-done.17) | copy-start | bytes 786436
  167.5 18.8 %collective-permute-start.24 = (bf16[64,2048]{1,0:T(8,128)(2,1)S(1)}, bf16[64,2048]{1,0:T(8,128)(2,1)S(1)}, u32[]{:S(2)}, u32[]{:S(2)}) collective-permute-start(bf16[64,2048]{1,0:T(8,128)(2,1)S(1)} %fusion.41), channel_id=1, source_target_pairs={{0,16},{8,24},{16,0},{24,8},{1,17},{9,25},{17,1},{25,9},{2,18},{10... | collective-permute-start | bytes 786440 | tf_op jit(solution)/shard_map/ppermute | solution.py:192
  172.3 20.7 %collective-permute-start.17 = (bf16[64,2048]{1,0:T(8,128)(2,1)S(1)}, bf16[64,2048]{1,0:T(8,128)(2,1)S(1)}, u32[]{:S(2)}, u32[]{:S(2)}) collective-permute-start(bf16[64,2048]{1,0:T(8,128)(2,1)S(1)} %fusion.45), channel_id=1, source_target_pairs={{0,24},{8,16},{16,8},{24,0},{1,25},{9,17},{17,9},{25,1},{2,26},{10... | collective-permute-start | bytes 786440 | tf_op jit(solution)/shard_map/ppermute | solution.py:192
  193.1 8.3 %collective-permute-start.32 = (bf16[64,2048]{1,0:T(8,128)(2,1)S(1)}, bf16[64,2048]{1,0:T(8,128)(2,1)S(1)}, u32[]{:S(2)}, u32[]{:S(2)}) collective-permute-start(bf16[64,2048]{1,0:T(8,128)(2,1)S(1)} %fusion.52), channel_id=1, source_target_pairs={{0,1},{1,0},{2,3},{3,2},{4,5},{5,4},{6,7},{7,6},{8,9},{9,8},{10,11... | collective-permute-start | bytes 786440 | tf_op jit(solution)/shard_map/ppermute | solution.py:192
  (3 other events, 2.6 us)
Sparse Core Ops, SparseCore 0:
  52.4 45.4 all-gather.1

commit v3 on v1

v3 whole, which is shorter than its diff:
```python
import functools
import math

import jax
import jax.numpy as jnp
from jax import lax
from jax.experimental import pallas as pl
from jax.experimental.pallas import tpu as pltpu
from jax.sharding import PartitionSpec as P

NOPE = 128
ROPE = 64
LAT = 512
VDIM = 128
CACHE = 384
WINDOW = 160
SINK = 4


EPSILON = 1e-06
EXTRA = 128
CHUNKS = 4


def rms_scale(values, gain_row):
    mean_square = jnp.mean(values * values, axis=-1, keepdims=True)
    return values * lax.rsqrt(mean_square + EPSILON) * gain_row


def rotate(values, cosine, sine_part):
    half_width = values.shape[-1] // 2
    first_half = values[..., :half_width]
    second_half = values[..., half_width:]
    return jnp.concatenate(
        [
            first_half * cosine - second_half * sine_part,
            second_half * cosine + first_half * sine_part,
        ],
        axis=-1,
    )


def dot(values, weight):
    return jnp.dot(values, weight, preferred_element_type=jnp.float32)


def transposed_dot(values, weight):
    return lax.dot_general(
        values, weight, (((1,), (1,)), ((), ())), preferred_element_type=jnp.float32
    )


WHOLE = pl.BlockSpec(memory_space=pltpu.VMEM)
SCALARS = pl.BlockSpec(memory_space=pltpu.SMEM)
PLACED = pl.BlockSpec(memory_space=pl.ANY)


def params(megabytes):
    return pltpu.CompilerParams(vmem_limit_bytes=megabytes << 20)


def tree_kernel(row_ref, lengths_ref, accepted_ref, parents_ref, closure_ref, turns_ref, places_ref):
    requests, size, _ = closure_ref.shape
    down = lax.broadcasted_iota(jnp.int32, (size, size), 0)
    across = lax.broadcasted_iota(jnp.int32, (size, size), 1)
    eye = (down == across).astype(jnp.bfloat16)
    closures = []
    for k in range(requests):
        parent_row = parents_ref[pl.ds(row_ref[0] ^ k, 1), :]
        links = (parent_row == down).astype(jnp.bfloat16) + eye
        closures.append(
            lax.dot_general(
                links, eye, (((0,), (0,)), ((), ())), preferred_element_type=jnp.float32
            )
        )
    for repeat in range(max(1, (size - 1).bit_length())):
        narrow = [closure.astype(jnp.bfloat16) for closure in closures]
        closures = [jnp.minimum(dot(each, each), 1.0) for each in narrow]
    step = -2.0 * math.log(10000.0) / ROPE
    frequency = jnp.exp(
        lax.broadcasted_iota(jnp.int32, (size, ROPE // 2), 1).astype(jnp.float32) * step
    )
    for k in range(requests):
        closure_ref[k] = closures[k]
        depth = jnp.sum(closures[k], axis=-1, keepdims=True) - 1.0
        angles = (lengths_ref[row_ref[0] ^ k].astype(jnp.float32) + depth) * frequency
        turns_ref[k, :, : ROPE // 2] = jnp.cos(angles)
        turns_ref[k, :, ROPE // 2 :] = jnp.sin(angles)
    own = closures[0].astype(jnp.bfloat16)
    depth_row = transposed_dot(jnp.ones((8, size), jnp.bfloat16), own)[:1] - 1.0
    chosen = (lax.broadcasted_iota(jnp.int32, (size, 1), 0) == accepted_ref[0]).astype(jnp.float32)
    path_mask = jnp.sum(chosen * closures[0], axis=0, keepdims=True)
    places_ref[...] = jnp.where(
        depth_row == down.astype(jnp.float32), path_mask, 0.0
    ).astype(jnp.bfloat16)


def tree_tables(row_index, lengths, accepted, parents):
    requests, size = parents.shape
    return pl.pallas_call(
        tree_kernel,
        out_shape=(
            jax.ShapeDtypeStruct((requests, size, size), jnp.float32),
            jax.ShapeDtypeStruct((requests, size, ROPE), jnp.float32),
            jax.ShapeDtypeStruct((size, size), jnp.bfloat16),
        ),
        in_specs=[SCALARS, SCALARS, SCALARS, WHOLE],
        out_specs=(WHOLE, WHOLE, WHOLE),
        compiler_params=params(16),
        name="trees",
    )(row_index, lengths, accepted, parents)


def attention_kernel(first, place, row_ref, lengths_ref, *refs):
    (
        first_ref,
        second_ref,
        cache_a_ref,
        cache_b_ref,
        closure_ref,
        turns_ref,
        places_ref,
        gain_ref,
        query_ref,
        latent_ref,
        latent_gain_ref,
        key_ref,
        value_ref,
        output_ref,
        keep_ref,
        send_ref,
    ) = refs[:16]
    size = first_ref.shape[0]
    heads = key_ref.shape[0]
    bf16 = jnp.bfloat16
    scale_factor = 1.0 / math.sqrt(NOPE + ROPE)
    rows = jnp.concatenate([first_ref[...], second_ref[...]], axis=0).astype(jnp.float32)
    rows = rms_scale(rows, gain_ref[...]).astype(bf16)
    turns = jnp.concatenate([turns_ref[place], turns_ref[place + 1]], axis=0)
    cosine, sine_part = turns[:, : ROPE // 2], turns[:, ROPE // 2 :]
    projected = transposed_dot(rows, latent_ref[...])
    content = rms_scale(projected[:, :LAT], latent_gain_ref[...]).astype(bf16)
    key_rope = rotate(projected[:, LAT:], cosine, sine_part).astype(bf16)
    if first:
        accepted_ref = refs[16]
        accepted_ref[0, :, :LAT] = dot(places_ref[...], content[:size]).astype(bf16)
        accepted_ref[0, :, LAT:] = dot(places_ref[...], key_rope[:size]).astype(bf16)
    queries = dot(rows, query_ref[...])
    query_latent, query_rope = [], []
    for h in range(heads):
        start = h * (NOPE + ROPE)
        query_latent.append(
            dot(queries[:, start : start + NOPE].astype(bf16), key_ref[h]).astype(bf16)
        )
        turned = queries[:, start + NOPE : start + NOPE + ROPE].astype(bf16).astype(jnp.float32)
        query_rope.append(rotate(turned, cosine, sine_part).astype(bf16))
    outs = [[], []]
    for r, cache_ref in enumerate((cache_a_ref, cache_b_ref)):
        part = slice(r * size, (r + 1) * size)
        latent_rows = jnp.concatenate([each[part] for each in query_latent], axis=0)
        rope_rows = jnp.concatenate([each[part] for each in query_rope], axis=0)
        old = dot(latent_rows, cache_ref[0, :LAT, :]) + dot(rope_rows, cache_ref[0, LAT:, :])
        new = transposed_dot(latent_rows, content[part]) + transposed_dot(rope_rows, key_rope[part])
        length = lengths_ref[row_ref[0] ^ (place + r)]
        spots = lax.broadcasted_iota(jnp.int32, (1, old.shape[1]), 1)
        allowed = (spots < length) & ((spots < SINK) | (spots >= length - WINDOW))
        related = jnp.concatenate([closure_ref[place + r]] * heads, axis=0) > 0.5
        old = jnp.where(allowed, old * scale_factor, -1e30)
        new = jnp.where(related, new * scale_factor, -1e30)
        peak = jnp.maximum(
            jnp.max(old, axis=-1, keepdims=True), jnp.max(new, axis=-1, keepdims=True)
        )
        old = jnp.exp(old - peak)
        new = jnp.exp(new - peak)
        total = jnp.sum(old, axis=-1, keepdims=True) + jnp.sum(new, axis=-1, keepdims=True)
        old = (old / total).astype(bf16)
        new = (new / total).astype(bf16)
        mixed = transposed_dot(old, cache_ref[0, :LAT, :]) + dot(new, content[part])
        for h in range(heads):
            outs[r].append(mixed[h * size : (h + 1) * size].astype(bf16))
    head_rows = [
        dot(jnp.concatenate([outs[0][h], outs[1][h]], axis=0), value_ref[h]).astype(bf16)
        for h in range(heads)
    ]
    head_rows = jnp.concatenate(head_rows, axis=1)
    partial = dot(head_rows, output_ref[...])
    keep_ref[...] = partial[:size]
    send_ref[...] = partial[size:].astype(bf16)


def attention_part(first, place, row_index, lengths, blocks, cache, tables, weights):
    size, width = blocks[0].shape
    slots, spots = cache.shape[1:]
    heads = weights[4].shape[0]
    closure, turns, places = tables

    def whole(array):
        rank = array.ndim
        return pl.BlockSpec(array.shape, lambda i, row, lens: (0,) * rank)

    def cached(k):
        return pl.BlockSpec((1, slots, spots), lambda i, row, lens: (row[0] ^ k, 0, 0))

    rest = [closure, turns, places, *weights]
    out_shape = [
        jax.ShapeDtypeStruct((size, width), jnp.float32),
        jax.ShapeDtypeStruct((size, width), jnp.bfloat16),
    ]
    if first:
        out_shape.append(jax.ShapeDtypeStruct((1, size, LAT + ROPE), jnp.bfloat16))
    rows = 2 * size
    flops = 2 * rows * width * (weights[1].shape[1] + LAT + ROPE + heads * VDIM)
    return pl.pallas_call(
        functools.partial(attention_kernel, first, place),
        out_shape=tuple(out_shape),
        grid_spec=pltpu.PrefetchScalarGridSpec(
            num_scalar_prefetch=2,
            grid=(1,),
            in_specs=[whole(blocks[0]), whole(blocks[1]), cached(place), cached(place + 1)]
            + [whole(each) for each in rest],
            out_specs=tuple(whole(each) for each in out_shape),
        ),
        compiler_params=params(32),
        cost_estimate=pl.CostEstimate(
            flops=flops,
            bytes_accessed=2 * width * (weights[1].shape[1] + LAT + ROPE + heads * VDIM),
            transcendentals=rows * heads * (spots + size),
        ),
        name="attention",
    )(row_index, lengths, blocks[0], blocks[1], cache, cache, *rest)


def join_kernel(hidden_ref, keep_ref, arrived_ref, gain_ref, named_ref, residual_ref, block_ref):
    width = hidden_ref.shape[1]
    total = keep_ref[...].astype(jnp.float32)
    for k in range(arrived_ref.shape[0]):
        total = total + arrived_ref[k].astype(jnp.float32)
    residual = hidden_ref[...].astype(jnp.float32) + total
    residual_ref[...] = residual
    block_ref[:, :width] = rms_scale(residual, gain_ref[...]).astype(jnp.bfloat16)
    block_ref[:, width:] = named_ref[...]


def joined(hidden, keep, arrived, gain, named):
    rows, width = hidden.shape
    return pl.pallas_call(
        join_kernel,
        out_shape=(
            jax.ShapeDtypeStruct((rows, width), jnp.float32),
            jax.ShapeDtypeStruct((rows, width + EXTRA), jnp.bfloat16),
        ),
        in_specs=[WHOLE] * 5,
        out_specs=(WHOLE, WHOLE),
        compiler_params=params(16),
        name="join",
    )(hidden, keep, arrived, gain, named)


def expert_kernel(shared, *refs):
    blocks, refs = refs[:4], refs[4:]
    own_ref, router_ref, gate_up_ref, down_ref = refs[:4]
    refs = refs[4:]
    if shared:
        shared_gate_up_ref, shared_down_ref = refs[:2]
        refs = refs[2:]
    keep_ref, send_ref = refs
    experts, width = router_ref.shape
    size = blocks[0].shape[0]
    rows = jnp.concatenate([ref[:, :width] for ref in blocks], axis=0)
    named = jnp.concatenate([ref[:, width:] for ref in blocks], axis=0)[:, :experts]
    logits = transposed_dot(rows, router_ref[...])
    raised = jnp.exp(logits - jnp.max(logits, axis=-1, keepdims=True))
    router = raised / jnp.sum(raised, axis=-1, keepdims=True)
    share = jnp.sum(router * named.astype(jnp.float32) * own_ref[...], axis=-1, keepdims=True)

    def inner(weights_ref):
        gate = transposed_dot(rows, weights_ref[0])
        upper = transposed_dot(rows, weights_ref[1])
        return (jax.nn.silu(gate) * upper).astype(jnp.bfloat16)

    routed_inner = inner(gate_up_ref)
    if shared:
        shared_inner = inner(shared_gate_up_ref)
    tile = width // CHUNKS
    for k in range(CHUNKS):
        part = slice(k * tile, (k + 1) * tile)
        result = share * dot(routed_inner, down_ref[:, part])
        if shared:
            result = result + dot(shared_inner, shared_down_ref[:, part])
        keep_ref[:, :, part] = result[: 2 * size].reshape(2, size, tile)
        send_ref[:, :, part] = result[2 * size :].astype(jnp.bfloat16).reshape(2, size, tile)


def expert_part(blocks, own_expert, router, routed_weights, shared_weights=()):
    size = blocks[0].shape[0]
    width = router.shape[1]
    units = sum(each.shape[0] for each in (*routed_weights, *shared_weights) if each.ndim == 2)
    operands = [*blocks, own_expert, router, *routed_weights, *shared_weights]
    return pl.pallas_call(
        functools.partial(expert_kernel, bool(shared_weights)),
        out_shape=(
            jax.ShapeDtypeStruct((2, size, width), jnp.float32),
            jax.ShapeDtypeStruct((2, size, width), jnp.bfloat16),
        ),
        in_specs=[WHOLE] * len(operands),
        out_specs=(WHOLE, WHOLE),
        compiler_params=params(32),
        cost_estimate=pl.CostEstimate(
            flops=24 * size * width * units,
            bytes_accessed=6 * width * units,
            transcendentals=4 * size * units,
        ),
        name="experts",
    )(*operands)


def swap(values, axis, size, bits):
    return lax.ppermute(values, axis, [(i, i ^ bits) for i in range(size)])


def body(
    sizes,
    hidden,
    latent_cache,
    lengths,
    parents,
    routes,
    accepted,
    input_gain,
    query_weight,
    latent_weight,
    latent_gain,
    key_absorb,
    value_absorb,
    output_weight,
    post_gain,
    router_weight,
    shared_gate_up,
    shared_down,
    expert_gate_up,
    expert_down,
):
    n_req, n_row, n_col = sizes
    experts = router_weight.shape[1]
    req_index = lax.axis_index("req")
    row_index = lax.axis_index("row")
    bf16 = jnp.bfloat16

    far = swap(hidden, "row", n_row, 2)
    near = swap(hidden, "row", n_row, 1)
    far_near = swap(far, "row", n_row, 1)

    row_scalar = row_index.astype(jnp.int32).reshape(1)
    tables = tree_tables(row_scalar, lengths, accepted, parents)
    cache = jnp.swapaxes(latent_cache, 1, 2)
    weights = (
        input_gain[None],
        query_weight,
        latent_weight.T,
        latent_gain[None],
        key_absorb,
        value_absorb,
        output_weight,
    )
    own_keep, own_send, accepted_latents = attention_part(
        True, 0, row_scalar, lengths, (hidden, near), cache, tables, weights
    )
    far_keep, far_send = attention_part(
        False, 2, row_scalar, lengths, (far, far_near), cache, tables, weights
    )

    def fold(keep, sent):
        return keep + swap(sent, "row", n_row, 1).astype(jnp.float32)

    from_far = swap(fold(far_keep, far_send).astype(bf16), "row", n_row, 2)
    partial = fold(own_keep, own_send) + from_far.astype(jnp.float32)
    partial, arrived = col_parts(partial, n_col)
    named = (routes[:, :, None] == jnp.arange(EXTRA, dtype=jnp.int32)).any(axis=1).astype(bf16)
    residual, block = joined(hidden, partial, arrived, post_gain[None], named)

    own_expert = jnp.arange(experts, dtype=jnp.int32) == req_index * n_row + row_index
    own_expert = own_expert.astype(jnp.float32)[None]
    router = router_weight.T
    routed_weights = (jnp.swapaxes(expert_gate_up[0], 1, 2), expert_down[0])
    shared_weights = (jnp.swapaxes(shared_gate_up, 1, 2), shared_down)
    distances = [*range(n_req - 1, 0, -1)]
    blocks = {s: swap(block, "req", n_req, s) for s in distances}
    blocks[0] = block
    total = None
    for s in [0, *distances]:
        far = swap(blocks[s], "row", n_row, 2)
        near = swap(blocks[s], "row", n_row, 1)
        far_near = swap(far, "row", n_row, 1)
        keep, send = expert_part(
            (blocks[s], far, near, far_near),
            own_expert,
            router,
            routed_weights,
            () if s else shared_weights,
        )
        from_near = swap(send, "row", n_row, 1).astype(jnp.float32)
        from_far = swap((keep[1] + from_near[1]).astype(bf16), "row", n_row, 2)
        part = keep[0] + from_near[0] + from_far.astype(jnp.float32)
        if s:
            part = swap(part.astype(bf16), "req", n_req, s).astype(jnp.float32)
        total = part if total is None else total + part
    total, arrived = col_parts(total, n_col)
    layer_output = residual + (total.astype(jnp.float32) + sum_up(arrived))
    return (layer_output.astype(bf16), accepted_latents)


def sum_up(parts):
    return jnp.sum(parts.astype(jnp.float32), axis=0)


def col_parts(values, n_col):
    bits = 1
    while 2 * bits < n_col:
        sent = values.astype(jnp.bfloat16)
        values = sent.astype(jnp.float32) + swap(sent, "col", n_col, bits).astype(jnp.float32)
        bits *= 2
    sent = values.astype(jnp.bfloat16)
    return sent, swap(sent, "col", n_col, bits)[None]


def solution(mesh):
    placed = (
        P(("req", "row"), None),
        P("req", None, None),
        P("req"),
        P("req", None),
        P(("req", "row"), None),
        P(("req", "row")),
        P(),
        P(None, ("row", "col")),
        P(),
        P(),
        P(("row", "col"), None, None),
        P(("row", "col"), None, None),
        P(("row", "col"), None),
        P(),
        P(),
        P(None, None, ("row", "col")),
        P(("row", "col"), None),
        P(("req", "row"), None, None, "col"),
        P(("req", "row"), "col", None),
    )
    sizes = (mesh.shape["req"], mesh.shape["row"], mesh.shape["col"])
    return jax.shard_map(
        functools.partial(body, sizes),
        mesh=mesh,
        in_specs=placed,
        out_specs=(P(("req", "row"), None), P(("req", "row"), None, None)),
        check_vma=False,
    )
```

time: 233 us -> 165 us (0.71)
  the two profiles are of different devices: /device:TPU:0 before, /device:TPU:8 now
where the time goes in v3:
time: 165 us
  waiting for transfers between devices  81.3 us (49%)
  starting transfers between devices  32.5 us (20%)
  Pallas kernels  29.2 us (18%)
  local copies, waits for them, and re-layouts  18.2 us (11%)
  other arithmetic  2.1 us (1%)
    ppermute x34, waiting for transfers between devices, swap(): return lax.ppermute(values, axis, [(i, i ^ bits) for i in range(size)])  81.3 us
    ppermute x34, starting transfers between devices, swap(): return lax.ppermute(values, axis, [(i, i ^ bits) for i in range(size)])  32.5 us
    unnamed x56, local copies, waits for them, and re-layouts  18.2 us
    pallas_call x4, Pallas kernels, expert_part(): pl.pallas_call(functools.partial(expert_kernel, bool(shared_weights)), ou...  17.8 us
    pallas_call x2, Pallas kernels, attention_part(): pl.pallas_call(functools.partial(attention_kernel, first, place), out_sha...  8.25 us
  transfers between devices with their start and end apart: 34, of which 13 were waited for; matrix products, arithmetic and copies ran while one was open for 1% of the time, Pallas kernels for 17%

profile of v3, /device:TPU:8, one launch (start us, length us, event | category | flops | bytes accessed | tf_op | source)
XLA Modules:
  0.0 164.8 jit_solution(8898724288866843654)
XLA Ops:
  0.6 1.6 collective-permute-start.2
  2.2 6.7 %collective-permute-done.2.refs_0_ = bf16[64,2048]{1,0:T(8,128)(2,1)S(1)} collective-permute-done((bf16[64,2048]{1,0:T(8,128)(2,1)}, bf16[64,2048]{1,0:T(8,128)(2,1)S(1)}, u32[]{:S(2)}, u32[]{:S(2)}) %collective-permute-start.2) | collective-permute-done | bytes 262176 | tf_op jit(solution)/shard_map/ppermute | solution.py:318
  9.0 0.5 collective-permute-start
  10.1 0.6 copy-done.22
  10.8 0.7 copy-done.24
  11.5 2.1 %trees.1 = (f32[4,64,64]{2,1,0:T(8,128)S(1)}, f32[4,64,64]{2,1,0:T(8,128)S(1)}, bf16[64,64]{1,0:T(8,128)(2,1)S(1)}) custom-call(s32[1]{0:T(128)} %bitcast.row_ref, s32[4]{0:T(128)S(1)} %copy-done.22, s32[1]{0:T(128)S(6)} %copy.22.accepted_ref, s32[4,64]{1,0:T(4,128)S(1)} %copy-done.24), custom_call_target="tpu_custom_call" | custom-call | tf_op jit(solution)/shard_map/trees/pallas_call | solution.py:100
  13.6 1.5 copy-done.3
  15.1 1.7 %copy-done.5 = bf16[2048,576]{0,1:T(8,128)(2,1)S(1)} copy-done((bf16[2048,576]{0,1:T(8,128)(2,1)S(1)}, bf16[2048,576]{0,1:T(8,128)(2,1)}, u32[]{:S(2)}) %copy-start.5) | copy-done | bytes 2359320
  16.8 1.4 copy-done.7
  18.2 1.2 copy-done.8
  19.4 0.9 copy-done.13
  20.3 0.9 copy-done.14
  21.3 0.7 copy-done.18
  22.0 0.7 copy-done.21
  22.7 0.7 copy-done.23
  23.3 3.8 %attention.3 = (f32[64,2048]{1,0:T(8,128)S(1)}, bf16[64,2048]{1,0:T(8,128)(2,1)S(1)}) custom-call(s32[1]{0:T(128)} %bitcast.row_ref, s32[4]{0:T(128)S(1)} %copy-done.23, bf16[64,2048]{1,0:T(8,128)(2,1)S(1)} %collective-permute-done.2.refs_0_, bf16[64,2048]{1,0:T(8,128)(2,1)S(1)} %collective-permute-done.3.refs_1_, bf16[4,576,384]{2,1,0:T(8,128)(2,1)S(1)} %bitcast.61, ...), custom_call_target="tpu_custom_call" | custom-call | flops 637534208 | bytes 4980736 | tf_op jit(solution)/shard_map/attention/pallas_call | solution.py:213
  27.3 4.4 %attention.2 = (f32[64,2048]{1,0:T(8,128)S(1)}, bf16[64,2048]{1,0:T(8,128)(2,1)S(1)}, bf16[1,64,576]{2,1,0:T(8,128)(2,1)}) custom-call(s32[1]{0:T(128)} %bitcast.row_ref, s32[4]{0:T(128)S(1)} %copy-done.23, bf16[64,2048]{1,0:T(8,128)(2,1)S(1)} %copy-done.15, bf16[64,2048]{1,0:T(8,128)(2,1)S(1)} %collective-permute-done.refs_1_, ...), custom_call_target="tpu_custom_call" | custom-call | flops 637534208 | bytes 4980736 | tf_op jit(solution)/shard_map/attention/pallas_call | solution.py:213
  31.8 0.5 collective-permute-start.1
  32.4 1.6 collective-permute-start.5
  33.9 6.7 %collective-permute-done.5 = bf16[64,2048]{1,0:T(8,128)(2,1)S(1)} collective-permute-done((bf16[64,2048]{1,0:T(8,128)(2,1)S(1)}, bf16[64,2048]{1,0:T(8,128)(2,1)S(1)}, u32[]{:S(2)}, u32[]{:S(2)}) %collective-permute-start.5) | collective-permute-done | bytes 262176 | tf_op jit(solution)/shard_map/ppermute | solution.py:318
  40.8 1.5 collective-permute-start.6
  42.4 5.8 %collective-permute-done.6 = bf16[64,2048]{1,0:T(8,128)(2,1)S(1)} collective-permute-done((bf16[64,2048]{1,0:T(8,128)(2,1)S(1)}, bf16[64,2048]{1,0:T(8,128)(2,1)S(1)}, u32[]{:S(2)}, u32[]{:S(2)}) %collective-permute-start.6) | collective-permute-done | bytes 262176 | tf_op jit(solution)/shard_map/ppermute | solution.py:318
  48.2 0.9 join.1
  49.2 0.8 copy-done.16
  50.0 1.5 collective-permute-start.7
  51.5 0.4 collective-permute-start.26
  51.9 2.6 %collective-permute-start.19 = (bf16[64,2176]{1,0:T(8,128)(2,1)}, bf16[64,2176]{1,0:T(8,128)(2,1)}, u32[]{:S(2)}, u32[]{:S(2)}) collective-permute-start(bf16[64,2176]{1,0:T(8,128)(2,1)} %get-tuple-element.28.refs_0_), channel_id=1, source_target_pairs={{0,16},{8,24},{16,0},{24,8},{1,17},{9,25},{17,1},{25,9},{2,18},{10... | collective-permute-start | bytes 835592 | tf_op jit(solution)/shard_map/ppermute | solution.py:318
  54.5 0.4 collective-permute-start.12
  55.0 2.1 %collective-permute-done.7.refs_1_ = bf16[64,2176]{1,0:T(8,128)(2,1)} collective-permute-done((bf16[64,2176]{1,0:T(8,128)(2,1)}, bf16[64,2176]{1,0:T(8,128)(2,1)}, u32[]{:S(2)}, u32[]{:S(2)}) %collective-permute-start.7) | collective-permute-done | bytes 278560 | tf_op jit(solution)/shard_map/ppermute | solution.py:318
  57.1 4.3 %collective-permute-done.26.refs_0_ = bf16[64,2176]{1,0:T(8,128)(2,1)} collective-permute-done((bf16[64,2176]{1,0:T(8,128)(2,1)}, bf16[64,2176]{1,0:T(8,128)(2,1)}, u32[]{:S(2)}, u32[]{:S(2)}) %collective-permute-start.26) | collective-permute-done | bytes 278560 | tf_op jit(solution)/shard_map/ppermute | solution.py:318
  61.4 0.5 collective-permute-start.27
  61.9 11.2 %collective-permute-done.19.refs_0_ = bf16[64,2176]{1,0:T(8,128)(2,1)} collective-permute-done((bf16[64,2176]{1,0:T(8,128)(2,1)}, bf16[64,2176]{1,0:T(8,128)(2,1)}, u32[]{:S(2)}, u32[]{:S(2)}) %collective-permute-start.19) | collective-permute-done | bytes 278560 | tf_op jit(solution)/shard_map/ppermute | solution.py:318
  73.1 0.5 collective-permute-start.20
  73.6 3.8 %collective-permute-done.12.refs_0_ = bf16[64,2176]{1,0:T(8,128)(2,1)S(1)} collective-permute-done((bf16[64,2176]{1,0:T(8,128)(2,1)}, bf16[64,2176]{1,0:T(8,128)(2,1)S(1)}, u32[]{:S(2)}, u32[]{:S(2)}) %collective-permute-start.12) | collective-permute-done | bytes 278560 | tf_op jit(solution)/shard_map/ppermute | solution.py:318
  77.4 0.5 collective-permute-start.13
  77.9 0.2 collective-permute-start.29
  78.1 1.8 %collective-permute-done.20.refs_1_ = bf16[64,2176]{1,0:T(8,128)(2,1)} collective-permute-done((bf16[64,2176]{1,0:T(8,128)(2,1)}, bf16[64,2176]{1,0:T(8,128)(2,1)}, u32[]{:S(2)}, u32[]{:S(2)}) %collective-permute-start.20) | collective-permute-done | bytes 278560 | tf_op jit(solution)/shard_map/ppermute | solution.py:318
  80.0 2.6 %copy-done = bf16[1,2,2048,704]{2,3,1,0:T(8,128)(2,1)S(1)} copy-done((bf16[1,2,2048,704]{2,3,1,0:T(8,128)(2,1)S(1)}, bf16[1,2,2048,704]{2,3,1,0:T(8,128)(2,1)}, u32[]{:S(2)}) %copy-start) | copy-done | bytes 5767192
  82.6 1.8 %copy-done.1 = bf16[1,704,2048]{2,1,0:T(8,128)(2,1)S(1)} copy-done((bf16[1,704,2048]{2,1,0:T(8,128)(2,1)S(1)}, bf16[1,704,2048]{2,1,0:T(8,128)(2,1)}, u32[]{:S(2)}) %copy-start.1) | copy-done | bytes 2883608
  84.4 1.8 %copy-done.10 = bf16[2,2048,352]{1,2,0:T(8,128)(2,1)S(1)} copy-done((bf16[2,2048,352]{1,2,0:T(8,128)(2,1)S(1)}, bf16[2,2048,352]{1,2,0:T(8,128)(2,1)}, u32[]{:S(2)}) %copy-start.10) | copy-done | bytes 2883608
  86.2 5.9 %experts.4 = (f32[2,64,2048]{2,1,0:T(8,128)S(1)}, bf16[2,64,2048]{2,1,0:T(8,128)(2,1)S(1)}) custom-call(bf16[64,2176]{1,0:T(8,128)(2,1)} %get-tuple-element.28.refs_0_, bf16[64,2176]{1,0:T(8,128)(2,1)} %collective-permute-done.7.refs_1_, bf16[64,2176]{1,0:T(8,128)(2,1)} %collective-permute-done.8.refs_2_, bf16[64,2176]{1,0:T(8,128)(2,1)} %collective-permute-done.9.refs_3_, ...), custom_call_target="tpu_custom_call" | custom-call | flops 3321888768 | bytes 12976128 | tf_op jit(solution)/shard_map/experts/pallas_call | solution.py:299
  92.1 0.6 collective-permute-start.14
  92.8 0.4 collective-permute-start.15
  93.2 4.5 %experts.7 = (f32[2,64,2048]{2,1,0:T(8,128)S(1)}, bf16[2,64,2048]{2,1,0:T(8,128)(2,1)S(1)}) custom-call(bf16[64,2176]{1,0:T(8,128)(2,1)} %collective-permute-done.26.refs_0_, bf16[64,2176]{1,0:T(8,128)(2,1)} %collective-permute-done.27.refs_1_, bf16[64,2176]{1,0:T(8,128)(2,1)S(1)} %collective-permute-done.28.refs_2_, ...), custom_call_target="tpu_custom_call" | custom-call | flops 2214592512 | bytes 8650752 | tf_op jit(solution)/shard_map/experts/pallas_call | solution.py:299
  97.7 0.1 collective-permute-start.30
  97.9 4.2 %experts.6 = (f32[2,64,2048]{2,1,0:T(8,128)S(1)}, bf16[2,64,2048]{2,1,0:T(8,128)(2,1)S(1)}) custom-call(bf16[64,2176]{1,0:T(8,128)(2,1)} %collective-permute-done.19.refs_0_, bf16[64,2176]{1,0:T(8,128)(2,1)} %collective-permute-done.20.refs_1_, bf16[64,2176]{1,0:T(8,128)(2,1)S(1)} %collective-permute-done.21.refs_2_, ...), custom_call_target="tpu_custom_call" | custom-call | flops 2214592512 | bytes 8650752 | tf_op jit(solution)/shard_map/experts/pallas_call | solution.py:299
  102.1 0.5 collective-permute-start.23
  102.6 3.2 %experts.5 = (f32[2,64,2048]{2,1,0:T(8,128)S(1)}, bf16[2,64,2048]{2,1,0:T(8,128)(2,1)S(1)}) custom-call(bf16[64,2176]{1,0:T(8,128)(2,1)S(1)} %collective-permute-done.12.refs_0_, bf16[64,2176]{1,0:T(8,128)(2,1)S(1)} %collective-permute-done.13.refs_1_, bf16[64,2176]{1,0:T(8,128)(2,1)S(1)} %collective-permute-done.14.refs_2_, ...), custom_call_target="tpu_custom_call" | custom-call | flops 2214592512 | bytes 8650752 | tf_op jit(solution)/shard_map/experts/pallas_call | solution.py:299
  105.9 0.1 collective-permute-start.16
  106.2 0.6 collective-permute-start.11
  106.9 1.6 collective-permute-start.31
  108.7 0.6 collective-permute-start.24
  109.4 1.6 collective-permute-start.17
  111.0 9.9 %collective-permute-done.31 = bf16[64,2048]{1,0:T(8,128)(2,1)S(1)} collective-permute-done((bf16[64,2048]{1,0:T(8,128)(2,1)S(1)}, bf16[64,2048]{1,0:T(8,128)(2,1)S(1)}, u32[]{:S(2)}, u32[]{:S(2)}) %collective-permute-start.31) | collective-permute-done | bytes 262176 | tf_op jit(solution)/shard_map/ppermute | solution.py:318
  121.0 5.3 %collective-permute-start.32 = (bf16[64,2048]{1,0:T(8,128)(2,1)S(1)}, bf16[64,2048]{1,0:T(8,128)(2,1)S(1)}, u32[]{:S(2)}, u32[]{:S(2)}) collective-permute-start(bf16[64,2048]{1,0:T(8,128)(2,1)S(1)} %fusion.3), channel_id=1, source_target_pairs={{0,8},{8,0},{16,24},{24,16},{1,9},{9,1},{17,25},{25,17},{2,10},{10... | collective-permute-start | bytes 786440 | tf_op jit(solution)/shard_map/ppermute | solution.py:318
  126.4 0.2 collective-permute-done.24
  126.6 6.4 %collective-permute-start.25 = (bf16[64,2048]{1,0:T(8,128)(2,1)S(1)}, bf16[64,2048]{1,0:T(8,128)(2,1)S(1)}, u32[]{:S(2)}, u32[]{:S(2)}) collective-permute-start(bf16[64,2048]{1,0:T(8,128)(2,1)S(1)} %fusion.7), channel_id=1, source_target_pairs={{0,16},{8,24},{16,0},{24,8},{1,17},{9,25},{17,1},{25,9},{2,18},{10... | collective-permute-start | bytes 786440 | tf_op jit(solution)/shard_map/ppermute | solution.py:318
  133.1 0.5 collective-permute-start.18
  133.6 14.4 %collective-permute-done.25 = bf16[64,2048]{1,0:T(8,128)(2,1)S(1)} collective-permute-done((bf16[64,2048]{1,0:T(8,128)(2,1)S(1)}, bf16[64,2048]{1,0:T(8,128)(2,1)S(1)}, u32[]{:S(2)}, u32[]{:S(2)}) %collective-permute-start.25) | collective-permute-done | bytes 262176 | tf_op jit(solution)/shard_map/ppermute | solution.py:318
  148.0 7.6 %collective-permute-done.18 = bf16[64,2048]{1,0:T(8,128)(2,1)S(1)} collective-permute-done((bf16[64,2048]{1,0:T(8,128)(2,1)S(1)}, bf16[64,2048]{1,0:T(8,128)(2,1)S(1)}, u32[]{:S(2)}, u32[]{:S(2)}) %collective-permute-start.18) | collective-permute-done | bytes 262176 | tf_op jit(solution)/shard_map/ppermute | solution.py:318
  155.6 0.2 fusion.18
  155.7 1.5 collective-permute-start.33
  157.3 6.7 %collective-permute-done.33 = bf16[64,2048]{1,0:T(8,128)(2,1)S(1)} collective-permute-done((bf16[64,2048]{1,0:T(8,128)(2,1)S(1)}, bf16[64,2048]{1,0:T(8,128)(2,1)S(1)}, u32[]{:S(2)}, u32[]{:S(2)}) %collective-permute-start.33) | collective-permute-done | bytes 262176 | tf_op jit(solution)/shard_map/ppermute | solution.py:318
  164.0 0.8 add_convert_fusion
  (87 shorter events, 1.4 us)
Async XLA Ops:
  0.6 8.3 %collective-permute-start.2 = (bf16[64,2048]{1,0:T(8,128)(2,1)}, bf16[64,2048]{1,0:T(8,128)(2,1)S(1)}, u32[]{:S(2)}, u32[]{:S(2)}) collective-permute-start(bf16[64,2048]{1,0:T(8,128)(2,1)} %hidden_ref.1), channel_id=1, source_target_pairs={{0,4},{2,6},{4,0},{6,2},{1,5},{3,7},{5,1},{7,3},{8,12},{10,14},{12... | collective-permute-start | bytes 786440 | tf_op jit(solution)/shard_map/ppermute | solution.py:318
  9.0 4.6 %collective-permute-start.3 = (bf16[64,2048]{1,0:T(8,128)(2,1)S(1)}, bf16[64,2048]{1,0:T(8,128)(2,1)S(1)}, u32[]{:S(2)}, u32[]{:S(2)}) collective-permute-start(bf16[64,2048]{1,0:T(8,128)(2,1)S(1)} %collective-permute-done.2.refs_0_), channel_id=1, source_target_pairs={{0,2},{2,0},{4,6},{6,4},{1,3},{3,1},{5,7},{7,5},{8,10},{10,8},{12,... | collective-permute-start | bytes 786440 | tf_op jit(solution)/shard_map/ppermute | solution.py:318
  9.0 18.3 %collective-permute-start = (bf16[64,2048]{1,0:T(8,128)(2,1)}, bf16[64,2048]{1,0:T(8,128)(2,1)S(1)}, u32[]{:S(2)}, u32[]{:S(2)}) collective-permute-start(bf16[64,2048]{1,0:T(8,128)(2,1)} %hidden_ref.1), channel_id=1, source_target_pairs={{0,2},{2,0},{4,6},{6,4},{1,3},{3,1},{5,7},{7,5},{8,10},{10,8},{12,... | collective-permute-start | bytes 786440 | tf_op jit(solution)/shard_map/ppermute | solution.py:318
  10.1 0.7 copy-start.22
  10.8 0.7 copy-start.24
  13.6 1.5 copy-start.3
  15.1 1.7 %copy-start.5 = (bf16[2048,576]{0,1:T(8,128)(2,1)S(1)}, bf16[2048,576]{0,1:T(8,128)(2,1)}, u32[]{:S(2)}) copy-start(bf16[2048,576]{0,1:T(8,128)(2,1)} %param.27) | copy-start | bytes 7077892
  16.8 1.4 copy-start.7
  18.2 1.2 copy-start.8
  19.4 0.9 copy-start.13
  20.3 0.9 copy-start.14
  21.3 0.7 copy-start.18
  22.0 0.7 copy-start.21
  22.7 0.7 copy-start.23
  23.3 4.0 %copy-start.4 = (bf16[4,384,576]{1,2,0:T(8,128)(2,1)S(1)}, bf16[4,384,576]{1,2,0:T(8,128)(2,1)}, u32[]{:S(2)}) copy-start(bf16[4,384,576]{1,2,0:T(8,128)(2,1)} %param.20) | copy-start | bytes 5308420
  23.3 4.0 %copy-start.6 = (bf16[2048,576]{0,1:T(8,128)(2,1)S(1)}, bf16[2048,576]{0,1:T(8,128)(2,1)}, u32[]{:S(2)}) copy-start(bf16[2048,576]{0,1:T(8,128)(2,1)} %param.27) | copy-start | bytes 7077892
  23.3 4.0 %copy-start.9 = (bf16[256,2048]{1,0:T(8,128)(2,1)S(1)}, bf16[256,2048]{1,0:T(8,128)(2,1)}, u32[]{:S(2)}) copy-start(bf16[256,2048]{1,0:T(8,128)(2,1)} %refs_13_.3) | copy-start | bytes 3145732
  23.3 4.0 %copy-start.15 = (bf16[64,2048]{1,0:T(8,128)(2,1)S(1)}, bf16[64,2048]{1,0:T(8,128)(2,1)}, u32[]{:S(2)}) copy-start(bf16[64,2048]{1,0:T(8,128)(2,1)} %hidden_ref.1) | copy-start | bytes 786436
  23.3 4.0 %copy-start.19 = (f32[2048]{0:T(1024)S(1)}, f32[2048]{0:T(1024)}, u32[]{:S(2)}) copy-start(f32[2048]{0:T(1024)} %param.25) | copy-start | bytes 24580
  27.2 5.1 %collective-permute-start.4 = (bf16[64,2048]{1,0:T(8,128)(2,1)S(1)}, bf16[64,2048]{1,0:T(8,128)(2,1)S(1)}, u32[]{:S(2)}, u32[]{:S(2)}) collective-permute-start(bf16[64,2048]{1,0:T(8,128)(2,1)S(1)} %get-tuple-element.26), channel_id=1, source_target_pairs={{0,2},{2,0},{4,6},{6,4},{1,3},{3,1},{5,7},{7,5},{8,10},{10,8},{12,... | collective-permute-start | bytes 786440 | tf_op jit(solution)/shard_map/ppermute | solution.py:318
  31.7 10.6 %copy-start.25 = (s32[64,6]{0,1:T(8,128)S(1)}, s32[64,6]{0,1:T(8,128)}, u32[]{:S(2)}) copy-start(s32[64,6]{0,1:T(8,128)} %param.23) | copy-start | bytes 4612
  31.7 16.5 %copy-start.20 = (f32[2048]{0:T(1024)S(1)}, f32[2048]{0:T(1024)}, u32[]{:S(2)}) copy-start(f32[2048]{0:T(1024)} %param.32) | copy-start | bytes 24580
  31.7 48.2 %copy-start.11 = (bf16[352,2048]{1,0:T(8,128)(2,1)S(1)}, bf16[352,2048]{1,0:T(8,128)(2,1)}, u32[]{:S(2)}) copy-start(bf16[352,2048]{1,0:T(8,128)(2,1)} %refs_9_.1) | copy-start | bytes 4325380
  31.7 48.2 %copy-start.12 = (bf16[2048,16]{0,1:T(8,128)(2,1)S(1)}, bf16[2048,16]{0,1:T(8,128)(2,1)}, u32[]{:S(2)}) copy-start(bf16[2048,16]{0,1:T(8,128)(2,1)} %param.33) | copy-start | bytes 196612
  31.8 2.2 %collective-permute-start.1 = (bf16[64,2048]{1,0:T(8,128)(2,1)S(1)}, bf16[64,2048]{1,0:T(8,128)(2,1)S(1)}, u32[]{:S(2)}, u32[]{:S(2)}) collective-permute-start(bf16[64,2048]{1,0:T(8,128)(2,1)S(1)} %get-tuple-element.24), channel_id=1, source_target_pairs={{0,2},{2,0},{4,6},{6,4},{1,3},{3,1},{5,7},{7,5},{8,10},{10,8},{12,... | collective-permute-start | bytes 786440 | tf_op jit(solution)/shard_map/ppermute | solution.py:318
  32.3 60.9 %slice-start = ((s8[5767168]{0:T(1024)(128)(4,1)}), s8[1572864]{0:T(1024)(128)(4,1)S(1)}, s32[]{:S(2)}) async-start(s8[5767168]{0:T(1024)(128)(4,1)} %bitcast.52), calls=%async_computation | async-start | bytes 3145728
  32.4 8.3 %collective-permute-start.5 = (bf16[64,2048]{1,0:T(8,128)(2,1)S(1)}, bf16[64,2048]{1,0:T(8,128)(2,1)S(1)}, u32[]{:S(2)}, u32[]{:S(2)}) collective-permute-start(bf16[64,2048]{1,0:T(8,128)(2,1)S(1)} %add_convert_fusion.2), channel_id=1, source_target_pairs={{0,4},{2,6},{4,0},{6,2},{1,5},{3,7},{5,1},{7,3},{8,12},{10,14},{12... | collective-permute-start | bytes 786440 | tf_op jit(solution)/shard_map/ppermute | solution.py:318
  40.8 7.5 %collective-permute-start.6 = (bf16[64,2048]{1,0:T(8,128)(2,1)S(1)}, bf16[64,2048]{1,0:T(8,128)(2,1)S(1)}, u32[]{:S(2)}, u32[]{:S(2)}) collective-permute-start(bf16[64,2048]{1,0:T(8,128)(2,1)S(1)} %add_convert_fusion.1.keep_ref), channel_id=1, source_target_pairs={{0,1},{1,0},{2,3},{3,2},{4,5},{5,4},{6,7},{7,6},{8,9},{9,8},{10,11... | collective-permute-start | bytes 786440 | tf_op jit(solution)/shard_map/ppermute | solution.py:318
  49.2 0.8 copy-start.16
  50.0 7.1 %collective-permute-start.7 = (bf16[64,2176]{1,0:T(8,128)(2,1)}, bf16[64,2176]{1,0:T(8,128)(2,1)}, u32[]{:S(2)}, u32[]{:S(2)}) collective-permute-start(bf16[64,2176]{1,0:T(8,128)(2,1)} %get-tuple-element.28.refs_0_), channel_id=1, source_target_pairs={{0,4},{2,6},{4,0},{6,2},{1,5},{3,7},{5,1},{7,3},{8,12},{10,14},{12... | collective-permute-start | bytes 835592 | tf_op jit(solution)/shard_map/ppermute | solution.py:318
  51.5 9.9 %collective-permute-start.26 = (bf16[64,2176]{1,0:T(8,128)(2,1)}, bf16[64,2176]{1,0:T(8,128)(2,1)}, u32[]{:S(2)}, u32[]{:S(2)}) collective-permute-start(bf16[64,2176]{1,0:T(8,128)(2,1)} %get-tuple-element.28.refs_0_), channel_id=1, source_target_pairs={{0,8},{8,0},{16,24},{24,16},{1,9},{9,1},{17,25},{25,17},{2,10},{10... | collective-permute-start | bytes 835592 | tf_op jit(solution)/shard_map/ppermute | solution.py:318
  51.9 21.1 %collective-permute-start.19 = (bf16[64,2176]{1,0:T(8,128)(2,1)}, bf16[64,2176]{1,0:T(8,128)(2,1)}, u32[]{:S(2)}, u32[]{:S(2)}) collective-permute-start(bf16[64,2176]{1,0:T(8,128)(2,1)} %get-tuple-element.28.refs_0_), channel_id=1, source_target_pairs={{0,16},{8,24},{16,0},{24,8},{1,17},{9,25},{17,1},{25,9},{2,18},{10... | collective-permute-start | bytes 835592 | tf_op jit(solution)/shard_map/ppermute | solution.py:318
  54.5 19.1 %collective-permute-start.8 = (bf16[64,2176]{1,0:T(8,128)(2,1)}, bf16[64,2176]{1,0:T(8,128)(2,1)}, u32[]{:S(2)}, u32[]{:S(2)}) collective-permute-start(bf16[64,2176]{1,0:T(8,128)(2,1)} %get-tuple-element.28.refs_0_), channel_id=1, source_target_pairs={{0,2},{2,0},{4,6},{6,4},{1,3},{3,1},{5,7},{7,5},{8,10},{10,8},{12,... | collective-permute-start | bytes 835592 | tf_op jit(solution)/shard_map/ppermute | solution.py:318
  54.5 22.9 %collective-permute-start.12 = (bf16[64,2176]{1,0:T(8,128)(2,1)}, bf16[64,2176]{1,0:T(8,128)(2,1)S(1)}, u32[]{:S(2)}, u32[]{:S(2)}) collective-permute-start(bf16[64,2176]{1,0:T(8,128)(2,1)} %get-tuple-element.28.refs_0_), channel_id=1, source_target_pairs={{0,24},{8,16},{16,8},{24,0},{1,25},{9,17},{17,9},{25,1},{2,26},{10... | collective-permute-start | bytes 835592 | tf_op jit(solution)/shard_map/ppermute | solution.py:318
  57.1 20.3 %collective-permute-start.9 = (bf16[64,2176]{1,0:T(8,128)(2,1)}, bf16[64,2176]{1,0:T(8,128)(2,1)}, u32[]{:S(2)}, u32[]{:S(2)}) collective-permute-start(bf16[64,2176]{1,0:T(8,128)(2,1)} %collective-permute-done.7.refs_1_), channel_id=1, source_target_pairs={{0,2},{2,0},{4,6},{6,4},{1,3},{3,1},{5,7},{7,5},{8,10},{10,8},{12,... | collective-permute-start | bytes 835592 | tf_op jit(solution)/shard_map/ppermute | solution.py:318
  61.4 16.5 %collective-permute-start.27 = (bf16[64,2176]{1,0:T(8,128)(2,1)}, bf16[64,2176]{1,0:T(8,128)(2,1)}, u32[]{:S(2)}, u32[]{:S(2)}) collective-permute-start(bf16[64,2176]{1,0:T(8,128)(2,1)} %collective-permute-done.26.refs_0_), channel_id=1, source_target_pairs={{0,4},{2,6},{4,0},{6,2},{1,5},{3,7},{5,1},{7,3},{8,12},{10,14},{12... | collective-permute-start | bytes 835592 | tf_op jit(solution)/shard_map/ppermute | solution.py:318
  73.1 6.9 %collective-permute-start.20 = (bf16[64,2176]{1,0:T(8,128)(2,1)}, bf16[64,2176]{1,0:T(8,128)(2,1)}, u32[]{:S(2)}, u32[]{:S(2)}) collective-permute-start(bf16[64,2176]{1,0:T(8,128)(2,1)} %collective-permute-done.19.refs_0_), channel_id=1, source_target_pairs={{0,4},{2,6},{4,0},{6,2},{1,5},{3,7},{5,1},{7,3},{8,12},{10,14},{12... | collective-permute-start | bytes 835592 | tf_op jit(solution)/shard_map/ppermute | solution.py:318
  73.6 18.6 %collective-permute-start.28 = (bf16[64,2176]{1,0:T(8,128)(2,1)}, bf16[64,2176]{1,0:T(8,128)(2,1)S(1)}, u32[]{:S(2)}, u32[]{:S(2)}) collective-permute-start(bf16[64,2176]{1,0:T(8,128)(2,1)} %collective-permute-done.26.refs_0_), channel_id=1, source_target_pairs={{0,2},{2,0},{4,6},{6,4},{1,3},{3,1},{5,7},{7,5},{8,10},{10,8},{12,... | collective-permute-start | bytes 835592 | tf_op jit(solution)/shard_map/ppermute | solution.py:318
  77.4 20.3 %collective-permute-start.21 = (bf16[64,2176]{1,0:T(8,128)(2,1)}, bf16[64,2176]{1,0:T(8,128)(2,1)S(1)}, u32[]{:S(2)}, u32[]{:S(2)}) collective-permute-start(bf16[64,2176]{1,0:T(8,128)(2,1)} %collective-permute-done.19.refs_0_), channel_id=1, source_target_pairs={{0,2},{2,0},{4,6},{6,4},{1,3},{3,1},{5,7},{7,5},{8,10},{10,8},{12,... | collective-permute-start | bytes 835592 | tf_op jit(solution)/shard_map/ppermute | solution.py:318
  77.4 15.3 %collective-permute-start.13 = (bf16[64,2176]{1,0:T(8,128)(2,1)S(1)}, bf16[64,2176]{1,0:T(8,128)(2,1)S(1)}, u32[]{:S(2)}, u32[]{:S(2)}) collective-permute-start(bf16[64,2176]{1,0:T(8,128)(2,1)S(1)} %collective-permute-done.12.refs_0_), channel_id=1, source_target_pairs={{0,4},{2,6},{4,0},{6,2},{1,5},{3,7},{5,1},{7,3},{8,12},{10,14},{12... | collective-permute-start | bytes 835592 | tf_op jit(solution)/shard_map/ppermute | solution.py:318
  77.9 14.9 %collective-permute-start.29 = (bf16[64,2176]{1,0:T(8,128)(2,1)}, bf16[64,2176]{1,0:T(8,128)(2,1)S(1)}, u32[]{:S(2)}, u32[]{:S(2)}) collective-permute-start(bf16[64,2176]{1,0:T(8,128)(2,1)} %collective-permute-done.27.refs_1_), channel_id=1, source_target_pairs={{0,2},{2,0},{4,6},{6,4},{1,3},{3,1},{5,7},{7,5},{8,10},{10,8},{12,... | collective-permute-start | bytes 835592 | tf_op jit(solution)/shard_map/ppermute | solution.py:318
  79.9 17.9 %collective-permute-start.22 = (bf16[64,2176]{1,0:T(8,128)(2,1)}, bf16[64,2176]{1,0:T(8,128)(2,1)S(1)}, u32[]{:S(2)}, u32[]{:S(2)}) collective-permute-start(bf16[64,2176]{1,0:T(8,128)(2,1)} %collective-permute-done.20.refs_1_), channel_id=1, source_target_pairs={{0,2},{2,0},{4,6},{6,4},{1,3},{3,1},{5,7},{7,5},{8,10},{10,8},{12,... | collective-permute-start | bytes 835592 | tf_op jit(solution)/shard_map/ppermute | solution.py:318
  79.9 2.6 %copy-start = (bf16[1,2,2048,704]{2,3,1,0:T(8,128)(2,1)S(1)}, bf16[1,2,2048,704]{2,3,1,0:T(8,128)(2,1)}, u32[]{:S(2)}) copy-start(bf16[1,2,2048,704]{2,3,1,0:T(8,128)(2,1)} %param.36) | copy-start | bytes 17301508
  82.6 1.8 %copy-start.1 = (bf16[1,704,2048]{2,1,0:T(8,128)(2,1)S(1)}, bf16[1,704,2048]{2,1,0:T(8,128)(2,1)}, u32[]{:S(2)}) copy-start(bf16[1,704,2048]{2,1,0:T(8,128)(2,1)} %param.37) | copy-start | bytes 8650756
  84.4 1.8 %copy-start.10 = (bf16[2,2048,352]{1,2,0:T(8,128)(2,1)S(1)}, bf16[2,2048,352]{1,2,0:T(8,128)(2,1)}, u32[]{:S(2)}) copy-start(bf16[2,2048,352]{1,2,0:T(8,128)(2,1)} %param.34) | copy-start | bytes 8650756
  86.2 7.0 %slice-start.1 = ((s8[5767168]{0:T(1024)(128)(4,1)}), s8[4194304]{0:T(1024)(128)(4,1)S(1)}, s32[]{:S(2)}) async-start(s8[5767168]{0:T(1024)(128)(4,1)} %bitcast.52), calls=%async_computation.1 | async-start | bytes 8388608
  86.2 7.0 %copy-start.2 = (bf16[1,704,2048]{2,1,0:T(8,128)(2,1)S(1)}, bf16[1,704,2048]{2,1,0:T(8,128)(2,1)}, u32[]{:S(2)}) copy-start(bf16[1,704,2048]{2,1,0:T(8,128)(2,1)} %param.37) | copy-start | bytes 8650756
  92.1 10.5 %collective-permute-start.14 = (bf16[64,2176]{1,0:T(8,128)(2,1)S(1)}, bf16[64,2176]{1,0:T(8,128)(2,1)S(1)}, u32[]{:S(2)}, u32[]{:S(2)}) collective-permute-start(bf16[64,2176]{1,0:T(8,128)(2,1)S(1)} %collective-permute-done.12.refs_0_), channel_id=1, source_target_pairs={{0,2},{2,0},{4,6},{6,4},{1,3},{3,1},{5,7},{7,5},{8,10},{10,8},{12,... | collective-permute-start | bytes 835592 | tf_op jit(solution)/shard_map/ppermute | solution.py:318
  92.7 13.3 %collective-permute-start.10 = (bf16[2,64,2048]{2,1,0:T(8,128)(2,1)S(1)}, bf16[2,64,2048]{2,1,0:T(8,128)(2,1)S(1)}, u32[]{:S(2)}, u32[]{:S(2)}) collective-permute-start(bf16[2,64,2048]{2,1,0:T(8,128)(2,1)S(1)} %get-tuple-element.30), channel_id=1, source_target_pairs={{0,2},{2,0},{4,6},{6,4},{1,3},{3,1},{5,7},{7,5},{8,10},{10,8},{12,... | collective-permute-start | bytes 1572872 | tf_op jit(solution)/shard_map/ppermute | solution.py:318
  92.8 9.8 %collective-permute-start.15 = (bf16[64,2176]{1,0:T(8,128)(2,1)S(1)}, bf16[64,2176]{1,0:T(8,128)(2,1)S(1)}, u32[]{:S(2)}, u32[]{:S(2)}) collective-permute-start(bf16[64,2176]{1,0:T(8,128)(2,1)S(1)} %collective-permute-done.13.refs_1_), channel_id=1, source_target_pairs={{0,2},{2,0},{4,6},{6,4},{1,3},{3,1},{5,7},{7,5},{8,10},{10,8},{12,... | collective-permute-start | bytes 835592 | tf_op jit(solution)/shard_map/ppermute | solution.py:318
  97.7 9.0 %collective-permute-start.30 = (bf16[2,64,2048]{2,1,0:T(8,128)(2,1)S(1)}, bf16[2,64,2048]{2,1,0:T(8,128)(2,1)S(1)}, u32[]{:S(2)}, u32[]{:S(2)}) collective-permute-start(bf16[2,64,2048]{2,1,0:T(8,128)(2,1)S(1)} %get-tuple-element.36), channel_id=1, source_target_pairs={{0,2},{2,0},{4,6},{6,4},{1,3},{3,1},{5,7},{7,5},{8,10},{10,8},{12,... | collective-permute-start | bytes 1572872 | tf_op jit(solution)/shard_map/ppermute | solution.py:318
  102.1 6.4 %collective-permute-start.23 = (bf16[2,64,2048]{2,1,0:T(8,128)(2,1)S(1)}, bf16[2,64,2048]{2,1,0:T(8,128)(2,1)S(1)}, u32[]{:S(2)}, u32[]{:S(2)}) collective-permute-start(bf16[2,64,2048]{2,1,0:T(8,128)(2,1)S(1)} %get-tuple-element.34), channel_id=1, source_target_pairs={{0,2},{2,0},{4,6},{6,4},{1,3},{3,1},{5,7},{7,5},{8,10},{10,8},{12,... | collective-permute-start | bytes 1572872 | tf_op jit(solution)/shard_map/ppermute | solution.py:318
  105.9 3.4 %collective-permute-start.16 = (bf16[2,64,2048]{2,1,0:T(8,128)(2,1)S(1)}, bf16[2,64,2048]{2,1,0:T(8,128)(2,1)S(1)}, u32[]{:S(2)}, u32[]{:S(2)}) collective-permute-start(bf16[2,64,2048]{2,1,0:T(8,128)(2,1)S(1)} %get-tuple-element.32), channel_id=1, source_target_pairs={{0,2},{2,0},{4,6},{6,4},{1,3},{3,1},{5,7},{7,5},{8,10},{10,8},{12,... | collective-permute-start | bytes 1572872 | tf_op jit(solution)/shard_map/ppermute | solution.py:318
  106.2 27.4 %collective-permute-start.11 = (bf16[64,2048]{1,0:T(8,128)(2,1)S(1)}, bf16[64,2048]{1,0:T(8,128)(2,1)S(1)}, u32[]{:S(2)}, u32[]{:S(2)}) collective-permute-start(bf16[64,2048]{1,0:T(8,128)(2,1)S(1)} %fusion.19), channel_id=1, source_target_pairs={{0,4},{2,6},{4,0},{6,2},{1,5},{3,7},{5,1},{7,3},{8,12},{10,14},{12... | collective-permute-start | bytes 786440 | tf_op jit(solution)/shard_map/ppermute | solution.py:318
  106.9 14.0 %collective-permute-start.31 = (bf16[64,2048]{1,0:T(8,128)(2,1)S(1)}, bf16[64,2048]{1,0:T(8,128)(2,1)S(1)}, u32[]{:S(2)}, u32[]{:S(2)}) collective-permute-start(bf16[64,2048]{1,0:T(8,128)(2,1)S(1)} %fusion.22), channel_id=1, source_target_pairs={{0,4},{2,6},{4,0},{6,2},{1,5},{3,7},{5,1},{7,3},{8,12},{10,14},{12... | collective-permute-start | bytes 786440 | tf_op jit(solution)/shard_map/ppermute | solution.py:318
  108.7 17.9 %collective-permute-start.24 = (bf16[64,2048]{1,0:T(8,128)(2,1)S(1)}, bf16[64,2048]{1,0:T(8,128)(2,1)S(1)}, u32[]{:S(2)}, u32[]{:S(2)}) collective-permute-start(bf16[64,2048]{1,0:T(8,128)(2,1)S(1)} %fusion.21), channel_id=1, source_target_pairs={{0,4},{2,6},{4,0},{6,2},{1,5},{3,7},{5,1},{7,3},{8,12},{10,14},{12... | collective-permute-start | bytes 786440 | tf_op jit(solution)/shard_map/ppermute | solution.py:318
  109.4 23.6 %collective-permute-start.17 = (bf16[64,2048]{1,0:T(8,128)(2,1)S(1)}, bf16[64,2048]{1,0:T(8,128)(2,1)S(1)}, u32[]{:S(2)}, u32[]{:S(2)}) collective-permute-start(bf16[64,2048]{1,0:T(8,128)(2,1)S(1)} %fusion.20), channel_id=1, source_target_pairs={{0,4},{2,6},{4,0},{6,2},{1,5},{3,7},{5,1},{7,3},{8,12},{10,14},{12... | collective-permute-start | bytes 786440 | tf_op jit(solution)/shard_map/ppermute | solution.py:318
  121.0 12.6 %collective-permute-start.32 = (bf16[64,2048]{1,0:T(8,128)(2,1)S(1)}, bf16[64,2048]{1,0:T(8,128)(2,1)S(1)}, u32[]{:S(2)}, u32[]{:S(2)}) collective-permute-start(bf16[64,2048]{1,0:T(8,128)(2,1)S(1)} %fusion.3), channel_id=1, source_target_pairs={{0,8},{8,0},{16,24},{24,16},{1,9},{9,1},{17,25},{25,17},{2,10},{10... | collective-permute-start | bytes 786440 | tf_op jit(solution)/shard_map/ppermute | solution.py:318
  126.6 37.4 %copy-start.17 = (f32[64,2048]{1,0:T(8,128)S(1)}, f32[64,2048]{1,0:T(8,128)}, u32[]{:S(2)}) copy-start(f32[64,2048]{1,0:T(8,128)} %copy-done.16) | copy-start | bytes 1572868
  126.6 21.3 %collective-permute-start.25 = (bf16[64,2048]{1,0:T(8,128)(2,1)S(1)}, bf16[64,2048]{1,0:T(8,128)(2,1)S(1)}, u32[]{:S(2)}, u32[]{:S(2)}) collective-permute-start(bf16[64,2048]{1,0:T(8,128)(2,1)S(1)} %fusion.7), channel_id=1, source_target_pairs={{0,16},{8,24},{16,0},{24,8},{1,17},{9,25},{17,1},{25,9},{2,18},{10... | collective-permute-start | bytes 786440 | tf_op jit(solution)/shard_map/ppermute | solution.py:318
  133.1 22.5 %collective-permute-start.18 = (bf16[64,2048]{1,0:T(8,128)(2,1)S(1)}, bf16[64,2048]{1,0:T(8,128)(2,1)S(1)}, u32[]{:S(2)}, u32[]{:S(2)}) collective-permute-start(bf16[64,2048]{1,0:T(8,128)(2,1)S(1)} %fusion.11), channel_id=1, source_target_pairs={{0,24},{8,16},{16,8},{24,0},{1,25},{9,17},{17,9},{25,1},{2,26},{10... | collective-permute-start | bytes 786440 | tf_op jit(solution)/shard_map/ppermute | solution.py:318
  155.7 8.3 %collective-permute-start.33 = (bf16[64,2048]{1,0:T(8,128)(2,1)S(1)}, bf16[64,2048]{1,0:T(8,128)(2,1)S(1)}, u32[]{:S(2)}, u32[]{:S(2)}) collective-permute-start(bf16[64,2048]{1,0:T(8,128)(2,1)S(1)} %fusion.18), channel_id=1, source_target_pairs={{0,1},{1,0},{2,3},{3,2},{4,5},{5,4},{6,7},{7,6},{8,9},{9,8},{10,11... | collective-permute-start | bytes 786440 | tf_op jit(solution)/shard_map/ppermute | solution.py:318

commit v4 on v3

--- a/solution.py
+++ b/solution.py
@@ -52,7 +52,10 @@
 
 WHOLE = pl.BlockSpec(memory_space=pltpu.VMEM)
 SCALARS = pl.BlockSpec(memory_space=pltpu.SMEM)
-PLACED = pl.BlockSpec(memory_space=pl.ANY)
+STORED = pl.BlockSpec(memory_space=pltpu.HBM)
+
+
+SMALL = pl.CostEstimate(flops=1, bytes_accessed=1, transcendentals=0)
 
 
 def params(megabytes):
@@ -83,9 +86,11 @@
     for k in range(requests):
         closure_ref[k] = closures[k]
         depth = jnp.sum(closures[k], axis=-1, keepdims=True) - 1.0
-        angles = (lengths_ref[row_ref[0] ^ k].astype(jnp.float32) + depth) * frequency
+        length = lengths_ref[row_ref[0] ^ k].astype(jnp.float32)
+        angles = (length + depth) * frequency
         turns_ref[k, :, : ROPE // 2] = jnp.cos(angles)
-        turns_ref[k, :, ROPE // 2 :] = jnp.sin(angles)
+        turns_ref[k, :, ROPE // 2 : ROPE] = jnp.sin(angles)
+        turns_ref[k, :, ROPE : ROPE + 1] = jnp.full((size, 1), length)
     own = closures[0].astype(jnp.bfloat16)
     depth_row = transposed_dot(jnp.ones((8, size), jnp.bfloat16), own)[:1] - 1.0
     chosen = (lax.broadcasted_iota(jnp.int32, (size, 1), 0) == accepted_ref[0]).astype(jnp.float32)
@@ -101,7 +106,7 @@
         tree_kernel,
         out_shape=(
             jax.ShapeDtypeStruct((requests, size, size), jnp.float32),
-            jax.ShapeDtypeStruct((requests, size, ROPE), jnp.float32),
+            jax.ShapeDtypeStruct((requests, size, ROPE + 1), jnp.float32),
             jax.ShapeDtypeStruct((size, size), jnp.bfloat16),
         ),
         in_specs=[SCALARS, SCALARS, SCALARS, WHOLE],
@@ -111,25 +116,31 @@
     )(row_index, lengths, accepted, parents)
 
 
-def attention_kernel(first, place, row_ref, lengths_ref, *refs):
-    (
-        first_ref,
-        second_ref,
-        cache_a_ref,
-        cache_b_ref,
-        closure_ref,
-        turns_ref,
-        places_ref,
-        gain_ref,
-        query_ref,
-        latent_ref,
-        latent_gain_ref,
-        key_ref,
-        value_ref,
-        output_ref,
-        keep_ref,
-        send_ref,
-    ) = refs[:16]
+def attention_kernel(first, place, row_ref, *refs):
+    first_ref, second_ref, closure_ref, turns_ref, places_ref, cache_hbm, *stored = refs[:13]
+    outs, scratch = refs[13 : 15 + first], refs[15 + first :]
+    keep_ref, send_ref = outs[:2]
+    *held, cache_ref, first_held, sems = scratch
+    gain_ref, query_ref, latent_ref, latent_gain_ref, key_ref, value_ref, output_ref = held
+    copies = [
+        pltpu.make_async_copy(stored[k], held[k], sems.at[k]) for k in (0, 2, 1, 3, 4, 5, 6)
+    ]
+    gain_copy, latent_copy, query_copy, latent_gain_copy, key_copy, value_copy, output_copy = copies
+    cache_copies = [
+        pltpu.make_async_copy(
+            cache_hbm.at[row_ref[0] ^ (place + r)], cache_ref.at[r], sems.at[7 + r]
+        )
+        for r in range(2)
+    ]
+    if first:
+        rows_copy = pltpu.make_async_copy(first_ref, first_held, sems.at[9])
+        rows_copy.start()
+        first_ref = first_held
+    for copy in (*copies[:5], *cache_copies, *copies[5:]):
+        copy.start()
+    if first:
+        rows_copy.wait()
+    gain_copy.wait()
     size = first_ref.shape[0]
     heads = key_ref.shape[0]
     bf16 = jnp.bfloat16
@@ -137,15 +148,19 @@
     rows = jnp.concatenate([first_ref[...], second_ref[...]], axis=0).astype(jnp.float32)
     rows = rms_scale(rows, gain_ref[...]).astype(bf16)
     turns = jnp.concatenate([turns_ref[place], turns_ref[place + 1]], axis=0)
-    cosine, sine_part = turns[:, : ROPE // 2], turns[:, ROPE // 2 :]
+    cosine, sine_part = turns[:, : ROPE // 2], turns[:, ROPE // 2 : ROPE]
+    latent_copy.wait()
     projected = transposed_dot(rows, latent_ref[...])
+    latent_gain_copy.wait()
     content = rms_scale(projected[:, :LAT], latent_gain_ref[...]).astype(bf16)
     key_rope = rotate(projected[:, LAT:], cosine, sine_part).astype(bf16)
     if first:
-        accepted_ref = refs[16]
+        accepted_ref = outs[2]
         accepted_ref[0, :, :LAT] = dot(places_ref[...], content[:size]).astype(bf16)
         accepted_ref[0, :, LAT:] = dot(places_ref[...], key_rope[:size]).astype(bf16)
+    query_copy.wait()
     queries = dot(rows, query_ref[...])
+    key_copy.wait()
     query_latent, query_rope = [], []
     for h in range(heads):
         start = h * (NOPE + ROPE)
@@ -154,15 +169,16 @@
         )
         turned = queries[:, start + NOPE : start + NOPE + ROPE].astype(bf16).astype(jnp.float32)
         query_rope.append(rotate(turned, cosine, sine_part).astype(bf16))
-    outs = [[], []]
-    for r, cache_ref in enumerate((cache_a_ref, cache_b_ref)):
+    mixed_rows = [[], []]
+    for r in range(2):
+        cache_copies[r].wait()
         part = slice(r * size, (r + 1) * size)
         latent_rows = jnp.concatenate([each[part] for each in query_latent], axis=0)
         rope_rows = jnp.concatenate([each[part] for each in query_rope], axis=0)
-        old = dot(latent_rows, cache_ref[0, :LAT, :]) + dot(rope_rows, cache_ref[0, LAT:, :])
+        old = dot(latent_rows, cache_ref[r, :LAT, :]) + dot(rope_rows, cache_ref[r, LAT:, :])
         new = transposed_dot(latent_rows, content[part]) + transposed_dot(rope_rows, key_rope[part])
-        length = lengths_ref[row_ref[0] ^ (place + r)]
-        spots = lax.broadcasted_iota(jnp.int32, (1, old.shape[1]), 1)
+        length = jnp.concatenate([turns_ref[place + r, :, ROPE : ROPE + 1]] * heads, axis=0)
+        spots = lax.broadcasted_iota(jnp.int32, old.shape, 1).astype(jnp.float32)
         allowed = (spots < length) & ((spots < SINK) | (spots >= length - WINDOW))
         related = jnp.concatenate([closure_ref[place + r]] * heads, axis=0) > 0.5
         old = jnp.where(allowed, old * scale_factor, -1e30)
@@ -175,33 +191,25 @@
         total = jnp.sum(old, axis=-1, keepdims=True) + jnp.sum(new, axis=-1, keepdims=True)
         old = (old / total).astype(bf16)
         new = (new / total).astype(bf16)
-        mixed = transposed_dot(old, cache_ref[0, :LAT, :]) + dot(new, content[part])
+        mixed = transposed_dot(old, cache_ref[r, :LAT, :]) + dot(new, content[part])
         for h in range(heads):
-            outs[r].append(mixed[h * size : (h + 1) * size].astype(bf16))
+            mixed_rows[r].append(mixed[h * size : (h + 1) * size].astype(bf16))
+    value_copy.wait()
     head_rows = [
-        dot(jnp.concatenate([outs[0][h], outs[1][h]], axis=0), value_ref[h]).astype(bf16)
+        dot(jnp.concatenate([mixed_rows[0][h], mixed_rows[1][h]], axis=0), value_ref[h]).astype(bf16)
         for h in range(heads)
     ]
     head_rows = jnp.concatenate(head_rows, axis=1)
+    output_copy.wait()
     partial = dot(head_rows, output_ref[...])
     keep_ref[...] = partial[:size]
     send_ref[...] = partial[size:].astype(bf16)
 
 
-def attention_part(first, place, row_index, lengths, blocks, cache, tables, weights):
+def attention_part(first, place, row_index, blocks, cache, tables, weights):
     size, width = blocks[0].shape
     slots, spots = cache.shape[1:]
     heads = weights[4].shape[0]
-    closure, turns, places = tables
-
-    def whole(array):
-        rank = array.ndim
-        return pl.BlockSpec(array.shape, lambda i, row, lens: (0,) * rank)
-
-    def cached(k):
-        return pl.BlockSpec((1, slots, spots), lambda i, row, lens: (row[0] ^ k, 0, 0))
-
-    rest = [closure, turns, places, *weights]
     out_shape = [
         jax.ShapeDtypeStruct((size, width), jnp.float32),
         jax.ShapeDtypeStruct((size, width), jnp.bfloat16),
@@ -209,25 +217,22 @@
     if first:
         out_shape.append(jax.ShapeDtypeStruct((1, size, LAT + ROPE), jnp.bfloat16))
     rows = 2 * size
-    flops = 2 * rows * width * (weights[1].shape[1] + LAT + ROPE + heads * VDIM)
+    columns = weights[1].shape[1] + LAT + ROPE + heads * VDIM
     return pl.pallas_call(
         functools.partial(attention_kernel, first, place),
         out_shape=tuple(out_shape),
-        grid_spec=pltpu.PrefetchScalarGridSpec(
-            num_scalar_prefetch=2,
-            grid=(1,),
-            in_specs=[whole(blocks[0]), whole(blocks[1]), cached(place), cached(place + 1)]
-            + [whole(each) for each in rest],
-            out_specs=tuple(whole(each) for each in out_shape),
-        ),
-        compiler_params=params(32),
-        cost_estimate=pl.CostEstimate(
-            flops=flops,
-            bytes_accessed=2 * width * (weights[1].shape[1] + LAT + ROPE + heads * VDIM),
-            transcendentals=rows * heads * (spots + size),
-        ),
+        in_specs=[SCALARS, STORED if first else WHOLE] + [WHOLE] * 4 + [STORED] * 8,
+        out_specs=(WHOLE,) * len(out_shape),
+        scratch_shapes=[
+            *(pltpu.VMEM(each.shape, each.dtype) for each in weights),
+            pltpu.VMEM((2, slots, spots), cache.dtype),
+            pltpu.VMEM((size, width), jnp.bfloat16),
+            pltpu.SemaphoreType.DMA((10,)),
+        ],
+        compiler_params=params(53),
+        cost_estimate=SMALL,
         name="attention",
-    )(row_index, lengths, blocks[0], blocks[1], cache, cache, *rest)
+    )(row_index, *blocks, *tables, cache, *weights)
 
 
 def join_kernel(hidden_ref, keep_ref, arrived_ref, gain_ref, named_ref, residual_ref, block_ref):
@@ -258,35 +263,58 @@
 
 def expert_kernel(shared, *refs):
     blocks, refs = refs[:4], refs[4:]
-    own_ref, router_ref, gate_up_ref, down_ref = refs[:4]
-    refs = refs[4:]
-    if shared:
-        shared_gate_up_ref, shared_down_ref = refs[:2]
-        refs = refs[2:]
-    keep_ref, send_ref = refs
+    own_ref, refs = refs[0], refs[1:]
+    count = 5 if shared else 3
+    stored, (keep_ref, send_ref), held, sems = (
+        refs[:count],
+        refs[count : count + 2],
+        refs[count + 2 : 2 * count + 2],
+        refs[-1],
+    )
+    router_ref, gate_up_ref, down_ref = held[:3]
     experts, width = router_ref.shape
+    router_copy = pltpu.make_async_copy(stored[0], router_ref, sems.at[0])
+    router_copy.start()
+    pairs = []
+    for k in range(1, count, 2):
+        pairs.append(
+            [
+                pltpu.make_async_copy(stored[k].at[0], held[k].at[0], sems.at[3 * k]),
+                pltpu.make_async_copy(stored[k].at[1], held[k].at[1], sems.at[3 * k + 1]),
+                pltpu.make_async_copy(stored[k + 1], held[k + 1], sems.at[3 * k + 2]),
+            ]
+        )
+    for copy in (copy for pair in pairs for copy in pair[:2]):
+        copy.start()
+    for pair in pairs:
+        pair[2].start()
     size = blocks[0].shape[0]
     rows = jnp.concatenate([ref[:, :width] for ref in blocks], axis=0)
     named = jnp.concatenate([ref[:, width:] for ref in blocks], axis=0)[:, :experts]
+    router_copy.wait()
     logits = transposed_dot(rows, router_ref[...])
     raised = jnp.exp(logits - jnp.max(logits, axis=-1, keepdims=True))
     router = raised / jnp.sum(raised, axis=-1, keepdims=True)
     share = jnp.sum(router * named.astype(jnp.float32) * own_ref[...], axis=-1, keepdims=True)
 
-    def inner(weights_ref):
+    def inner(weights_ref, copies):
+        copies[0].wait()
         gate = transposed_dot(rows, weights_ref[0])
+        copies[1].wait()
         upper = transposed_dot(rows, weights_ref[1])
         return (jax.nn.silu(gate) * upper).astype(jnp.bfloat16)
 
-    routed_inner = inner(gate_up_ref)
+    routed_inner = inner(gate_up_ref, pairs[0])
     if shared:
-        shared_inner = inner(shared_gate_up_ref)
+        shared_inner = inner(held[3], pairs[1])
+    for pair in pairs:
+        pair[2].wait()
     tile = width // CHUNKS
     for k in range(CHUNKS):
         part = slice(k * tile, (k + 1) * tile)
         result = share * dot(routed_inner, down_ref[:, part])
         if shared:
-            result = result + dot(shared_inner, shared_down_ref[:, part])
+            result = result + dot(shared_inner, held[4][:, part])
         keep_ref[:, :, part] = result[: 2 * size].reshape(2, size, tile)
         send_ref[:, :, part] = result[2 * size :].astype(jnp.bfloat16).reshape(2, size, tile)
 
@@ -295,23 +323,27 @@
     size = blocks[0].shape[0]
     width = router.shape[1]
     units = sum(each.shape[0] for each in (*routed_weights, *shared_weights) if each.ndim == 2)
-    operands = [*blocks, own_expert, router, *routed_weights, *shared_weights]
+    stored = [router, *routed_weights, *shared_weights]
     return pl.pallas_call(
         functools.partial(expert_kernel, bool(shared_weights)),
         out_shape=(
             jax.ShapeDtypeStruct((2, size, width), jnp.float32),
             jax.ShapeDtypeStruct((2, size, width), jnp.bfloat16),
         ),
-        in_specs=[WHOLE] * len(operands),
+        in_specs=[WHOLE] * 5 + [STORED] * len(stored),
         out_specs=(WHOLE, WHOLE),
-        compiler_params=params(32),
-        cost_estimate=pl.CostEstimate(
-            flops=24 * size * width * units,
-            bytes_accessed=6 * width * units,
-            transcendentals=4 * size * units,
-        ),
+        scratch_shapes=[
+            *(pltpu.VMEM(each.shape, each.dtype) for each in stored),
+            pltpu.SemaphoreType.DMA((12,)),
+        ],
+        compiler_params=params(50),
+        cost_estimate=SMALL,
         name="experts",
-    )(*operands)
+    )(*blocks, own_expert, *stored)
+
+
+def after(values, *others):
+    return lax.optimization_barrier((values, *others))[0]
 
 
 def swap(values, axis, size, bits):
@@ -348,7 +380,6 @@
 
     far = swap(hidden, "row", n_row, 2)
     near = swap(hidden, "row", n_row, 1)
-    far_near = swap(far, "row", n_row, 1)
 
     row_scalar = row_index.astype(jnp.int32).reshape(1)
     tables = tree_tables(row_scalar, lengths, accepted, parents)
@@ -363,10 +394,12 @@
         output_weight,
     )
     own_keep, own_send, accepted_latents = attention_part(
-        True, 0, row_scalar, lengths, (hidden, near), cache, tables, weights
-    )
+        True, 0, row_scalar, (hidden, near), cache, tables, weights
+    )
+    far = after(far, own_send)
+    far_near = swap(far, "row", n_row, 1)
     far_keep, far_send = attention_part(
-        False, 2, row_scalar, lengths, (far, far_near), cache, tables, weights
+        False, 2, row_scalar, (far, far_near), cache, tables, weights
     )
 
     def fold(keep, sent):
@@ -383,27 +416,35 @@
     router = router_weight.T
     routed_weights = (jnp.swapaxes(expert_gate_up[0], 1, 2), expert_down[0])
     shared_weights = (jnp.swapaxes(shared_gate_up, 1, 2), shared_down)
-    distances = [*range(n_req - 1, 0, -1)]
-    blocks = {s: swap(block, "req", n_req, s) for s in distances}
-    blocks[0] = block
-    total = None
-    for s in [0, *distances]:
-        far = swap(blocks[s], "row", n_row, 2)
-        near = swap(blocks[s], "row", n_row, 1)
+    distances = [0, 1, *range(n_req - 1, 1, -1)]
+    blocks = [block]
+    for k, s in enumerate(distances[1:], 1):
+        source = block if k < 3 else after(block, blocks[k - 2])
+        blocks.append(swap(source, "req", n_req, s))
+    sends, parts = [], []
+    for k, s in enumerate(distances):
+        far = swap(after(blocks[k], *sends[: max(0, k - 2)]), "row", n_row, 2)
+        near = swap(blocks[k], "row", n_row, 1)
+        if k == 0:
+            far = after(far, *blocks[1:3])
+        elif k > 2:
+            far = after(far, *sends, *parts[: k - 1])
         far_near = swap(far, "row", n_row, 1)
         keep, send = expert_part(
-            (blocks[s], far, near, far_near),
+            (blocks[k], far, near, far_near),
             own_expert,
             router,
             routed_weights,
             () if s else shared_weights,
         )
-        from_near = swap(send, "row", n_row, 1).astype(jnp.float32)
-        from_far = swap((keep[1] + from_near[1]).astype(bf16), "row", n_row, 2)
-        part = keep[0] + from_near[0] + from_far.astype(jnp.float32)
-        if s:
-            part = swap(part.astype(bf16), "req", n_req, s).astype(jnp.float32)
-        total = part if total is None else total + part
+        sends.append(send)
+        from_near = swap(send, "row", n_row, 1)
+        from_far = swap((keep[1] + from_near[1].astype(jnp.float32)).astype(bf16), "row", n_row, 2)
+        part = keep[0] + from_near[0].astype(jnp.float32) + from_far.astype(jnp.float32)
+        parts.append(part.astype(bf16) if s else part)
+    total = parts[0]
+    for s, part in zip(distances[1:], parts[1:]):
+        total = total + swap(part, "req", n_req, s).astype(jnp.float32)
     total, arrived = col_parts(total, n_col)
     layer_output = residual + (total.astype(jnp.float32) + sum_up(arrived))
     return (layer_output.astype(bf16), accepted_latents)

time: 165 us -> 162 us (0.982)
  the two profiles are of different devices: /device:TPU:8 before, /device:TPU:0 now
where the time goes in v4:
time: 162 us
  waiting for transfers between devices  86.1 us (53%)
  Pallas kernels  42.9 us (26%)
  starting transfers between devices  23.2 us (14%)
  local copies, waits for them, and re-layouts  5.1 us (3%)
  other arithmetic  2.73 us (2%)
    ppermute x34, waiting for transfers between devices, swap(): return lax.ppermute(values, axis, [(i, i ^ bits) for i in range(size)])  86.1 us
    pallas_call x4, Pallas kernels, expert_part(): pl.pallas_call(functools.partial(expert_kernel, bool(shared_weights)), ou...  25.1 us
    ppermute x34, starting transfers between devices, swap(): return lax.ppermute(values, axis, [(i, i ^ bits) for i in range(size)])  23.2 us
    pallas_call x2, Pallas kernels, attention_part(): pl.pallas_call(functools.partial(attention_kernel, first, place), out_sha...  15.4 us
    unnamed x24, local copies, waits for them, and re-layouts  5.1 us
  transfers between devices with their start and end apart: 34, of which 18 were waited for; matrix products, arithmetic and copies ran while one was open for 1% of the time, Pallas kernels for 22%

profile of v4, /device:TPU:0, one launch (start us, length us, event | category | flops | bytes accessed | tf_op | source)
XLA Modules:
  0.0 161.6 jit_solution(7706066853881650260)
XLA Ops:
  0.6 0.5 collective-permute-start
  1.1 2.6 %collective-permute-start.2 = (bf16[64,2048]{1,0:T(8,128)(2,1)}, bf16[64,2048]{1,0:T(8,128)(2,1)S(1)}, u32[]{:S(2)}, u32[]{:S(2)}) collective-permute-start(bf16[64,2048]{1,0:T(8,128)(2,1)} %hidden_ref.1), channel_id=1, source_target_pairs={{0,4},{2,6},{4,0},{6,2},{1,5},{3,7},{5,1},{7,3},{8,12},{10,14},{12... | collective-permute-start | bytes 786440 | tf_op jit(solution)/shard_map/ppermute | solution.py:350
  4.4 0.7 copy-done.6
  5.1 0.7 copy-done.7
  5.7 2.1 %trees.1 = (f32[4,64,64]{2,1,0:T(8,128)S(1)}, f32[4,64,65]{2,1,0:T(8,128)S(1)}, bf16[64,64]{1,0:T(8,128)(2,1)S(1)}) custom-call(s32[1]{0:T(128)} %bitcast.row_ref, s32[4]{0:T(128)S(1)} %copy-done.7, s32[1]{0:T(128)S(6)} %copy.22.accepted_ref, s32[4,64]{1,0:T(4,128)S(1)} %copy-done.6), custom_call_target="tpu_custom_call" | custom-call | tf_op jit(solution)/shard_map/trees/pallas_call | solution.py:105
  7.9 0.7 copy-done.9
  8.6 0.9 copy-done.1
  9.5 0.7 copy-done.3
  10.2 0.7 copy-done.5
  10.9 7.7 %attention.2 = (f32[64,2048]{1,0:T(8,128)}, bf16[64,2048]{1,0:T(8,128)(2,1)S(1)}, bf16[1,64,576]{2,1,0:T(8,128)(2,1)}) custom-call(s32[1]{0:T(128)} %bitcast.row_ref, bf16[64,2048]{1,0:T(8,128)(2,1)S(1)} %copy-done.1, bf16[64,2048]{1,0:T(8,128)(2,1)} %copy-done.9, f32[4,64,64]{2,1,0:T(8,128)S(1)} %get-tuple-element.25.refs_2_, ...), custom_call_target="tpu_custom_call" | custom-call | flops 1 | bytes 1 | tf_op jit(solution)/shard_map/attention/pallas_call | solution.py:221
  18.7 0.2 collective-permute-start.3
  18.9 1.4 collective-permute-done.3.refs_1_
  20.3 0.7 copy-done.10
  21.0 7.7 %attention.3 = (f32[64,2048]{1,0:T(8,128)}, bf16[64,2048]{1,0:T(8,128)(2,1)S(1)}) custom-call(s32[1]{0:T(128)} %bitcast.row_ref, bf16[64,2048]{1,0:T(8,128)(2,1)S(1)} %collective-permute-done.2.refs_0_, bf16[64,2048]{1,0:T(8,128)(2,1)} %copy-done.10, f32[4,64,64]{2,1,0:T(8,128)S(1)} %get-tuple-element.25.refs_2_, ...), custom_call_target="tpu_custom_call" | custom-call | flops 1 | bytes 1 | tf_op jit(solution)/shard_map/attention/pallas_call | solution.py:221
  28.7 0.2 collective-permute-start.4
  29.0 0.3 collective-permute-start.1
  29.3 1.0 collective-permute-done.4
  30.3 1.1 add_convert_fusion.7
  31.4 0.1 collective-permute-start.5
  31.6 8.3 %collective-permute-done.5 = bf16[64,2048]{1,0:T(8,128)(2,1)S(1)} collective-permute-done((bf16[64,2048]{1,0:T(8,128)(2,1)S(1)}, bf16[64,2048]{1,0:T(8,128)(2,1)S(1)}, u32[]{:S(2)}, u32[]{:S(2)}) %collective-permute-start.5) | collective-permute-done | bytes 262176 | tf_op jit(solution)/shard_map/ppermute | solution.py:350
  39.9 0.1 add_convert_fusion.6.keep_ref
  40.0 1.6 collective-permute-start.6
  41.5 0.1 fusion.7
  41.7 5.9 %collective-permute-done.6 = bf16[64,2048]{1,0:T(8,128)(2,1)S(1)} collective-permute-done((bf16[64,2048]{1,0:T(8,128)(2,1)S(1)}, bf16[64,2048]{1,0:T(8,128)(2,1)S(1)}, u32[]{:S(2)}, u32[]{:S(2)}) %collective-permute-start.6) | collective-permute-done | bytes 262176 | tf_op jit(solution)/shard_map/ppermute | solution.py:350
  47.6 0.2 join.1
  47.8 3.7 %collective-permute-start.9 = (bf16[64,2176]{1,0:T(8,128)(2,1)S(1)}, bf16[64,2176]{1,0:T(8,128)(2,1)S(1)}, u32[]{:S(2)}, u32[]{:S(2)}) collective-permute-start(bf16[64,2176]{1,0:T(8,128)(2,1)S(1)} %get-tuple-element.42.refs_0_), channel_id=1, source_target_pairs={{0,24},{8,16},{16,8},{24,0},{1,25},{9,17},{17,9},{25,1},{2,26},{10... | collective-permute-start | bytes 835592 | tf_op jit(solution)/shard_map/ppermute | solution.py:350
  51.5 0.5 collective-permute-start.7
  52.0 7.3 %collective-permute-done.9.refs_0_ = bf16[64,2176]{1,0:T(8,128)(2,1)S(1)} collective-permute-done((bf16[64,2176]{1,0:T(8,128)(2,1)S(1)}, bf16[64,2176]{1,0:T(8,128)(2,1)S(1)}, u32[]{:S(2)}, u32[]{:S(2)}) %collective-permute-start.9) | collective-permute-done | bytes 278560 | tf_op jit(solution)/shard_map/ppermute | solution.py:350
  59.3 3.5 %collective-permute-done.8.refs_0_ = bf16[64,2176]{1,0:T(8,128)(2,1)S(1)} collective-permute-done((bf16[64,2176]{1,0:T(8,128)(2,1)S(1)}, bf16[64,2176]{1,0:T(8,128)(2,1)S(1)}, u32[]{:S(2)}, u32[]{:S(2)}) %collective-permute-start.8) | collective-permute-done | bytes 278560 | tf_op jit(solution)/shard_map/ppermute | solution.py:350
  62.8 0.7 collective-permute-start.20
  63.5 1.3 collective-permute-start.14
  64.9 7.7 %experts.4 = (f32[2,64,2048]{2,1,0:T(8,128)S(1)}, bf16[2,64,2048]{2,1,0:T(8,128)(2,1)S(1)}) custom-call(bf16[64,2176]{1,0:T(8,128)(2,1)S(1)} %get-tuple-element.42.refs_0_, bf16[64,2176]{1,0:T(8,128)(2,1)S(1)} %collective-permute-done.7.refs_1_, bf16[64,2176]{1,0:T(8,128)(2,1)S(1)} %collective-permute-done.10.refs_2_, ...), custom_call_target="tpu_custom_call" | custom-call | flops 1 | bytes 1 | tf_op jit(solution)/shard_map/experts/pallas_call | solution.py:327
  72.6 0.6 collective-permute-start.12
  73.2 4.7 %collective-permute-done.14.refs_1_ = bf16[64,2176]{1,0:T(8,128)(2,1)S(1)} collective-permute-done((bf16[64,2176]{1,0:T(8,128)(2,1)S(1)}, bf16[64,2176]{1,0:T(8,128)(2,1)S(1)}, u32[]{:S(2)}, u32[]{:S(2)}) %collective-permute-start.14) | collective-permute-done | bytes 278560 | tf_op jit(solution)/shard_map/ppermute | solution.py:350
  77.8 0.6 collective-permute-start.26
  78.5 0.2 collective-permute-start.21
  78.7 0.3 collective-permute-start.22
  79.0 0.4 collective-permute-done.16.refs_3_
  79.4 5.9 %experts.5 = (f32[2,64,2048]{2,1,0:T(8,128)S(1)}, bf16[2,64,2048]{2,1,0:T(8,128)(2,1)S(1)}) custom-call(bf16[64,2176]{1,0:T(8,128)(2,1)S(1)} %collective-permute-done.8.refs_0_, bf16[64,2176]{1,0:T(8,128)(2,1)S(1)} %collective-permute-done.14.refs_1_, bf16[64,2176]{1,0:T(8,128)(2,1)S(1)} %collective-permute-done.15.refs_2_, ...), custom_call_target="tpu_custom_call" | custom-call | flops 1 | bytes 1 | tf_op jit(solution)/shard_map/experts/pallas_call | solution.py:327
  85.3 0.2 collective-permute-start.17
  85.5 8.3 %collective-permute-done.26.refs_0_ = bf16[64,2176]{1,0:T(8,128)(2,1)S(1)} collective-permute-done((bf16[64,2176]{1,0:T(8,128)(2,1)S(1)}, bf16[64,2176]{1,0:T(8,128)(2,1)S(1)}, u32[]{:S(2)}, u32[]{:S(2)}) %collective-permute-start.26) | collective-permute-done | bytes 278560 | tf_op jit(solution)/shard_map/ppermute | solution.py:350
  93.8 0.7 collective-permute-start.27
  94.5 5.7 %experts.6 = (f32[2,64,2048]{2,1,0:T(8,128)S(1)}, bf16[2,64,2048]{2,1,0:T(8,128)(2,1)S(1)}) custom-call(bf16[64,2176]{1,0:T(8,128)(2,1)S(1)} %collective-permute-done.9.refs_0_, bf16[64,2176]{1,0:T(8,128)(2,1)S(1)} %collective-permute-done.20.refs_1_, bf16[64,2176]{1,0:T(8,128)(2,1)S(1)} %collective-permute-done.21.refs_2_, ...), custom_call_target="tpu_custom_call" | custom-call | flops 1 | bytes 1 | tf_op jit(solution)/shard_map/experts/pallas_call | solution.py:327
  100.2 0.5 collective-permute-start.23
  100.8 1.4 collective-permute-start.13
  102.3 0.8 collective-permute-start.18
  103.1 7.0 %collective-permute-done.13 = bf16[64,2048]{1,0:T(8,128)(2,1)S(1)} collective-permute-done((bf16[64,2048]{1,0:T(8,128)(2,1)S(1)}, bf16[64,2048]{1,0:T(8,128)(2,1)S(1)}, u32[]{:S(2)}, u32[]{:S(2)}) %collective-permute-start.13) | collective-permute-done | bytes 262176 | tf_op jit(solution)/shard_map/ppermute | solution.py:350
  110.2 4.6 %collective-permute-done.18 = bf16[64,2048]{1,0:T(8,128)(2,1)S(1)} collective-permute-done((bf16[64,2048]{1,0:T(8,128)(2,1)S(1)}, bf16[64,2048]{1,0:T(8,128)(2,1)S(1)}, u32[]{:S(2)}, u32[]{:S(2)}) %collective-permute-start.18) | collective-permute-done | bytes 262176 | tf_op jit(solution)/shard_map/ppermute | solution.py:350
  114.8 0.1 fusion.2
  115.0 1.5 collective-permute-done.29.refs_3_
  116.5 5.7 %experts.7 = (f32[2,64,2048]{2,1,0:T(8,128)S(1)}, bf16[2,64,2048]{2,1,0:T(8,128)(2,1)S(1)}) custom-call(bf16[64,2176]{1,0:T(8,128)(2,1)S(1)} %collective-permute-done.26.refs_0_, bf16[64,2176]{1,0:T(8,128)(2,1)S(1)} %collective-permute-done.27.refs_1_, bf16[64,2176]{1,0:T(8,128)(2,1)S(1)} %collective-permute-done.28.refs_2_, ...), custom_call_target="tpu_custom_call" | custom-call | flops 1 | bytes 1 | tf_op jit(solution)/shard_map/experts/pallas_call | solution.py:327
  122.2 0.2 collective-permute-start.30
  122.5 1.4 collective-permute-start.24
  123.9 0.3 collective-permute-done.30
  124.2 1.4 collective-permute-start.31
  125.6 6.0 %collective-permute-done.24 = bf16[64,2048]{1,0:T(8,128)(2,1)S(1)} collective-permute-done((bf16[64,2048]{1,0:T(8,128)(2,1)S(1)}, bf16[64,2048]{1,0:T(8,128)(2,1)S(1)}, u32[]{:S(2)}, u32[]{:S(2)}) %collective-permute-start.24) | collective-permute-done | bytes 262176 | tf_op jit(solution)/shard_map/ppermute | solution.py:350
  131.8 1.5 collective-permute-start.25
  133.2 3.5 %collective-permute-done.31 = bf16[64,2048]{1,0:T(8,128)(2,1)S(1)} collective-permute-done((bf16[64,2048]{1,0:T(8,128)(2,1)S(1)}, bf16[64,2048]{1,0:T(8,128)(2,1)S(1)}, u32[]{:S(2)}, u32[]{:S(2)}) %collective-permute-start.31) | collective-permute-done | bytes 262176 | tf_op jit(solution)/shard_map/ppermute | solution.py:350
  136.9 6.0 %collective-permute-done.25 = bf16[64,2048]{1,0:T(8,128)(2,1)S(1)} collective-permute-done((bf16[64,2048]{1,0:T(8,128)(2,1)S(1)}, bf16[64,2048]{1,0:T(8,128)(2,1)S(1)}, u32[]{:S(2)}, u32[]{:S(2)}) %collective-permute-start.25) | collective-permute-done | bytes 262176 | tf_op jit(solution)/shard_map/ppermute | solution.py:350
  142.9 11.0 %collective-permute-done.32 = bf16[64,2048]{1,0:T(8,128)(2,1)S(1)} collective-permute-done((bf16[64,2048]{1,0:T(8,128)(2,1)S(1)}, bf16[64,2048]{1,0:T(8,128)(2,1)S(1)}, u32[]{:S(2)}, u32[]{:S(2)}) %collective-permute-start.32) | collective-permute-done | bytes 262176 | tf_op jit(solution)/shard_map/ppermute | solution.py:350
  154.0 0.1 add_convert_fusion.1
  154.1 1.5 collective-permute-start.33
  155.6 5.2 %collective-permute-done.33 = bf16[64,2048]{1,0:T(8,128)(2,1)S(1)} collective-permute-done((bf16[64,2048]{1,0:T(8,128)(2,1)S(1)}, bf16[64,2048]{1,0:T(8,128)(2,1)S(1)}, u32[]{:S(2)}, u32[]{:S(2)}) %collective-permute-start.33) | collective-permute-done | bytes 262176 | tf_op jit(solution)/shard_map/ppermute | solution.py:350
  160.8 0.8 add_convert_fusion
  (51 shorter events, 0.7 us)
Async XLA Ops:
  0.6 7.2 %collective-permute-start = (bf16[64,2048]{1,0:T(8,128)(2,1)}, bf16[64,2048]{1,0:T(8,128)(2,1)S(1)}, u32[]{:S(2)}, u32[]{:S(2)}) collective-permute-start(bf16[64,2048]{1,0:T(8,128)(2,1)} %hidden_ref.1), channel_id=1, source_target_pairs={{0,2},{2,0},{4,6},{6,4},{1,3},{3,1},{5,7},{7,5},{8,10},{10,8},{12,... | collective-permute-start | bytes 786440 | tf_op jit(solution)/shard_map/ppermute | solution.py:350
  1.1 17.5 %collective-permute-start.2 = (bf16[64,2048]{1,0:T(8,128)(2,1)}, bf16[64,2048]{1,0:T(8,128)(2,1)S(1)}, u32[]{:S(2)}, u32[]{:S(2)}) collective-permute-start(bf16[64,2048]{1,0:T(8,128)(2,1)} %hidden_ref.1), channel_id=1, source_target_pairs={{0,4},{2,6},{4,0},{6,2},{1,5},{3,7},{5,1},{7,3},{8,12},{10,14},{12... | collective-permute-start | bytes 786440 | tf_op jit(solution)/shard_map/ppermute | solution.py:350
  4.4 0.7 copy-start.6
  5.1 0.7 copy-start.7
  7.9 0.7 copy-start.9
  8.6 0.9 copy-start.1
  9.5 0.7 copy-start.3
  10.2 0.7 copy-start.5
  18.7 21.2 %copy-start.8 = (f32[64,2048]{1,0:T(8,128)S(1)}, f32[64,2048]{1,0:T(8,128)}, u32[]{:S(2)}) copy-start(f32[64,2048]{1,0:T(8,128)} %get-tuple-element.28) | copy-start | bytes 1572868
  18.7 1.6 collective-permute-start.3
  20.3 0.7 copy-start.10
  28.7 12.8 %copy-start.11 = (s32[64,6]{0,1:T(8,128)S(1)}, s32[64,6]{0,1:T(8,128)}, u32[]{:S(2)}) copy-start(s32[64,6]{0,1:T(8,128)} %param.23) | copy-start | bytes 4612
  28.7 18.9 %copy-start.2 = (bf16[64,2048]{1,0:T(8,128)(2,1)S(1)}, bf16[64,2048]{1,0:T(8,128)(2,1)}, u32[]{:S(2)}) copy-start(bf16[64,2048]{1,0:T(8,128)(2,1)} %hidden_ref.1) | copy-start | bytes 786436
  28.7 18.9 %copy-start.4 = (f32[2048]{0:T(1024)S(1)}, f32[2048]{0:T(1024)}, u32[]{:S(2)}) copy-start(f32[2048]{0:T(1024)} %param.32) | copy-start | bytes 24580
  28.7 36.1 %copy-start = (bf16[2048,16]{0,1:T(8,128)(2,1)S(1)}, bf16[2048,16]{0,1:T(8,128)(2,1)}, u32[]{:S(2)}) copy-start(bf16[2048,16]{0,1:T(8,128)(2,1)} %param.33) | copy-start | bytes 196612
  28.7 1.6 collective-permute-start.4
  29.0 2.6 %collective-permute-start.1 = (bf16[64,2048]{1,0:T(8,128)(2,1)S(1)}, bf16[64,2048]{1,0:T(8,128)(2,1)S(1)}, u32[]{:S(2)}, u32[]{:S(2)}) collective-permute-start(bf16[64,2048]{1,0:T(8,128)(2,1)S(1)} %get-tuple-element.29), channel_id=1, source_target_pairs={{0,2},{2,0},{4,6},{6,4},{1,3},{3,1},{5,7},{7,5},{8,10},{10,8},{12,... | collective-permute-start | bytes 786440 | tf_op jit(solution)/shard_map/ppermute | solution.py:350
  31.4 8.4 %collective-permute-start.5 = (bf16[64,2048]{1,0:T(8,128)(2,1)S(1)}, bf16[64,2048]{1,0:T(8,128)(2,1)S(1)}, u32[]{:S(2)}, u32[]{:S(2)}) collective-permute-start(bf16[64,2048]{1,0:T(8,128)(2,1)S(1)} %add_convert_fusion.7), channel_id=1, source_target_pairs={{0,4},{2,6},{4,0},{6,2},{1,5},{3,7},{5,1},{7,3},{8,12},{10,14},{12... | collective-permute-start | bytes 786440 | tf_op jit(solution)/shard_map/ppermute | solution.py:350
  40.0 7.6 %collective-permute-start.6 = (bf16[64,2048]{1,0:T(8,128)(2,1)S(1)}, bf16[64,2048]{1,0:T(8,128)(2,1)S(1)}, u32[]{:S(2)}, u32[]{:S(2)}) collective-permute-start(bf16[64,2048]{1,0:T(8,128)(2,1)S(1)} %add_convert_fusion.6.keep_ref), channel_id=1, source_target_pairs={{0,1},{1,0},{2,3},{3,2},{4,5},{5,4},{6,7},{7,6},{8,9},{9,8},{10,11... | collective-permute-start | bytes 786440 | tf_op jit(solution)/shard_map/ppermute | solution.py:350
  47.8 11.5 %collective-permute-start.9 = (bf16[64,2176]{1,0:T(8,128)(2,1)S(1)}, bf16[64,2176]{1,0:T(8,128)(2,1)S(1)}, u32[]{:S(2)}, u32[]{:S(2)}) collective-permute-start(bf16[64,2176]{1,0:T(8,128)(2,1)S(1)} %get-tuple-element.42.refs_0_), channel_id=1, source_target_pairs={{0,24},{8,16},{16,8},{24,0},{1,25},{9,17},{17,9},{25,1},{2,26},{10... | collective-permute-start | bytes 835592 | tf_op jit(solution)/shard_map/ppermute | solution.py:350
  51.5 11.3 %collective-permute-start.8 = (bf16[64,2176]{1,0:T(8,128)(2,1)S(1)}, bf16[64,2176]{1,0:T(8,128)(2,1)S(1)}, u32[]{:S(2)}, u32[]{:S(2)}) collective-permute-start(bf16[64,2176]{1,0:T(8,128)(2,1)S(1)} %get-tuple-element.42.refs_0_), channel_id=1, source_target_pairs={{0,8},{8,0},{16,24},{24,16},{1,9},{9,1},{17,25},{25,17},{2,10},{10... | collective-permute-start | bytes 835592 | tf_op jit(solution)/shard_map/ppermute | solution.py:350
  51.5 11.3 %collective-permute-start.7 = (bf16[64,2176]{1,0:T(8,128)(2,1)S(1)}, bf16[64,2176]{1,0:T(8,128)(2,1)S(1)}, u32[]{:S(2)}, u32[]{:S(2)}) collective-permute-start(bf16[64,2176]{1,0:T(8,128)(2,1)S(1)} %get-tuple-element.42.refs_0_), channel_id=1, source_target_pairs={{0,4},{2,6},{4,0},{6,2},{1,5},{3,7},{5,1},{7,3},{8,12},{10,14},{12... | collective-permute-start | bytes 835592 | tf_op jit(solution)/shard_map/ppermute | solution.py:350
  52.0 12.8 %collective-permute-start.10 = (bf16[64,2176]{1,0:T(8,128)(2,1)S(1)}, bf16[64,2176]{1,0:T(8,128)(2,1)S(1)}, u32[]{:S(2)}, u32[]{:S(2)}) collective-permute-start(bf16[64,2176]{1,0:T(8,128)(2,1)S(1)} %get-tuple-element.42.refs_0_), channel_id=1, source_target_pairs={{0,2},{2,0},{4,6},{6,4},{1,3},{3,1},{5,7},{7,5},{8,10},{10,8},{12,... | collective-permute-start | bytes 835592 | tf_op jit(solution)/shard_map/ppermute | solution.py:350
  62.8 2.0 %collective-permute-start.11 = (bf16[64,2176]{1,0:T(8,128)(2,1)S(1)}, bf16[64,2176]{1,0:T(8,128)(2,1)S(1)}, u32[]{:S(2)}, u32[]{:S(2)}) collective-permute-start(bf16[64,2176]{1,0:T(8,128)(2,1)S(1)} %collective-permute-done.7.refs_1_), channel_id=1, source_target_pairs={{0,2},{2,0},{4,6},{6,4},{1,3},{3,1},{5,7},{7,5},{8,10},{10,8},{12,... | collective-permute-start | bytes 835592 | tf_op jit(solution)/shard_map/ppermute | solution.py:350
  62.8 15.7 %collective-permute-start.20 = (bf16[64,2176]{1,0:T(8,128)(2,1)S(1)}, bf16[64,2176]{1,0:T(8,128)(2,1)S(1)}, u32[]{:S(2)}, u32[]{:S(2)}) collective-permute-start(bf16[64,2176]{1,0:T(8,128)(2,1)S(1)} %collective-permute-done.9.refs_0_), channel_id=1, source_target_pairs={{0,4},{2,6},{4,0},{6,2},{1,5},{3,7},{5,1},{7,3},{8,12},{10,14},{12... | collective-permute-start | bytes 835592 | tf_op jit(solution)/shard_map/ppermute | solution.py:350
  63.5 14.3 %collective-permute-start.14 = (bf16[64,2176]{1,0:T(8,128)(2,1)S(1)}, bf16[64,2176]{1,0:T(8,128)(2,1)S(1)}, u32[]{:S(2)}, u32[]{:S(2)}) collective-permute-start(bf16[64,2176]{1,0:T(8,128)(2,1)S(1)} %collective-permute-done.8.refs_0_), channel_id=1, source_target_pairs={{0,4},{2,6},{4,0},{6,2},{1,5},{3,7},{5,1},{7,3},{8,12},{10,14},{12... | collective-permute-start | bytes 835592 | tf_op jit(solution)/shard_map/ppermute | solution.py:350
  64.8 13.9 %collective-permute-start.15 = (bf16[64,2176]{1,0:T(8,128)(2,1)S(1)}, bf16[64,2176]{1,0:T(8,128)(2,1)S(1)}, u32[]{:S(2)}, u32[]{:S(2)}) collective-permute-start(bf16[64,2176]{1,0:T(8,128)(2,1)S(1)} %collective-permute-done.8.refs_0_), channel_id=1, source_target_pairs={{0,2},{2,0},{4,6},{6,4},{1,3},{3,1},{5,7},{7,5},{8,10},{10,8},{12,... | collective-permute-start | bytes 835592 | tf_op jit(solution)/shard_map/ppermute | solution.py:350
  72.6 28.2 %collective-permute-start.12 = (bf16[2,64,2048]{2,1,0:T(8,128)(2,1)S(1)}, bf16[2,64,2048]{2,1,0:T(8,128)(2,1)S(1)}, u32[]{:S(2)}, u32[]{:S(2)}) collective-permute-start(bf16[2,64,2048]{2,1,0:T(8,128)(2,1)S(1)} %get-tuple-element.37), channel_id=1, source_target_pairs={{0,2},{2,0},{4,6},{6,4},{1,3},{3,1},{5,7},{7,5},{8,10},{10,8},{12,... | collective-permute-start | bytes 1572872 | tf_op jit(solution)/shard_map/ppermute | solution.py:350
  77.8 1.6 collective-permute-start.16
  77.8 15.9 %collective-permute-start.26 = (bf16[64,2176]{1,0:T(8,128)(2,1)S(1)}, bf16[64,2176]{1,0:T(8,128)(2,1)S(1)}, u32[]{:S(2)}, u32[]{:S(2)}) collective-permute-start(bf16[64,2176]{1,0:T(8,128)(2,1)S(1)} %get-tuple-element.42.refs_0_), channel_id=1, source_target_pairs={{0,16},{8,24},{16,0},{24,8},{1,17},{9,25},{17,1},{25,9},{2,18},{10... | collective-permute-start | bytes 835592 | tf_op jit(solution)/shard_map/ppermute | solution.py:350
  78.5 16.0 %collective-permute-start.21 = (bf16[64,2176]{1,0:T(8,128)(2,1)S(1)}, bf16[64,2176]{1,0:T(8,128)(2,1)S(1)}, u32[]{:S(2)}, u32[]{:S(2)}) collective-permute-start(bf16[64,2176]{1,0:T(8,128)(2,1)S(1)} %collective-permute-done.9.refs_0_), channel_id=1, source_target_pairs={{0,2},{2,0},{4,6},{6,4},{1,3},{3,1},{5,7},{7,5},{8,10},{10,8},{12,... | collective-permute-start | bytes 835592 | tf_op jit(solution)/shard_map/ppermute | solution.py:350
  78.7 15.8 %collective-permute-start.22 = (bf16[64,2176]{1,0:T(8,128)(2,1)S(1)}, bf16[64,2176]{1,0:T(8,128)(2,1)S(1)}, u32[]{:S(2)}, u32[]{:S(2)}) collective-permute-start(bf16[64,2176]{1,0:T(8,128)(2,1)S(1)} %collective-permute-done.20.refs_1_), channel_id=1, source_target_pairs={{0,2},{2,0},{4,6},{6,4},{1,3},{3,1},{5,7},{7,5},{8,10},{10,8},{12,... | collective-permute-start | bytes 835592 | tf_op jit(solution)/shard_map/ppermute | solution.py:350
  85.3 16.9 %collective-permute-start.17 = (bf16[2,64,2048]{2,1,0:T(8,128)(2,1)S(1)}, bf16[2,64,2048]{2,1,0:T(8,128)(2,1)S(1)}, u32[]{:S(2)}, u32[]{:S(2)}) collective-permute-start(bf16[2,64,2048]{2,1,0:T(8,128)(2,1)S(1)} %get-tuple-element.39), channel_id=1, source_target_pairs={{0,2},{2,0},{4,6},{6,4},{1,3},{3,1},{5,7},{7,5},{8,10},{10,8},{12,... | collective-permute-start | bytes 1572872 | tf_op jit(solution)/shard_map/ppermute | solution.py:350
  93.8 21.1 %collective-permute-start.27 = (bf16[64,2176]{1,0:T(8,128)(2,1)S(1)}, bf16[64,2176]{1,0:T(8,128)(2,1)S(1)}, u32[]{:S(2)}, u32[]{:S(2)}) collective-permute-start(bf16[64,2176]{1,0:T(8,128)(2,1)S(1)} %collective-permute-done.26.refs_0_), channel_id=1, source_target_pairs={{0,4},{2,6},{4,0},{6,2},{1,5},{3,7},{5,1},{7,3},{8,12},{10,14},{12... | collective-permute-start | bytes 835592 | tf_op jit(solution)/shard_map/ppermute | solution.py:350
  94.5 20.5 %collective-permute-start.28 = (bf16[64,2176]{1,0:T(8,128)(2,1)S(1)}, bf16[64,2176]{1,0:T(8,128)(2,1)S(1)}, u32[]{:S(2)}, u32[]{:S(2)}) collective-permute-start(bf16[64,2176]{1,0:T(8,128)(2,1)S(1)} %collective-permute-done.26.refs_0_), channel_id=1, source_target_pairs={{0,2},{2,0},{4,6},{6,4},{1,3},{3,1},{5,7},{7,5},{8,10},{10,8},{12,... | collective-permute-start | bytes 835592 | tf_op jit(solution)/shard_map/ppermute | solution.py:350
  100.2 22.2 %collective-permute-start.23 = (bf16[2,64,2048]{2,1,0:T(8,128)(2,1)S(1)}, bf16[2,64,2048]{2,1,0:T(8,128)(2,1)S(1)}, u32[]{:S(2)}, u32[]{:S(2)}) collective-permute-start(bf16[2,64,2048]{2,1,0:T(8,128)(2,1)S(1)} %get-tuple-element.41), channel_id=1, source_target_pairs={{0,2},{2,0},{4,6},{6,4},{1,3},{3,1},{5,7},{7,5},{8,10},{10,8},{12,... | collective-permute-start | bytes 1572872 | tf_op jit(solution)/shard_map/ppermute | solution.py:350
  100.8 9.2 %collective-permute-start.13 = (bf16[64,2048]{1,0:T(8,128)(2,1)S(1)}, bf16[64,2048]{1,0:T(8,128)(2,1)S(1)}, u32[]{:S(2)}, u32[]{:S(2)}) collective-permute-start(bf16[64,2048]{1,0:T(8,128)(2,1)S(1)} %fusion.3), channel_id=1, source_target_pairs={{0,4},{2,6},{4,0},{6,2},{1,5},{3,7},{5,1},{7,3},{8,12},{10,14},{12... | collective-permute-start | bytes 786440 | tf_op jit(solution)/shard_map/ppermute | solution.py:350
  102.3 12.5 %collective-permute-start.18 = (bf16[64,2048]{1,0:T(8,128)(2,1)S(1)}, bf16[64,2048]{1,0:T(8,128)(2,1)S(1)}, u32[]{:S(2)}, u32[]{:S(2)}) collective-permute-start(bf16[64,2048]{1,0:T(8,128)(2,1)S(1)} %fusion.4), channel_id=1, source_target_pairs={{0,4},{2,6},{4,0},{6,2},{1,5},{3,7},{5,1},{7,3},{8,12},{10,14},{12... | collective-permute-start | bytes 786440 | tf_op jit(solution)/shard_map/ppermute | solution.py:350
  114.9 1.6 %collective-permute-start.29 = (bf16[64,2176]{1,0:T(8,128)(2,1)S(1)}, bf16[64,2176]{1,0:T(8,128)(2,1)S(1)}, u32[]{:S(2)}, u32[]{:S(2)}) collective-permute-start(bf16[64,2176]{1,0:T(8,128)(2,1)S(1)} %collective-permute-done.27.refs_1_), channel_id=1, source_target_pairs={{0,2},{2,0},{4,6},{6,4},{1,3},{3,1},{5,7},{7,5},{8,10},{10,8},{12,... | collective-permute-start | bytes 835592 | tf_op jit(solution)/shard_map/ppermute | solution.py:350
  122.2 2.0 %collective-permute-start.30 = (bf16[2,64,2048]{2,1,0:T(8,128)(2,1)S(1)}, bf16[2,64,2048]{2,1,0:T(8,128)(2,1)S(1)}, u32[]{:S(2)}, u32[]{:S(2)}) collective-permute-start(bf16[2,64,2048]{2,1,0:T(8,128)(2,1)S(1)} %get-tuple-element.46), channel_id=1, source_target_pairs={{0,2},{2,0},{4,6},{6,4},{1,3},{3,1},{5,7},{7,5},{8,10},{10,8},{12,... | collective-permute-start | bytes 1572872 | tf_op jit(solution)/shard_map/ppermute | solution.py:350
  122.5 9.2 %collective-permute-start.24 = (bf16[64,2048]{1,0:T(8,128)(2,1)S(1)}, bf16[64,2048]{1,0:T(8,128)(2,1)S(1)}, u32[]{:S(2)}, u32[]{:S(2)}) collective-permute-start(bf16[64,2048]{1,0:T(8,128)(2,1)S(1)} %fusion.5), channel_id=1, source_target_pairs={{0,4},{2,6},{4,0},{6,2},{1,5},{3,7},{5,1},{7,3},{8,12},{10,14},{12... | collective-permute-start | bytes 786440 | tf_op jit(solution)/shard_map/ppermute | solution.py:350
  123.9 19.1 %collective-permute-start.19 = (bf16[64,2048]{1,0:T(8,128)(2,1)S(1)}, bf16[64,2048]{1,0:T(8,128)(2,1)S(1)}, u32[]{:S(2)}, u32[]{:S(2)}) collective-permute-start(bf16[64,2048]{1,0:T(8,128)(2,1)S(1)} %fusion.2), channel_id=1, source_target_pairs={{0,8},{8,0},{16,24},{24,16},{1,9},{9,1},{17,25},{25,17},{2,10},{10... | collective-permute-start | bytes 786440 | tf_op jit(solution)/shard_map/ppermute | solution.py:350
  124.2 12.5 %collective-permute-start.31 = (bf16[64,2048]{1,0:T(8,128)(2,1)S(1)}, bf16[64,2048]{1,0:T(8,128)(2,1)S(1)}, u32[]{:S(2)}, u32[]{:S(2)}) collective-permute-start(bf16[64,2048]{1,0:T(8,128)(2,1)S(1)} %fusion.6), channel_id=1, source_target_pairs={{0,4},{2,6},{4,0},{6,2},{1,5},{3,7},{5,1},{7,3},{8,12},{10,14},{12... | collective-permute-start | bytes 786440 | tf_op jit(solution)/shard_map/ppermute | solution.py:350
  131.8 11.2 %collective-permute-start.25 = (bf16[64,2048]{1,0:T(8,128)(2,1)S(1)}, bf16[64,2048]{1,0:T(8,128)(2,1)S(1)}, u32[]{:S(2)}, u32[]{:S(2)}) collective-permute-start(bf16[64,2048]{1,0:T(8,128)(2,1)S(1)} %fusion.1), channel_id=1, source_target_pairs={{0,24},{8,16},{16,8},{24,0},{1,25},{9,17},{17,9},{25,1},{2,26},{10... | collective-permute-start | bytes 786440 | tf_op jit(solution)/shard_map/ppermute | solution.py:350
  136.8 17.1 %collective-permute-start.32 = (bf16[64,2048]{1,0:T(8,128)(2,1)S(1)}, bf16[64,2048]{1,0:T(8,128)(2,1)S(1)}, u32[]{:S(2)}, u32[]{:S(2)}) collective-permute-start(bf16[64,2048]{1,0:T(8,128)(2,1)S(1)} %fusion), channel_id=1, source_target_pairs={{0,16},{8,24},{16,0},{24,8},{1,17},{9,25},{17,1},{25,9},{2,18},{10... | collective-permute-start | bytes 786440 | tf_op jit(solution)/shard_map/ppermute | solution.py:350
  154.1 6.7 %collective-permute-start.33 = (bf16[64,2048]{1,0:T(8,128)(2,1)S(1)}, bf16[64,2048]{1,0:T(8,128)(2,1)S(1)}, u32[]{:S(2)}, u32[]{:S(2)}) collective-permute-start(bf16[64,2048]{1,0:T(8,128)(2,1)S(1)} %add_convert_fusion.1), channel_id=1, source_target_pairs={{0,1},{1,0},{2,3},{3,2},{4,5},{5,4},{6,7},{7,6},{8,9},{9,8},{10,11... | collective-permute-start | bytes 786440 | tf_op jit(solution)/shard_map/ppermute | solution.py:350

commit v5 on v3

--- a/solution.py
+++ b/solution.py
@@ -52,15 +52,23 @@
 
 WHOLE = pl.BlockSpec(memory_space=pltpu.VMEM)
 SCALARS = pl.BlockSpec(memory_space=pltpu.SMEM)
-PLACED = pl.BlockSpec(memory_space=pl.ANY)
+
+
+SMALL = pl.CostEstimate(flops=1, bytes_accessed=1, transcendentals=0)
+LONG = pl.CostEstimate(flops=20000000000, bytes_accessed=1, transcendentals=0)
+LONGER = pl.CostEstimate(flops=30000000000, bytes_accessed=1, transcendentals=0)
 
 
 def params(megabytes):
     return pltpu.CompilerParams(vmem_limit_bytes=megabytes << 20)
 
 
-def tree_kernel(row_ref, lengths_ref, accepted_ref, parents_ref, closure_ref, turns_ref, places_ref):
+def tree_kernel(
+    row_ref, lengths_ref, accepted_ref, parents_ref, closure_ref, turns_ref, places_ref, expert_ref
+):
     requests, size, _ = closure_ref.shape
+    expert_ids = lax.broadcasted_iota(jnp.int32, expert_ref.shape, 1)
+    expert_ref[...] = (expert_ids == row_ref[1]).astype(jnp.float32)
     down = lax.broadcasted_iota(jnp.int32, (size, size), 0)
     across = lax.broadcasted_iota(jnp.int32, (size, size), 1)
     eye = (down == across).astype(jnp.bfloat16)
@@ -83,9 +91,11 @@
     for k in range(requests):
         closure_ref[k] = closures[k]
         depth = jnp.sum(closures[k], axis=-1, keepdims=True) - 1.0
-        angles = (lengths_ref[row_ref[0] ^ k].astype(jnp.float32) + depth) * frequency
+        length = lengths_ref[row_ref[0] ^ k].astype(jnp.float32)
+        angles = (length + depth) * frequency
         turns_ref[k, :, : ROPE // 2] = jnp.cos(angles)
-        turns_ref[k, :, ROPE // 2 :] = jnp.sin(angles)
+        turns_ref[k, :, ROPE // 2 : ROPE] = jnp.sin(angles)
+        turns_ref[k, :, ROPE : ROPE + 1] = jnp.full((size, 1), length)
     own = closures[0].astype(jnp.bfloat16)
     depth_row = transposed_dot(jnp.ones((8, size), jnp.bfloat16), own)[:1] - 1.0
     chosen = (lax.broadcasted_iota(jnp.int32, (size, 1), 0) == accepted_ref[0]).astype(jnp.float32)
@@ -95,28 +105,29 @@
     ).astype(jnp.bfloat16)
 
 
-def tree_tables(row_index, lengths, accepted, parents):
+def tree_tables(indices, lengths, accepted, parents, experts):
     requests, size = parents.shape
     return pl.pallas_call(
         tree_kernel,
         out_shape=(
             jax.ShapeDtypeStruct((requests, size, size), jnp.float32),
-            jax.ShapeDtypeStruct((requests, size, ROPE), jnp.float32),
+            jax.ShapeDtypeStruct((requests, size, ROPE + 1), jnp.float32),
             jax.ShapeDtypeStruct((size, size), jnp.bfloat16),
+            jax.ShapeDtypeStruct((1, experts), jnp.float32),
         ),
         in_specs=[SCALARS, SCALARS, SCALARS, WHOLE],
-        out_specs=(WHOLE, WHOLE, WHOLE),
+        out_specs=(WHOLE, WHOLE, WHOLE, WHOLE),
         compiler_params=params(16),
+        cost_estimate=LONG,
         name="trees",
-    )(row_index, lengths, accepted, parents)
-
-
-def attention_kernel(first, place, row_ref, lengths_ref, *refs):
+    )(indices, lengths, accepted, parents)
+
+
+def attention_kernel(first, place, row_ref, *refs):
     (
         first_ref,
         second_ref,
-        cache_a_ref,
-        cache_b_ref,
+        cache_ref,
         closure_ref,
         turns_ref,
         places_ref,
@@ -129,7 +140,7 @@
         output_ref,
         keep_ref,
         send_ref,
-    ) = refs[:16]
+    ) = refs[:15]
     size = first_ref.shape[0]
     heads = key_ref.shape[0]
     bf16 = jnp.bfloat16
@@ -137,12 +148,12 @@
     rows = jnp.concatenate([first_ref[...], second_ref[...]], axis=0).astype(jnp.float32)
     rows = rms_scale(rows, gain_ref[...]).astype(bf16)
     turns = jnp.concatenate([turns_ref[place], turns_ref[place + 1]], axis=0)
-    cosine, sine_part = turns[:, : ROPE // 2], turns[:, ROPE // 2 :]
+    cosine, sine_part = turns[:, : ROPE // 2], turns[:, ROPE // 2 : ROPE]
     projected = transposed_dot(rows, latent_ref[...])
     content = rms_scale(projected[:, :LAT], latent_gain_ref[...]).astype(bf16)
     key_rope = rotate(projected[:, LAT:], cosine, sine_part).astype(bf16)
     if first:
-        accepted_ref = refs[16]
+        accepted_ref = refs[15]
         accepted_ref[0, :, :LAT] = dot(places_ref[...], content[:size]).astype(bf16)
         accepted_ref[0, :, LAT:] = dot(places_ref[...], key_rope[:size]).astype(bf16)
     queries = dot(rows, query_ref[...])
@@ -155,14 +166,15 @@
         turned = queries[:, start + NOPE : start + NOPE + ROPE].astype(bf16).astype(jnp.float32)
         query_rope.append(rotate(turned, cosine, sine_part).astype(bf16))
     outs = [[], []]
-    for r, cache_ref in enumerate((cache_a_ref, cache_b_ref)):
+    for r in range(2):
+        spot = row_ref[0] ^ (place + r)
         part = slice(r * size, (r + 1) * size)
         latent_rows = jnp.concatenate([each[part] for each in query_latent], axis=0)
         rope_rows = jnp.concatenate([each[part] for each in query_rope], axis=0)
-        old = dot(latent_rows, cache_ref[0, :LAT, :]) + dot(rope_rows, cache_ref[0, LAT:, :])
+        old = dot(latent_rows, cache_ref[spot, :LAT, :]) + dot(rope_rows, cache_ref[spot, LAT:, :])
         new = transposed_dot(latent_rows, content[part]) + transposed_dot(rope_rows, key_rope[part])
-        length = lengths_ref[row_ref[0] ^ (place + r)]
-        spots = lax.broadcasted_iota(jnp.int32, (1, old.shape[1]), 1)
+        length = jnp.concatenate([turns_ref[place + r, :, ROPE : ROPE + 1]] * heads, axis=0)
+        spots = lax.broadcasted_iota(jnp.int32, old.shape, 1).astype(jnp.float32)
         allowed = (spots < length) & ((spots < SINK) | (spots >= length - WINDOW))
         related = jnp.concatenate([closure_ref[place + r]] * heads, axis=0) > 0.5
         old = jnp.where(allowed, old * scale_factor, -1e30)
@@ -175,7 +187,7 @@
         total = jnp.sum(old, axis=-1, keepdims=True) + jnp.sum(new, axis=-1, keepdims=True)
         old = (old / total).astype(bf16)
         new = (new / total).astype(bf16)
-        mixed = transposed_dot(old, cache_ref[0, :LAT, :]) + dot(new, content[part])
+        mixed = transposed_dot(old, cache_ref[spot, :LAT, :]) + dot(new, content[part])
         for h in range(heads):
             outs[r].append(mixed[h * size : (h + 1) * size].astype(bf16))
     head_rows = [
@@ -188,46 +200,23 @@
     send_ref[...] = partial[size:].astype(bf16)
 
 
-def attention_part(first, place, row_index, lengths, blocks, cache, tables, weights):
+def attention_part(first, place, row_index, blocks, cache, tables, weights):
     size, width = blocks[0].shape
-    slots, spots = cache.shape[1:]
-    heads = weights[4].shape[0]
-    closure, turns, places = tables
-
-    def whole(array):
-        rank = array.ndim
-        return pl.BlockSpec(array.shape, lambda i, row, lens: (0,) * rank)
-
-    def cached(k):
-        return pl.BlockSpec((1, slots, spots), lambda i, row, lens: (row[0] ^ k, 0, 0))
-
-    rest = [closure, turns, places, *weights]
     out_shape = [
         jax.ShapeDtypeStruct((size, width), jnp.float32),
         jax.ShapeDtypeStruct((size, width), jnp.bfloat16),
     ]
     if first:
         out_shape.append(jax.ShapeDtypeStruct((1, size, LAT + ROPE), jnp.bfloat16))
-    rows = 2 * size
-    flops = 2 * rows * width * (weights[1].shape[1] + LAT + ROPE + heads * VDIM)
     return pl.pallas_call(
         functools.partial(attention_kernel, first, place),
         out_shape=tuple(out_shape),
-        grid_spec=pltpu.PrefetchScalarGridSpec(
-            num_scalar_prefetch=2,
-            grid=(1,),
-            in_specs=[whole(blocks[0]), whole(blocks[1]), cached(place), cached(place + 1)]
-            + [whole(each) for each in rest],
-            out_specs=tuple(whole(each) for each in out_shape),
-        ),
-        compiler_params=params(32),
-        cost_estimate=pl.CostEstimate(
-            flops=flops,
-            bytes_accessed=2 * width * (weights[1].shape[1] + LAT + ROPE + heads * VDIM),
-            transcendentals=rows * heads * (spots + size),
-        ),
+        in_specs=[SCALARS] + [WHOLE] * 13,
+        out_specs=(WHOLE,) * len(out_shape),
+        compiler_params=params(12),
+        cost_estimate=SMALL,
         name="attention",
-    )(row_index, lengths, blocks[0], blocks[1], cache, cache, *rest)
+    )(row_index, *blocks, cache, *tables, *weights)
 
 
 def join_kernel(hidden_ref, keep_ref, arrived_ref, gain_ref, named_ref, residual_ref, block_ref):
@@ -252,6 +241,7 @@
         in_specs=[WHOLE] * 5,
         out_specs=(WHOLE, WHOLE),
         compiler_params=params(16),
+        cost_estimate=LONGER,
         name="join",
     )(hidden, keep, arrived, gain, named)
 
@@ -304,14 +294,14 @@
         ),
         in_specs=[WHOLE] * len(operands),
         out_specs=(WHOLE, WHOLE),
-        compiler_params=params(32),
-        cost_estimate=pl.CostEstimate(
-            flops=24 * size * width * units,
-            bytes_accessed=6 * width * units,
-            transcendentals=4 * size * units,
-        ),
+        compiler_params=params(12),
+        cost_estimate=SMALL,
         name="experts",
     )(*operands)
+
+
+def after(values, *others):
+    return lax.optimization_barrier((values, *others))[0]
 
 
 def swap(values, axis, size, bits):
@@ -341,17 +331,16 @@
     expert_down,
 ):
     n_req, n_row, n_col = sizes
-    experts = router_weight.shape[1]
     req_index = lax.axis_index("req")
     row_index = lax.axis_index("row")
     bf16 = jnp.bfloat16
 
     far = swap(hidden, "row", n_row, 2)
     near = swap(hidden, "row", n_row, 1)
-    far_near = swap(far, "row", n_row, 1)
-
-    row_scalar = row_index.astype(jnp.int32).reshape(1)
-    tables = tree_tables(row_scalar, lengths, accepted, parents)
+
+    experts = router_weight.shape[1]
+    indices = jnp.stack([row_index, req_index * n_row + row_index]).astype(jnp.int32)
+    *tables, own_expert = tree_tables(indices, lengths, accepted, parents, experts)
     cache = jnp.swapaxes(latent_cache, 1, 2)
     weights = (
         input_gain[None],
@@ -363,10 +352,12 @@
         output_weight,
     )
     own_keep, own_send, accepted_latents = attention_part(
-        True, 0, row_scalar, lengths, (hidden, near), cache, tables, weights
-    )
+        True, 0, indices, (hidden, near), cache, tables, weights
+    )
+    far = after(far, own_send)
+    far_near = swap(far, "row", n_row, 1)
     far_keep, far_send = attention_part(
-        False, 2, row_scalar, lengths, (far, far_near), cache, tables, weights
+        False, 2, indices, (far, far_near), cache, tables, weights
     )
 
     def fold(keep, sent):
@@ -378,32 +369,38 @@
     named = (routes[:, :, None] == jnp.arange(EXTRA, dtype=jnp.int32)).any(axis=1).astype(bf16)
     residual, block = joined(hidden, partial, arrived, post_gain[None], named)
 
-    own_expert = jnp.arange(experts, dtype=jnp.int32) == req_index * n_row + row_index
-    own_expert = own_expert.astype(jnp.float32)[None]
     router = router_weight.T
     routed_weights = (jnp.swapaxes(expert_gate_up[0], 1, 2), expert_down[0])
     shared_weights = (jnp.swapaxes(shared_gate_up, 1, 2), shared_down)
-    distances = [*range(n_req - 1, 0, -1)]
-    blocks = {s: swap(block, "req", n_req, s) for s in distances}
-    blocks[0] = block
-    total = None
-    for s in [0, *distances]:
-        far = swap(blocks[s], "row", n_row, 2)
-        near = swap(blocks[s], "row", n_row, 1)
+    distances = [0, 1, *range(n_req - 1, 1, -1)]
+    blocks = [block]
+    for k, s in enumerate(distances[1:], 1):
+        source = block if k < 3 else after(block, blocks[k - 2])
+        blocks.append(swap(source, "req", n_req, s))
+    sends, parts = [], []
+    for k, s in enumerate(distances):
+        far = swap(after(blocks[k], *sends[: max(0, k - 2)]), "row", n_row, 2)
+        near = swap(blocks[k], "row", n_row, 1)
+        if k == 0:
+            far = after(far, *blocks[1:3])
+        elif k > 2:
+            far = after(far, *sends, *parts[: k - 1])
         far_near = swap(far, "row", n_row, 1)
         keep, send = expert_part(
-            (blocks[s], far, near, far_near),
+            (blocks[k], far, near, far_near),
             own_expert,
             router,
             routed_weights,
             () if s else shared_weights,
         )
-        from_near = swap(send, "row", n_row, 1).astype(jnp.float32)
-        from_far = swap((keep[1] + from_near[1]).astype(bf16), "row", n_row, 2)
-        part = keep[0] + from_near[0] + from_far.astype(jnp.float32)
-        if s:
-            part = swap(part.astype(bf16), "req", n_req, s).astype(jnp.float32)
-        total = part if total is None else total + part
+        sends.append(send)
+        from_near = swap(send, "row", n_row, 1)
+        from_far = swap((keep[1] + from_near[1].astype(jnp.float32)).astype(bf16), "row", n_row, 2)
+        part = keep[0] + from_near[0].astype(jnp.float32) + from_far.astype(jnp.float32)
+        parts.append(part.astype(bf16) if s else part)
+    total = parts[0]
+    for s, part in zip(distances[1:], parts[1:]):
+        total = total + swap(part, "req", n_req, s).astype(jnp.float32)
     total, arrived = col_parts(total, n_col)
     layer_output = residual + (total.astype(jnp.float32) + sum_up(arrived))
     return (layer_output.astype(bf16), accepted_latents)

time: 165 us -> 141 us (0.85)
  the two profiles are of different devices: /device:TPU:8 before, /device:TPU:0 now
where the time goes in v5:
time: 141 us
  waiting for transfers between devices  87.8 us (62%)
  Pallas kernels  25 us (18%)
  starting transfers between devices  22.6 us (16%)
  local copies, waits for them, and re-layouts  2.28 us (2%)
  other arithmetic  1.89 us (1%)
  between operations  1.62 us (1%)
    ppermute x34, waiting for transfers between devices, swap(): return lax.ppermute(values, axis, [(i, i ^ bits) for i in range(size)])  87.8 us
    ppermute x34, starting transfers between devices, swap(): return lax.ppermute(values, axis, [(i, i ^ bits) for i in range(size)])  22.6 us
    pallas_call x4, Pallas kernels, expert_part(): pl.pallas_call(functools.partial(expert_kernel, bool(shared_weights)), ou...  14.5 us
    pallas_call x2, Pallas kernels, attention_part(): pl.pallas_call(functools.partial(attention_kernel, first, place), out_sha...  8.21 us
  transfers between devices with their start and end apart: 34, of which 19 were waited for; matrix products, arithmetic and copies ran while one was open for 1% of the time, Pallas kernels for 15%

profile of v5, /device:TPU:0, one launch (start us, length us, event | category | flops | bytes accessed | tf_op | source)
XLA Modules:
  0.0 141.3 jit_solution(13000744489228692955)
XLA Ops:
  0.6 0.5 collective-permute-start
  1.1 2.6 %collective-permute-start.2 = (bf16[64,2048]{1,0:T(8,128)(2,1)}, bf16[64,2048]{1,0:T(8,128)(2,1)S(1)}, u32[]{:S(2)}, u32[]{:S(2)}) collective-permute-start(bf16[64,2048]{1,0:T(8,128)(2,1)} %hidden_ref.1), channel_id=1, source_target_pairs={{0,4},{2,6},{4,0},{6,2},{1,5},{3,7},{5,1},{7,3},{8,12},{10,14},{12... | collective-permute-start | bytes 786440 | tf_op jit(solution)/shard_map/ppermute | solution.py:308
  4.5 0.7 copy-done.14
  5.2 0.7 copy-done.15
  5.9 2.1 %trees.1 = (f32[4,64,64]{2,1,0:T(8,128)S(1)}, f32[4,64,65]{2,1,0:T(8,128)S(1)}, bf16[64,64]{1,0:T(8,128)(2,1)S(1)}, f32[1,16]{1,0:T(1,128)S(1)}) custom-call(s32[2]{0:T(128)S(1)} %pad_add_fusion.row_ref, s32[4]{0:T(128)S(1)} %copy-done.15, s32[1]{0:T(128)S(6)} %copy.22.accepted_ref, s32[4,64]{1,0:T(4,128)S(1)} %copy-done.14), custom_call_target="tpu_custom_call" | custom-call | flops 20000000000 | bytes 1 | tf_op jit(solution)/shard_map/trees/pallas_call | solution.py:110
  8.0 0.4 copy-done.3
  8.5 0.3 copy-done.4
  8.8 0.1 copy-done.9
  8.9 4.4 %attention.2 = (f32[64,2048]{1,0:T(8,128)S(1)}, bf16[64,2048]{1,0:T(8,128)(2,1)S(1)}, bf16[1,64,576]{2,1,0:T(8,128)(2,1)}) custom-call(s32[2]{0:T(128)S(1)} %pad_add_fusion.row_ref, bf16[64,2048]{1,0:T(8,128)(2,1)S(1)} %copy-done.10, bf16[64,2048]{1,0:T(8,128)(2,1)S(1)} %collective-permute-done.refs_1_, bf16[4,576,384]{2,1,0:T(8,128)(2,1)S(1)} %bitcast.48, ...), custom_call_target="tpu_custom_call" | custom-call | flops 1 | bytes 1 | tf_op jit(solution)/shard_map/attention/pallas_call | solution.py:211
  13.3 0.2 collective-permute-start.3
  13.5 1.4 collective-permute-done.3.refs_1_
  14.8 3.8 %attention.3 = (f32[64,2048]{1,0:T(8,128)S(1)}, bf16[64,2048]{1,0:T(8,128)(2,1)S(1)}) custom-call(s32[2]{0:T(128)S(1)} %pad_add_fusion.row_ref, bf16[64,2048]{1,0:T(8,128)(2,1)S(1)} %collective-permute-done.2.refs_0_, bf16[64,2048]{1,0:T(8,128)(2,1)S(1)} %collective-permute-done.3.refs_1_, bf16[4,576,384]{2,1,0:T(8,128)(2,1)S(1)} %bitcast.49, ...), custom_call_target="tpu_custom_call" | custom-call | flops 1 | bytes 1 | tf_op jit(solution)/shard_map/attention/pallas_call | solution.py:211
  18.7 0.2 collective-permute-start.4
  18.9 0.3 collective-permute-start.1
  19.3 1.0 collective-permute-done.4
  20.4 0.1 collective-permute-start.5
  20.5 0.2 collective-permute-done.1
  20.7 8.1 %collective-permute-done.5 = bf16[64,2048]{1,0:T(8,128)(2,1)S(1)} collective-permute-done((bf16[64,2048]{1,0:T(8,128)(2,1)S(1)}, bf16[64,2048]{1,0:T(8,128)(2,1)S(1)}, u32[]{:S(2)}, u32[]{:S(2)}) %collective-permute-start.5) | collective-permute-done | bytes 262176 | tf_op jit(solution)/shard_map/ppermute | solution.py:308
  28.8 0.1 add_convert_fusion.6.keep_ref
  28.9 1.6 %collective-permute-start.6 = (bf16[64,2048]{1,0:T(8,128)(2,1)S(1)}, bf16[64,2048]{1,0:T(8,128)(2,1)S(1)}, u32[]{:S(2)}, u32[]{:S(2)}) collective-permute-start(bf16[64,2048]{1,0:T(8,128)(2,1)S(1)} %add_convert_fusion.6.keep_ref), channel_id=1, source_target_pairs={{0,1},{1,0},{2,3},{3,2},{4,5},{5,4},{6,7},{7,6},{8,9},{9,8},{10,11... | collective-permute-start | bytes 786440 | tf_op jit(solution)/shard_map/ppermute | solution.py:308
  30.4 0.1 fusion.7
  30.6 5.9 %collective-permute-done.6 = bf16[64,2048]{1,0:T(8,128)(2,1)S(1)} collective-permute-done((bf16[64,2048]{1,0:T(8,128)(2,1)S(1)}, bf16[64,2048]{1,0:T(8,128)(2,1)S(1)}, u32[]{:S(2)}, u32[]{:S(2)}) %collective-permute-start.6) | collective-permute-done | bytes 262176 | tf_op jit(solution)/shard_map/ppermute | solution.py:308
  36.5 0.2 join.1
  36.8 3.7 %collective-permute-start.9 = (bf16[64,2176]{1,0:T(8,128)(2,1)S(1)}, bf16[64,2176]{1,0:T(8,128)(2,1)S(1)}, u32[]{:S(2)}, u32[]{:S(2)}) collective-permute-start(bf16[64,2176]{1,0:T(8,128)(2,1)S(1)} %get-tuple-element.44.refs_0_), channel_id=1, source_target_pairs={{0,24},{8,16},{16,8},{24,0},{1,25},{9,17},{17,9},{25,1},{2,26},{10... | collective-permute-start | bytes 835592 | tf_op jit(solution)/shard_map/ppermute | solution.py:308
  40.4 0.5 collective-permute-start.7
  41.0 7.3 %collective-permute-done.9.refs_0_ = bf16[64,2176]{1,0:T(8,128)(2,1)S(1)} collective-permute-done((bf16[64,2176]{1,0:T(8,128)(2,1)S(1)}, bf16[64,2176]{1,0:T(8,128)(2,1)S(1)}, u32[]{:S(2)}, u32[]{:S(2)}) %collective-permute-start.9) | collective-permute-done | bytes 278560 | tf_op jit(solution)/shard_map/ppermute | solution.py:308
  48.2 3.5 %collective-permute-done.8.refs_0_ = bf16[64,2176]{1,0:T(8,128)(2,1)S(1)} collective-permute-done((bf16[64,2176]{1,0:T(8,128)(2,1)S(1)}, bf16[64,2176]{1,0:T(8,128)(2,1)S(1)}, u32[]{:S(2)}, u32[]{:S(2)}) %collective-permute-start.8) | collective-permute-done | bytes 278560 | tf_op jit(solution)/shard_map/ppermute | solution.py:308
  51.8 0.7 collective-permute-start.14
  52.5 1.3 collective-permute-start.20
  53.9 4.6 %experts.4 = (f32[2,64,2048]{2,1,0:T(8,128)S(1)}, bf16[2,64,2048]{2,1,0:T(8,128)(2,1)S(1)}) custom-call(bf16[64,2176]{1,0:T(8,128)(2,1)S(1)} %get-tuple-element.44.refs_0_, bf16[64,2176]{1,0:T(8,128)(2,1)S(1)} %collective-permute-done.7.refs_1_, bf16[64,2176]{1,0:T(8,128)(2,1)S(1)} %collective-permute-done.10.refs_2_, ...), custom_call_target="tpu_custom_call" | custom-call | flops 1 | bytes 1 | tf_op jit(solution)/shard_map/experts/pallas_call | solution.py:289
  58.5 0.6 collective-permute-start.12
  59.0 2.2 %collective-permute-done.14.refs_1_ = bf16[64,2176]{1,0:T(8,128)(2,1)S(1)} collective-permute-done((bf16[64,2176]{1,0:T(8,128)(2,1)S(1)}, bf16[64,2176]{1,0:T(8,128)(2,1)S(1)}, u32[]{:S(2)}, u32[]{:S(2)}) %collective-permute-start.14) | collective-permute-done | bytes 278560 | tf_op jit(solution)/shard_map/ppermute | solution.py:308
  61.2 0.7 collective-permute-start.26
  61.9 4.9 %collective-permute-done.20.refs_1_ = bf16[64,2176]{1,0:T(8,128)(2,1)S(1)} collective-permute-done((bf16[64,2176]{1,0:T(8,128)(2,1)S(1)}, bf16[64,2176]{1,0:T(8,128)(2,1)S(1)}, u32[]{:S(2)}, u32[]{:S(2)}) %collective-permute-start.20) | collective-permute-done | bytes 278560 | tf_op jit(solution)/shard_map/ppermute | solution.py:308
  66.8 0.5 collective-permute-start.22
  67.3 3.4 %experts.5 = (f32[2,64,2048]{2,1,0:T(8,128)S(1)}, bf16[2,64,2048]{2,1,0:T(8,128)(2,1)S(1)}) custom-call(bf16[64,2176]{1,0:T(8,128)(2,1)S(1)} %collective-permute-done.8.refs_0_, bf16[64,2176]{1,0:T(8,128)(2,1)S(1)} %collective-permute-done.14.refs_1_, bf16[64,2176]{1,0:T(8,128)(2,1)S(1)} %collective-permute-done.15.refs_2_, ...), custom_call_target="tpu_custom_call" | custom-call | flops 1 | bytes 1 | tf_op jit(solution)/shard_map/experts/pallas_call | solution.py:289
  70.7 0.1 collective-permute-start.17
  70.8 6.3 %collective-permute-done.26.refs_0_ = bf16[64,2176]{1,0:T(8,128)(2,1)S(1)} collective-permute-done((bf16[64,2176]{1,0:T(8,128)(2,1)S(1)}, bf16[64,2176]{1,0:T(8,128)(2,1)S(1)}, u32[]{:S(2)}, u32[]{:S(2)}) %collective-permute-start.26) | collective-permute-done | bytes 278560 | tf_op jit(solution)/shard_map/ppermute | solution.py:308
  77.1 0.7 collective-permute-start.27
  77.9 3.2 %experts.6 = (f32[2,64,2048]{2,1,0:T(8,128)S(1)}, bf16[2,64,2048]{2,1,0:T(8,128)(2,1)S(1)}) custom-call(bf16[64,2176]{1,0:T(8,128)(2,1)S(1)} %collective-permute-done.9.refs_0_, bf16[64,2176]{1,0:T(8,128)(2,1)S(1)} %collective-permute-done.20.refs_1_, bf16[64,2176]{1,0:T(8,128)(2,1)S(1)} %collective-permute-done.21.refs_2_, ...), custom_call_target="tpu_custom_call" | custom-call | flops 1 | bytes 1 | tf_op jit(solution)/shard_map/experts/pallas_call | solution.py:289
  81.1 0.6 collective-permute-start.23
  81.8 1.4 collective-permute-start.13
  83.2 0.8 collective-permute-start.18
  84.0 8.0 %collective-permute-done.13 = bf16[64,2048]{1,0:T(8,128)(2,1)S(1)} collective-permute-done((bf16[64,2048]{1,0:T(8,128)(2,1)S(1)}, bf16[64,2048]{1,0:T(8,128)(2,1)S(1)}, u32[]{:S(2)}, u32[]{:S(2)}) %collective-permute-start.13) | collective-permute-done | bytes 262176 | tf_op jit(solution)/shard_map/ppermute | solution.py:308
  92.0 0.1 bitcast_add_fusion.3
  92.1 4.6 %collective-permute-done.18 = bf16[64,2048]{1,0:T(8,128)(2,1)S(1)} collective-permute-done((bf16[64,2048]{1,0:T(8,128)(2,1)S(1)}, bf16[64,2048]{1,0:T(8,128)(2,1)S(1)}, u32[]{:S(2)}, u32[]{:S(2)}) %collective-permute-start.18) | collective-permute-done | bytes 262176 | tf_op jit(solution)/shard_map/ppermute | solution.py:308
  96.7 0.1 fusion.2
  96.9 1.5 %collective-permute-done.29.refs_3_ = bf16[64,2176]{1,0:T(8,128)(2,1)S(1)} collective-permute-done((bf16[64,2176]{1,0:T(8,128)(2,1)S(1)}, bf16[64,2176]{1,0:T(8,128)(2,1)S(1)}, u32[]{:S(2)}, u32[]{:S(2)}) %collective-permute-start.29) | collective-permute-done | bytes 278560 | tf_op jit(solution)/shard_map/ppermute | solution.py:308
  98.4 3.2 %experts.7 = (f32[2,64,2048]{2,1,0:T(8,128)S(1)}, bf16[2,64,2048]{2,1,0:T(8,128)(2,1)S(1)}) custom-call(bf16[64,2176]{1,0:T(8,128)(2,1)S(1)} %collective-permute-done.26.refs_0_, bf16[64,2176]{1,0:T(8,128)(2,1)S(1)} %collective-permute-done.27.refs_1_, bf16[64,2176]{1,0:T(8,128)(2,1)S(1)} %collective-permute-done.28.refs_2_, ...), custom_call_target="tpu_custom_call" | custom-call | flops 1 | bytes 1 | tf_op jit(solution)/shard_map/experts/pallas_call | solution.py:289
  101.6 0.2 collective-permute-start.30
  101.9 0.8 collective-permute-start.24
  102.7 0.9 collective-permute-done.30
  103.7 0.8 collective-permute-start.31
  104.5 6.6 %collective-permute-done.24 = bf16[64,2048]{1,0:T(8,128)(2,1)S(1)} collective-permute-done((bf16[64,2048]{1,0:T(8,128)(2,1)S(1)}, bf16[64,2048]{1,0:T(8,128)(2,1)S(1)}, u32[]{:S(2)}, u32[]{:S(2)}) %collective-permute-start.24) | collective-permute-done | bytes 262176 | tf_op jit(solution)/shard_map/ppermute | solution.py:308
  111.1 0.1 fusion.1
  111.2 2.0 %collective-permute-start.25 = (bf16[64,2048]{1,0:T(8,128)(2,1)S(1)}, bf16[64,2048]{1,0:T(8,128)(2,1)S(1)}, u32[]{:S(2)}, u32[]{:S(2)}) collective-permute-start(bf16[64,2048]{1,0:T(8,128)(2,1)S(1)} %fusion.1), channel_id=1, source_target_pairs={{0,24},{8,16},{16,8},{24,0},{1,25},{9,17},{17,9},{25,1},{2,26},{10... | collective-permute-start | bytes 786440 | tf_op jit(solution)/shard_map/ppermute | solution.py:308
  113.2 3.0 %collective-permute-done.31 = bf16[64,2048]{1,0:T(8,128)(2,1)S(1)} collective-permute-done((bf16[64,2048]{1,0:T(8,128)(2,1)S(1)}, bf16[64,2048]{1,0:T(8,128)(2,1)S(1)}, u32[]{:S(2)}, u32[]{:S(2)}) %collective-permute-start.31) | collective-permute-done | bytes 262176 | tf_op jit(solution)/shard_map/ppermute | solution.py:308
  116.2 0.1 fusion
  116.3 5.6 %collective-permute-done.25 = bf16[64,2048]{1,0:T(8,128)(2,1)S(1)} collective-permute-done((bf16[64,2048]{1,0:T(8,128)(2,1)S(1)}, bf16[64,2048]{1,0:T(8,128)(2,1)S(1)}, u32[]{:S(2)}, u32[]{:S(2)}) %collective-permute-start.25) | collective-permute-done | bytes 262176 | tf_op jit(solution)/shard_map/ppermute | solution.py:308
  121.9 12.0 %collective-permute-done.32 = bf16[64,2048]{1,0:T(8,128)(2,1)S(1)} collective-permute-done((bf16[64,2048]{1,0:T(8,128)(2,1)S(1)}, bf16[64,2048]{1,0:T(8,128)(2,1)S(1)}, u32[]{:S(2)}, u32[]{:S(2)}) %collective-permute-start.32) | collective-permute-done | bytes 262176 | tf_op jit(solution)/shard_map/ppermute | solution.py:308
  133.9 0.1 add_convert_fusion.1
  134.0 1.6 %collective-permute-start.33 = (bf16[64,2048]{1,0:T(8,128)(2,1)S(1)}, bf16[64,2048]{1,0:T(8,128)(2,1)S(1)}, u32[]{:S(2)}, u32[]{:S(2)}) collective-permute-start(bf16[64,2048]{1,0:T(8,128)(2,1)S(1)} %add_convert_fusion.1), channel_id=1, source_target_pairs={{0,1},{1,0},{2,3},{3,2},{4,5},{5,4},{6,7},{7,6},{8,9},{9,8},{10,11... | collective-permute-start | bytes 786440 | tf_op jit(solution)/shard_map/ppermute | solution.py:308
  135.6 4.9 %collective-permute-done.33 = bf16[64,2048]{1,0:T(8,128)(2,1)S(1)} collective-permute-done((bf16[64,2048]{1,0:T(8,128)(2,1)S(1)}, bf16[64,2048]{1,0:T(8,128)(2,1)S(1)}, u32[]{:S(2)}, u32[]{:S(2)}) %collective-permute-start.33) | collective-permute-done | bytes 262176 | tf_op jit(solution)/shard_map/ppermute | solution.py:308
  140.5 0.8 add_convert_fusion
  (66 shorter events, 0.8 us)
Async XLA Ops:
  0.6 7.4 %collective-permute-start = (bf16[64,2048]{1,0:T(8,128)(2,1)}, bf16[64,2048]{1,0:T(8,128)(2,1)S(1)}, u32[]{:S(2)}, u32[]{:S(2)}) collective-permute-start(bf16[64,2048]{1,0:T(8,128)(2,1)} %hidden_ref.1), channel_id=1, source_target_pairs={{0,2},{2,0},{4,6},{6,4},{1,3},{3,1},{5,7},{7,5},{8,10},{10,8},{12,... | collective-permute-start | bytes 786440 | tf_op jit(solution)/shard_map/ppermute | solution.py:308
  1.1 12.2 %collective-permute-start.2 = (bf16[64,2048]{1,0:T(8,128)(2,1)}, bf16[64,2048]{1,0:T(8,128)(2,1)S(1)}, u32[]{:S(2)}, u32[]{:S(2)}) collective-permute-start(bf16[64,2048]{1,0:T(8,128)(2,1)} %hidden_ref.1), channel_id=1, source_target_pairs={{0,4},{2,6},{4,0},{6,2},{1,5},{3,7},{5,1},{7,3},{8,12},{10,14},{12... | collective-permute-start | bytes 786440 | tf_op jit(solution)/shard_map/ppermute | solution.py:308
  4.5 0.7 copy-start.14
  5.2 0.7 copy-start.15
  5.8 2.2 %copy-start.1 = (bf16[2048,576]{0,1:T(8,128)(2,1)S(1)}, bf16[2048,576]{0,1:T(8,128)(2,1)}, u32[]{:S(2)}) copy-start(bf16[2048,576]{0,1:T(8,128)(2,1)} %param.27) | copy-start | bytes 7077892
  5.8 2.2 %copy-start.2 = (bf16[4,384,576]{1,2,0:T(8,128)(2,1)S(1)}, bf16[4,384,576]{1,2,0:T(8,128)(2,1)}, u32[]{:S(2)}) copy-start(bf16[4,384,576]{1,2,0:T(8,128)(2,1)} %param.20) | copy-start | bytes 5308420
  5.8 2.6 %copy-start.3 = (bf16[2048,384]{1,0:T(8,128)(2,1)S(1)}, bf16[2048,384]{1,0:T(8,128)(2,1)}, u32[]{:S(2)}) copy-start(bf16[2048,384]{1,0:T(8,128)(2,1)} %refs_7_.3) | copy-start | bytes 4718596
  5.8 2.9 %copy-start.4 = (bf16[256,2048]{1,0:T(8,128)(2,1)S(1)}, bf16[256,2048]{1,0:T(8,128)(2,1)}, u32[]{:S(2)}) copy-start(bf16[256,2048]{1,0:T(8,128)(2,1)} %refs_12_.3) | copy-start | bytes 3145732
  5.8 2.9 %copy-start.8 = (bf16[2,128,512]{2,1,0:T(8,128)(2,1)S(1)}, bf16[2,128,512]{2,1,0:T(8,128)(2,1)}, u32[]{:S(2)}) copy-start(bf16[2,128,512]{2,1,0:T(8,128)(2,1)} %refs_10_.3) | copy-start | bytes 786436
  5.8 3.0 %copy-start.9 = (bf16[2,512,128]{2,1,0:T(8,128)(2,1)S(1)}, bf16[2,512,128]{2,1,0:T(8,128)(2,1)}, u32[]{:S(2)}) copy-start(bf16[2,512,128]{2,1,0:T(8,128)(2,1)} %refs_11_.3) | copy-start | bytes 786436
  5.8 3.1 %copy-start.10 = (bf16[64,2048]{1,0:T(8,128)(2,1)S(1)}, bf16[64,2048]{1,0:T(8,128)(2,1)}, u32[]{:S(2)}) copy-start(bf16[64,2048]{1,0:T(8,128)(2,1)} %hidden_ref.1) | copy-start | bytes 786436
  5.9 3.1 %copy-start.11 = (f32[2048]{0:T(1024)S(1)}, f32[2048]{0:T(1024)}, u32[]{:S(2)}) copy-start(f32[2048]{0:T(1024)} %param.25) | copy-start | bytes 24580
  5.9 3.1 %copy-start.12 = (f32[512]{0:T(512)S(1)}, f32[512]{0:T(512)}, u32[]{:S(2)}) copy-start(f32[512]{0:T(512)} %param.28) | copy-start | bytes 6148
  13.3 1.5 %collective-permute-start.3 = (bf16[64,2048]{1,0:T(8,128)(2,1)S(1)}, bf16[64,2048]{1,0:T(8,128)(2,1)S(1)}, u32[]{:S(2)}, u32[]{:S(2)}) collective-permute-start(bf16[64,2048]{1,0:T(8,128)(2,1)S(1)} %collective-permute-done.2.refs_0_), channel_id=1, source_target_pairs={{0,2},{2,0},{4,6},{6,4},{1,3},{3,1},{5,7},{7,5},{8,10},{10,8},{12,... | collective-permute-start | bytes 786440 | tf_op jit(solution)/shard_map/ppermute | solution.py:308
  18.7 11.8 %copy-start.16 = (s32[64,6]{0,1:T(8,128)S(1)}, s32[64,6]{0,1:T(8,128)}, u32[]{:S(2)}) copy-start(s32[64,6]{0,1:T(8,128)} %param.23) | copy-start | bytes 4612
  18.7 17.8 %copy-start.13 = (f32[2048]{0:T(1024)S(1)}, f32[2048]{0:T(1024)}, u32[]{:S(2)}) copy-start(f32[2048]{0:T(1024)} %param.32) | copy-start | bytes 24580
  18.7 1.6 %collective-permute-start.4 = (bf16[64,2048]{1,0:T(8,128)(2,1)S(1)}, bf16[64,2048]{1,0:T(8,128)(2,1)S(1)}, u32[]{:S(2)}, u32[]{:S(2)}) collective-permute-start(bf16[64,2048]{1,0:T(8,128)(2,1)S(1)} %get-tuple-element.33), channel_id=1, source_target_pairs={{0,2},{2,0},{4,6},{6,4},{1,3},{3,1},{5,7},{7,5},{8,10},{10,8},{12,... | collective-permute-start | bytes 786440 | tf_op jit(solution)/shard_map/ppermute | solution.py:308
  18.9 1.7 %collective-permute-start.1 = (bf16[64,2048]{1,0:T(8,128)(2,1)S(1)}, bf16[64,2048]{1,0:T(8,128)(2,1)S(1)}, u32[]{:S(2)}, u32[]{:S(2)}) collective-permute-start(bf16[64,2048]{1,0:T(8,128)(2,1)S(1)} %get-tuple-element.30), channel_id=1, source_target_pairs={{0,2},{2,0},{4,6},{6,4},{1,3},{3,1},{5,7},{7,5},{8,10},{10,8},{12,... | collective-permute-start | bytes 786440 | tf_op jit(solution)/shard_map/ppermute | solution.py:308
  20.4 8.4 %collective-permute-start.5 = (bf16[64,2048]{1,0:T(8,128)(2,1)S(1)}, bf16[64,2048]{1,0:T(8,128)(2,1)S(1)}, u32[]{:S(2)}, u32[]{:S(2)}) collective-permute-start(bf16[64,2048]{1,0:T(8,128)(2,1)S(1)} %add_convert_fusion.7), channel_id=1, source_target_pairs={{0,4},{2,6},{4,0},{6,2},{1,5},{3,7},{5,1},{7,3},{8,12},{10,14},{12... | collective-permute-start | bytes 786440 | tf_op jit(solution)/shard_map/ppermute | solution.py:308
  28.9 7.6 %collective-permute-start.6 = (bf16[64,2048]{1,0:T(8,128)(2,1)S(1)}, bf16[64,2048]{1,0:T(8,128)(2,1)S(1)}, u32[]{:S(2)}, u32[]{:S(2)}) collective-permute-start(bf16[64,2048]{1,0:T(8,128)(2,1)S(1)} %add_convert_fusion.6.keep_ref), channel_id=1, source_target_pairs={{0,1},{1,0},{2,3},{3,2},{4,5},{5,4},{6,7},{7,6},{8,9},{9,8},{10,11... | collective-permute-start | bytes 786440 | tf_op jit(solution)/shard_map/ppermute | solution.py:308
  36.5 17.3 %slice-start = ((s8[5767168]{0:T(1024)(128)(4,1)}), s8[4194304]{0:T(1024)(128)(4,1)S(1)}, s32[]{:S(2)}) async-start(s8[5767168]{0:T(1024)(128)(4,1)} %bitcast.36), calls=%async_computation | async-start | bytes 8388608
  36.5 17.3 %slice-start.1 = ((s8[5767168]{0:T(1024)(128)(4,1)}), s8[1572864]{0:T(1024)(128)(4,1)S(1)}, s32[]{:S(2)}) async-start(s8[5767168]{0:T(1024)(128)(4,1)} %bitcast.36), calls=%async_computation.1 | async-start | bytes 3145728
  36.5 17.3 %copy-start = (bf16[1,704,2048]{2,1,0:T(8,128)(2,1)S(1)}, bf16[1,704,2048]{2,1,0:T(8,128)(2,1)}, u32[]{:S(2)}) copy-start(bf16[1,704,2048]{2,1,0:T(8,128)(2,1)} %param.37) | copy-start | bytes 8650756
  36.5 17.3 %copy-start.5 = (bf16[2,2048,352]{1,2,0:T(8,128)(2,1)S(1)}, bf16[2,2048,352]{1,2,0:T(8,128)(2,1)}, u32[]{:S(2)}) copy-start(bf16[2,2048,352]{1,2,0:T(8,128)(2,1)} %param.34) | copy-start | bytes 8650756
  36.5 17.3 %copy-start.6 = (bf16[352,2048]{1,0:T(8,128)(2,1)S(1)}, bf16[352,2048]{1,0:T(8,128)(2,1)}, u32[]{:S(2)}) copy-start(bf16[352,2048]{1,0:T(8,128)(2,1)} %refs_9_.1) | copy-start | bytes 4325380
  36.5 17.3 %copy-start.7 = (bf16[2048,16]{0,1:T(8,128)(2,1)S(1)}, bf16[2048,16]{0,1:T(8,128)(2,1)}, u32[]{:S(2)}) copy-start(bf16[2048,16]{0,1:T(8,128)(2,1)} %param.33) | copy-start | bytes 196612
  36.8 11.5 %collective-permute-start.9 = (bf16[64,2176]{1,0:T(8,128)(2,1)S(1)}, bf16[64,2176]{1,0:T(8,128)(2,1)S(1)}, u32[]{:S(2)}, u32[]{:S(2)}) collective-permute-start(bf16[64,2176]{1,0:T(8,128)(2,1)S(1)} %get-tuple-element.44.refs_0_), channel_id=1, source_target_pairs={{0,24},{8,16},{16,8},{24,0},{1,25},{9,17},{17,9},{25,1},{2,26},{10... | collective-permute-start | bytes 835592 | tf_op jit(solution)/shard_map/ppermute | solution.py:308
  40.4 11.3 %collective-permute-start.8 = (bf16[64,2176]{1,0:T(8,128)(2,1)S(1)}, bf16[64,2176]{1,0:T(8,128)(2,1)S(1)}, u32[]{:S(2)}, u32[]{:S(2)}) collective-permute-start(bf16[64,2176]{1,0:T(8,128)(2,1)S(1)} %get-tuple-element.44.refs_0_), channel_id=1, source_target_pairs={{0,8},{8,0},{16,24},{24,16},{1,9},{9,1},{17,25},{25,17},{2,10},{10... | collective-permute-start | bytes 835592 | tf_op jit(solution)/shard_map/ppermute | solution.py:308
  40.4 11.3 %collective-permute-start.7 = (bf16[64,2176]{1,0:T(8,128)(2,1)S(1)}, bf16[64,2176]{1,0:T(8,128)(2,1)S(1)}, u32[]{:S(2)}, u32[]{:S(2)}) collective-permute-start(bf16[64,2176]{1,0:T(8,128)(2,1)S(1)} %get-tuple-element.44.refs_0_), channel_id=1, source_target_pairs={{0,4},{2,6},{4,0},{6,2},{1,5},{3,7},{5,1},{7,3},{8,12},{10,14},{12... | collective-permute-start | bytes 835592 | tf_op jit(solution)/shard_map/ppermute | solution.py:308
  40.9 12.8 %collective-permute-start.10 = (bf16[64,2176]{1,0:T(8,128)(2,1)S(1)}, bf16[64,2176]{1,0:T(8,128)(2,1)S(1)}, u32[]{:S(2)}, u32[]{:S(2)}) collective-permute-start(bf16[64,2176]{1,0:T(8,128)(2,1)S(1)} %get-tuple-element.44.refs_0_), channel_id=1, source_target_pairs={{0,2},{2,0},{4,6},{6,4},{1,3},{3,1},{5,7},{7,5},{8,10},{10,8},{12,... | collective-permute-start | bytes 835592 | tf_op jit(solution)/shard_map/ppermute | solution.py:308
  51.7 2.0 %collective-permute-start.11 = (bf16[64,2176]{1,0:T(8,128)(2,1)S(1)}, bf16[64,2176]{1,0:T(8,128)(2,1)S(1)}, u32[]{:S(2)}, u32[]{:S(2)}) collective-permute-start(bf16[64,2176]{1,0:T(8,128)(2,1)S(1)} %collective-permute-done.7.refs_1_), channel_id=1, source_target_pairs={{0,2},{2,0},{4,6},{6,4},{1,3},{3,1},{5,7},{7,5},{8,10},{10,8},{12,... | collective-permute-start | bytes 835592 | tf_op jit(solution)/shard_map/ppermute | solution.py:308
  51.8 9.5 %collective-permute-start.14 = (bf16[64,2176]{1,0:T(8,128)(2,1)S(1)}, bf16[64,2176]{1,0:T(8,128)(2,1)S(1)}, u32[]{:S(2)}, u32[]{:S(2)}) collective-permute-start(bf16[64,2176]{1,0:T(8,128)(2,1)S(1)} %collective-permute-done.8.refs_0_), channel_id=1, source_target_pairs={{0,4},{2,6},{4,0},{6,2},{1,5},{3,7},{5,1},{7,3},{8,12},{10,14},{12... | collective-permute-start | bytes 835592 | tf_op jit(solution)/shard_map/ppermute | solution.py:308
  52.5 14.3 %collective-permute-start.20 = (bf16[64,2176]{1,0:T(8,128)(2,1)S(1)}, bf16[64,2176]{1,0:T(8,128)(2,1)S(1)}, u32[]{:S(2)}, u32[]{:S(2)}) collective-permute-start(bf16[64,2176]{1,0:T(8,128)(2,1)S(1)} %collective-permute-done.9.refs_0_), channel_id=1, source_target_pairs={{0,4},{2,6},{4,0},{6,2},{1,5},{3,7},{5,1},{7,3},{8,12},{10,14},{12... | collective-permute-start | bytes 835592 | tf_op jit(solution)/shard_map/ppermute | solution.py:308
  53.8 13.0 %collective-permute-start.15 = (bf16[64,2176]{1,0:T(8,128)(2,1)S(1)}, bf16[64,2176]{1,0:T(8,128)(2,1)S(1)}, u32[]{:S(2)}, u32[]{:S(2)}) collective-permute-start(bf16[64,2176]{1,0:T(8,128)(2,1)S(1)} %collective-permute-done.8.refs_0_), channel_id=1, source_target_pairs={{0,2},{2,0},{4,6},{6,4},{1,3},{3,1},{5,7},{7,5},{8,10},{10,8},{12,... | collective-permute-start | bytes 835592 | tf_op jit(solution)/shard_map/ppermute | solution.py:308
  58.5 23.2 %collective-permute-start.12 = (bf16[2,64,2048]{2,1,0:T(8,128)(2,1)S(1)}, bf16[2,64,2048]{2,1,0:T(8,128)(2,1)S(1)}, u32[]{:S(2)}, u32[]{:S(2)}) collective-permute-start(bf16[2,64,2048]{2,1,0:T(8,128)(2,1)S(1)} %get-tuple-element.39), channel_id=1, source_target_pairs={{0,2},{2,0},{4,6},{6,4},{1,3},{3,1},{5,7},{7,5},{8,10},{10,8},{12,... | collective-permute-start | bytes 1572872 | tf_op jit(solution)/shard_map/ppermute | solution.py:308
  61.2 6.1 %collective-permute-start.16 = (bf16[64,2176]{1,0:T(8,128)(2,1)S(1)}, bf16[64,2176]{1,0:T(8,128)(2,1)S(1)}, u32[]{:S(2)}, u32[]{:S(2)}) collective-permute-start(bf16[64,2176]{1,0:T(8,128)(2,1)S(1)} %collective-permute-done.14.refs_1_), channel_id=1, source_target_pairs={{0,2},{2,0},{4,6},{6,4},{1,3},{3,1},{5,7},{7,5},{8,10},{10,8},{12,... | collective-permute-start | bytes 835592 | tf_op jit(solution)/shard_map/ppermute | solution.py:308
  61.2 15.9 %collective-permute-start.26 = (bf16[64,2176]{1,0:T(8,128)(2,1)S(1)}, bf16[64,2176]{1,0:T(8,128)(2,1)S(1)}, u32[]{:S(2)}, u32[]{:S(2)}) collective-permute-start(bf16[64,2176]{1,0:T(8,128)(2,1)S(1)} %get-tuple-element.44.refs_0_), channel_id=1, source_target_pairs={{0,16},{8,24},{16,0},{24,8},{1,17},{9,25},{17,1},{25,9},{2,18},{10... | collective-permute-start | bytes 835592 | tf_op jit(solution)/shard_map/ppermute | solution.py:308
  66.8 11.1 %collective-permute-start.21 = (bf16[64,2176]{1,0:T(8,128)(2,1)S(1)}, bf16[64,2176]{1,0:T(8,128)(2,1)S(1)}, u32[]{:S(2)}, u32[]{:S(2)}) collective-permute-start(bf16[64,2176]{1,0:T(8,128)(2,1)S(1)} %collective-permute-done.9.refs_0_), channel_id=1, source_target_pairs={{0,2},{2,0},{4,6},{6,4},{1,3},{3,1},{5,7},{7,5},{8,10},{10,8},{12,... | collective-permute-start | bytes 835592 | tf_op jit(solution)/shard_map/ppermute | solution.py:308
  66.8 11.1 %collective-permute-start.22 = (bf16[64,2176]{1,0:T(8,128)(2,1)S(1)}, bf16[64,2176]{1,0:T(8,128)(2,1)S(1)}, u32[]{:S(2)}, u32[]{:S(2)}) collective-permute-start(bf16[64,2176]{1,0:T(8,128)(2,1)S(1)} %collective-permute-done.20.refs_1_), channel_id=1, source_target_pairs={{0,2},{2,0},{4,6},{6,4},{1,3},{3,1},{5,7},{7,5},{8,10},{10,8},{12,... | collective-permute-start | bytes 835592 | tf_op jit(solution)/shard_map/ppermute | solution.py:308
  70.7 12.4 %collective-permute-start.17 = (bf16[2,64,2048]{2,1,0:T(8,128)(2,1)S(1)}, bf16[2,64,2048]{2,1,0:T(8,128)(2,1)S(1)}, u32[]{:S(2)}, u32[]{:S(2)}) collective-permute-start(bf16[2,64,2048]{2,1,0:T(8,128)(2,1)S(1)} %get-tuple-element.41), channel_id=1, source_target_pairs={{0,2},{2,0},{4,6},{6,4},{1,3},{3,1},{5,7},{7,5},{8,10},{10,8},{12,... | collective-permute-start | bytes 1572872 | tf_op jit(solution)/shard_map/ppermute | solution.py:308
  77.1 19.6 %collective-permute-start.27 = (bf16[64,2176]{1,0:T(8,128)(2,1)S(1)}, bf16[64,2176]{1,0:T(8,128)(2,1)S(1)}, u32[]{:S(2)}, u32[]{:S(2)}) collective-permute-start(bf16[64,2176]{1,0:T(8,128)(2,1)S(1)} %collective-permute-done.26.refs_0_), channel_id=1, source_target_pairs={{0,4},{2,6},{4,0},{6,2},{1,5},{3,7},{5,1},{7,3},{8,12},{10,14},{12... | collective-permute-start | bytes 835592 | tf_op jit(solution)/shard_map/ppermute | solution.py:308
  77.9 19.0 %collective-permute-start.28 = (bf16[64,2176]{1,0:T(8,128)(2,1)S(1)}, bf16[64,2176]{1,0:T(8,128)(2,1)S(1)}, u32[]{:S(2)}, u32[]{:S(2)}) collective-permute-start(bf16[64,2176]{1,0:T(8,128)(2,1)S(1)} %collective-permute-done.26.refs_0_), channel_id=1, source_target_pairs={{0,2},{2,0},{4,6},{6,4},{1,3},{3,1},{5,7},{7,5},{8,10},{10,8},{12,... | collective-permute-start | bytes 835592 | tf_op jit(solution)/shard_map/ppermute | solution.py:308
  81.1 20.7 %collective-permute-start.23 = (bf16[2,64,2048]{2,1,0:T(8,128)(2,1)S(1)}, bf16[2,64,2048]{2,1,0:T(8,128)(2,1)S(1)}, u32[]{:S(2)}, u32[]{:S(2)}) collective-permute-start(bf16[2,64,2048]{2,1,0:T(8,128)(2,1)S(1)} %get-tuple-element.43), channel_id=1, source_target_pairs={{0,2},{2,0},{4,6},{6,4},{1,3},{3,1},{5,7},{7,5},{8,10},{10,8},{12,... | collective-permute-start | bytes 1572872 | tf_op jit(solution)/shard_map/ppermute | solution.py:308
  81.8 10.2 %collective-permute-start.13 = (bf16[64,2048]{1,0:T(8,128)(2,1)S(1)}, bf16[64,2048]{1,0:T(8,128)(2,1)S(1)}, u32[]{:S(2)}, u32[]{:S(2)}) collective-permute-start(bf16[64,2048]{1,0:T(8,128)(2,1)S(1)} %fusion.3), channel_id=1, source_target_pairs={{0,4},{2,6},{4,0},{6,2},{1,5},{3,7},{5,1},{7,3},{8,12},{10,14},{12... | collective-permute-start | bytes 786440 | tf_op jit(solution)/shard_map/ppermute | solution.py:308
  83.2 13.5 %collective-permute-start.18 = (bf16[64,2048]{1,0:T(8,128)(2,1)S(1)}, bf16[64,2048]{1,0:T(8,128)(2,1)S(1)}, u32[]{:S(2)}, u32[]{:S(2)}) collective-permute-start(bf16[64,2048]{1,0:T(8,128)(2,1)S(1)} %fusion.4), channel_id=1, source_target_pairs={{0,4},{2,6},{4,0},{6,2},{1,5},{3,7},{5,1},{7,3},{8,12},{10,14},{12... | collective-permute-start | bytes 786440 | tf_op jit(solution)/shard_map/ppermute | solution.py:308
  96.8 1.6 %collective-permute-start.29 = (bf16[64,2176]{1,0:T(8,128)(2,1)S(1)}, bf16[64,2176]{1,0:T(8,128)(2,1)S(1)}, u32[]{:S(2)}, u32[]{:S(2)}) collective-permute-start(bf16[64,2176]{1,0:T(8,128)(2,1)S(1)} %collective-permute-done.27.refs_1_), channel_id=1, source_target_pairs={{0,2},{2,0},{4,6},{6,4},{1,3},{3,1},{5,7},{7,5},{8,10},{10,8},{12,... | collective-permute-start | bytes 835592 | tf_op jit(solution)/shard_map/ppermute | solution.py:308
  101.6 2.0 %collective-permute-start.30 = (bf16[2,64,2048]{2,1,0:T(8,128)(2,1)S(1)}, bf16[2,64,2048]{2,1,0:T(8,128)(2,1)S(1)}, u32[]{:S(2)}, u32[]{:S(2)}) collective-permute-start(bf16[2,64,2048]{2,1,0:T(8,128)(2,1)S(1)} %get-tuple-element.48), channel_id=1, source_target_pairs={{0,2},{2,0},{4,6},{6,4},{1,3},{3,1},{5,7},{7,5},{8,10},{10,8},{12,... | collective-permute-start | bytes 1572872 | tf_op jit(solution)/shard_map/ppermute | solution.py:308
  101.9 9.2 %collective-permute-start.24 = (bf16[64,2048]{1,0:T(8,128)(2,1)S(1)}, bf16[64,2048]{1,0:T(8,128)(2,1)S(1)}, u32[]{:S(2)}, u32[]{:S(2)}) collective-permute-start(bf16[64,2048]{1,0:T(8,128)(2,1)S(1)} %fusion.5), channel_id=1, source_target_pairs={{0,4},{2,6},{4,0},{6,2},{1,5},{3,7},{5,1},{7,3},{8,12},{10,14},{12... | collective-permute-start | bytes 786440 | tf_op jit(solution)/shard_map/ppermute | solution.py:308
  102.7 19.2 %collective-permute-start.19 = (bf16[64,2048]{1,0:T(8,128)(2,1)S(1)}, bf16[64,2048]{1,0:T(8,128)(2,1)S(1)}, u32[]{:S(2)}, u32[]{:S(2)}) collective-permute-start(bf16[64,2048]{1,0:T(8,128)(2,1)S(1)} %fusion.2), channel_id=1, source_target_pairs={{0,8},{8,0},{16,24},{24,16},{1,9},{9,1},{17,25},{25,17},{2,10},{10... | collective-permute-start | bytes 786440 | tf_op jit(solution)/shard_map/ppermute | solution.py:308
  103.7 12.5 %collective-permute-start.31 = (bf16[64,2048]{1,0:T(8,128)(2,1)S(1)}, bf16[64,2048]{1,0:T(8,128)(2,1)S(1)}, u32[]{:S(2)}, u32[]{:S(2)}) collective-permute-start(bf16[64,2048]{1,0:T(8,128)(2,1)S(1)} %fusion.6), channel_id=1, source_target_pairs={{0,4},{2,6},{4,0},{6,2},{1,5},{3,7},{5,1},{7,3},{8,12},{10,14},{12... | collective-permute-start | bytes 786440 | tf_op jit(solution)/shard_map/ppermute | solution.py:308
  111.2 10.7 %collective-permute-start.25 = (bf16[64,2048]{1,0:T(8,128)(2,1)S(1)}, bf16[64,2048]{1,0:T(8,128)(2,1)S(1)}, u32[]{:S(2)}, u32[]{:S(2)}) collective-permute-start(bf16[64,2048]{1,0:T(8,128)(2,1)S(1)} %fusion.1), channel_id=1, source_target_pairs={{0,24},{8,16},{16,8},{24,0},{1,25},{9,17},{17,9},{25,1},{2,26},{10... | collective-permute-start | bytes 786440 | tf_op jit(solution)/shard_map/ppermute | solution.py:308
  116.3 17.6 %collective-permute-start.32 = (bf16[64,2048]{1,0:T(8,128)(2,1)S(1)}, bf16[64,2048]{1,0:T(8,128)(2,1)S(1)}, u32[]{:S(2)}, u32[]{:S(2)}) collective-permute-start(bf16[64,2048]{1,0:T(8,128)(2,1)S(1)} %fusion), channel_id=1, source_target_pairs={{0,16},{8,24},{16,0},{24,8},{1,17},{9,25},{17,1},{25,9},{2,18},{10... | collective-permute-start | bytes 786440 | tf_op jit(solution)/shard_map/ppermute | solution.py:308
  134.0 6.4 %collective-permute-start.33 = (bf16[64,2048]{1,0:T(8,128)(2,1)S(1)}, bf16[64,2048]{1,0:T(8,128)(2,1)S(1)}, u32[]{:S(2)}, u32[]{:S(2)}) collective-permute-start(bf16[64,2048]{1,0:T(8,128)(2,1)S(1)} %add_convert_fusion.1), channel_id=1, source_target_pairs={{0,1},{1,0},{2,3},{3,2},{4,5},{5,4},{6,7},{7,6},{8,9},{9,8},{10,11... | collective-permute-start | bytes 786440 | tf_op jit(solution)/shard_map/ppermute | solution.py:308

commit v6 on v5

--- a/solution.py
+++ b/solution.py
@@ -219,45 +219,86 @@
     )(row_index, *blocks, cache, *tables, *weights)
 
 
-def join_kernel(hidden_ref, keep_ref, arrived_ref, gain_ref, named_ref, residual_ref, block_ref):
-    width = hidden_ref.shape[1]
+def join_kernel(
+    row_ref,
+    hidden_ref,
+    keep_ref,
+    arrived_ref,
+    gain_ref,
+    named_ref,
+    residual_ref,
+    block_ref,
+    own_ref,
+):
     total = keep_ref[...].astype(jnp.float32)
     for k in range(arrived_ref.shape[0]):
         total = total + arrived_ref[k].astype(jnp.float32)
     residual = hidden_ref[...].astype(jnp.float32) + total
-    residual_ref[...] = residual
-    block_ref[:, :width] = rms_scale(residual, gain_ref[...]).astype(jnp.bfloat16)
-    block_ref[:, width:] = named_ref[...]
-
-
-def joined(hidden, keep, arrived, gain, named):
+    parts, _, part_width = residual_ref.shape
+    normed = rms_scale(residual, gain_ref[...]).astype(jnp.bfloat16)
+    for k in range(parts):
+        part = slice(k * part_width, (k + 1) * part_width)
+        residual_ref[k ^ row_ref[2]] = residual[:, part]
+        block_ref[k ^ row_ref[2], :, :part_width] = normed[:, part]
+        block_ref[k, :, part_width:] = named_ref[...]
+    own_ref[...] = block_ref[:1]
+
+
+def joined(indices, parts, hidden, keep, arrived, gain, named):
     rows, width = hidden.shape
+    block_width = width // parts + EXTRA
     return pl.pallas_call(
         join_kernel,
         out_shape=(
-            jax.ShapeDtypeStruct((rows, width), jnp.float32),
-            jax.ShapeDtypeStruct((rows, width + EXTRA), jnp.bfloat16),
+            jax.ShapeDtypeStruct((parts, rows, width // parts), jnp.float32),
+            jax.ShapeDtypeStruct((parts, rows, block_width), jnp.bfloat16),
+            jax.ShapeDtypeStruct((1, rows, block_width), jnp.bfloat16),
         ),
-        in_specs=[WHOLE] * 5,
-        out_specs=(WHOLE, WHOLE),
+        in_specs=[SCALARS] + [WHOLE] * 5,
+        out_specs=(WHOLE, WHOLE, WHOLE),
         compiler_params=params(16),
         cost_estimate=LONGER,
         name="join",
-    )(hidden, keep, arrived, gain, named)
-
-
-def expert_kernel(shared, *refs):
-    blocks, refs = refs[:4], refs[4:]
+    )(indices, hidden, keep, arrived, gain, named)
+
+
+def finish_kernel(row_ref, own_ref, others_ref, out_ref):
+    parts, _, width = others_ref.shape
+    for k in range(parts + 1):
+        values = own_ref[...] if k == 0 else others_ref[k - 1]
+        start = pl.multiple_of((row_ref[2] ^ k) * width, 128)
+        out_ref[:, pl.ds(start, width)] = values
+
+
+def finished(indices, own, others):
+    rows, width = own.shape
+    return pl.pallas_call(
+        finish_kernel,
+        out_shape=jax.ShapeDtypeStruct((rows, width * (1 + others.shape[0])), own.dtype),
+        in_specs=[SCALARS, WHOLE, WHOLE],
+        out_specs=WHOLE,
+        compiler_params=params(12),
+        name="finish",
+    )(indices, own, others)
+
+
+def expert_kernel(shared, far_first, *refs):
+    row_ref, blocks, refs = refs[0], refs[1:5], refs[5:]
     own_ref, router_ref, gate_up_ref, down_ref = refs[:4]
     refs = refs[4:]
     if shared:
         shared_gate_up_ref, shared_down_ref = refs[:2]
         refs = refs[2:]
-    keep_ref, send_ref = refs
+    keep_ref, send_ref, rows_ref = refs
     experts, width = router_ref.shape
-    size = blocks[0].shape[0]
-    rows = jnp.concatenate([ref[:, :width] for ref in blocks], axis=0)
-    named = jnp.concatenate([ref[:, width:] for ref in blocks], axis=0)[:, :experts]
+    parts, size, _ = blocks[0].shape
+    part_width = width // parts
+    for b, ref in enumerate(blocks):
+        for k in range(parts):
+            start = pl.multiple_of((k ^ row_ref[2]) * part_width, 128)
+            rows_ref[b * size : (b + 1) * size, pl.ds(start, part_width)] = ref[k, :, :part_width]
+    rows = rows_ref[...]
+    named = jnp.concatenate([ref[0, :, part_width:] for ref in blocks], axis=0)[:, :experts]
     logits = transposed_dot(rows, router_ref[...])
     raised = jnp.exp(logits - jnp.max(logits, axis=-1, keepdims=True))
     router = raised / jnp.sum(raised, axis=-1, keepdims=True)
@@ -277,23 +318,31 @@
         result = share * dot(routed_inner, down_ref[:, part])
         if shared:
             result = result + dot(shared_inner, shared_down_ref[:, part])
-        keep_ref[:, :, part] = result[: 2 * size].reshape(2, size, tile)
-        send_ref[:, :, part] = result[2 * size :].astype(jnp.bfloat16).reshape(2, size, tile)
-
-
-def expert_part(blocks, own_expert, router, routed_weights, shared_weights=()):
-    size = blocks[0].shape[0]
+        place = (k * tile // part_width) ^ row_ref[2]
+        inside = slice(k * tile % part_width, k * tile % part_width + tile)
+        spot = (slice(None), place) if far_first else (place, slice(None))
+        spot = (*spot, slice(None), inside)
+        keep_ref[spot] = result[: 2 * size].reshape(2, size, tile)
+        send_ref[spot] = result[2 * size :].astype(jnp.bfloat16).reshape(2, size, tile)
+
+
+def expert_part(
+    indices, parts, far_first, blocks, own_expert, router, routed_weights, shared_weights=()
+):
+    size = blocks[0].shape[1]
     width = router.shape[1]
     units = sum(each.shape[0] for each in (*routed_weights, *shared_weights) if each.ndim == 2)
-    operands = [*blocks, own_expert, router, *routed_weights, *shared_weights]
+    out_shape = (*((2, parts) if far_first else (parts, 2)), size, width // parts)
+    operands = [indices, *blocks, own_expert, router, *routed_weights, *shared_weights]
     return pl.pallas_call(
-        functools.partial(expert_kernel, bool(shared_weights)),
+        functools.partial(expert_kernel, bool(shared_weights), far_first),
         out_shape=(
-            jax.ShapeDtypeStruct((2, size, width), jnp.float32),
-            jax.ShapeDtypeStruct((2, size, width), jnp.bfloat16),
+            jax.ShapeDtypeStruct(out_shape, jnp.float32),
+            jax.ShapeDtypeStruct(out_shape, jnp.bfloat16),
         ),
-        in_specs=[WHOLE] * len(operands),
+        in_specs=[SCALARS] + [WHOLE] * (len(operands) - 1),
         out_specs=(WHOLE, WHOLE),
+        scratch_shapes=[pltpu.VMEM((4 * size, width), jnp.bfloat16)],
         compiler_params=params(12),
         cost_estimate=SMALL,
         name="experts",
@@ -339,7 +388,7 @@
     near = swap(hidden, "row", n_row, 1)
 
     experts = router_weight.shape[1]
-    indices = jnp.stack([row_index, req_index * n_row + row_index]).astype(jnp.int32)
+    indices = jnp.stack([row_index, req_index * n_row + row_index, lax.axis_index("col")]).astype(jnp.int32)
     *tables, own_expert = tree_tables(indices, lengths, accepted, parents, experts)
     cache = jnp.swapaxes(latent_cache, 1, 2)
     weights = (
@@ -367,26 +416,34 @@
     partial = fold(own_keep, own_send) + from_far.astype(jnp.float32)
     partial, arrived = col_parts(partial, n_col)
     named = (routes[:, :, None] == jnp.arange(EXTRA, dtype=jnp.int32)).any(axis=1).astype(bf16)
-    residual, block = joined(hidden, partial, arrived, post_gain[None], named)
+    residual, block, own_part = joined(indices, n_col, hidden, partial, arrived, post_gain[None], named)
 
     router = router_weight.T
     routed_weights = (jnp.swapaxes(expert_gate_up[0], 1, 2), expert_down[0])
     shared_weights = (jnp.swapaxes(shared_gate_up, 1, 2), shared_down)
     distances = [0, 1, *range(n_req - 1, 1, -1)]
-    blocks = [block]
-    for k, s in enumerate(distances[1:], 1):
-        source = block if k < 3 else after(block, blocks[k - 2])
-        blocks.append(swap(source, "req", n_req, s))
-    sends, parts = [], []
+    blocks = [block, swap(block, "req", n_req, 1)]
+    fars = [swap(each, "row", n_row, 2) for each in blocks]
+    rest = [swap(own_part, "req", n_req, s) for s in distances[2:]]
+    if rest:
+        rest = after(jnp.concatenate(rest, axis=0)[None], fars[0], blocks[1])
+        rest_far = swap(rest, "row", n_row, 2)
+        rest, rest_far = col_gather(rest, n_col), col_gather(rest_far, n_col)
+        blocks += [rest[:, k] for k in range(rest.shape[1])]
+        fars += [rest_far[:, k] for k in range(rest.shape[1])]
+    sends, folds, parts = [], [], []
     for k, s in enumerate(distances):
-        far = swap(after(blocks[k], *sends[: max(0, k - 2)]), "row", n_row, 2)
         near = swap(blocks[k], "row", n_row, 1)
-        if k == 0:
-            far = after(far, *blocks[1:3])
-        elif k > 2:
-            far = after(far, *sends, *parts[: k - 1])
+        far = fars[k]
+        if k > 1:
+            far = after(far, *sends, *folds[: k - 1])
+        elif k == 1:
+            far = after(far, *sends)
         far_near = swap(far, "row", n_row, 1)
         keep, send = expert_part(
+            indices,
+            n_col,
+            k < 3,
             (blocks[k], far, near, far_near),
             own_expert,
             router,
@@ -394,20 +451,41 @@
             () if s else shared_weights,
         )
         sends.append(send)
-        from_near = swap(send, "row", n_row, 1)
-        from_far = swap((keep[1] + from_near[1].astype(jnp.float32)).astype(bf16), "row", n_row, 2)
-        part = keep[0] + from_near[0].astype(jnp.float32) + from_far.astype(jnp.float32)
+        near_sum = keep + swap(send, "row", n_row, 1).astype(jnp.float32)
+        if k < 3:
+            fold = near_sum[1].astype(bf16)
+            part = near_sum[0] + swap(fold, "row", n_row, 2).astype(jnp.float32)
+            part = col_scatter(part, n_col)[0]
+        else:
+            fold = near_sum[n_col // 2 :].astype(bf16)
+            part = col_scatter(near_sum, n_col)[0]
+            part = part[0] + swap(part[1].astype(bf16), "row", n_row, 2).astype(jnp.float32)
+        folds.append(fold)
         parts.append(part.astype(bf16) if s else part)
     total = parts[0]
     for s, part in zip(distances[1:], parts[1:]):
         total = total + swap(part, "req", n_req, s).astype(jnp.float32)
-    total, arrived = col_parts(total, n_col)
-    layer_output = residual + (total.astype(jnp.float32) + sum_up(arrived))
-    return (layer_output.astype(bf16), accepted_latents)
-
-
-def sum_up(parts):
-    return jnp.sum(parts.astype(jnp.float32), axis=0)
+    own = (residual[0] + total).astype(bf16)
+    others = col_gather(own[None], n_col)
+    layer_output = finished(indices, own, others[1:])
+    return (layer_output, accepted_latents)
+
+
+def col_gather(values, n_col):
+    bits = 1
+    while bits < n_col:
+        values = jnp.concatenate([values, swap(values, "col", n_col, bits)], axis=0)
+        bits *= 2
+    return values
+
+
+def col_scatter(values, n_col):
+    bits = n_col // 2
+    while bits:
+        received = swap(values[bits:].astype(jnp.bfloat16), "col", n_col, bits)
+        values = values[:bits] + received.astype(jnp.float32)
+        bits //= 2
+    return values
 
 
 def col_parts(values, n_col):

time: 141 us -> 125 us (0.89)
  waiting for transfers between devices: 87.8 us -> 54.8 us
  starting transfers between devices: 22.6 us -> 35 us
  Pallas kernels: 25 us -> 29.3 us
    ppermute x34 -> x39, waiting for transfers between devices: 87.8 us -> 54.8 us  [swap(): return lax.ppermute(values, axis, [(i, i ^ bits) for i in range(size)])]
    ppermute x34 -> x39, starting transfers between devices: 22.6 us -> 35 us  [swap(): return lax.ppermute(values, axis, [(i, i ^ bits) for i in range(size)])]
    pallas_call x5 -> x6, Pallas kernels: 14.7 us -> 18.9 us  [the longest x4 16.9 us: expert_part(): pl.pallas_call(functools.partial(expert_kernel, bool(shared_weights), far...]
  transfers between devices with their start and end apart: 34 -> 39, of which waited for: 19 -> 18; matrix products, arithmetic and copies ran while one was open for 1% -> 1% of each run, Pallas kernels for 15% -> 19%
where the time goes in v6:
time: 125 us
  waiting for transfers between devices  54.8 us (44%)
  starting transfers between devices  35 us (28%)
  Pallas kernels  29.3 us (23%)
  local copies, waits for them, and re-layouts  2.68 us (2%)
  between operations  1.83 us (1%)
  other arithmetic  1.53 us (1%)
    ppermute x39, waiting for transfers between devices, swap(): return lax.ppermute(values, axis, [(i, i ^ bits) for i in range(size)])  54.8 us
    ppermute x39, starting transfers between devices, swap(): return lax.ppermute(values, axis, [(i, i ^ bits) for i in range(size)])  35 us
    pallas_call x4, Pallas kernels, expert_part(): pl.pallas_call(functools.partial(expert_kernel, bool(shared_weights), far...  16.9 us
    pallas_call x2, Pallas kernels, attention_part(): pl.pallas_call(functools.partial(attention_kernel, first, place), out_sha...  8.2 us
  transfers between devices with their start and end apart: 39, of which 18 were waited for; matrix products, arithmetic and copies ran while one was open for 1% of the time, Pallas kernels for 19%

profile of v6, /device:TPU:0, one launch (start us, length us, event | category | flops | bytes accessed | tf_op | source)
XLA Modules:
  0.0 125.1 jit_solution(7302537574936926522)
XLA Ops:
  0.6 0.5 collective-permute-start
  1.1 2.6 %collective-permute-start.2 = (bf16[64,2048]{1,0:T(8,128)(2,1)}, bf16[64,2048]{1,0:T(8,128)(2,1)S(1)}, u32[]{:S(2)}, u32[]{:S(2)}) collective-permute-start(bf16[64,2048]{1,0:T(8,128)(2,1)} %hidden_ref.1), channel_id=1, source_target_pairs={{0,4},{2,6},{4,0},{6,2},{1,5},{3,7},{5,1},{7,3},{8,12},{10,14},{12... | collective-permute-start | bytes 786440 | tf_op jit(solution)/shard_map/ppermute | solution.py:357
  4.5 0.7 copy-done.14
  5.2 0.7 copy-done.15
  5.9 2.1 %trees.1 = (f32[4,64,64]{2,1,0:T(8,128)S(1)}, f32[4,64,65]{2,1,0:T(8,128)S(1)}, bf16[64,64]{1,0:T(8,128)(2,1)S(1)}, f32[1,16]{1,0:T(1,128)S(1)}) custom-call(s32[3]{0:T(128)S(1)} %pad_add_fusion.row_ref.refs_0_, s32[4]{0:T(128)S(1)} %copy-done.15, s32[1]{0:T(128)S(6)} %copy.24.accepted_ref, s32[4,64]{1,0:T(4,128)S(1)} %copy-done.14), custom_call_target="tpu_custom_call" | custom-call | flops 20000000000 | bytes 1 | tf_op jit(solution)/shard_map/trees/pallas_call | solution.py:110
  8.1 0.4 copy-done.3
  8.5 0.3 copy-done.4
  8.9 4.4 %attention.2 = (f32[64,2048]{1,0:T(8,128)S(1)}, bf16[64,2048]{1,0:T(8,128)(2,1)S(1)}, bf16[1,64,576]{2,1,0:T(8,128)(2,1)}) custom-call(s32[3]{0:T(128)S(1)} %pad_add_fusion.row_ref.refs_0_, bf16[64,2048]{1,0:T(8,128)(2,1)S(1)} %copy-done.10, bf16[64,2048]{1,0:T(8,128)(2,1)S(1)} %collective-permute-done.refs_1_, bf16[4,576,384]{2,1,0:T(8,128)(2,1)S(1)} %bitcast.82, ...), custom_call_target="tpu_custom_call" | custom-call | flops 1 | bytes 1 | tf_op jit(solution)/shard_map/attention/pallas_call | solution.py:211
  13.3 0.2 collective-permute-start.3
  13.5 1.4 %collective-permute-done.3.refs_1_ = bf16[64,2048]{1,0:T(8,128)(2,1)S(1)} collective-permute-done((bf16[64,2048]{1,0:T(8,128)(2,1)S(1)}, bf16[64,2048]{1,0:T(8,128)(2,1)S(1)}, u32[]{:S(2)}, u32[]{:S(2)}) %collective-permute-start.3) | collective-permute-done | bytes 262176 | tf_op jit(solution)/shard_map/ppermute | solution.py:357
  14.8 3.8 %attention.3 = (f32[64,2048]{1,0:T(8,128)S(1)}, bf16[64,2048]{1,0:T(8,128)(2,1)S(1)}) custom-call(s32[3]{0:T(128)S(1)} %pad_add_fusion.row_ref.refs_0_, bf16[64,2048]{1,0:T(8,128)(2,1)S(1)} %collective-permute-done.2.refs_0_, bf16[64,2048]{1,0:T(8,128)(2,1)S(1)} %collective-permute-done.3.refs_1_, bf16[4,576,384]{2,1,0:T(8,128)(2,1)S(1)} %bitcast.83, ...), custom_call_target="tpu_custom_call" | custom-call | flops 1 | bytes 1 | tf_op jit(solution)/shard_map/attention/pallas_call | solution.py:211
  18.7 0.2 collective-permute-start.4
  18.9 0.3 collective-permute-start.1
  19.3 1.0 collective-permute-done.4
  20.4 0.1 collective-permute-start.5
  20.5 0.2 collective-permute-done.1
  20.7 8.1 %collective-permute-done.5 = bf16[64,2048]{1,0:T(8,128)(2,1)S(1)} collective-permute-done((bf16[64,2048]{1,0:T(8,128)(2,1)S(1)}, bf16[64,2048]{1,0:T(8,128)(2,1)S(1)}, u32[]{:S(2)}, u32[]{:S(2)}) %collective-permute-start.5) | collective-permute-done | bytes 262176 | tf_op jit(solution)/shard_map/ppermute | solution.py:357
  28.9 1.6 %collective-permute-start.6 = (bf16[64,2048]{1,0:T(8,128)(2,1)S(1)}, bf16[64,2048]{1,0:T(8,128)(2,1)S(1)}, u32[]{:S(2)}, u32[]{:S(2)}) collective-permute-start(bf16[64,2048]{1,0:T(8,128)(2,1)S(1)} %add_convert_fusion.keep_ref), channel_id=1, source_target_pairs={{0,1},{1,0},{2,3},{3,2},{4,5},{5,4},{6,7},{7,6},{8,9},{9,8},{10,11... | collective-permute-start | bytes 786440 | tf_op jit(solution)/shard_map/ppermute | solution.py:357
  30.5 0.1 fusion.16
  30.6 5.9 %collective-permute-done.6 = bf16[64,2048]{1,0:T(8,128)(2,1)S(1)} collective-permute-done((bf16[64,2048]{1,0:T(8,128)(2,1)S(1)}, bf16[64,2048]{1,0:T(8,128)(2,1)S(1)}, u32[]{:S(2)}, u32[]{:S(2)}) %collective-permute-start.6) | collective-permute-done | bytes 262176 | tf_op jit(solution)/shard_map/ppermute | solution.py:357
  36.6 0.8 join.1
  37.4 1.6 %collective-permute-start.13 = (bf16[2,64,1152]{2,1,0:T(8,128)(2,1)S(1)}, bf16[2,64,1152]{2,1,0:T(8,128)(2,1)S(1)}, u32[]{:S(2)}, u32[]{:S(2)}) collective-permute-start(bf16[2,64,1152]{2,1,0:T(8,128)(2,1)S(1)} %get-tuple-element.36.refs_1_), channel_id=1, source_target_pairs={{0,8},{8,0},{16,24},{24,16},{1,9},{9,1},{17,25},{25,17},{2,10},{10... | collective-permute-start | bytes 884744 | tf_op jit(solution)/shard_map/ppermute | solution.py:357
  39.0 0.5 collective-permute-start.7
  39.5 2.6 %collective-permute-start.22 = (bf16[1,64,1152]{2,1,0:T(8,128)(2,1)S(1)}, bf16[1,64,1152]{2,1,0:T(8,128)(2,1)S(1)}, u32[]{:S(2)}, u32[]{:S(2)}) collective-permute-start(bf16[1,64,1152]{2,1,0:T(8,128)(2,1)S(1)} %get-tuple-element.43), channel_id=1, source_target_pairs={{0,16},{8,24},{16,0},{24,8},{1,17},{9,25},{17,1},{25,9},{2,18},{10... | collective-permute-start | bytes 442376 | tf_op jit(solution)/shard_map/ppermute | solution.py:357
  42.1 0.3 collective-permute-start.21
  42.4 6.2 %collective-permute-done.13.refs_1_ = bf16[2,64,1152]{2,1,0:T(8,128)(2,1)S(1)} collective-permute-done((bf16[2,64,1152]{2,1,0:T(8,128)(2,1)S(1)}, bf16[2,64,1152]{2,1,0:T(8,128)(2,1)S(1)}, u32[]{:S(2)}, u32[]{:S(2)}) %collective-permute-start.13) | collective-permute-done | bytes 294944 | tf_op jit(solution)/shard_map/ppermute | solution.py:357
  48.6 4.6 %collective-permute-done.21 = bf16[1,64,1152]{2,1,0:T(8,128)(2,1)S(1)} collective-permute-done((bf16[1,64,1152]{2,1,0:T(8,128)(2,1)S(1)}, bf16[1,64,1152]{2,1,0:T(8,128)(2,1)S(1)}, u32[]{:S(2)}, u32[]{:S(2)}) %collective-permute-start.21) | collective-permute-done | bytes 147488 | tf_op jit(solution)/shard_map/ppermute | solution.py:357
  53.2 0.5 collective-permute-start.24
  53.8 1.5 %collective-permute-start.23 = (bf16[1,2,64,1152]{3,2,0,1:T(8,128)(2,1)S(1)}, bf16[1,2,64,1152]{3,2,0,1:T(8,128)(2,1)S(1)}, u32[]{:S(2)}, u32[]{:S(2)}) collective-permute-start(bf16[1,2,64,1152]{3,2,0,1:T(8,128)(2,1)S(1)} %maximum_bitcast_fusion), channel_id=1, source_target_pairs={{0,1},{1,0},{2,3},{3,2},{4,5},{5,4},{6,7},{7,6},{8,9},{9,8},{10,11... | collective-permute-start | bytes 884744 | tf_op jit(solution)/shard_map/ppermute | solution.py:357
  55.5 5.2 %experts.4 = (f32[2,2,64,1024]{3,2,1,0:T(8,128)S(1)}, bf16[2,2,64,1024]{3,2,1,0:T(8,128)(2,1)S(1)}) custom-call(s32[3]{0:T(128)S(1)} %pad_add_fusion.row_ref.refs_0_, bf16[2,64,1152]{2,1,0:T(8,128)(2,1)S(1)} %get-tuple-element.36.refs_1_, bf16[2,64,1152]{2,1,0:T(8,128)(2,1)S(1)} %collective-permute-done.7.refs_2_, ...), custom_call_target="tpu_custom_call" | custom-call | flops 1 | bytes 1 | tf_op jit(solution)/shard_map/experts/pallas_call | solution.py:337
  60.7 0.5 collective-permute-start.10
  61.3 0.2 collective-permute-done.24
  61.5 1.5 %collective-permute-start.25 = (bf16[1,2,64,1152]{3,2,0,1:T(8,128)(2,1)S(1)}, bf16[1,2,64,1152]{3,2,0,1:T(8,128)(2,1)S(1)}, u32[]{:S(2)}, u32[]{:S(2)}) collective-permute-start(bf16[1,2,64,1152]{3,2,0,1:T(8,128)(2,1)S(1)} %collective-permute-done.24), channel_id=1, source_target_pairs={{0,1},{1,0},{2,3},{3,2},{4,5},{5,4},{6,7},{7,6},{8,9},{9,8},{10,11... | collective-permute-start | bytes 884744 | tf_op jit(solution)/shard_map/ppermute | solution.py:357
  63.3 4.0 %experts.5 = (f32[2,2,64,1024]{3,2,1,0:T(8,128)S(1)}, bf16[2,2,64,1024]{3,2,1,0:T(8,128)(2,1)S(1)}) custom-call(s32[3]{0:T(128)S(1)} %pad_add_fusion.row_ref.refs_0_, bf16[2,64,1152]{2,1,0:T(8,128)(2,1)S(1)} %collective-permute-done.13.refs_1_, bf16[2,64,1152]{2,1,0:T(8,128)(2,1)S(1)} %collective-permute-done.14.refs_2_, ...), custom_call_target="tpu_custom_call" | custom-call | flops 1 | bytes 1 | tf_op jit(solution)/shard_map/experts/pallas_call | solution.py:337
  67.3 0.6 collective-permute-start.17
  67.9 2.8 %collective-permute-done.25 = bf16[1,2,64,1152]{3,2,0,1:T(8,128)(2,1)S(1)} collective-permute-done((bf16[1,2,64,1152]{3,2,0,1:T(8,128)(2,1)S(1)}, bf16[1,2,64,1152]{3,2,0,1:T(8,128)(2,1)S(1)}, u32[]{:S(2)}, u32[]{:S(2)}) %collective-permute-start.25) | collective-permute-done | bytes 294944 | tf_op jit(solution)/shard_map/ppermute | solution.py:357
  70.8 0.2 convert_add_fusion.3
  71.0 1.6 %collective-permute-start.11 = (bf16[2,64,1024]{2,1,0:T(8,128)(2,1)S(1)}, bf16[2,64,1024]{2,1,0:T(8,128)(2,1)S(1)}, u32[]{:S(2)}, u32[]{:S(2)}) collective-permute-start(bf16[2,64,1024]{2,1,0:T(8,128)(2,1)S(1)} %fusion.3), channel_id=1, source_target_pairs={{0,4},{2,6},{4,0},{6,2},{1,5},{3,7},{5,1},{7,3},{8,12},{10,14},{12... | collective-permute-start | bytes 786440 | tf_op jit(solution)/shard_map/ppermute | solution.py:357
  72.7 3.8 %experts.6 = (f32[2,2,64,1024]{3,2,1,0:T(8,128)S(1)}, bf16[2,2,64,1024]{3,2,1,0:T(8,128)(2,1)S(1)}) custom-call(s32[3]{0:T(128)S(1)} %pad_add_fusion.row_ref.refs_0_, bf16[2,64,1152]{2,1,0:T(8,128)(2,1)S(1)} %get-tuple-element.54.refs_1_, bf16[2,64,1152]{2,1,0:T(8,128)(2,1)S(1)} %get-tuple-element.45.refs_2_, ...), custom_call_target="tpu_custom_call" | custom-call | flops 1 | bytes 1 | tf_op jit(solution)/shard_map/experts/pallas_call | solution.py:337
  76.5 0.2 collective-permute-start.28
  76.7 0.2 convert_add_fusion.2
  77.0 1.5 %collective-permute-start.18 = (bf16[2,64,1024]{2,1,0:T(8,128)(2,1)S(1)}, bf16[2,64,1024]{2,1,0:T(8,128)(2,1)S(1)}, u32[]{:S(2)}, u32[]{:S(2)}) collective-permute-start(bf16[2,64,1024]{2,1,0:T(8,128)(2,1)S(1)} %fusion.4), channel_id=1, source_target_pairs={{0,4},{2,6},{4,0},{6,2},{1,5},{3,7},{5,1},{7,3},{8,12},{10,14},{12... | collective-permute-start | bytes 786440 | tf_op jit(solution)/shard_map/ppermute | solution.py:357
  78.6 0.4 collective-permute-start.33
  79.0 0.7 collective-permute-done.11
  79.9 0.6 collective-permute-start.12
  80.4 5.2 %collective-permute-done.18 = bf16[2,64,1024]{2,1,0:T(8,128)(2,1)S(1)} collective-permute-done((bf16[2,64,1024]{2,1,0:T(8,128)(2,1)S(1)}, bf16[2,64,1024]{2,1,0:T(8,128)(2,1)S(1)}, u32[]{:S(2)}, u32[]{:S(2)}) %collective-permute-start.18) | collective-permute-done | bytes 262176 | tf_op jit(solution)/shard_map/ppermute | solution.py:357
  85.7 0.6 collective-permute-start.19
  86.3 3.8 %experts.7 = (f32[2,2,64,1024]{3,2,1,0:T(8,128)S(1)}, bf16[2,2,64,1024]{3,2,1,0:T(8,128)(2,1)S(1)}) custom-call(s32[3]{0:T(128)S(1)} %pad_add_fusion.row_ref.refs_0_, bf16[2,64,1152]{2,1,0:T(8,128)(2,1)S(1)} %get-tuple-element.55.refs_1_, bf16[2,64,1152]{2,1,0:T(8,128)(2,1)S(1)} %get-tuple-element.48.refs_2_, ...), custom_call_target="tpu_custom_call" | custom-call | flops 1 | bytes 1 | tf_op jit(solution)/shard_map/experts/pallas_call | solution.py:337
  90.2 0.2 convert_add_fusion.1
  90.5 1.6 %collective-permute-start.29 = (bf16[2,64,1024]{2,1,0:T(8,128)(2,1)S(1)}, bf16[2,64,1024]{2,1,0:T(8,128)(2,1)S(1)}, u32[]{:S(2)}, u32[]{:S(2)}) collective-permute-start(bf16[2,64,1024]{2,1,0:T(8,128)(2,1)S(1)} %fusion.5), channel_id=1, source_target_pairs={{0,4},{2,6},{4,0},{6,2},{1,5},{3,7},{5,1},{7,3},{8,12},{10,14},{12... | collective-permute-start | bytes 786440 | tf_op jit(solution)/shard_map/ppermute | solution.py:357
  92.1 0.1 convert_add_fusion
  92.3 1.6 %collective-permute-start.35 = (bf16[1,2,64,1024]{3,2,1,0:T(8,128)(2,1)S(1)}, bf16[1,2,64,1024]{3,2,1,0:T(8,128)(2,1)S(1)}, u32[]{:S(2)}, u32[]{:S(2)}) collective-permute-start(bf16[1,2,64,1024]{3,2,1,0:T(8,128)(2,1)S(1)} %slice.173), channel_id=1, source_target_pairs={{0,1},{1,0},{2,3},{3,2},{4,5},{5,4},{6,7},{7,6},{8,9},{9,8},{10,11... | collective-permute-start | bytes 786440 | tf_op jit(solution)/shard_map/ppermute | solution.py:357
  93.9 2.0 %collective-permute-start.20 = (bf16[64,1024]{1,0:T(8,128)(2,1)S(1)}, bf16[64,1024]{1,0:T(8,128)(2,1)S(1)}, u32[]{:S(2)}, u32[]{:S(2)}) collective-permute-start(bf16[64,1024]{1,0:T(8,128)(2,1)S(1)} %fusion.17), channel_id=1, source_target_pairs={{0,8},{8,0},{16,24},{24,16},{1,9},{9,1},{17,25},{25,17},{2,10},{10... | collective-permute-start | bytes 393224 | tf_op jit(solution)/shard_map/ppermute | solution.py:357
  95.9 3.4 %collective-permute-done.29 = bf16[2,64,1024]{2,1,0:T(8,128)(2,1)S(1)} collective-permute-done((bf16[2,64,1024]{2,1,0:T(8,128)(2,1)S(1)}, bf16[2,64,1024]{2,1,0:T(8,128)(2,1)S(1)}, u32[]{:S(2)}, u32[]{:S(2)}) %collective-permute-start.29) | collective-permute-done | bytes 262176 | tf_op jit(solution)/shard_map/ppermute | solution.py:357
  99.3 1.6 %collective-permute-start.30 = (bf16[1,64,1024]{2,1,0:T(8,128)(2,1)S(1)}, bf16[1,64,1024]{2,1,0:T(8,128)(2,1)S(1)}, u32[]{:S(2)}, u32[]{:S(2)}) collective-permute-start(bf16[1,64,1024]{2,1,0:T(8,128)(2,1)S(1)} %slice.174), channel_id=1, source_target_pairs={{0,1},{1,0},{2,3},{3,2},{4,5},{5,4},{6,7},{7,6},{8,9},{9,8},{10,11... | collective-permute-start | bytes 393224 | tf_op jit(solution)/shard_map/ppermute | solution.py:357
  101.0 1.6 %collective-permute-start.36 = (bf16[64,1024]{1,0:T(8,128)(2,1)S(1)}, bf16[64,1024]{1,0:T(8,128)(2,1)S(1)}, u32[]{:S(2)}, u32[]{:S(2)}) collective-permute-start(bf16[64,1024]{1,0:T(8,128)(2,1)S(1)} %fusion.19), channel_id=1, source_target_pairs={{0,4},{2,6},{4,0},{6,2},{1,5},{3,7},{5,1},{7,3},{8,12},{10,14},{12... | collective-permute-start | bytes 393224 | tf_op jit(solution)/shard_map/ppermute | solution.py:357
  102.6 1.9 %collective-permute-done.30 = bf16[1,64,1024]{2,1,0:T(8,128)(2,1)S(1)} collective-permute-done((bf16[1,64,1024]{2,1,0:T(8,128)(2,1)S(1)}, bf16[1,64,1024]{2,1,0:T(8,128)(2,1)S(1)}, u32[]{:S(2)}, u32[]{:S(2)}) %collective-permute-start.30) | collective-permute-done | bytes 131104 | tf_op jit(solution)/shard_map/ppermute | solution.py:357
  104.5 4.7 %collective-permute-start.31 = (bf16[64,1024]{1,0:T(8,128)(2,1)S(1)}, bf16[64,1024]{1,0:T(8,128)(2,1)S(1)}, u32[]{:S(2)}, u32[]{:S(2)}) collective-permute-start(bf16[64,1024]{1,0:T(8,128)(2,1)S(1)} %fusion.18), channel_id=1, source_target_pairs={{0,24},{8,16},{16,8},{24,0},{1,25},{9,17},{17,9},{25,1},{2,26},{10... | collective-permute-start | bytes 393224 | tf_op jit(solution)/shard_map/ppermute | solution.py:357
  109.4 3.9 %collective-permute-done.31 = bf16[64,1024]{1,0:T(8,128)(2,1)S(1)} collective-permute-done((bf16[64,1024]{1,0:T(8,128)(2,1)S(1)}, bf16[64,1024]{1,0:T(8,128)(2,1)S(1)}, u32[]{:S(2)}, u32[]{:S(2)}) %collective-permute-start.31) | collective-permute-done | bytes 131104 | tf_op jit(solution)/shard_map/ppermute | solution.py:357
  113.2 5.5 %collective-permute-done.37 = bf16[64,1024]{1,0:T(8,128)(2,1)S(1)} collective-permute-done((bf16[64,1024]{1,0:T(8,128)(2,1)S(1)}, bf16[64,1024]{1,0:T(8,128)(2,1)S(1)}, u32[]{:S(2)}, u32[]{:S(2)}) %collective-permute-start.37) | collective-permute-done | bytes 131104 | tf_op jit(solution)/shard_map/ppermute | solution.py:357
  118.7 0.1 fusion.15.own_ref
  118.8 1.4 %collective-permute-start.38 = (bf16[1,64,1024]{2,1,0:T(8,128)(2,1)S(1)}, bf16[1,64,1024]{2,1,0:T(8,128)(2,1)S(1)}, u32[]{:S(2)}, u32[]{:S(2)}) collective-permute-start(bf16[1,64,1024]{2,1,0:T(8,128)(2,1)S(1)} %bitcast.89), channel_id=1, source_target_pairs={{0,1},{1,0},{2,3},{3,2},{4,5},{5,4},{6,7},{7,6},{8,9},{9,8},{10,11... | collective-permute-start | bytes 393224 | tf_op jit(solution)/shard_map/ppermute | solution.py:357
  120.3 3.6 %collective-permute-done.38.others_ref = bf16[1,64,1024]{2,1,0:T(8,128)(2,1)S(1)} collective-permute-done((bf16[1,64,1024]{2,1,0:T(8,128)(2,1)S(1)}, bf16[1,64,1024]{2,1,0:T(8,128)(2,1)S(1)}, u32[]{:S(2)}, u32[]{:S(2)}) %collective-permute-start.38) | collective-permute-done | bytes 131104 | tf_op jit(solution)/shard_map/ppermute | solution.py:357
  123.9 1.3 %finish.1 = bf16[64,2048]{1,0:T(8,128)(2,1)} custom-call(s32[3]{0:T(128)S(1)} %pad_add_fusion.row_ref.refs_0_, bf16[64,1024]{1,0:T(8,128)(2,1)S(1)} %fusion.15.own_ref, bf16[1,64,1024]{2,1,0:T(8,128)(2,1)S(1)} %collective-permute-done.38.others_ref), custom_call_target="tpu_custom_call" | custom-call | tf_op jit(solution)/shard_map/finish/pallas_call | solution.py:275
  (94 shorter events, 2.0 us)
Async XLA Ops:
  0.6 7.4 %collective-permute-start = (bf16[64,2048]{1,0:T(8,128)(2,1)}, bf16[64,2048]{1,0:T(8,128)(2,1)S(1)}, u32[]{:S(2)}, u32[]{:S(2)}) collective-permute-start(bf16[64,2048]{1,0:T(8,128)(2,1)} %hidden_ref.1), channel_id=1, source_target_pairs={{0,2},{2,0},{4,6},{6,4},{1,3},{3,1},{5,7},{7,5},{8,10},{10,8},{12,... | collective-permute-start | bytes 786440 | tf_op jit(solution)/shard_map/ppermute | solution.py:357
  1.1 12.2 %collective-permute-start.2 = (bf16[64,2048]{1,0:T(8,128)(2,1)}, bf16[64,2048]{1,0:T(8,128)(2,1)S(1)}, u32[]{:S(2)}, u32[]{:S(2)}) collective-permute-start(bf16[64,2048]{1,0:T(8,128)(2,1)} %hidden_ref.1), channel_id=1, source_target_pairs={{0,4},{2,6},{4,0},{6,2},{1,5},{3,7},{5,1},{7,3},{8,12},{10,14},{12... | collective-permute-start | bytes 786440 | tf_op jit(solution)/shard_map/ppermute | solution.py:357
  4.5 0.7 copy-start.14
  5.2 0.7 copy-start.15
  5.8 2.2 %copy-start.1 = (bf16[2048,576]{0,1:T(8,128)(2,1)S(1)}, bf16[2048,576]{0,1:T(8,128)(2,1)}, u32[]{:S(2)}) copy-start(bf16[2048,576]{0,1:T(8,128)(2,1)} %param.27) | copy-start | bytes 7077892
  5.8 2.2 %copy-start.2 = (bf16[4,384,576]{1,2,0:T(8,128)(2,1)S(1)}, bf16[4,384,576]{1,2,0:T(8,128)(2,1)}, u32[]{:S(2)}) copy-start(bf16[4,384,576]{1,2,0:T(8,128)(2,1)} %param.20) | copy-start | bytes 5308420
  5.8 2.6 %copy-start.3 = (bf16[2048,384]{1,0:T(8,128)(2,1)S(1)}, bf16[2048,384]{1,0:T(8,128)(2,1)}, u32[]{:S(2)}) copy-start(bf16[2048,384]{1,0:T(8,128)(2,1)} %refs_7_.3) | copy-start | bytes 4718596
  5.8 2.9 %copy-start.4 = (bf16[256,2048]{1,0:T(8,128)(2,1)S(1)}, bf16[256,2048]{1,0:T(8,128)(2,1)}, u32[]{:S(2)}) copy-start(bf16[256,2048]{1,0:T(8,128)(2,1)} %refs_12_.3) | copy-start | bytes 3145732
  5.8 2.9 %copy-start.8 = (bf16[2,128,512]{2,1,0:T(8,128)(2,1)S(1)}, bf16[2,128,512]{2,1,0:T(8,128)(2,1)}, u32[]{:S(2)}) copy-start(bf16[2,128,512]{2,1,0:T(8,128)(2,1)} %refs_10_.4) | copy-start | bytes 786436
  5.8 3.0 %copy-start.9 = (bf16[2,512,128]{2,1,0:T(8,128)(2,1)S(1)}, bf16[2,512,128]{2,1,0:T(8,128)(2,1)}, u32[]{:S(2)}) copy-start(bf16[2,512,128]{2,1,0:T(8,128)(2,1)} %refs_11_.3) | copy-start | bytes 786436
  5.8 3.1 %copy-start.10 = (bf16[64,2048]{1,0:T(8,128)(2,1)S(1)}, bf16[64,2048]{1,0:T(8,128)(2,1)}, u32[]{:S(2)}) copy-start(bf16[64,2048]{1,0:T(8,128)(2,1)} %hidden_ref.1) | copy-start | bytes 786436
  5.9 3.1 %copy-start.11 = (f32[2048]{0:T(1024)S(1)}, f32[2048]{0:T(1024)}, u32[]{:S(2)}) copy-start(f32[2048]{0:T(1024)} %param.25) | copy-start | bytes 24580
  5.9 3.1 %copy-start.12 = (f32[512]{0:T(512)S(1)}, f32[512]{0:T(512)}, u32[]{:S(2)}) copy-start(f32[512]{0:T(512)} %param.28) | copy-start | bytes 6148
  13.3 1.5 %collective-permute-start.3 = (bf16[64,2048]{1,0:T(8,128)(2,1)S(1)}, bf16[64,2048]{1,0:T(8,128)(2,1)S(1)}, u32[]{:S(2)}, u32[]{:S(2)}) collective-permute-start(bf16[64,2048]{1,0:T(8,128)(2,1)S(1)} %collective-permute-done.2.refs_0_), channel_id=1, source_target_pairs={{0,2},{2,0},{4,6},{6,4},{1,3},{3,1},{5,7},{7,5},{8,10},{10,8},{12,... | collective-permute-start | bytes 786440 | tf_op jit(solution)/shard_map/ppermute | solution.py:357
  18.7 11.8 %copy-start.16 = (s32[64,6]{0,1:T(8,128)S(1)}, s32[64,6]{0,1:T(8,128)}, u32[]{:S(2)}) copy-start(s32[64,6]{0,1:T(8,128)} %param.23) | copy-start | bytes 4612
  18.7 17.8 %copy-start.13 = (f32[2048]{0:T(1024)S(1)}, f32[2048]{0:T(1024)}, u32[]{:S(2)}) copy-start(f32[2048]{0:T(1024)} %param.32) | copy-start | bytes 24580
  18.7 1.6 %collective-permute-start.4 = (bf16[64,2048]{1,0:T(8,128)(2,1)S(1)}, bf16[64,2048]{1,0:T(8,128)(2,1)S(1)}, u32[]{:S(2)}, u32[]{:S(2)}) collective-permute-start(bf16[64,2048]{1,0:T(8,128)(2,1)S(1)} %get-tuple-element.34), channel_id=1, source_target_pairs={{0,2},{2,0},{4,6},{6,4},{1,3},{3,1},{5,7},{7,5},{8,10},{10,8},{12,... | collective-permute-start | bytes 786440 | tf_op jit(solution)/shard_map/ppermute | solution.py:357
  18.9 1.7 %collective-permute-start.1 = (bf16[64,2048]{1,0:T(8,128)(2,1)S(1)}, bf16[64,2048]{1,0:T(8,128)(2,1)S(1)}, u32[]{:S(2)}, u32[]{:S(2)}) collective-permute-start(bf16[64,2048]{1,0:T(8,128)(2,1)S(1)} %get-tuple-element.31), channel_id=1, source_target_pairs={{0,2},{2,0},{4,6},{6,4},{1,3},{3,1},{5,7},{7,5},{8,10},{10,8},{12,... | collective-permute-start | bytes 786440 | tf_op jit(solution)/shard_map/ppermute | solution.py:357
  20.4 8.4 %collective-permute-start.5 = (bf16[64,2048]{1,0:T(8,128)(2,1)S(1)}, bf16[64,2048]{1,0:T(8,128)(2,1)S(1)}, u32[]{:S(2)}, u32[]{:S(2)}) collective-permute-start(bf16[64,2048]{1,0:T(8,128)(2,1)S(1)} %add_convert_fusion.1), channel_id=1, source_target_pairs={{0,4},{2,6},{4,0},{6,2},{1,5},{3,7},{5,1},{7,3},{8,12},{10,14},{12... | collective-permute-start | bytes 786440 | tf_op jit(solution)/shard_map/ppermute | solution.py:357
  28.9 7.6 %collective-permute-start.6 = (bf16[64,2048]{1,0:T(8,128)(2,1)S(1)}, bf16[64,2048]{1,0:T(8,128)(2,1)S(1)}, u32[]{:S(2)}, u32[]{:S(2)}) collective-permute-start(bf16[64,2048]{1,0:T(8,128)(2,1)S(1)} %add_convert_fusion.keep_ref), channel_id=1, source_target_pairs={{0,1},{1,0},{2,3},{3,2},{4,5},{5,4},{6,7},{7,6},{8,9},{9,8},{10,11... | collective-permute-start | bytes 786440 | tf_op jit(solution)/shard_map/ppermute | solution.py:357
  36.5 18.9 %slice-start = ((s8[5767168]{0:T(1024)(128)(4,1)}), s8[4194304]{0:T(1024)(128)(4,1)S(1)}, s32[]{:S(2)}) async-start(s8[5767168]{0:T(1024)(128)(4,1)} %bitcast.70), calls=%async_computation | async-start | bytes 8388608
  36.5 18.9 %slice-start.1 = ((s8[5767168]{0:T(1024)(128)(4,1)}), s8[1572864]{0:T(1024)(128)(4,1)S(1)}, s32[]{:S(2)}) async-start(s8[5767168]{0:T(1024)(128)(4,1)} %bitcast.70), calls=%async_computation.1 | async-start | bytes 3145728
  36.5 18.9 %copy-start = (bf16[1,704,2048]{2,1,0:T(8,128)(2,1)S(1)}, bf16[1,704,2048]{2,1,0:T(8,128)(2,1)}, u32[]{:S(2)}) copy-start(bf16[1,704,2048]{2,1,0:T(8,128)(2,1)} %param.37) | copy-start | bytes 8650756
  36.5 18.9 %copy-start.5 = (bf16[2,2048,352]{1,2,0:T(8,128)(2,1)S(1)}, bf16[2,2048,352]{1,2,0:T(8,128)(2,1)}, u32[]{:S(2)}) copy-start(bf16[2,2048,352]{1,2,0:T(8,128)(2,1)} %param.34) | copy-start | bytes 8650756
  36.5 18.9 %copy-start.6 = (bf16[352,2048]{1,0:T(8,128)(2,1)S(1)}, bf16[352,2048]{1,0:T(8,128)(2,1)}, u32[]{:S(2)}) copy-start(bf16[352,2048]{1,0:T(8,128)(2,1)} %refs_10_.5) | copy-start | bytes 4325380
  36.6 18.9 %copy-start.7 = (bf16[2048,16]{0,1:T(8,128)(2,1)S(1)}, bf16[2048,16]{0,1:T(8,128)(2,1)}, u32[]{:S(2)}) copy-start(bf16[2048,16]{0,1:T(8,128)(2,1)} %param.33) | copy-start | bytes 196612
  37.4 11.1 %collective-permute-start.13 = (bf16[2,64,1152]{2,1,0:T(8,128)(2,1)S(1)}, bf16[2,64,1152]{2,1,0:T(8,128)(2,1)S(1)}, u32[]{:S(2)}, u32[]{:S(2)}) collective-permute-start(bf16[2,64,1152]{2,1,0:T(8,128)(2,1)S(1)} %get-tuple-element.36.refs_1_), channel_id=1, source_target_pairs={{0,8},{8,0},{16,24},{24,16},{1,9},{9,1},{17,25},{25,17},{2,10},{10... | collective-permute-start | bytes 884744 | tf_op jit(solution)/shard_map/ppermute | solution.py:357
  39.0 9.5 %collective-permute-start.7 = (bf16[2,64,1152]{2,1,0:T(8,128)(2,1)S(1)}, bf16[2,64,1152]{2,1,0:T(8,128)(2,1)S(1)}, u32[]{:S(2)}, u32[]{:S(2)}) collective-permute-start(bf16[2,64,1152]{2,1,0:T(8,128)(2,1)S(1)} %get-tuple-element.36.refs_1_), channel_id=1, source_target_pairs={{0,4},{2,6},{4,0},{6,2},{1,5},{3,7},{5,1},{7,3},{8,12},{10,14},{12... | collective-permute-start | bytes 884744 | tf_op jit(solution)/shard_map/ppermute | solution.py:357
  39.5 9.1 %collective-permute-start.22 = (bf16[1,64,1152]{2,1,0:T(8,128)(2,1)S(1)}, bf16[1,64,1152]{2,1,0:T(8,128)(2,1)S(1)}, u32[]{:S(2)}, u32[]{:S(2)}) collective-permute-start(bf16[1,64,1152]{2,1,0:T(8,128)(2,1)S(1)} %get-tuple-element.43), channel_id=1, source_target_pairs={{0,16},{8,24},{16,0},{24,8},{1,17},{9,25},{17,1},{25,9},{2,18},{10... | collective-permute-start | bytes 442376 | tf_op jit(solution)/shard_map/ppermute | solution.py:357
  42.1 11.1 %collective-permute-start.21 = (bf16[1,64,1152]{2,1,0:T(8,128)(2,1)S(1)}, bf16[1,64,1152]{2,1,0:T(8,128)(2,1)S(1)}, u32[]{:S(2)}, u32[]{:S(2)}) collective-permute-start(bf16[1,64,1152]{2,1,0:T(8,128)(2,1)S(1)} %get-tuple-element.43), channel_id=1, source_target_pairs={{0,24},{8,16},{16,8},{24,0},{1,25},{9,17},{17,9},{25,1},{2,26},{10... | collective-permute-start | bytes 442376 | tf_op jit(solution)/shard_map/ppermute | solution.py:357
  42.4 13.0 %collective-permute-start.8 = (bf16[2,64,1152]{2,1,0:T(8,128)(2,1)S(1)}, bf16[2,64,1152]{2,1,0:T(8,128)(2,1)S(1)}, u32[]{:S(2)}, u32[]{:S(2)}) collective-permute-start(bf16[2,64,1152]{2,1,0:T(8,128)(2,1)S(1)} %get-tuple-element.36.refs_1_), channel_id=1, source_target_pairs={{0,2},{2,0},{4,6},{6,4},{1,3},{3,1},{5,7},{7,5},{8,10},{10,8},{12,... | collective-permute-start | bytes 884744 | tf_op jit(solution)/shard_map/ppermute | solution.py:357
  48.5 12.7 %collective-permute-start.14 = (bf16[2,64,1152]{2,1,0:T(8,128)(2,1)S(1)}, bf16[2,64,1152]{2,1,0:T(8,128)(2,1)S(1)}, u32[]{:S(2)}, u32[]{:S(2)}) collective-permute-start(bf16[2,64,1152]{2,1,0:T(8,128)(2,1)S(1)} %collective-permute-done.13.refs_1_), channel_id=1, source_target_pairs={{0,4},{2,6},{4,0},{6,2},{1,5},{3,7},{5,1},{7,3},{8,12},{10,14},{12... | collective-permute-start | bytes 884744 | tf_op jit(solution)/shard_map/ppermute | solution.py:357
  48.5 6.9 %collective-permute-start.9 = (bf16[2,64,1152]{2,1,0:T(8,128)(2,1)S(1)}, bf16[2,64,1152]{2,1,0:T(8,128)(2,1)S(1)}, u32[]{:S(2)}, u32[]{:S(2)}) collective-permute-start(bf16[2,64,1152]{2,1,0:T(8,128)(2,1)S(1)} %collective-permute-done.7.refs_2_), channel_id=1, source_target_pairs={{0,2},{2,0},{4,6},{6,4},{1,3},{3,1},{5,7},{7,5},{8,10},{10,8},{12,... | collective-permute-start | bytes 884744 | tf_op jit(solution)/shard_map/ppermute | solution.py:357
  53.2 8.3 %collective-permute-start.24 = (bf16[1,2,64,1152]{3,2,0,1:T(8,128)(2,1)S(1)}, bf16[1,2,64,1152]{3,2,0,1:T(8,128)(2,1)S(1)}, u32[]{:S(2)}, u32[]{:S(2)}) collective-permute-start(bf16[1,2,64,1152]{3,2,0,1:T(8,128)(2,1)S(1)} %maximum_bitcast_fusion), channel_id=1, source_target_pairs={{0,4},{2,6},{4,0},{6,2},{1,5},{3,7},{5,1},{7,3},{8,12},{10,14},{12... | collective-permute-start | bytes 884744 | tf_op jit(solution)/shard_map/ppermute | solution.py:357
  53.8 9.2 %collective-permute-start.23 = (bf16[1,2,64,1152]{3,2,0,1:T(8,128)(2,1)S(1)}, bf16[1,2,64,1152]{3,2,0,1:T(8,128)(2,1)S(1)}, u32[]{:S(2)}, u32[]{:S(2)}) collective-permute-start(bf16[1,2,64,1152]{3,2,0,1:T(8,128)(2,1)S(1)} %maximum_bitcast_fusion), channel_id=1, source_target_pairs={{0,1},{1,0},{2,3},{3,2},{4,5},{5,4},{6,7},{7,6},{8,9},{9,8},{10,11... | collective-permute-start | bytes 884744 | tf_op jit(solution)/shard_map/ppermute | solution.py:357
  55.3 7.9 %collective-permute-start.15 = (bf16[2,64,1152]{2,1,0:T(8,128)(2,1)S(1)}, bf16[2,64,1152]{2,1,0:T(8,128)(2,1)S(1)}, u32[]{:S(2)}, u32[]{:S(2)}) collective-permute-start(bf16[2,64,1152]{2,1,0:T(8,128)(2,1)S(1)} %collective-permute-done.13.refs_1_), channel_id=1, source_target_pairs={{0,2},{2,0},{4,6},{6,4},{1,3},{3,1},{5,7},{7,5},{8,10},{10,8},{12,... | collective-permute-start | bytes 884744 | tf_op jit(solution)/shard_map/ppermute | solution.py:357
  60.7 10.1 %collective-permute-start.10 = (bf16[2,2,64,1024]{3,2,1,0:T(8,128)(2,1)S(1)}, bf16[2,2,64,1024]{3,2,1,0:T(8,128)(2,1)S(1)}, u32[]{:S(2)}, u32[]{:S(2)}) collective-permute-start(bf16[2,2,64,1024]{3,2,1,0:T(8,128)(2,1)S(1)} %get-tuple-element.39), channel_id=1, source_target_pairs={{0,2},{2,0},{4,6},{6,4},{1,3},{3,1},{5,7},{7,5},{8,10},{10,8},{12,... | collective-permute-start | bytes 1572872 | tf_op jit(solution)/shard_map/ppermute | solution.py:357
  61.2 2.0 %collective-permute-start.16 = (bf16[2,64,1152]{2,1,0:T(8,128)(2,1)S(1)}, bf16[2,64,1152]{2,1,0:T(8,128)(2,1)S(1)}, u32[]{:S(2)}, u32[]{:S(2)}) collective-permute-start(bf16[2,64,1152]{2,1,0:T(8,128)(2,1)S(1)} %collective-permute-done.14.refs_2_), channel_id=1, source_target_pairs={{0,2},{2,0},{4,6},{6,4},{1,3},{3,1},{5,7},{7,5},{8,10},{10,8},{12,... | collective-permute-start | bytes 884744 | tf_op jit(solution)/shard_map/ppermute | solution.py:357
  61.5 9.1 %collective-permute-start.25 = (bf16[1,2,64,1152]{3,2,0,1:T(8,128)(2,1)S(1)}, bf16[1,2,64,1152]{3,2,0,1:T(8,128)(2,1)S(1)}, u32[]{:S(2)}, u32[]{:S(2)}) collective-permute-start(bf16[1,2,64,1152]{3,2,0,1:T(8,128)(2,1)S(1)} %collective-permute-done.24), channel_id=1, source_target_pairs={{0,1},{1,0},{2,3},{3,2},{4,5},{5,4},{6,7},{7,6},{8,9},{9,8},{10,11... | collective-permute-start | bytes 884744 | tf_op jit(solution)/shard_map/ppermute | solution.py:357
  63.1 9.5 %collective-permute-start.26 = (bf16[2,64,1152]{2,1,0:T(8,128)(2,1)S(1)}, bf16[2,64,1152]{2,1,0:T(8,128)(2,1)S(1)}, u32[]{:S(2)}, u32[]{:S(2)}) collective-permute-start(bf16[2,64,1152]{2,1,0:T(8,128)(2,1)S(1)} %get-tuple-element.54.refs_1_), channel_id=1, source_target_pairs={{0,2},{2,0},{4,6},{6,4},{1,3},{3,1},{5,7},{7,5},{8,10},{10,8},{12,... | collective-permute-start | bytes 884744 | tf_op jit(solution)/shard_map/ppermute | solution.py:357
  67.3 9.4 %collective-permute-start.17 = (bf16[2,2,64,1024]{3,2,1,0:T(8,128)(2,1)S(1)}, bf16[2,2,64,1024]{3,2,1,0:T(8,128)(2,1)S(1)}, u32[]{:S(2)}, u32[]{:S(2)}) collective-permute-start(bf16[2,2,64,1024]{3,2,1,0:T(8,128)(2,1)S(1)} %get-tuple-element.42), channel_id=1, source_target_pairs={{0,2},{2,0},{4,6},{6,4},{1,3},{3,1},{5,7},{7,5},{8,10},{10,8},{12,... | collective-permute-start | bytes 1572872 | tf_op jit(solution)/shard_map/ppermute | solution.py:357
  71.0 1.7 %collective-permute-start.27 = (bf16[2,64,1152]{2,1,0:T(8,128)(2,1)S(1)}, bf16[2,64,1152]{2,1,0:T(8,128)(2,1)S(1)}, u32[]{:S(2)}, u32[]{:S(2)}) collective-permute-start(bf16[2,64,1152]{2,1,0:T(8,128)(2,1)S(1)} %get-tuple-element.45.refs_2_), channel_id=1, source_target_pairs={{0,2},{2,0},{4,6},{6,4},{1,3},{3,1},{5,7},{7,5},{8,10},{10,8},{12,... | collective-permute-start | bytes 884744 | tf_op jit(solution)/shard_map/ppermute | solution.py:357
  71.0 8.7 %collective-permute-start.11 = (bf16[2,64,1024]{2,1,0:T(8,128)(2,1)S(1)}, bf16[2,64,1024]{2,1,0:T(8,128)(2,1)S(1)}, u32[]{:S(2)}, u32[]{:S(2)}) collective-permute-start(bf16[2,64,1024]{2,1,0:T(8,128)(2,1)S(1)} %fusion.3), channel_id=1, source_target_pairs={{0,4},{2,6},{4,0},{6,2},{1,5},{3,7},{5,1},{7,3},{8,12},{10,14},{12... | collective-permute-start | bytes 786440 | tf_op jit(solution)/shard_map/ppermute | solution.py:357
  76.5 13.7 %collective-permute-start.28 = (bf16[2,2,64,1024]{3,2,1,0:T(8,128)(2,1)S(1)}, bf16[2,2,64,1024]{3,2,1,0:T(8,128)(2,1)S(1)}, u32[]{:S(2)}, u32[]{:S(2)}) collective-permute-start(bf16[2,2,64,1024]{3,2,1,0:T(8,128)(2,1)S(1)} %get-tuple-element.47), channel_id=1, source_target_pairs={{0,2},{2,0},{4,6},{6,4},{1,3},{3,1},{5,7},{7,5},{8,10},{10,8},{12,... | collective-permute-start | bytes 1572872 | tf_op jit(solution)/shard_map/ppermute | solution.py:357
  77.0 8.6 %collective-permute-start.18 = (bf16[2,64,1024]{2,1,0:T(8,128)(2,1)S(1)}, bf16[2,64,1024]{2,1,0:T(8,128)(2,1)S(1)}, u32[]{:S(2)}, u32[]{:S(2)}) collective-permute-start(bf16[2,64,1024]{2,1,0:T(8,128)(2,1)S(1)} %fusion.4), channel_id=1, source_target_pairs={{0,4},{2,6},{4,0},{6,2},{1,5},{3,7},{5,1},{7,3},{8,12},{10,14},{12... | collective-permute-start | bytes 786440 | tf_op jit(solution)/shard_map/ppermute | solution.py:357
  78.5 7.8 %collective-permute-start.32 = (bf16[2,64,1152]{2,1,0:T(8,128)(2,1)S(1)}, bf16[2,64,1152]{2,1,0:T(8,128)(2,1)S(1)}, u32[]{:S(2)}, u32[]{:S(2)}) collective-permute-start(bf16[2,64,1152]{2,1,0:T(8,128)(2,1)S(1)} %get-tuple-element.55.refs_1_), channel_id=1, source_target_pairs={{0,2},{2,0},{4,6},{6,4},{1,3},{3,1},{5,7},{7,5},{8,10},{10,8},{12,... | collective-permute-start | bytes 884744 | tf_op jit(solution)/shard_map/ppermute | solution.py:357
  78.6 7.7 %collective-permute-start.33 = (bf16[2,64,1152]{2,1,0:T(8,128)(2,1)S(1)}, bf16[2,64,1152]{2,1,0:T(8,128)(2,1)S(1)}, u32[]{:S(2)}, u32[]{:S(2)}) collective-permute-start(bf16[2,64,1152]{2,1,0:T(8,128)(2,1)S(1)} %get-tuple-element.48.refs_2_), channel_id=1, source_target_pairs={{0,2},{2,0},{4,6},{6,4},{1,3},{3,1},{5,7},{7,5},{8,10},{10,8},{12,... | collective-permute-start | bytes 884744 | tf_op jit(solution)/shard_map/ppermute | solution.py:357
  79.9 29.5 %collective-permute-start.12 = (bf16[1,64,1024]{2,1,0:T(8,128)(2,1)S(1)}, bf16[1,64,1024]{2,1,0:T(8,128)(2,1)S(1)}, u32[]{:S(2)}, u32[]{:S(2)}) collective-permute-start(bf16[1,64,1024]{2,1,0:T(8,128)(2,1)S(1)} %slice.176), channel_id=1, source_target_pairs={{0,1},{1,0},{2,3},{3,2},{4,5},{5,4},{6,7},{7,6},{8,9},{9,8},{10,11... | collective-permute-start | bytes 393224 | tf_op jit(solution)/shard_map/ppermute | solution.py:357
  85.7 8.2 %collective-permute-start.19 = (bf16[1,64,1024]{2,1,0:T(8,128)(2,1)S(1)}, bf16[1,64,1024]{2,1,0:T(8,128)(2,1)S(1)}, u32[]{:S(2)}, u32[]{:S(2)}) collective-permute-start(bf16[1,64,1024]{2,1,0:T(8,128)(2,1)S(1)} %slice.175), channel_id=1, source_target_pairs={{0,1},{1,0},{2,3},{3,2},{4,5},{5,4},{6,7},{7,6},{8,9},{9,8},{10,11... | collective-permute-start | bytes 393224 | tf_op jit(solution)/shard_map/ppermute | solution.py:357
  90.1 2.0 %collective-permute-start.34 = (bf16[2,2,64,1024]{3,2,1,0:T(8,128)(2,1)S(1)}, bf16[2,2,64,1024]{3,2,1,0:T(8,128)(2,1)S(1)}, u32[]{:S(2)}, u32[]{:S(2)}) collective-permute-start(bf16[2,2,64,1024]{3,2,1,0:T(8,128)(2,1)S(1)} %get-tuple-element.50), channel_id=1, source_target_pairs={{0,2},{2,0},{4,6},{6,4},{1,3},{3,1},{5,7},{7,5},{8,10},{10,8},{12,... | collective-permute-start | bytes 1572872 | tf_op jit(solution)/shard_map/ppermute | solution.py:357
  90.5 8.8 %collective-permute-start.29 = (bf16[2,64,1024]{2,1,0:T(8,128)(2,1)S(1)}, bf16[2,64,1024]{2,1,0:T(8,128)(2,1)S(1)}, u32[]{:S(2)}, u32[]{:S(2)}) collective-permute-start(bf16[2,64,1024]{2,1,0:T(8,128)(2,1)S(1)} %fusion.5), channel_id=1, source_target_pairs={{0,4},{2,6},{4,0},{6,2},{1,5},{3,7},{5,1},{7,3},{8,12},{10,14},{12... | collective-permute-start | bytes 786440 | tf_op jit(solution)/shard_map/ppermute | solution.py:357
  92.3 8.6 %collective-permute-start.35 = (bf16[1,2,64,1024]{3,2,1,0:T(8,128)(2,1)S(1)}, bf16[1,2,64,1024]{3,2,1,0:T(8,128)(2,1)S(1)}, u32[]{:S(2)}, u32[]{:S(2)}) collective-permute-start(bf16[1,2,64,1024]{3,2,1,0:T(8,128)(2,1)S(1)} %slice.173), channel_id=1, source_target_pairs={{0,1},{1,0},{2,3},{3,2},{4,5},{5,4},{6,7},{7,6},{8,9},{9,8},{10,11... | collective-permute-start | bytes 786440 | tf_op jit(solution)/shard_map/ppermute | solution.py:357
  93.9 15.4 %collective-permute-start.20 = (bf16[64,1024]{1,0:T(8,128)(2,1)S(1)}, bf16[64,1024]{1,0:T(8,128)(2,1)S(1)}, u32[]{:S(2)}, u32[]{:S(2)}) collective-permute-start(bf16[64,1024]{1,0:T(8,128)(2,1)S(1)} %fusion.17), channel_id=1, source_target_pairs={{0,8},{8,0},{16,24},{24,16},{1,9},{9,1},{17,25},{25,17},{2,10},{10... | collective-permute-start | bytes 393224 | tf_op jit(solution)/shard_map/ppermute | solution.py:357
  99.3 5.2 %collective-permute-start.30 = (bf16[1,64,1024]{2,1,0:T(8,128)(2,1)S(1)}, bf16[1,64,1024]{2,1,0:T(8,128)(2,1)S(1)}, u32[]{:S(2)}, u32[]{:S(2)}) collective-permute-start(bf16[1,64,1024]{2,1,0:T(8,128)(2,1)S(1)} %slice.174), channel_id=1, source_target_pairs={{0,1},{1,0},{2,3},{3,2},{4,5},{5,4},{6,7},{7,6},{8,9},{9,8},{10,11... | collective-permute-start | bytes 393224 | tf_op jit(solution)/shard_map/ppermute | solution.py:357
  101.0 8.2 %collective-permute-start.36 = (bf16[64,1024]{1,0:T(8,128)(2,1)S(1)}, bf16[64,1024]{1,0:T(8,128)(2,1)S(1)}, u32[]{:S(2)}, u32[]{:S(2)}) collective-permute-start(bf16[64,1024]{1,0:T(8,128)(2,1)S(1)} %fusion.19), channel_id=1, source_target_pairs={{0,4},{2,6},{4,0},{6,2},{1,5},{3,7},{5,1},{7,3},{8,12},{10,14},{12... | collective-permute-start | bytes 393224 | tf_op jit(solution)/shard_map/ppermute | solution.py:357
  104.5 8.7 %collective-permute-start.31 = (bf16[64,1024]{1,0:T(8,128)(2,1)S(1)}, bf16[64,1024]{1,0:T(8,128)(2,1)S(1)}, u32[]{:S(2)}, u32[]{:S(2)}) collective-permute-start(bf16[64,1024]{1,0:T(8,128)(2,1)S(1)} %fusion.18), channel_id=1, source_target_pairs={{0,24},{8,16},{16,8},{24,0},{1,25},{9,17},{17,9},{25,1},{2,26},{10... | collective-permute-start | bytes 393224 | tf_op jit(solution)/shard_map/ppermute | solution.py:357
  109.3 9.5 %collective-permute-start.37 = (bf16[64,1024]{1,0:T(8,128)(2,1)S(1)}, bf16[64,1024]{1,0:T(8,128)(2,1)S(1)}, u32[]{:S(2)}, u32[]{:S(2)}) collective-permute-start(bf16[64,1024]{1,0:T(8,128)(2,1)S(1)} %fusion.7), channel_id=1, source_target_pairs={{0,16},{8,24},{16,0},{24,8},{1,17},{9,25},{17,1},{25,9},{2,18},{10... | collective-permute-start | bytes 393224 | tf_op jit(solution)/shard_map/ppermute | solution.py:357
  118.8 5.0 %collective-permute-start.38 = (bf16[1,64,1024]{2,1,0:T(8,128)(2,1)S(1)}, bf16[1,64,1024]{2,1,0:T(8,128)(2,1)S(1)}, u32[]{:S(2)}, u32[]{:S(2)}) collective-permute-start(bf16[1,64,1024]{2,1,0:T(8,128)(2,1)S(1)} %bitcast.89), channel_id=1, source_target_pairs={{0,1},{1,0},{2,3},{3,2},{4,5},{5,4},{6,7},{7,6},{8,9},{9,8},{10,11... | collective-permute-start | bytes 393224 | tf_op jit(solution)/shard_map/ppermute | solution.py:357

commit v7 on v6

--- a/solution.py
+++ b/solution.py
@@ -422,23 +422,24 @@
     routed_weights = (jnp.swapaxes(expert_gate_up[0], 1, 2), expert_down[0])
     shared_weights = (jnp.swapaxes(shared_gate_up, 1, 2), shared_down)
     distances = [0, 1, *range(n_req - 1, 1, -1)]
-    blocks = [block, swap(block, "req", n_req, 1)]
-    fars = [swap(each, "row", n_row, 2) for each in blocks]
+    fars = [swap(block, "row", n_row, 2)]
+    blocks = [block, swap(after(block, fars[0]), "req", n_req, 1)]
+    fars.append(swap(blocks[1], "row", n_row, 2))
     rest = [swap(own_part, "req", n_req, s) for s in distances[2:]]
     if rest:
-        rest = after(jnp.concatenate(rest, axis=0)[None], fars[0], blocks[1])
+        rest = after(jnp.concatenate(rest, axis=0)[None], fars[0])
         rest_far = swap(rest, "row", n_row, 2)
         rest, rest_far = col_gather(rest, n_col), col_gather(rest_far, n_col)
         blocks += [rest[:, k] for k in range(rest.shape[1])]
         fars += [rest_far[:, k] for k in range(rest.shape[1])]
-    sends, folds, parts = [], [], []
+    sends, folds, sums, returns = [], [], [], []
     for k, s in enumerate(distances):
         near = swap(blocks[k], "row", n_row, 1)
         far = fars[k]
-        if k > 1:
+        if k > 2:
+            far = after(far, *sends, *folds, *returns[: k - 2])
+        elif k:
             far = after(far, *sends, *folds[: k - 1])
-        elif k == 1:
-            far = after(far, *sends)
         far_near = swap(far, "row", n_row, 1)
         keep, send = expert_part(
             indices,
@@ -452,16 +453,21 @@
         )
         sends.append(send)
         near_sum = keep + swap(send, "row", n_row, 1).astype(jnp.float32)
+        fold = near_sum[1] if k < 3 else near_sum[n_col // 2 :]
+        folds.append(fold.astype(bf16))
+        sums.append(near_sum)
         if k < 3:
-            fold = near_sum[1].astype(bf16)
-            part = near_sum[0] + swap(fold, "row", n_row, 2).astype(jnp.float32)
-            part = col_scatter(part, n_col)[0]
+            returns.append(swap(folds[k], "row", n_row, 2))
+    parts = []
+    last = col_scatter(sums[-1], n_col)[0] if n_req > 3 else None
+    for k, near_sum in enumerate(sums):
+        if k < 3:
+            from_far = after(returns[k], *((), [last], folds[-1:])[k]) if n_req > 3 else returns[k]
+            part = col_scatter(near_sum[0] + from_far.astype(jnp.float32), n_col)[0]
         else:
-            fold = near_sum[n_col // 2 :].astype(bf16)
-            part = col_scatter(near_sum, n_col)[0]
+            part = last if k == n_req - 1 else col_scatter(near_sum, n_col)[0]
             part = part[0] + swap(part[1].astype(bf16), "row", n_row, 2).astype(jnp.float32)
-        folds.append(fold)
-        parts.append(part.astype(bf16) if s else part)
+        parts.append(part.astype(bf16) if k else part)
     total = parts[0]
     for s, part in zip(distances[1:], parts[1:]):
         total = total + swap(part, "req", n_req, s).astype(jnp.float32)

time: 125 us -> 134 us (1.072)
  waiting for transfers between devices: 54.8 us -> 66.8 us
  starting transfers between devices: 35 us -> 31.3 us
    ppermute x39, waiting for transfers between devices: 54.8 us -> 66.8 us  [swap(): return lax.ppermute(values, axis, [(i, i ^ bits) for i in range(size)])]
    ppermute x39, starting transfers between devices: 35 us -> 31.3 us  [swap(): return lax.ppermute(values, axis, [(i, i ^ bits) for i in range(size)])]
  transfers between devices with their start and end apart: 39 -> 39, of which waited for: 18 -> 23; matrix products, arithmetic and copies ran while one was open for 1% -> 1% of each run, Pallas kernels for 19% -> 15%
where the time goes in v7:
time: 134 us; the launch traced here: 133 us
  waiting for transfers between devices  66.8 us (50%)
  starting transfers between devices  31.3 us (23%)
  Pallas kernels  29.1 us (22%)
  local copies, waits for them, and re-layouts  2.67 us (2%)
  between operations  1.77 us (1%)
  other arithmetic  1.62 us (1%)
    ppermute x39, waiting for transfers between devices, swap(): return lax.ppermute(values, axis, [(i, i ^ bits) for i in range(size)])  66.8 us
    ppermute x39, starting transfers between devices, swap(): return lax.ppermute(values, axis, [(i, i ^ bits) for i in range(size)])  31.3 us
    pallas_call x4, Pallas kernels, expert_part(): pl.pallas_call(functools.partial(expert_kernel, bool(shared_weights), far...  16.7 us
    pallas_call x2, Pallas kernels, attention_part(): pl.pallas_call(functools.partial(attention_kernel, first, place), out_sha...  8.2 us
  transfers between devices with their start and end apart: 39, of which 23 were waited for; matrix products, arithmetic and copies ran while one was open for 1% of the time, Pallas kernels for 15%

profile of v7, /device:TPU:0, one launch (start us, length us, event | category | flops | bytes accessed | tf_op | source)
XLA Modules:
  0.0 133.3 jit_solution(5357967879175516122)
XLA Ops:
  0.6 0.5 collective-permute-start
  1.1 2.6 %collective-permute-start.2 = (bf16[64,2048]{1,0:T(8,128)(2,1)}, bf16[64,2048]{1,0:T(8,128)(2,1)S(1)}, u32[]{:S(2)}, u32[]{:S(2)}) collective-permute-start(bf16[64,2048]{1,0:T(8,128)(2,1)} %hidden_ref.1), channel_id=1, source_target_pairs={{0,4},{2,6},{4,0},{6,2},{1,5},{3,7},{5,1},{7,3},{8,12},{10,14},{12... | collective-permute-start | bytes 786440 | tf_op jit(solution)/shard_map/ppermute | solution.py:357
  4.5 0.7 copy-done.14
  5.2 0.7 copy-done.15
  5.9 2.1 %trees.1 = (f32[4,64,64]{2,1,0:T(8,128)S(1)}, f32[4,64,65]{2,1,0:T(8,128)S(1)}, bf16[64,64]{1,0:T(8,128)(2,1)S(1)}, f32[1,16]{1,0:T(1,128)S(1)}) custom-call(s32[3]{0:T(128)S(1)} %pad_add_fusion.row_ref.refs_0_, s32[4]{0:T(128)S(1)} %copy-done.15, s32[1]{0:T(128)S(6)} %copy.24.accepted_ref, s32[4,64]{1,0:T(4,128)S(1)} %copy-done.14), custom_call_target="tpu_custom_call" | custom-call | flops 20000000000 | bytes 1 | tf_op jit(solution)/shard_map/trees/pallas_call | solution.py:110
  8.1 0.4 copy-done.3
  8.5 0.3 copy-done.4
  8.9 4.4 %attention.2 = (f32[64,2048]{1,0:T(8,128)S(1)}, bf16[64,2048]{1,0:T(8,128)(2,1)S(1)}, bf16[1,64,576]{2,1,0:T(8,128)(2,1)}) custom-call(s32[3]{0:T(128)S(1)} %pad_add_fusion.row_ref.refs_0_, bf16[64,2048]{1,0:T(8,128)(2,1)S(1)} %copy-done.10, bf16[64,2048]{1,0:T(8,128)(2,1)S(1)} %collective-permute-done.refs_1_, bf16[4,576,384]{2,1,0:T(8,128)(2,1)S(1)} %bitcast.82, ...), custom_call_target="tpu_custom_call" | custom-call | flops 1 | bytes 1 | tf_op jit(solution)/shard_map/attention/pallas_call | solution.py:211
  13.5 1.4 %collective-permute-done.3.refs_1_ = bf16[64,2048]{1,0:T(8,128)(2,1)S(1)} collective-permute-done((bf16[64,2048]{1,0:T(8,128)(2,1)S(1)}, bf16[64,2048]{1,0:T(8,128)(2,1)S(1)}, u32[]{:S(2)}, u32[]{:S(2)}) %collective-permute-start.3) | collective-permute-done | bytes 262176 | tf_op jit(solution)/shard_map/ppermute | solution.py:357
  14.8 3.8 %attention.3 = (f32[64,2048]{1,0:T(8,128)S(1)}, bf16[64,2048]{1,0:T(8,128)(2,1)S(1)}) custom-call(s32[3]{0:T(128)S(1)} %pad_add_fusion.row_ref.refs_0_, bf16[64,2048]{1,0:T(8,128)(2,1)S(1)} %collective-permute-done.2.refs_0_, bf16[64,2048]{1,0:T(8,128)(2,1)S(1)} %collective-permute-done.3.refs_1_, bf16[4,576,384]{2,1,0:T(8,128)(2,1)S(1)} %bitcast.83, ...), custom_call_target="tpu_custom_call" | custom-call | flops 1 | bytes 1 | tf_op jit(solution)/shard_map/attention/pallas_call | solution.py:211
  18.7 0.2 collective-permute-start.4
  18.9 0.3 collective-permute-start.1
  19.3 1.0 collective-permute-done.4
  20.7 8.1 %collective-permute-done.5 = bf16[64,2048]{1,0:T(8,128)(2,1)S(1)} collective-permute-done((bf16[64,2048]{1,0:T(8,128)(2,1)S(1)}, bf16[64,2048]{1,0:T(8,128)(2,1)S(1)}, u32[]{:S(2)}, u32[]{:S(2)}) %collective-permute-start.5) | collective-permute-done | bytes 262176 | tf_op jit(solution)/shard_map/ppermute | solution.py:357
  28.9 1.6 %collective-permute-start.6 = (bf16[64,2048]{1,0:T(8,128)(2,1)S(1)}, bf16[64,2048]{1,0:T(8,128)(2,1)S(1)}, u32[]{:S(2)}, u32[]{:S(2)}) collective-permute-start(bf16[64,2048]{1,0:T(8,128)(2,1)S(1)} %add_convert_fusion.keep_ref), channel_id=1, source_target_pairs={{0,1},{1,0},{2,3},{3,2},{4,5},{5,4},{6,7},{7,6},{8,9},{9,8},{10,11... | collective-permute-start | bytes 786440 | tf_op jit(solution)/shard_map/ppermute | solution.py:357
  30.6 5.9 %collective-permute-done.6 = bf16[64,2048]{1,0:T(8,128)(2,1)S(1)} collective-permute-done((bf16[64,2048]{1,0:T(8,128)(2,1)S(1)}, bf16[64,2048]{1,0:T(8,128)(2,1)S(1)}, u32[]{:S(2)}, u32[]{:S(2)}) %collective-permute-start.6) | collective-permute-done | bytes 262176 | tf_op jit(solution)/shard_map/ppermute | solution.py:357
  36.5 0.8 join.1
  37.3 0.6 collective-permute-start.7
  37.9 3.6 %collective-permute-start.21 = (bf16[1,64,1152]{2,1,0:T(8,128)(2,1)S(1)}, bf16[1,64,1152]{2,1,0:T(8,128)(2,1)S(1)}, u32[]{:S(2)}, u32[]{:S(2)}) collective-permute-start(bf16[1,64,1152]{2,1,0:T(8,128)(2,1)S(1)} %get-tuple-element.46), channel_id=1, source_target_pairs={{0,24},{8,16},{16,8},{24,0},{1,25},{9,17},{17,9},{25,1},{2,26},{10... | collective-permute-start | bytes 442376 | tf_op jit(solution)/shard_map/ppermute | solution.py:357
  41.5 3.2 %collective-permute-done.7.refs_2_ = bf16[2,64,1152]{2,1,0:T(8,128)(2,1)S(1)} collective-permute-done((bf16[2,64,1152]{2,1,0:T(8,128)(2,1)S(1)}, bf16[2,64,1152]{2,1,0:T(8,128)(2,1)S(1)}, u32[]{:S(2)}, u32[]{:S(2)}) %collective-permute-start.7) | collective-permute-done | bytes 294944 | tf_op jit(solution)/shard_map/ppermute | solution.py:357
  44.7 0.8 collective-permute-done.21
  45.6 6.7 %collective-permute-done.22 = bf16[1,64,1152]{2,1,0:T(8,128)(2,1)S(1)} collective-permute-done((bf16[1,64,1152]{2,1,0:T(8,128)(2,1)S(1)}, bf16[1,64,1152]{2,1,0:T(8,128)(2,1)S(1)}, u32[]{:S(2)}, u32[]{:S(2)}) %collective-permute-start.22) | collective-permute-done | bytes 147488 | tf_op jit(solution)/shard_map/ppermute | solution.py:357
  52.4 1.6 %collective-permute-start.24 = (bf16[1,2,64,1152]{3,2,0,1:T(8,128)(2,1)S(1)}, bf16[1,2,64,1152]{3,2,0,1:T(8,128)(2,1)S(1)}, u32[]{:S(2)}, u32[]{:S(2)}) collective-permute-start(bf16[1,2,64,1152]{3,2,0,1:T(8,128)(2,1)S(1)} %maximum_bitcast_fusion), channel_id=1, source_target_pairs={{0,4},{2,6},{4,0},{6,2},{1,5},{3,7},{5,1},{7,3},{8,12},{10,14},{12... | collective-permute-start | bytes 884744 | tf_op jit(solution)/shard_map/ppermute | solution.py:357
  54.0 1.5 %collective-permute-start.23 = (bf16[1,2,64,1152]{3,2,0,1:T(8,128)(2,1)S(1)}, bf16[1,2,64,1152]{3,2,0,1:T(8,128)(2,1)S(1)}, u32[]{:S(2)}, u32[]{:S(2)}) collective-permute-start(bf16[1,2,64,1152]{3,2,0,1:T(8,128)(2,1)S(1)} %maximum_bitcast_fusion), channel_id=1, source_target_pairs={{0,1},{1,0},{2,3},{3,2},{4,5},{5,4},{6,7},{7,6},{8,9},{9,8},{10,11... | collective-permute-start | bytes 884744 | tf_op jit(solution)/shard_map/ppermute | solution.py:357
  55.6 5.2 %experts.4 = (f32[2,2,64,1024]{3,2,1,0:T(8,128)S(1)}, bf16[2,2,64,1024]{3,2,1,0:T(8,128)(2,1)S(1)}) custom-call(s32[3]{0:T(128)S(1)} %pad_add_fusion.row_ref.refs_0_, bf16[2,64,1152]{2,1,0:T(8,128)(2,1)S(1)} %get-tuple-element.42.refs_1_, bf16[2,64,1152]{2,1,0:T(8,128)(2,1)S(1)} %collective-permute-done.7.refs_2_, ...), custom_call_target="tpu_custom_call" | custom-call | flops 1 | bytes 1 | tf_op jit(solution)/shard_map/experts/pallas_call | solution.py:337
  60.9 1.1 collective-permute-start.14
  62.0 1.5 %collective-permute-start.25 = (bf16[1,2,64,1152]{3,2,0,1:T(8,128)(2,1)S(1)}, bf16[1,2,64,1152]{3,2,0,1:T(8,128)(2,1)S(1)}, u32[]{:S(2)}, u32[]{:S(2)}) collective-permute-start(bf16[1,2,64,1152]{3,2,0,1:T(8,128)(2,1)S(1)} %collective-permute-done.24), channel_id=1, source_target_pairs={{0,1},{1,0},{2,3},{3,2},{4,5},{5,4},{6,7},{7,6},{8,9},{9,8},{10,11... | collective-permute-start | bytes 884744 | tf_op jit(solution)/shard_map/ppermute | solution.py:357
  63.6 0.5 collective-permute-start.15
  64.1 6.2 %collective-permute-done.14.refs_2_ = bf16[2,64,1152]{2,1,0:T(8,128)(2,1)S(1)} collective-permute-done((bf16[2,64,1152]{2,1,0:T(8,128)(2,1)S(1)}, bf16[2,64,1152]{2,1,0:T(8,128)(2,1)S(1)}, u32[]{:S(2)}, u32[]{:S(2)}) %collective-permute-start.14) | collective-permute-done | bytes 294944 | tf_op jit(solution)/shard_map/ppermute | solution.py:357
  70.3 0.2 collective-permute-done.25
  70.6 0.3 convert_add_fusion.3
  71.0 0.9 collective-permute-done.16.refs_4_
  71.9 3.8 %experts.5 = (f32[2,2,64,1024]{3,2,1,0:T(8,128)S(1)}, bf16[2,2,64,1024]{3,2,1,0:T(8,128)(2,1)S(1)}) custom-call(s32[3]{0:T(128)S(1)} %pad_add_fusion.row_ref.refs_0_, bf16[2,64,1152]{2,1,0:T(8,128)(2,1)S(1)} %collective-permute-done.13.refs_1_, bf16[2,64,1152]{2,1,0:T(8,128)(2,1)S(1)} %collective-permute-done.14.refs_2_, ...), custom_call_target="tpu_custom_call" | custom-call | flops 1 | bytes 1 | tf_op jit(solution)/shard_map/experts/pallas_call | solution.py:337
  75.7 0.2 collective-permute-start.17
  76.0 0.4 collective-permute-start.27
  76.5 0.6 collective-permute-start.11
  77.1 1.0 collective-permute-done.27.refs_4_
  78.1 3.8 %experts.6 = (f32[2,2,64,1024]{3,2,1,0:T(8,128)S(1)}, bf16[2,2,64,1024]{3,2,1,0:T(8,128)(2,1)S(1)}) custom-call(s32[3]{0:T(128)S(1)} %pad_add_fusion.row_ref.refs_0_, bf16[2,64,1152]{2,1,0:T(8,128)(2,1)S(1)} %get-tuple-element.58.refs_1_, bf16[2,64,1152]{2,1,0:T(8,128)(2,1)S(1)} %get-tuple-element.48.refs_2_, ...), custom_call_target="tpu_custom_call" | custom-call | flops 1 | bytes 1 | tf_op jit(solution)/shard_map/experts/pallas_call | solution.py:337
  82.0 0.2 collective-permute-start.28
  82.4 1.6 %collective-permute-done.28 = bf16[2,2,64,1024]{3,2,1,0:T(8,128)(2,1)S(1)} collective-permute-done((bf16[2,2,64,1024]{3,2,1,0:T(8,128)(2,1)S(1)}, bf16[2,2,64,1024]{3,2,1,0:T(8,128)(2,1)S(1)}, u32[]{:S(2)}, u32[]{:S(2)}) %collective-permute-start.28) | collective-permute-done | bytes 524320 | tf_op jit(solution)/shard_map/ppermute | solution.py:357
  84.2 0.9 collective-permute-done.11
  85.1 1.6 %collective-permute-done.31.refs_4_ = bf16[2,64,1152]{2,1,0:T(8,128)(2,1)S(1)} collective-permute-done((bf16[2,64,1152]{2,1,0:T(8,128)(2,1)S(1)}, bf16[2,64,1152]{2,1,0:T(8,128)(2,1)S(1)}, u32[]{:S(2)}, u32[]{:S(2)}) %collective-permute-start.31) | collective-permute-done | bytes 294944 | tf_op jit(solution)/shard_map/ppermute | solution.py:357
  86.7 3.8 %experts.7 = (f32[2,2,64,1024]{3,2,1,0:T(8,128)S(1)}, bf16[2,2,64,1024]{3,2,1,0:T(8,128)(2,1)S(1)}) custom-call(s32[3]{0:T(128)S(1)} %pad_add_fusion.row_ref.refs_0_, bf16[2,64,1152]{2,1,0:T(8,128)(2,1)S(1)} %get-tuple-element.59.refs_1_, bf16[2,64,1152]{2,1,0:T(8,128)(2,1)S(1)} %get-tuple-element.51.refs_2_, ...), custom_call_target="tpu_custom_call" | custom-call | flops 1 | bytes 1 | tf_op jit(solution)/shard_map/experts/pallas_call | solution.py:337
  90.5 0.2 collective-permute-start.32
  90.7 0.7 collective-permute-start.18
  91.5 0.6 collective-permute-start.12
  92.1 7.2 %collective-permute-done.18 = bf16[2,64,1024]{2,1,0:T(8,128)(2,1)S(1)} collective-permute-done((bf16[2,64,1024]{2,1,0:T(8,128)(2,1)S(1)}, bf16[2,64,1024]{2,1,0:T(8,128)(2,1)S(1)}, u32[]{:S(2)}, u32[]{:S(2)}) %collective-permute-start.18) | collective-permute-done | bytes 262176 | tf_op jit(solution)/shard_map/ppermute | solution.py:357
  99.4 0.6 collective-permute-start.19
  100.0 0.6 collective-permute-start.29
  100.8 1.6 %collective-permute-start.35 = (bf16[1,2,64,1024]{3,2,1,0:T(8,128)(2,1)S(1)}, bf16[1,2,64,1024]{3,2,1,0:T(8,128)(2,1)S(1)}, u32[]{:S(2)}, u32[]{:S(2)}) collective-permute-start(bf16[1,2,64,1024]{3,2,1,0:T(8,128)(2,1)S(1)} %slice.174), channel_id=1, source_target_pairs={{0,1},{1,0},{2,3},{3,2},{4,5},{5,4},{6,7},{7,6},{8,9},{9,8},{10,11... | collective-permute-start | bytes 786440 | tf_op jit(solution)/shard_map/ppermute | solution.py:357
  102.4 3.5 %collective-permute-done.19 = bf16[1,64,1024]{2,1,0:T(8,128)(2,1)S(1)} collective-permute-done((bf16[1,64,1024]{2,1,0:T(8,128)(2,1)S(1)}, bf16[1,64,1024]{2,1,0:T(8,128)(2,1)S(1)}, u32[]{:S(2)}, u32[]{:S(2)}) %collective-permute-start.19) | collective-permute-done | bytes 131104 | tf_op jit(solution)/shard_map/ppermute | solution.py:357
  105.9 2.0 %collective-permute-start.20 = (bf16[64,1024]{1,0:T(8,128)(2,1)S(1)}, bf16[64,1024]{1,0:T(8,128)(2,1)S(1)}, u32[]{:S(2)}, u32[]{:S(2)}) collective-permute-start(bf16[64,1024]{1,0:T(8,128)(2,1)S(1)} %fusion.17), channel_id=1, source_target_pairs={{0,8},{8,0},{16,24},{24,16},{1,9},{9,1},{17,25},{25,17},{2,10},{10... | collective-permute-start | bytes 393224 | tf_op jit(solution)/shard_map/ppermute | solution.py:357
  108.0 1.1 collective-permute-start.33
  109.2 2.3 %collective-permute-done.35 = bf16[1,2,64,1024]{3,2,1,0:T(8,128)(2,1)S(1)} collective-permute-done((bf16[1,2,64,1024]{3,2,1,0:T(8,128)(2,1)S(1)}, bf16[1,2,64,1024]{3,2,1,0:T(8,128)(2,1)S(1)}, u32[]{:S(2)}, u32[]{:S(2)}) %collective-permute-start.35) | collective-permute-done | bytes 262176 | tf_op jit(solution)/shard_map/ppermute | solution.py:357
  111.6 0.5 collective-permute-start.36
  112.1 1.0 collective-permute-done.33
  113.1 2.5 %collective-permute-start.34 = (bf16[64,1024]{1,0:T(8,128)(2,1)S(1)}, bf16[64,1024]{1,0:T(8,128)(2,1)S(1)}, u32[]{:S(2)}, u32[]{:S(2)}) collective-permute-start(bf16[64,1024]{1,0:T(8,128)(2,1)S(1)} %fusion.18), channel_id=1, source_target_pairs={{0,24},{8,16},{16,8},{24,0},{1,25},{9,17},{17,9},{25,1},{2,26},{10... | collective-permute-start | bytes 393224 | tf_op jit(solution)/shard_map/ppermute | solution.py:357
  115.7 0.9 collective-permute-done.36
  116.6 3.0 %collective-permute-start.37 = (bf16[64,1024]{1,0:T(8,128)(2,1)S(1)}, bf16[64,1024]{1,0:T(8,128)(2,1)S(1)}, u32[]{:S(2)}, u32[]{:S(2)}) collective-permute-start(bf16[64,1024]{1,0:T(8,128)(2,1)S(1)} %fusion.7), channel_id=1, source_target_pairs={{0,16},{8,24},{16,0},{24,8},{1,17},{9,25},{17,1},{25,9},{2,18},{10... | collective-permute-start | bytes 393224 | tf_op jit(solution)/shard_map/ppermute | solution.py:357
  119.6 1.3 collective-permute-done.34
  120.9 6.0 %collective-permute-done.37 = bf16[64,1024]{1,0:T(8,128)(2,1)S(1)} collective-permute-done((bf16[64,1024]{1,0:T(8,128)(2,1)S(1)}, bf16[64,1024]{1,0:T(8,128)(2,1)S(1)}, u32[]{:S(2)}, u32[]{:S(2)}) %collective-permute-start.37) | collective-permute-done | bytes 131104 | tf_op jit(solution)/shard_map/ppermute | solution.py:357
  127.0 0.3 collective-permute-start.38
  127.3 4.7 %collective-permute-done.38.others_ref = bf16[1,64,1024]{2,1,0:T(8,128)(2,1)S(1)} collective-permute-done((bf16[1,64,1024]{2,1,0:T(8,128)(2,1)S(1)}, bf16[1,64,1024]{2,1,0:T(8,128)(2,1)S(1)}, u32[]{:S(2)}, u32[]{:S(2)}) %collective-permute-start.38) | collective-permute-done | bytes 131104 | tf_op jit(solution)/shard_map/ppermute | solution.py:357
  132.1 1.3 finish.1
  (94 shorter events, 2.8 us)
Async XLA Ops:
  0.6 7.4 %collective-permute-start = (bf16[64,2048]{1,0:T(8,128)(2,1)}, bf16[64,2048]{1,0:T(8,128)(2,1)S(1)}, u32[]{:S(2)}, u32[]{:S(2)}) collective-permute-start(bf16[64,2048]{1,0:T(8,128)(2,1)} %hidden_ref.1), channel_id=1, source_target_pairs={{0,2},{2,0},{4,6},{6,4},{1,3},{3,1},{5,7},{7,5},{8,10},{10,8},{12,... | collective-permute-start | bytes 786440 | tf_op jit(solution)/shard_map/ppermute | solution.py:357
  1.1 12.2 %collective-permute-start.2 = (bf16[64,2048]{1,0:T(8,128)(2,1)}, bf16[64,2048]{1,0:T(8,128)(2,1)S(1)}, u32[]{:S(2)}, u32[]{:S(2)}) collective-permute-start(bf16[64,2048]{1,0:T(8,128)(2,1)} %hidden_ref.1), channel_id=1, source_target_pairs={{0,4},{2,6},{4,0},{6,2},{1,5},{3,7},{5,1},{7,3},{8,12},{10,14},{12... | collective-permute-start | bytes 786440 | tf_op jit(solution)/shard_map/ppermute | solution.py:357
  4.5 0.7 copy-start.14
  5.2 0.7 copy-start.15
  5.8 2.2 %copy-start.1 = (bf16[2048,576]{0,1:T(8,128)(2,1)S(1)}, bf16[2048,576]{0,1:T(8,128)(2,1)}, u32[]{:S(2)}) copy-start(bf16[2048,576]{0,1:T(8,128)(2,1)} %param.27) | copy-start | bytes 7077892
  5.8 2.2 %copy-start.2 = (bf16[4,384,576]{1,2,0:T(8,128)(2,1)S(1)}, bf16[4,384,576]{1,2,0:T(8,128)(2,1)}, u32[]{:S(2)}) copy-start(bf16[4,384,576]{1,2,0:T(8,128)(2,1)} %param.20) | copy-start | bytes 5308420
  5.8 2.6 %copy-start.3 = (bf16[2048,384]{1,0:T(8,128)(2,1)S(1)}, bf16[2048,384]{1,0:T(8,128)(2,1)}, u32[]{:S(2)}) copy-start(bf16[2048,384]{1,0:T(8,128)(2,1)} %refs_7_.3) | copy-start | bytes 4718596
  5.8 2.9 %copy-start.4 = (bf16[256,2048]{1,0:T(8,128)(2,1)S(1)}, bf16[256,2048]{1,0:T(8,128)(2,1)}, u32[]{:S(2)}) copy-start(bf16[256,2048]{1,0:T(8,128)(2,1)} %refs_12_.3) | copy-start | bytes 3145732
  5.8 2.9 %copy-start.8 = (bf16[2,128,512]{2,1,0:T(8,128)(2,1)S(1)}, bf16[2,128,512]{2,1,0:T(8,128)(2,1)}, u32[]{:S(2)}) copy-start(bf16[2,128,512]{2,1,0:T(8,128)(2,1)} %refs_10_.4) | copy-start | bytes 786436
  5.8 3.0 %copy-start.9 = (bf16[2,512,128]{2,1,0:T(8,128)(2,1)S(1)}, bf16[2,512,128]{2,1,0:T(8,128)(2,1)}, u32[]{:S(2)}) copy-start(bf16[2,512,128]{2,1,0:T(8,128)(2,1)} %refs_11_.3) | copy-start | bytes 786436
  5.8 3.1 %copy-start.10 = (bf16[64,2048]{1,0:T(8,128)(2,1)S(1)}, bf16[64,2048]{1,0:T(8,128)(2,1)}, u32[]{:S(2)}) copy-start(bf16[64,2048]{1,0:T(8,128)(2,1)} %hidden_ref.1) | copy-start | bytes 786436
  5.9 3.1 %copy-start.11 = (f32[2048]{0:T(1024)S(1)}, f32[2048]{0:T(1024)}, u32[]{:S(2)}) copy-start(f32[2048]{0:T(1024)} %param.25) | copy-start | bytes 24580
  5.9 3.1 %copy-start.12 = (f32[512]{0:T(512)S(1)}, f32[512]{0:T(512)}, u32[]{:S(2)}) copy-start(f32[512]{0:T(512)} %param.28) | copy-start | bytes 6148
  13.3 1.5 %collective-permute-start.3 = (bf16[64,2048]{1,0:T(8,128)(2,1)S(1)}, bf16[64,2048]{1,0:T(8,128)(2,1)S(1)}, u32[]{:S(2)}, u32[]{:S(2)}) collective-permute-start(bf16[64,2048]{1,0:T(8,128)(2,1)S(1)} %collective-permute-done.2.refs_0_), channel_id=1, source_target_pairs={{0,2},{2,0},{4,6},{6,4},{1,3},{3,1},{5,7},{7,5},{8,10},{10,8},{12,... | collective-permute-start | bytes 786440 | tf_op jit(solution)/shard_map/ppermute | solution.py:357
  18.7 11.8 %copy-start.16 = (s32[64,6]{0,1:T(8,128)S(1)}, s32[64,6]{0,1:T(8,128)}, u32[]{:S(2)}) copy-start(s32[64,6]{0,1:T(8,128)} %param.23) | copy-start | bytes 4612
  18.7 17.8 %copy-start.13 = (f32[2048]{0:T(1024)S(1)}, f32[2048]{0:T(1024)}, u32[]{:S(2)}) copy-start(f32[2048]{0:T(1024)} %param.32) | copy-start | bytes 24580
  18.7 1.6 %collective-permute-start.4 = (bf16[64,2048]{1,0:T(8,128)(2,1)S(1)}, bf16[64,2048]{1,0:T(8,128)(2,1)S(1)}, u32[]{:S(2)}, u32[]{:S(2)}) collective-permute-start(bf16[64,2048]{1,0:T(8,128)(2,1)S(1)} %get-tuple-element.36), channel_id=1, source_target_pairs={{0,2},{2,0},{4,6},{6,4},{1,3},{3,1},{5,7},{7,5},{8,10},{10,8},{12,... | collective-permute-start | bytes 786440 | tf_op jit(solution)/shard_map/ppermute | solution.py:357
  18.9 1.7 %collective-permute-start.1 = (bf16[64,2048]{1,0:T(8,128)(2,1)S(1)}, bf16[64,2048]{1,0:T(8,128)(2,1)S(1)}, u32[]{:S(2)}, u32[]{:S(2)}) collective-permute-start(bf16[64,2048]{1,0:T(8,128)(2,1)S(1)} %get-tuple-element.33), channel_id=1, source_target_pairs={{0,2},{2,0},{4,6},{6,4},{1,3},{3,1},{5,7},{7,5},{8,10},{10,8},{12,... | collective-permute-start | bytes 786440 | tf_op jit(solution)/shard_map/ppermute | solution.py:357
  20.4 8.4 %collective-permute-start.5 = (bf16[64,2048]{1,0:T(8,128)(2,1)S(1)}, bf16[64,2048]{1,0:T(8,128)(2,1)S(1)}, u32[]{:S(2)}, u32[]{:S(2)}) collective-permute-start(bf16[64,2048]{1,0:T(8,128)(2,1)S(1)} %add_convert_fusion.1), channel_id=1, source_target_pairs={{0,4},{2,6},{4,0},{6,2},{1,5},{3,7},{5,1},{7,3},{8,12},{10,14},{12... | collective-permute-start | bytes 786440 | tf_op jit(solution)/shard_map/ppermute | solution.py:357
  28.9 7.6 %collective-permute-start.6 = (bf16[64,2048]{1,0:T(8,128)(2,1)S(1)}, bf16[64,2048]{1,0:T(8,128)(2,1)S(1)}, u32[]{:S(2)}, u32[]{:S(2)}) collective-permute-start(bf16[64,2048]{1,0:T(8,128)(2,1)S(1)} %add_convert_fusion.keep_ref), channel_id=1, source_target_pairs={{0,1},{1,0},{2,3},{3,2},{4,5},{5,4},{6,7},{7,6},{8,9},{9,8},{10,11... | collective-permute-start | bytes 786440 | tf_op jit(solution)/shard_map/ppermute | solution.py:357
  36.5 19.0 %slice-start = ((s8[5767168]{0:T(1024)(128)(4,1)}), s8[4194304]{0:T(1024)(128)(4,1)S(1)}, s32[]{:S(2)}) async-start(s8[5767168]{0:T(1024)(128)(4,1)} %bitcast.70), calls=%async_computation | async-start | bytes 8388608
  36.5 19.0 %slice-start.1 = ((s8[5767168]{0:T(1024)(128)(4,1)}), s8[1572864]{0:T(1024)(128)(4,1)S(1)}, s32[]{:S(2)}) async-start(s8[5767168]{0:T(1024)(128)(4,1)} %bitcast.70), calls=%async_computation.1 | async-start | bytes 3145728
  36.5 19.0 %copy-start = (bf16[1,704,2048]{2,1,0:T(8,128)(2,1)S(1)}, bf16[1,704,2048]{2,1,0:T(8,128)(2,1)}, u32[]{:S(2)}) copy-start(bf16[1,704,2048]{2,1,0:T(8,128)(2,1)} %param.37) | copy-start | bytes 8650756
  36.5 19.0 %copy-start.5 = (bf16[2,2048,352]{1,2,0:T(8,128)(2,1)S(1)}, bf16[2,2048,352]{1,2,0:T(8,128)(2,1)}, u32[]{:S(2)}) copy-start(bf16[2,2048,352]{1,2,0:T(8,128)(2,1)} %param.34) | copy-start | bytes 8650756
  36.5 19.0 %copy-start.6 = (bf16[352,2048]{1,0:T(8,128)(2,1)S(1)}, bf16[352,2048]{1,0:T(8,128)(2,1)}, u32[]{:S(2)}) copy-start(bf16[352,2048]{1,0:T(8,128)(2,1)} %refs_10_.5) | copy-start | bytes 4325380
  36.5 19.0 %copy-start.7 = (bf16[2048,16]{0,1:T(8,128)(2,1)S(1)}, bf16[2048,16]{0,1:T(8,128)(2,1)}, u32[]{:S(2)}) copy-start(bf16[2048,16]{0,1:T(8,128)(2,1)} %param.33) | copy-start | bytes 196612
  37.3 7.4 %collective-permute-start.7 = (bf16[2,64,1152]{2,1,0:T(8,128)(2,1)S(1)}, bf16[2,64,1152]{2,1,0:T(8,128)(2,1)S(1)}, u32[]{:S(2)}, u32[]{:S(2)}) collective-permute-start(bf16[2,64,1152]{2,1,0:T(8,128)(2,1)S(1)} %get-tuple-element.42.refs_1_), channel_id=1, source_target_pairs={{0,4},{2,6},{4,0},{6,2},{1,5},{3,7},{5,1},{7,3},{8,12},{10,14},{12... | collective-permute-start | bytes 884744 | tf_op jit(solution)/shard_map/ppermute | solution.py:357
  37.9 7.6 %collective-permute-start.21 = (bf16[1,64,1152]{2,1,0:T(8,128)(2,1)S(1)}, bf16[1,64,1152]{2,1,0:T(8,128)(2,1)S(1)}, u32[]{:S(2)}, u32[]{:S(2)}) collective-permute-start(bf16[1,64,1152]{2,1,0:T(8,128)(2,1)S(1)} %get-tuple-element.46), channel_id=1, source_target_pairs={{0,24},{8,16},{16,8},{24,0},{1,25},{9,17},{17,9},{25,1},{2,26},{10... | collective-permute-start | bytes 442376 | tf_op jit(solution)/shard_map/ppermute | solution.py:357
  41.5 10.8 %collective-permute-start.22 = (bf16[1,64,1152]{2,1,0:T(8,128)(2,1)S(1)}, bf16[1,64,1152]{2,1,0:T(8,128)(2,1)S(1)}, u32[]{:S(2)}, u32[]{:S(2)}) collective-permute-start(bf16[1,64,1152]{2,1,0:T(8,128)(2,1)S(1)} %get-tuple-element.46), channel_id=1, source_target_pairs={{0,16},{8,24},{16,0},{24,8},{1,17},{9,25},{17,1},{25,9},{2,18},{10... | collective-permute-start | bytes 442376 | tf_op jit(solution)/shard_map/ppermute | solution.py:357
  41.5 14.0 %collective-permute-start.8 = (bf16[2,64,1152]{2,1,0:T(8,128)(2,1)S(1)}, bf16[2,64,1152]{2,1,0:T(8,128)(2,1)S(1)}, u32[]{:S(2)}, u32[]{:S(2)}) collective-permute-start(bf16[2,64,1152]{2,1,0:T(8,128)(2,1)S(1)} %get-tuple-element.42.refs_1_), channel_id=1, source_target_pairs={{0,2},{2,0},{4,6},{6,4},{1,3},{3,1},{5,7},{7,5},{8,10},{10,8},{12,... | collective-permute-start | bytes 884744 | tf_op jit(solution)/shard_map/ppermute | solution.py:357
  44.7 10.8 %collective-permute-start.9 = (bf16[2,64,1152]{2,1,0:T(8,128)(2,1)S(1)}, bf16[2,64,1152]{2,1,0:T(8,128)(2,1)S(1)}, u32[]{:S(2)}, u32[]{:S(2)}) collective-permute-start(bf16[2,64,1152]{2,1,0:T(8,128)(2,1)S(1)} %collective-permute-done.7.refs_2_), channel_id=1, source_target_pairs={{0,2},{2,0},{4,6},{6,4},{1,3},{3,1},{5,7},{7,5},{8,10},{10,8},{12,... | collective-permute-start | bytes 884744 | tf_op jit(solution)/shard_map/ppermute | solution.py:357
  52.3 8.5 %collective-permute-start.13 = (bf16[2,64,1152]{2,1,0:T(8,128)(2,1)S(1)}, bf16[2,64,1152]{2,1,0:T(8,128)(2,1)S(1)}, u32[]{:S(2)}, u32[]{:S(2)}) collective-permute-start(bf16[2,64,1152]{2,1,0:T(8,128)(2,1)S(1)} %get-tuple-element.42.refs_1_), channel_id=1, source_target_pairs={{0,8},{8,0},{16,24},{24,16},{1,9},{9,1},{17,25},{25,17},{2,10},{10... | collective-permute-start | bytes 884744 | tf_op jit(solution)/shard_map/ppermute | solution.py:357
  52.4 9.6 %collective-permute-start.24 = (bf16[1,2,64,1152]{3,2,0,1:T(8,128)(2,1)S(1)}, bf16[1,2,64,1152]{3,2,0,1:T(8,128)(2,1)S(1)}, u32[]{:S(2)}, u32[]{:S(2)}) collective-permute-start(bf16[1,2,64,1152]{3,2,0,1:T(8,128)(2,1)S(1)} %maximum_bitcast_fusion), channel_id=1, source_target_pairs={{0,4},{2,6},{4,0},{6,2},{1,5},{3,7},{5,1},{7,3},{8,12},{10,14},{12... | collective-permute-start | bytes 884744 | tf_op jit(solution)/shard_map/ppermute | solution.py:357
  54.0 9.4 %collective-permute-start.23 = (bf16[1,2,64,1152]{3,2,0,1:T(8,128)(2,1)S(1)}, bf16[1,2,64,1152]{3,2,0,1:T(8,128)(2,1)S(1)}, u32[]{:S(2)}, u32[]{:S(2)}) collective-permute-start(bf16[1,2,64,1152]{3,2,0,1:T(8,128)(2,1)S(1)} %maximum_bitcast_fusion), channel_id=1, source_target_pairs={{0,1},{1,0},{2,3},{3,2},{4,5},{5,4},{6,7},{7,6},{8,9},{9,8},{10,11... | collective-permute-start | bytes 884744 | tf_op jit(solution)/shard_map/ppermute | solution.py:357
  60.8 9.8 %collective-permute-start.10 = (bf16[2,2,64,1024]{3,2,1,0:T(8,128)(2,1)S(1)}, bf16[2,2,64,1024]{3,2,1,0:T(8,128)(2,1)S(1)}, u32[]{:S(2)}, u32[]{:S(2)}) collective-permute-start(bf16[2,2,64,1024]{3,2,1,0:T(8,128)(2,1)S(1)} %get-tuple-element.41), channel_id=1, source_target_pairs={{0,2},{2,0},{4,6},{6,4},{1,3},{3,1},{5,7},{7,5},{8,10},{10,8},{12,... | collective-permute-start | bytes 1572872 | tf_op jit(solution)/shard_map/ppermute | solution.py:357
  60.9 9.4 %collective-permute-start.14 = (bf16[2,64,1152]{2,1,0:T(8,128)(2,1)S(1)}, bf16[2,64,1152]{2,1,0:T(8,128)(2,1)S(1)}, u32[]{:S(2)}, u32[]{:S(2)}) collective-permute-start(bf16[2,64,1152]{2,1,0:T(8,128)(2,1)S(1)} %collective-permute-done.13.refs_1_), channel_id=1, source_target_pairs={{0,4},{2,6},{4,0},{6,2},{1,5},{3,7},{5,1},{7,3},{8,12},{10,14},{12... | collective-permute-start | bytes 884744 | tf_op jit(solution)/shard_map/ppermute | solution.py:357
  62.0 8.5 %collective-permute-start.25 = (bf16[1,2,64,1152]{3,2,0,1:T(8,128)(2,1)S(1)}, bf16[1,2,64,1152]{3,2,0,1:T(8,128)(2,1)S(1)}, u32[]{:S(2)}, u32[]{:S(2)}) collective-permute-start(bf16[1,2,64,1152]{3,2,0,1:T(8,128)(2,1)S(1)} %collective-permute-done.24), channel_id=1, source_target_pairs={{0,1},{1,0},{2,3},{3,2},{4,5},{5,4},{6,7},{7,6},{8,9},{9,8},{10,11... | collective-permute-start | bytes 884744 | tf_op jit(solution)/shard_map/ppermute | solution.py:357
  63.5 13.6 %collective-permute-start.26 = (bf16[2,64,1152]{2,1,0:T(8,128)(2,1)S(1)}, bf16[2,64,1152]{2,1,0:T(8,128)(2,1)S(1)}, u32[]{:S(2)}, u32[]{:S(2)}) collective-permute-start(bf16[2,64,1152]{2,1,0:T(8,128)(2,1)S(1)} %get-tuple-element.58.refs_1_), channel_id=1, source_target_pairs={{0,2},{2,0},{4,6},{6,4},{1,3},{3,1},{5,7},{7,5},{8,10},{10,8},{12,... | collective-permute-start | bytes 884744 | tf_op jit(solution)/shard_map/ppermute | solution.py:357
  63.6 7.4 %collective-permute-start.15 = (bf16[2,64,1152]{2,1,0:T(8,128)(2,1)S(1)}, bf16[2,64,1152]{2,1,0:T(8,128)(2,1)S(1)}, u32[]{:S(2)}, u32[]{:S(2)}) collective-permute-start(bf16[2,64,1152]{2,1,0:T(8,128)(2,1)S(1)} %collective-permute-done.13.refs_1_), channel_id=1, source_target_pairs={{0,2},{2,0},{4,6},{6,4},{1,3},{3,1},{5,7},{7,5},{8,10},{10,8},{12,... | collective-permute-start | bytes 884744 | tf_op jit(solution)/shard_map/ppermute | solution.py:357
  70.3 1.6 %collective-permute-start.16 = (bf16[2,64,1152]{2,1,0:T(8,128)(2,1)S(1)}, bf16[2,64,1152]{2,1,0:T(8,128)(2,1)S(1)}, u32[]{:S(2)}, u32[]{:S(2)}) collective-permute-start(bf16[2,64,1152]{2,1,0:T(8,128)(2,1)S(1)} %collective-permute-done.14.refs_2_), channel_id=1, source_target_pairs={{0,2},{2,0},{4,6},{6,4},{1,3},{3,1},{5,7},{7,5},{8,10},{10,8},{12,... | collective-permute-start | bytes 884744 | tf_op jit(solution)/shard_map/ppermute | solution.py:357
  75.7 6.4 %collective-permute-start.17 = (bf16[2,2,64,1024]{3,2,1,0:T(8,128)(2,1)S(1)}, bf16[2,2,64,1024]{3,2,1,0:T(8,128)(2,1)S(1)}, u32[]{:S(2)}, u32[]{:S(2)}) collective-permute-start(bf16[2,2,64,1024]{3,2,1,0:T(8,128)(2,1)S(1)} %get-tuple-element.45), channel_id=1, source_target_pairs={{0,2},{2,0},{4,6},{6,4},{1,3},{3,1},{5,7},{7,5},{8,10},{10,8},{12,... | collective-permute-start | bytes 1572872 | tf_op jit(solution)/shard_map/ppermute | solution.py:357
  76.0 2.2 %collective-permute-start.27 = (bf16[2,64,1152]{2,1,0:T(8,128)(2,1)S(1)}, bf16[2,64,1152]{2,1,0:T(8,128)(2,1)S(1)}, u32[]{:S(2)}, u32[]{:S(2)}) collective-permute-start(bf16[2,64,1152]{2,1,0:T(8,128)(2,1)S(1)} %get-tuple-element.48.refs_2_), channel_id=1, source_target_pairs={{0,2},{2,0},{4,6},{6,4},{1,3},{3,1},{5,7},{7,5},{8,10},{10,8},{12,... | collective-permute-start | bytes 884744 | tf_op jit(solution)/shard_map/ppermute | solution.py:357
  76.4 8.7 %collective-permute-start.30 = (bf16[2,64,1152]{2,1,0:T(8,128)(2,1)S(1)}, bf16[2,64,1152]{2,1,0:T(8,128)(2,1)S(1)}, u32[]{:S(2)}, u32[]{:S(2)}) collective-permute-start(bf16[2,64,1152]{2,1,0:T(8,128)(2,1)S(1)} %get-tuple-element.59.refs_1_), channel_id=1, source_target_pairs={{0,2},{2,0},{4,6},{6,4},{1,3},{3,1},{5,7},{7,5},{8,10},{10,8},{12,... | collective-permute-start | bytes 884744 | tf_op jit(solution)/shard_map/ppermute | solution.py:357
  76.5 8.6 %collective-permute-start.11 = (bf16[2,64,1024]{2,1,0:T(8,128)(2,1)S(1)}, bf16[2,64,1024]{2,1,0:T(8,128)(2,1)S(1)}, u32[]{:S(2)}, u32[]{:S(2)}) collective-permute-start(bf16[2,64,1024]{2,1,0:T(8,128)(2,1)S(1)} %fusion.3), channel_id=1, source_target_pairs={{0,4},{2,6},{4,0},{6,2},{1,5},{3,7},{5,1},{7,3},{8,12},{10,14},{12... | collective-permute-start | bytes 786440 | tf_op jit(solution)/shard_map/ppermute | solution.py:357
  82.0 2.0 %collective-permute-start.28 = (bf16[2,2,64,1024]{3,2,1,0:T(8,128)(2,1)S(1)}, bf16[2,2,64,1024]{3,2,1,0:T(8,128)(2,1)S(1)}, u32[]{:S(2)}, u32[]{:S(2)}) collective-permute-start(bf16[2,2,64,1024]{3,2,1,0:T(8,128)(2,1)S(1)} %get-tuple-element.50), channel_id=1, source_target_pairs={{0,2},{2,0},{4,6},{6,4},{1,3},{3,1},{5,7},{7,5},{8,10},{10,8},{12,... | collective-permute-start | bytes 1572872 | tf_op jit(solution)/shard_map/ppermute | solution.py:357
  85.1 1.6 %collective-permute-start.31 = (bf16[2,64,1152]{2,1,0:T(8,128)(2,1)S(1)}, bf16[2,64,1152]{2,1,0:T(8,128)(2,1)S(1)}, u32[]{:S(2)}, u32[]{:S(2)}) collective-permute-start(bf16[2,64,1152]{2,1,0:T(8,128)(2,1)S(1)} %get-tuple-element.51.refs_2_), channel_id=1, source_target_pairs={{0,2},{2,0},{4,6},{6,4},{1,3},{3,1},{5,7},{7,5},{8,10},{10,8},{12,... | collective-permute-start | bytes 884744 | tf_op jit(solution)/shard_map/ppermute | solution.py:357
  90.5 10.1 %collective-permute-start.32 = (bf16[2,2,64,1024]{3,2,1,0:T(8,128)(2,1)S(1)}, bf16[2,2,64,1024]{3,2,1,0:T(8,128)(2,1)S(1)}, u32[]{:S(2)}, u32[]{:S(2)}) collective-permute-start(bf16[2,2,64,1024]{3,2,1,0:T(8,128)(2,1)S(1)} %get-tuple-element.53), channel_id=1, source_target_pairs={{0,2},{2,0},{4,6},{6,4},{1,3},{3,1},{5,7},{7,5},{8,10},{10,8},{12,... | collective-permute-start | bytes 1572872 | tf_op jit(solution)/shard_map/ppermute | solution.py:357
  90.7 8.6 %collective-permute-start.18 = (bf16[2,64,1024]{2,1,0:T(8,128)(2,1)S(1)}, bf16[2,64,1024]{2,1,0:T(8,128)(2,1)S(1)}, u32[]{:S(2)}, u32[]{:S(2)}) collective-permute-start(bf16[2,64,1024]{2,1,0:T(8,128)(2,1)S(1)} %fusion.4), channel_id=1, source_target_pairs={{0,4},{2,6},{4,0},{6,2},{1,5},{3,7},{5,1},{7,3},{8,12},{10,14},{12... | collective-permute-start | bytes 786440 | tf_op jit(solution)/shard_map/ppermute | solution.py:357
  91.5 28.1 %collective-permute-start.12 = (bf16[1,64,1024]{2,1,0:T(8,128)(2,1)S(1)}, bf16[1,64,1024]{2,1,0:T(8,128)(2,1)S(1)}, u32[]{:S(2)}, u32[]{:S(2)}) collective-permute-start(bf16[1,64,1024]{2,1,0:T(8,128)(2,1)S(1)} %slice.177), channel_id=1, source_target_pairs={{0,1},{1,0},{2,3},{3,2},{4,5},{5,4},{6,7},{7,6},{8,9},{9,8},{10,11... | collective-permute-start | bytes 393224 | tf_op jit(solution)/shard_map/ppermute | solution.py:357
  99.4 6.5 %collective-permute-start.19 = (bf16[1,64,1024]{2,1,0:T(8,128)(2,1)S(1)}, bf16[1,64,1024]{2,1,0:T(8,128)(2,1)S(1)}, u32[]{:S(2)}, u32[]{:S(2)}) collective-permute-start(bf16[1,64,1024]{2,1,0:T(8,128)(2,1)S(1)} %slice.176), channel_id=1, source_target_pairs={{0,1},{1,0},{2,3},{3,2},{4,5},{5,4},{6,7},{7,6},{8,9},{9,8},{10,11... | collective-permute-start | bytes 393224 | tf_op jit(solution)/shard_map/ppermute | solution.py:357
  100.0 7.9 %collective-permute-start.29 = (bf16[2,64,1024]{2,1,0:T(8,128)(2,1)S(1)}, bf16[2,64,1024]{2,1,0:T(8,128)(2,1)S(1)}, u32[]{:S(2)}, u32[]{:S(2)}) collective-permute-start(bf16[2,64,1024]{2,1,0:T(8,128)(2,1)S(1)} %fusion.5), channel_id=1, source_target_pairs={{0,4},{2,6},{4,0},{6,2},{1,5},{3,7},{5,1},{7,3},{8,12},{10,14},{12... | collective-permute-start | bytes 786440 | tf_op jit(solution)/shard_map/ppermute | solution.py:357
  100.8 10.6 %collective-permute-start.35 = (bf16[1,2,64,1024]{3,2,1,0:T(8,128)(2,1)S(1)}, bf16[1,2,64,1024]{3,2,1,0:T(8,128)(2,1)S(1)}, u32[]{:S(2)}, u32[]{:S(2)}) collective-permute-start(bf16[1,2,64,1024]{3,2,1,0:T(8,128)(2,1)S(1)} %slice.174), channel_id=1, source_target_pairs={{0,1},{1,0},{2,3},{3,2},{4,5},{5,4},{6,7},{7,6},{8,9},{9,8},{10,11... | collective-permute-start | bytes 786440 | tf_op jit(solution)/shard_map/ppermute | solution.py:357
  105.9 13.7 %collective-permute-start.20 = (bf16[64,1024]{1,0:T(8,128)(2,1)S(1)}, bf16[64,1024]{1,0:T(8,128)(2,1)S(1)}, u32[]{:S(2)}, u32[]{:S(2)}) collective-permute-start(bf16[64,1024]{1,0:T(8,128)(2,1)S(1)} %fusion.17), channel_id=1, source_target_pairs={{0,8},{8,0},{16,24},{24,16},{1,9},{9,1},{17,25},{25,17},{2,10},{10... | collective-permute-start | bytes 393224 | tf_op jit(solution)/shard_map/ppermute | solution.py:357
  108.0 5.0 %collective-permute-start.33 = (bf16[1,64,1024]{2,1,0:T(8,128)(2,1)S(1)}, bf16[1,64,1024]{2,1,0:T(8,128)(2,1)S(1)}, u32[]{:S(2)}, u32[]{:S(2)}) collective-permute-start(bf16[1,64,1024]{2,1,0:T(8,128)(2,1)S(1)} %slice.175), channel_id=1, source_target_pairs={{0,1},{1,0},{2,3},{3,2},{4,5},{5,4},{6,7},{7,6},{8,9},{9,8},{10,11... | collective-permute-start | bytes 393224 | tf_op jit(solution)/shard_map/ppermute | solution.py:357
  111.6 5.0 %collective-permute-start.36 = (bf16[64,1024]{1,0:T(8,128)(2,1)S(1)}, bf16[64,1024]{1,0:T(8,128)(2,1)S(1)}, u32[]{:S(2)}, u32[]{:S(2)}) collective-permute-start(bf16[64,1024]{1,0:T(8,128)(2,1)S(1)} %fusion.19), channel_id=1, source_target_pairs={{0,4},{2,6},{4,0},{6,2},{1,5},{3,7},{5,1},{7,3},{8,12},{10,14},{12... | collective-permute-start | bytes 393224 | tf_op jit(solution)/shard_map/ppermute | solution.py:357
  113.1 7.8 %collective-permute-start.34 = (bf16[64,1024]{1,0:T(8,128)(2,1)S(1)}, bf16[64,1024]{1,0:T(8,128)(2,1)S(1)}, u32[]{:S(2)}, u32[]{:S(2)}) collective-permute-start(bf16[64,1024]{1,0:T(8,128)(2,1)S(1)} %fusion.18), channel_id=1, source_target_pairs={{0,24},{8,16},{16,8},{24,0},{1,25},{9,17},{17,9},{25,1},{2,26},{10... | collective-permute-start | bytes 393224 | tf_op jit(solution)/shard_map/ppermute | solution.py:357
  116.6 10.3 %collective-permute-start.37 = (bf16[64,1024]{1,0:T(8,128)(2,1)S(1)}, bf16[64,1024]{1,0:T(8,128)(2,1)S(1)}, u32[]{:S(2)}, u32[]{:S(2)}) collective-permute-start(bf16[64,1024]{1,0:T(8,128)(2,1)S(1)} %fusion.7), channel_id=1, source_target_pairs={{0,16},{8,24},{16,0},{24,8},{1,17},{9,25},{17,1},{25,9},{2,18},{10... | collective-permute-start | bytes 393224 | tf_op jit(solution)/shard_map/ppermute | solution.py:357
  127.0 5.0 %collective-permute-start.38 = (bf16[1,64,1024]{2,1,0:T(8,128)(2,1)S(1)}, bf16[1,64,1024]{2,1,0:T(8,128)(2,1)S(1)}, u32[]{:S(2)}, u32[]{:S(2)}) collective-permute-start(bf16[1,64,1024]{2,1,0:T(8,128)(2,1)S(1)} %bitcast.89), channel_id=1, source_target_pairs={{0,1},{1,0},{2,3},{3,2},{4,5},{5,4},{6,7},{7,6},{8,9},{9,8},{10,11... | collective-permute-start | bytes 393224 | tf_op jit(solution)/shard_map/ppermute | solution.py:357

commit v8 on v7

--- a/solution.py
+++ b/solution.py
@@ -422,12 +422,11 @@
     routed_weights = (jnp.swapaxes(expert_gate_up[0], 1, 2), expert_down[0])
     shared_weights = (jnp.swapaxes(shared_gate_up, 1, 2), shared_down)
     distances = [0, 1, *range(n_req - 1, 1, -1)]
-    fars = [swap(block, "row", n_row, 2)]
-    blocks = [block, swap(after(block, fars[0]), "req", n_req, 1)]
-    fars.append(swap(blocks[1], "row", n_row, 2))
+    blocks = [block, swap(block, "req", n_req, 1)]
+    fars = [swap(each, "row", n_row, 2) for each in blocks]
     rest = [swap(own_part, "req", n_req, s) for s in distances[2:]]
     if rest:
-        rest = after(jnp.concatenate(rest, axis=0)[None], fars[0])
+        rest = after(jnp.concatenate(rest, axis=0)[None], fars[0], blocks[1])
         rest_far = swap(rest, "row", n_row, 2)
         rest, rest_far = col_gather(rest, n_col), col_gather(rest_far, n_col)
         blocks += [rest[:, k] for k in range(rest.shape[1])]
@@ -436,11 +435,9 @@
     for k, s in enumerate(distances):
         near = swap(blocks[k], "row", n_row, 1)
         far = fars[k]
-        if k > 2:
-            far = after(far, *sends, *folds, *returns[: k - 2])
-        elif k:
-            far = after(far, *sends, *folds[: k - 1])
         far_near = swap(far, "row", n_row, 1)
+        if k:
+            far_near = after(far_near, *sends, *folds[: k - 1], *returns[: max(0, k - 2)])
         keep, send = expert_part(
             indices,
             n_col,
@@ -459,13 +456,12 @@
         if k < 3:
             returns.append(swap(folds[k], "row", n_row, 2))
     parts = []
-    last = col_scatter(sums[-1], n_col)[0] if n_req > 3 else None
     for k, near_sum in enumerate(sums):
         if k < 3:
-            from_far = after(returns[k], *((), [last], folds[-1:])[k]) if n_req > 3 else returns[k]
+            from_far = after(returns[k], *folds[-1:]) if k else returns[k]
             part = col_scatter(near_sum[0] + from_far.astype(jnp.float32), n_col)[0]
         else:
-            part = last if k == n_req - 1 else col_scatter(near_sum, n_col)[0]
+            part = col_scatter(near_sum, n_col)[0]
             part = part[0] + swap(part[1].astype(bf16), "row", n_row, 2).astype(jnp.float32)
         parts.append(part.astype(bf16) if k else part)
     total = parts[0]

time: 134 us -> 126 us (0.940)
  waiting for transfers between devices: 66.8 us -> 59 us
    ppermute x39, waiting for transfers between devices: 66.8 us -> 59 us  [swap(): return lax.ppermute(values, axis, [(i, i ^ bits) for i in range(size)])]
  transfers between devices with their start and end apart: 39 -> 39, of which waited for: 23 -> 21; matrix products, arithmetic and copies ran while one was open for 1% -> 1% of each run, Pallas kernels for 15% -> 19%
where the time goes in v8:
time: 126 us
  waiting for transfers between devices  59 us (47%)
  starting transfers between devices  31.9 us (25%)
  Pallas kernels  29.3 us (23%)
  local copies, waits for them, and re-layouts  2.68 us (2%)
  between operations  1.8 us (1%)
  other arithmetic  1.52 us (1%)
    ppermute x39, waiting for transfers between devices, swap(): return lax.ppermute(values, axis, [(i, i ^ bits) for i in range(size)])  59 us
    ppermute x39, starting transfers between devices, swap(): return lax.ppermute(values, axis, [(i, i ^ bits) for i in range(size)])  31.9 us
    pallas_call x4, Pallas kernels, expert_part(): pl.pallas_call(functools.partial(expert_kernel, bool(shared_weights), far...  16.9 us
    pallas_call x2, Pallas kernels, attention_part(): pl.pallas_call(functools.partial(attention_kernel, first, place), out_sha...  8.2 us
  transfers between devices with their start and end apart: 39, of which 21 were waited for; matrix products, arithmetic and copies ran while one was open for 1% of the time, Pallas kernels for 19%

profile of v8, /device:TPU:0, one launch (start us, length us, event | category | flops | bytes accessed | tf_op | source)
XLA Modules:
  0.0 126.2 jit_solution(15277283687467641100)
XLA Ops:
  0.6 0.5 collective-permute-start
  1.1 2.6 %collective-permute-start.2 = (bf16[64,2048]{1,0:T(8,128)(2,1)}, bf16[64,2048]{1,0:T(8,128)(2,1)S(1)}, u32[]{:S(2)}, u32[]{:S(2)}) collective-permute-start(bf16[64,2048]{1,0:T(8,128)(2,1)} %hidden_ref.1), channel_id=1, source_target_pairs={{0,4},{2,6},{4,0},{6,2},{1,5},{3,7},{5,1},{7,3},{8,12},{10,14},{12... | collective-permute-start | bytes 786440 | tf_op jit(solution)/shard_map/ppermute | solution.py:357
  4.5 0.7 copy-done.14
  5.2 0.7 copy-done.15
  5.9 2.1 %trees.1 = (f32[4,64,64]{2,1,0:T(8,128)S(1)}, f32[4,64,65]{2,1,0:T(8,128)S(1)}, bf16[64,64]{1,0:T(8,128)(2,1)S(1)}, f32[1,16]{1,0:T(1,128)S(1)}) custom-call(s32[3]{0:T(128)S(1)} %pad_add_fusion.row_ref.refs_0_, s32[4]{0:T(128)S(1)} %copy-done.15, s32[1]{0:T(128)S(6)} %copy.24.accepted_ref, s32[4,64]{1,0:T(4,128)S(1)} %copy-done.14), custom_call_target="tpu_custom_call" | custom-call | flops 20000000000 | bytes 1 | tf_op jit(solution)/shard_map/trees/pallas_call | solution.py:110
  8.1 0.4 copy-done.3
  8.5 0.3 copy-done.4
  8.9 4.4 %attention.2 = (f32[64,2048]{1,0:T(8,128)S(1)}, bf16[64,2048]{1,0:T(8,128)(2,1)S(1)}, bf16[1,64,576]{2,1,0:T(8,128)(2,1)}) custom-call(s32[3]{0:T(128)S(1)} %pad_add_fusion.row_ref.refs_0_, bf16[64,2048]{1,0:T(8,128)(2,1)S(1)} %copy-done.10, bf16[64,2048]{1,0:T(8,128)(2,1)S(1)} %collective-permute-done.refs_1_, bf16[4,576,384]{2,1,0:T(8,128)(2,1)S(1)} %bitcast.82, ...), custom_call_target="tpu_custom_call" | custom-call | flops 1 | bytes 1 | tf_op jit(solution)/shard_map/attention/pallas_call | solution.py:211
  13.5 1.4 %collective-permute-done.3.refs_1_ = bf16[64,2048]{1,0:T(8,128)(2,1)S(1)} collective-permute-done((bf16[64,2048]{1,0:T(8,128)(2,1)S(1)}, bf16[64,2048]{1,0:T(8,128)(2,1)S(1)}, u32[]{:S(2)}, u32[]{:S(2)}) %collective-permute-start.3) | collective-permute-done | bytes 262176 | tf_op jit(solution)/shard_map/ppermute | solution.py:357
  14.8 3.8 %attention.3 = (f32[64,2048]{1,0:T(8,128)S(1)}, bf16[64,2048]{1,0:T(8,128)(2,1)S(1)}) custom-call(s32[3]{0:T(128)S(1)} %pad_add_fusion.row_ref.refs_0_, bf16[64,2048]{1,0:T(8,128)(2,1)S(1)} %collective-permute-done.2.refs_0_, bf16[64,2048]{1,0:T(8,128)(2,1)S(1)} %collective-permute-done.3.refs_1_, bf16[4,576,384]{2,1,0:T(8,128)(2,1)S(1)} %bitcast.83, ...), custom_call_target="tpu_custom_call" | custom-call | flops 1 | bytes 1 | tf_op jit(solution)/shard_map/attention/pallas_call | solution.py:211
  18.7 0.2 collective-permute-start.4
  18.9 0.3 collective-permute-start.1
  19.3 1.0 collective-permute-done.4
  20.7 8.1 %collective-permute-done.5 = bf16[64,2048]{1,0:T(8,128)(2,1)S(1)} collective-permute-done((bf16[64,2048]{1,0:T(8,128)(2,1)S(1)}, bf16[64,2048]{1,0:T(8,128)(2,1)S(1)}, u32[]{:S(2)}, u32[]{:S(2)}) %collective-permute-start.5) | collective-permute-done | bytes 262176 | tf_op jit(solution)/shard_map/ppermute | solution.py:357
  28.9 1.6 %collective-permute-start.6 = (bf16[64,2048]{1,0:T(8,128)(2,1)S(1)}, bf16[64,2048]{1,0:T(8,128)(2,1)S(1)}, u32[]{:S(2)}, u32[]{:S(2)}) collective-permute-start(bf16[64,2048]{1,0:T(8,128)(2,1)S(1)} %add_convert_fusion.keep_ref), channel_id=1, source_target_pairs={{0,1},{1,0},{2,3},{3,2},{4,5},{5,4},{6,7},{7,6},{8,9},{9,8},{10,11... | collective-permute-start | bytes 786440 | tf_op jit(solution)/shard_map/ppermute | solution.py:357
  30.6 5.9 %collective-permute-done.6 = bf16[64,2048]{1,0:T(8,128)(2,1)S(1)} collective-permute-done((bf16[64,2048]{1,0:T(8,128)(2,1)S(1)}, bf16[64,2048]{1,0:T(8,128)(2,1)S(1)}, u32[]{:S(2)}, u32[]{:S(2)}) %collective-permute-start.6) | collective-permute-done | bytes 262176 | tf_op jit(solution)/shard_map/ppermute | solution.py:357
  36.6 0.8 join.1
  37.4 0.6 collective-permute-start.7
  38.0 3.6 %collective-permute-start.19 = (bf16[1,64,1152]{2,1,0:T(8,128)(2,1)S(1)}, bf16[1,64,1152]{2,1,0:T(8,128)(2,1)S(1)}, u32[]{:S(2)}, u32[]{:S(2)}) collective-permute-start(bf16[1,64,1152]{2,1,0:T(8,128)(2,1)S(1)} %get-tuple-element.45), channel_id=1, source_target_pairs={{0,24},{8,16},{16,8},{24,0},{1,25},{9,17},{17,9},{25,1},{2,26},{10... | collective-permute-start | bytes 442376 | tf_op jit(solution)/shard_map/ppermute | solution.py:357
  41.5 0.8 collective-permute-start.13
  42.4 2.4 %collective-permute-done.7.refs_2_ = bf16[2,64,1152]{2,1,0:T(8,128)(2,1)S(1)} collective-permute-done((bf16[2,64,1152]{2,1,0:T(8,128)(2,1)S(1)}, bf16[2,64,1152]{2,1,0:T(8,128)(2,1)S(1)}, u32[]{:S(2)}, u32[]{:S(2)}) %collective-permute-start.7) | collective-permute-done | bytes 294944 | tf_op jit(solution)/shard_map/ppermute | solution.py:357
  44.8 1.8 %collective-permute-done.19 = bf16[1,64,1152]{2,1,0:T(8,128)(2,1)S(1)} collective-permute-done((bf16[1,64,1152]{2,1,0:T(8,128)(2,1)S(1)}, bf16[1,64,1152]{2,1,0:T(8,128)(2,1)S(1)}, u32[]{:S(2)}, u32[]{:S(2)}) %collective-permute-start.19) | collective-permute-done | bytes 147488 | tf_op jit(solution)/shard_map/ppermute | solution.py:357
  46.5 5.8 %collective-permute-done.20 = bf16[1,64,1152]{2,1,0:T(8,128)(2,1)S(1)} collective-permute-done((bf16[1,64,1152]{2,1,0:T(8,128)(2,1)S(1)}, bf16[1,64,1152]{2,1,0:T(8,128)(2,1)S(1)}, u32[]{:S(2)}, u32[]{:S(2)}) %collective-permute-start.20) | collective-permute-done | bytes 147488 | tf_op jit(solution)/shard_map/ppermute | solution.py:357
  52.4 1.1 collective-permute-done.13.refs_1_
  53.5 1.3 collective-permute-start.14
  54.8 0.8 collective-permute-start.22
  55.5 1.3 %collective-permute-start.21 = (bf16[1,2,64,1152]{3,2,0,1:T(8,128)(2,1)S(1)}, bf16[1,2,64,1152]{3,2,0,1:T(8,128)(2,1)S(1)}, u32[]{:S(2)}, u32[]{:S(2)}) collective-permute-start(bf16[1,2,64,1152]{3,2,0,1:T(8,128)(2,1)S(1)} %maximum_bitcast_fusion), channel_id=1, source_target_pairs={{0,1},{1,0},{2,3},{3,2},{4,5},{5,4},{6,7},{7,6},{8,9},{9,8},{10,11... | collective-permute-start | bytes 884744 | tf_op jit(solution)/shard_map/ppermute | solution.py:357
  57.0 5.2 %experts.4 = (f32[2,2,64,1024]{3,2,1,0:T(8,128)S(1)}, bf16[2,2,64,1024]{3,2,1,0:T(8,128)(2,1)S(1)}) custom-call(s32[3]{0:T(128)S(1)} %pad_add_fusion.row_ref.refs_0_, bf16[2,64,1152]{2,1,0:T(8,128)(2,1)S(1)} %get-tuple-element.38.refs_1_, bf16[2,64,1152]{2,1,0:T(8,128)(2,1)S(1)} %collective-permute-done.7.refs_2_, ...), custom_call_target="tpu_custom_call" | custom-call | flops 1 | bytes 1 | tf_op jit(solution)/shard_map/experts/pallas_call | solution.py:337
  62.2 0.5 collective-permute-start.10
  62.7 0.7 collective-permute-done.14.refs_2_
  63.4 3.2 %collective-permute-done.22 = bf16[1,2,64,1152]{3,2,0,1:T(8,128)(2,1)S(1)} collective-permute-done((bf16[1,2,64,1152]{3,2,0,1:T(8,128)(2,1)S(1)}, bf16[1,2,64,1152]{3,2,0,1:T(8,128)(2,1)S(1)}, u32[]{:S(2)}, u32[]{:S(2)}) %collective-permute-start.22) | collective-permute-done | bytes 294944 | tf_op jit(solution)/shard_map/ppermute | solution.py:357
  66.6 1.7 %collective-permute-start.23 = (bf16[1,2,64,1152]{3,2,0,1:T(8,128)(2,1)S(1)}, bf16[1,2,64,1152]{3,2,0,1:T(8,128)(2,1)S(1)}, u32[]{:S(2)}, u32[]{:S(2)}) collective-permute-start(bf16[1,2,64,1152]{3,2,0,1:T(8,128)(2,1)S(1)} %collective-permute-done.22), channel_id=1, source_target_pairs={{0,1},{1,0},{2,3},{3,2},{4,5},{5,4},{6,7},{7,6},{8,9},{9,8},{10,11... | collective-permute-start | bytes 884744 | tf_op jit(solution)/shard_map/ppermute | solution.py:357
  68.5 4.0 %experts.5 = (f32[2,2,64,1024]{3,2,1,0:T(8,128)S(1)}, bf16[2,2,64,1024]{3,2,1,0:T(8,128)(2,1)S(1)}) custom-call(s32[3]{0:T(128)S(1)} %pad_add_fusion.row_ref.refs_0_, bf16[2,64,1152]{2,1,0:T(8,128)(2,1)S(1)} %collective-permute-done.13.refs_1_, bf16[2,64,1152]{2,1,0:T(8,128)(2,1)S(1)} %collective-permute-done.14.refs_2_, ...), custom_call_target="tpu_custom_call" | custom-call | flops 1 | bytes 1 | tf_op jit(solution)/shard_map/experts/pallas_call | solution.py:337
  72.5 0.6 collective-permute-start.17
  73.1 0.2 collective-permute-done.23
  73.5 0.2 convert_add_fusion.3
  73.7 1.8 %collective-permute-start.11 = (bf16[2,64,1024]{2,1,0:T(8,128)(2,1)S(1)}, bf16[2,64,1024]{2,1,0:T(8,128)(2,1)S(1)}, u32[]{:S(2)}, u32[]{:S(2)}) collective-permute-start(bf16[2,64,1024]{2,1,0:T(8,128)(2,1)S(1)} %fusion.3), channel_id=1, source_target_pairs={{0,4},{2,6},{4,0},{6,2},{1,5},{3,7},{5,1},{7,3},{8,12},{10,14},{12... | collective-permute-start | bytes 786440 | tf_op jit(solution)/shard_map/ppermute | solution.py:357
  75.5 0.2 collective-permute-start.24
  75.7 0.3 collective-permute-start.25
  76.0 3.8 %experts.6 = (f32[2,2,64,1024]{3,2,1,0:T(8,128)S(1)}, bf16[2,2,64,1024]{3,2,1,0:T(8,128)(2,1)S(1)}) custom-call(s32[3]{0:T(128)S(1)} %pad_add_fusion.row_ref.refs_0_, bf16[2,64,1152]{2,1,0:T(8,128)(2,1)S(1)} %get-tuple-element.58.refs_1_, bf16[2,64,1152]{2,1,0:T(8,128)(2,1)S(1)} %get-tuple-element.56.refs_2_, ...), custom_call_target="tpu_custom_call" | custom-call | flops 1 | bytes 1 | tf_op jit(solution)/shard_map/experts/pallas_call | solution.py:337
  79.9 0.3 collective-permute-start.31
  80.1 2.3 %collective-permute-done.11 = bf16[2,64,1024]{2,1,0:T(8,128)(2,1)S(1)} collective-permute-done((bf16[2,64,1024]{2,1,0:T(8,128)(2,1)S(1)}, bf16[2,64,1024]{2,1,0:T(8,128)(2,1)S(1)}, u32[]{:S(2)}, u32[]{:S(2)}) %collective-permute-start.11) | collective-permute-done | bytes 262176 | tf_op jit(solution)/shard_map/ppermute | solution.py:357
  82.6 1.7 %collective-permute-start.12 = (bf16[1,64,1024]{2,1,0:T(8,128)(2,1)S(1)}, bf16[1,64,1024]{2,1,0:T(8,128)(2,1)S(1)}, u32[]{:S(2)}, u32[]{:S(2)}) collective-permute-start(bf16[1,64,1024]{2,1,0:T(8,128)(2,1)S(1)} %slice.177), channel_id=1, source_target_pairs={{0,1},{1,0},{2,3},{3,2},{4,5},{5,4},{6,7},{7,6},{8,9},{9,8},{10,11... | collective-permute-start | bytes 393224 | tf_op jit(solution)/shard_map/ppermute | solution.py:357
  84.5 1.6 %collective-permute-start.18 = (bf16[2,64,1024]{2,1,0:T(8,128)(2,1)S(1)}, bf16[2,64,1024]{2,1,0:T(8,128)(2,1)S(1)}, u32[]{:S(2)}, u32[]{:S(2)}) collective-permute-start(bf16[2,64,1024]{2,1,0:T(8,128)(2,1)S(1)} %fusion.4), channel_id=1, source_target_pairs={{0,4},{2,6},{4,0},{6,2},{1,5},{3,7},{5,1},{7,3},{8,12},{10,14},{12... | collective-permute-start | bytes 786440 | tf_op jit(solution)/shard_map/ppermute | solution.py:357
  86.1 3.8 %experts.7 = (f32[2,2,64,1024]{3,2,1,0:T(8,128)S(1)}, bf16[2,2,64,1024]{3,2,1,0:T(8,128)(2,1)S(1)}) custom-call(s32[3]{0:T(128)S(1)} %pad_add_fusion.row_ref.refs_0_, bf16[2,64,1152]{2,1,0:T(8,128)(2,1)S(1)} %get-tuple-element.59.refs_1_, bf16[2,64,1152]{2,1,0:T(8,128)(2,1)S(1)} %get-tuple-element.57.refs_2_, ...), custom_call_target="tpu_custom_call" | custom-call | flops 1 | bytes 1 | tf_op jit(solution)/shard_map/experts/pallas_call | solution.py:337
  90.0 0.2 convert_add_fusion
  90.3 0.6 collective-permute-start.32
  90.9 1.1 collective-permute-done.28
  92.1 0.6 collective-permute-start.35
  92.9 1.5 %collective-permute-start.29 = (bf16[1,64,1024]{2,1,0:T(8,128)(2,1)S(1)}, bf16[1,64,1024]{2,1,0:T(8,128)(2,1)S(1)}, u32[]{:S(2)}, u32[]{:S(2)}) collective-permute-start(bf16[1,64,1024]{2,1,0:T(8,128)(2,1)S(1)} %slice.176), channel_id=1, source_target_pairs={{0,1},{1,0},{2,3},{3,2},{4,5},{5,4},{6,7},{7,6},{8,9},{9,8},{10,11... | collective-permute-start | bytes 393224 | tf_op jit(solution)/shard_map/ppermute | solution.py:357
  94.4 4.7 %collective-permute-done.32 = bf16[2,64,1024]{2,1,0:T(8,128)(2,1)S(1)} collective-permute-done((bf16[2,64,1024]{2,1,0:T(8,128)(2,1)S(1)}, bf16[2,64,1024]{2,1,0:T(8,128)(2,1)S(1)}, u32[]{:S(2)}, u32[]{:S(2)}) %collective-permute-start.32) | collective-permute-done | bytes 262176 | tf_op jit(solution)/shard_map/ppermute | solution.py:357
  99.1 0.6 collective-permute-start.33
  99.8 4.4 %collective-permute-done.29 = bf16[1,64,1024]{2,1,0:T(8,128)(2,1)S(1)} collective-permute-done((bf16[1,64,1024]{2,1,0:T(8,128)(2,1)S(1)}, bf16[1,64,1024]{2,1,0:T(8,128)(2,1)S(1)}, u32[]{:S(2)}, u32[]{:S(2)}) %collective-permute-start.29) | collective-permute-done | bytes 131104 | tf_op jit(solution)/shard_map/ppermute | solution.py:357
  104.2 0.7 collective-permute-start.30
  105.0 0.6 collective-permute-start.36
  105.6 0.5 collective-permute-done.33
  106.2 2.0 %collective-permute-start.34 = (bf16[64,1024]{1,0:T(8,128)(2,1)S(1)}, bf16[64,1024]{1,0:T(8,128)(2,1)S(1)}, u32[]{:S(2)}, u32[]{:S(2)}) collective-permute-start(bf16[64,1024]{1,0:T(8,128)(2,1)S(1)} %fusion.18), channel_id=1, source_target_pairs={{0,24},{8,16},{16,8},{24,0},{1,25},{9,17},{17,9},{25,1},{2,26},{10... | collective-permute-start | bytes 393224 | tf_op jit(solution)/shard_map/ppermute | solution.py:357
  108.1 1.9 %collective-permute-done.36 = bf16[64,1024]{1,0:T(8,128)(2,1)S(1)} collective-permute-done((bf16[64,1024]{1,0:T(8,128)(2,1)S(1)}, bf16[64,1024]{1,0:T(8,128)(2,1)S(1)}, u32[]{:S(2)}, u32[]{:S(2)}) %collective-permute-start.36) | collective-permute-done | bytes 131104 | tf_op jit(solution)/shard_map/ppermute | solution.py:357
  110.1 1.8 %collective-permute-start.37 = (bf16[64,1024]{1,0:T(8,128)(2,1)S(1)}, bf16[64,1024]{1,0:T(8,128)(2,1)S(1)}, u32[]{:S(2)}, u32[]{:S(2)}) collective-permute-start(bf16[64,1024]{1,0:T(8,128)(2,1)S(1)} %fusion.7), channel_id=1, source_target_pairs={{0,16},{8,24},{16,0},{24,8},{1,17},{9,25},{17,1},{25,9},{2,18},{10... | collective-permute-start | bytes 393224 | tf_op jit(solution)/shard_map/ppermute | solution.py:357
  111.9 2.3 %collective-permute-done.34 = bf16[64,1024]{1,0:T(8,128)(2,1)S(1)} collective-permute-done((bf16[64,1024]{1,0:T(8,128)(2,1)S(1)}, bf16[64,1024]{1,0:T(8,128)(2,1)S(1)}, u32[]{:S(2)}, u32[]{:S(2)}) %collective-permute-start.34) | collective-permute-done | bytes 131104 | tf_op jit(solution)/shard_map/ppermute | solution.py:357
  114.2 5.6 %collective-permute-done.37 = bf16[64,1024]{1,0:T(8,128)(2,1)S(1)} collective-permute-done((bf16[64,1024]{1,0:T(8,128)(2,1)S(1)}, bf16[64,1024]{1,0:T(8,128)(2,1)S(1)}, u32[]{:S(2)}, u32[]{:S(2)}) %collective-permute-start.37) | collective-permute-done | bytes 131104 | tf_op jit(solution)/shard_map/ppermute | solution.py:357
  119.9 0.6 collective-permute-start.38
  120.5 4.4 %collective-permute-done.38.others_ref = bf16[1,64,1024]{2,1,0:T(8,128)(2,1)S(1)} collective-permute-done((bf16[1,64,1024]{2,1,0:T(8,128)(2,1)S(1)}, bf16[1,64,1024]{2,1,0:T(8,128)(2,1)S(1)}, u32[]{:S(2)}, u32[]{:S(2)}) %collective-permute-start.38) | collective-permute-done | bytes 131104 | tf_op jit(solution)/shard_map/ppermute | solution.py:357
  124.9 1.3 %finish.1 = bf16[64,2048]{1,0:T(8,128)(2,1)} custom-call(s32[3]{0:T(128)S(1)} %pad_add_fusion.row_ref.refs_0_, bf16[64,1024]{1,0:T(8,128)(2,1)S(1)} %fusion.15.own_ref, bf16[1,64,1024]{2,1,0:T(8,128)(2,1)S(1)} %collective-permute-done.38.others_ref), custom_call_target="tpu_custom_call" | custom-call | tf_op jit(solution)/shard_map/finish/pallas_call | solution.py:275
  (94 shorter events, 2.6 us)
Async XLA Ops:
  0.6 7.4 %collective-permute-start = (bf16[64,2048]{1,0:T(8,128)(2,1)}, bf16[64,2048]{1,0:T(8,128)(2,1)S(1)}, u32[]{:S(2)}, u32[]{:S(2)}) collective-permute-start(bf16[64,2048]{1,0:T(8,128)(2,1)} %hidden_ref.1), channel_id=1, source_target_pairs={{0,2},{2,0},{4,6},{6,4},{1,3},{3,1},{5,7},{7,5},{8,10},{10,8},{12,... | collective-permute-start | bytes 786440 | tf_op jit(solution)/shard_map/ppermute | solution.py:357
  1.1 12.2 %collective-permute-start.2 = (bf16[64,2048]{1,0:T(8,128)(2,1)}, bf16[64,2048]{1,0:T(8,128)(2,1)S(1)}, u32[]{:S(2)}, u32[]{:S(2)}) collective-permute-start(bf16[64,2048]{1,0:T(8,128)(2,1)} %hidden_ref.1), channel_id=1, source_target_pairs={{0,4},{2,6},{4,0},{6,2},{1,5},{3,7},{5,1},{7,3},{8,12},{10,14},{12... | collective-permute-start | bytes 786440 | tf_op jit(solution)/shard_map/ppermute | solution.py:357
  4.5 0.7 copy-start.14
  5.2 0.7 copy-start.15
  5.8 2.2 %copy-start.1 = (bf16[2048,576]{0,1:T(8,128)(2,1)S(1)}, bf16[2048,576]{0,1:T(8,128)(2,1)}, u32[]{:S(2)}) copy-start(bf16[2048,576]{0,1:T(8,128)(2,1)} %param.27) | copy-start | bytes 7077892
  5.8 2.2 %copy-start.2 = (bf16[4,384,576]{1,2,0:T(8,128)(2,1)S(1)}, bf16[4,384,576]{1,2,0:T(8,128)(2,1)}, u32[]{:S(2)}) copy-start(bf16[4,384,576]{1,2,0:T(8,128)(2,1)} %param.20) | copy-start | bytes 5308420
  5.8 2.6 %copy-start.3 = (bf16[2048,384]{1,0:T(8,128)(2,1)S(1)}, bf16[2048,384]{1,0:T(8,128)(2,1)}, u32[]{:S(2)}) copy-start(bf16[2048,384]{1,0:T(8,128)(2,1)} %refs_7_.3) | copy-start | bytes 4718596
  5.8 2.9 %copy-start.4 = (bf16[256,2048]{1,0:T(8,128)(2,1)S(1)}, bf16[256,2048]{1,0:T(8,128)(2,1)}, u32[]{:S(2)}) copy-start(bf16[256,2048]{1,0:T(8,128)(2,1)} %refs_12_.3) | copy-start | bytes 3145732
  5.8 2.9 %copy-start.8 = (bf16[2,128,512]{2,1,0:T(8,128)(2,1)S(1)}, bf16[2,128,512]{2,1,0:T(8,128)(2,1)}, u32[]{:S(2)}) copy-start(bf16[2,128,512]{2,1,0:T(8,128)(2,1)} %refs_10_.4) | copy-start | bytes 786436
  5.8 3.0 %copy-start.9 = (bf16[2,512,128]{2,1,0:T(8,128)(2,1)S(1)}, bf16[2,512,128]{2,1,0:T(8,128)(2,1)}, u32[]{:S(2)}) copy-start(bf16[2,512,128]{2,1,0:T(8,128)(2,1)} %refs_11_.3) | copy-start | bytes 786436
  5.8 3.1 %copy-start.10 = (bf16[64,2048]{1,0:T(8,128)(2,1)S(1)}, bf16[64,2048]{1,0:T(8,128)(2,1)}, u32[]{:S(2)}) copy-start(bf16[64,2048]{1,0:T(8,128)(2,1)} %hidden_ref.1) | copy-start | bytes 786436
  5.9 3.1 %copy-start.11 = (f32[2048]{0:T(1024)S(1)}, f32[2048]{0:T(1024)}, u32[]{:S(2)}) copy-start(f32[2048]{0:T(1024)} %param.25) | copy-start | bytes 24580
  5.9 3.1 %copy-start.12 = (f32[512]{0:T(512)S(1)}, f32[512]{0:T(512)}, u32[]{:S(2)}) copy-start(f32[512]{0:T(512)} %param.28) | copy-start | bytes 6148
  13.3 1.5 %collective-permute-start.3 = (bf16[64,2048]{1,0:T(8,128)(2,1)S(1)}, bf16[64,2048]{1,0:T(8,128)(2,1)S(1)}, u32[]{:S(2)}, u32[]{:S(2)}) collective-permute-start(bf16[64,2048]{1,0:T(8,128)(2,1)S(1)} %collective-permute-done.2.refs_0_), channel_id=1, source_target_pairs={{0,2},{2,0},{4,6},{6,4},{1,3},{3,1},{5,7},{7,5},{8,10},{10,8},{12,... | collective-permute-start | bytes 786440 | tf_op jit(solution)/shard_map/ppermute | solution.py:357
  18.7 11.8 %copy-start.16 = (s32[64,6]{0,1:T(8,128)S(1)}, s32[64,6]{0,1:T(8,128)}, u32[]{:S(2)}) copy-start(s32[64,6]{0,1:T(8,128)} %param.23) | copy-start | bytes 4612
  18.7 17.8 %copy-start.13 = (f32[2048]{0:T(1024)S(1)}, f32[2048]{0:T(1024)}, u32[]{:S(2)}) copy-start(f32[2048]{0:T(1024)} %param.32) | copy-start | bytes 24580
  18.7 1.6 %collective-permute-start.4 = (bf16[64,2048]{1,0:T(8,128)(2,1)S(1)}, bf16[64,2048]{1,0:T(8,128)(2,1)S(1)}, u32[]{:S(2)}, u32[]{:S(2)}) collective-permute-start(bf16[64,2048]{1,0:T(8,128)(2,1)S(1)} %get-tuple-element.36), channel_id=1, source_target_pairs={{0,2},{2,0},{4,6},{6,4},{1,3},{3,1},{5,7},{7,5},{8,10},{10,8},{12,... | collective-permute-start | bytes 786440 | tf_op jit(solution)/shard_map/ppermute | solution.py:357
  18.9 1.7 %collective-permute-start.1 = (bf16[64,2048]{1,0:T(8,128)(2,1)S(1)}, bf16[64,2048]{1,0:T(8,128)(2,1)S(1)}, u32[]{:S(2)}, u32[]{:S(2)}) collective-permute-start(bf16[64,2048]{1,0:T(8,128)(2,1)S(1)} %get-tuple-element.33), channel_id=1, source_target_pairs={{0,2},{2,0},{4,6},{6,4},{1,3},{3,1},{5,7},{7,5},{8,10},{10,8},{12,... | collective-permute-start | bytes 786440 | tf_op jit(solution)/shard_map/ppermute | solution.py:357
  20.4 8.4 %collective-permute-start.5 = (bf16[64,2048]{1,0:T(8,128)(2,1)S(1)}, bf16[64,2048]{1,0:T(8,128)(2,1)S(1)}, u32[]{:S(2)}, u32[]{:S(2)}) collective-permute-start(bf16[64,2048]{1,0:T(8,128)(2,1)S(1)} %add_convert_fusion.1), channel_id=1, source_target_pairs={{0,4},{2,6},{4,0},{6,2},{1,5},{3,7},{5,1},{7,3},{8,12},{10,14},{12... | collective-permute-start | bytes 786440 | tf_op jit(solution)/shard_map/ppermute | solution.py:357
  28.9 7.6 %collective-permute-start.6 = (bf16[64,2048]{1,0:T(8,128)(2,1)S(1)}, bf16[64,2048]{1,0:T(8,128)(2,1)S(1)}, u32[]{:S(2)}, u32[]{:S(2)}) collective-permute-start(bf16[64,2048]{1,0:T(8,128)(2,1)S(1)} %add_convert_fusion.keep_ref), channel_id=1, source_target_pairs={{0,1},{1,0},{2,3},{3,2},{4,5},{5,4},{6,7},{7,6},{8,9},{9,8},{10,11... | collective-permute-start | bytes 786440 | tf_op jit(solution)/shard_map/ppermute | solution.py:357
  36.5 20.4 %slice-start = ((s8[5767168]{0:T(1024)(128)(4,1)}), s8[4194304]{0:T(1024)(128)(4,1)S(1)}, s32[]{:S(2)}) async-start(s8[5767168]{0:T(1024)(128)(4,1)} %bitcast.70), calls=%async_computation | async-start | bytes 8388608
  36.5 20.4 %slice-start.1 = ((s8[5767168]{0:T(1024)(128)(4,1)}), s8[1572864]{0:T(1024)(128)(4,1)S(1)}, s32[]{:S(2)}) async-start(s8[5767168]{0:T(1024)(128)(4,1)} %bitcast.70), calls=%async_computation.1 | async-start | bytes 3145728
  36.5 20.4 %copy-start = (bf16[1,704,2048]{2,1,0:T(8,128)(2,1)S(1)}, bf16[1,704,2048]{2,1,0:T(8,128)(2,1)}, u32[]{:S(2)}) copy-start(bf16[1,704,2048]{2,1,0:T(8,128)(2,1)} %param.37) | copy-start | bytes 8650756
  36.5 20.4 %copy-start.5 = (bf16[2,2048,352]{1,2,0:T(8,128)(2,1)S(1)}, bf16[2,2048,352]{1,2,0:T(8,128)(2,1)}, u32[]{:S(2)}) copy-start(bf16[2,2048,352]{1,2,0:T(8,128)(2,1)} %param.34) | copy-start | bytes 8650756
  36.5 20.4 %copy-start.6 = (bf16[352,2048]{1,0:T(8,128)(2,1)S(1)}, bf16[352,2048]{1,0:T(8,128)(2,1)}, u32[]{:S(2)}) copy-start(bf16[352,2048]{1,0:T(8,128)(2,1)} %refs_10_.5) | copy-start | bytes 4325380
  36.6 20.4 %copy-start.7 = (bf16[2048,16]{0,1:T(8,128)(2,1)S(1)}, bf16[2048,16]{0,1:T(8,128)(2,1)}, u32[]{:S(2)}) copy-start(bf16[2048,16]{0,1:T(8,128)(2,1)} %param.33) | copy-start | bytes 196612
  37.4 7.4 %collective-permute-start.7 = (bf16[2,64,1152]{2,1,0:T(8,128)(2,1)S(1)}, bf16[2,64,1152]{2,1,0:T(8,128)(2,1)S(1)}, u32[]{:S(2)}, u32[]{:S(2)}) collective-permute-start(bf16[2,64,1152]{2,1,0:T(8,128)(2,1)S(1)} %get-tuple-element.38.refs_1_), channel_id=1, source_target_pairs={{0,4},{2,6},{4,0},{6,2},{1,5},{3,7},{5,1},{7,3},{8,12},{10,14},{12... | collective-permute-start | bytes 884744 | tf_op jit(solution)/shard_map/ppermute | solution.py:357
  38.0 8.6 %collective-permute-start.19 = (bf16[1,64,1152]{2,1,0:T(8,128)(2,1)S(1)}, bf16[1,64,1152]{2,1,0:T(8,128)(2,1)S(1)}, u32[]{:S(2)}, u32[]{:S(2)}) collective-permute-start(bf16[1,64,1152]{2,1,0:T(8,128)(2,1)S(1)} %get-tuple-element.45), channel_id=1, source_target_pairs={{0,24},{8,16},{16,8},{24,0},{1,25},{9,17},{17,9},{25,1},{2,26},{10... | collective-permute-start | bytes 442376 | tf_op jit(solution)/shard_map/ppermute | solution.py:357
  41.5 10.8 %collective-permute-start.20 = (bf16[1,64,1152]{2,1,0:T(8,128)(2,1)S(1)}, bf16[1,64,1152]{2,1,0:T(8,128)(2,1)S(1)}, u32[]{:S(2)}, u32[]{:S(2)}) collective-permute-start(bf16[1,64,1152]{2,1,0:T(8,128)(2,1)S(1)} %get-tuple-element.45), channel_id=1, source_target_pairs={{0,16},{8,24},{16,0},{24,8},{1,17},{9,25},{17,1},{25,9},{2,18},{10... | collective-permute-start | bytes 442376 | tf_op jit(solution)/shard_map/ppermute | solution.py:357
  41.5 12.0 %collective-permute-start.13 = (bf16[2,64,1152]{2,1,0:T(8,128)(2,1)S(1)}, bf16[2,64,1152]{2,1,0:T(8,128)(2,1)S(1)}, u32[]{:S(2)}, u32[]{:S(2)}) collective-permute-start(bf16[2,64,1152]{2,1,0:T(8,128)(2,1)S(1)} %get-tuple-element.38.refs_1_), channel_id=1, source_target_pairs={{0,8},{8,0},{16,24},{24,16},{1,9},{9,1},{17,25},{25,17},{2,10},{10... | collective-permute-start | bytes 884744 | tf_op jit(solution)/shard_map/ppermute | solution.py:357
  42.4 14.5 %collective-permute-start.8 = (bf16[2,64,1152]{2,1,0:T(8,128)(2,1)S(1)}, bf16[2,64,1152]{2,1,0:T(8,128)(2,1)S(1)}, u32[]{:S(2)}, u32[]{:S(2)}) collective-permute-start(bf16[2,64,1152]{2,1,0:T(8,128)(2,1)S(1)} %get-tuple-element.38.refs_1_), channel_id=1, source_target_pairs={{0,2},{2,0},{4,6},{6,4},{1,3},{3,1},{5,7},{7,5},{8,10},{10,8},{12,... | collective-permute-start | bytes 884744 | tf_op jit(solution)/shard_map/ppermute | solution.py:357
  44.8 12.1 %collective-permute-start.9 = (bf16[2,64,1152]{2,1,0:T(8,128)(2,1)S(1)}, bf16[2,64,1152]{2,1,0:T(8,128)(2,1)S(1)}, u32[]{:S(2)}, u32[]{:S(2)}) collective-permute-start(bf16[2,64,1152]{2,1,0:T(8,128)(2,1)S(1)} %collective-permute-done.7.refs_2_), channel_id=1, source_target_pairs={{0,2},{2,0},{4,6},{6,4},{1,3},{3,1},{5,7},{7,5},{8,10},{10,8},{12,... | collective-permute-start | bytes 884744 | tf_op jit(solution)/shard_map/ppermute | solution.py:357
  53.5 9.9 %collective-permute-start.14 = (bf16[2,64,1152]{2,1,0:T(8,128)(2,1)S(1)}, bf16[2,64,1152]{2,1,0:T(8,128)(2,1)S(1)}, u32[]{:S(2)}, u32[]{:S(2)}) collective-permute-start(bf16[2,64,1152]{2,1,0:T(8,128)(2,1)S(1)} %collective-permute-done.13.refs_1_), channel_id=1, source_target_pairs={{0,4},{2,6},{4,0},{6,2},{1,5},{3,7},{5,1},{7,3},{8,12},{10,14},{12... | collective-permute-start | bytes 884744 | tf_op jit(solution)/shard_map/ppermute | solution.py:357
  54.8 11.8 %collective-permute-start.22 = (bf16[1,2,64,1152]{3,2,0,1:T(8,128)(2,1)S(1)}, bf16[1,2,64,1152]{3,2,0,1:T(8,128)(2,1)S(1)}, u32[]{:S(2)}, u32[]{:S(2)}) collective-permute-start(bf16[1,2,64,1152]{3,2,0,1:T(8,128)(2,1)S(1)} %maximum_bitcast_fusion), channel_id=1, source_target_pairs={{0,4},{2,6},{4,0},{6,2},{1,5},{3,7},{5,1},{7,3},{8,12},{10,14},{12... | collective-permute-start | bytes 884744 | tf_op jit(solution)/shard_map/ppermute | solution.py:357
  55.5 12.7 %collective-permute-start.21 = (bf16[1,2,64,1152]{3,2,0,1:T(8,128)(2,1)S(1)}, bf16[1,2,64,1152]{3,2,0,1:T(8,128)(2,1)S(1)}, u32[]{:S(2)}, u32[]{:S(2)}) collective-permute-start(bf16[1,2,64,1152]{3,2,0,1:T(8,128)(2,1)S(1)} %maximum_bitcast_fusion), channel_id=1, source_target_pairs={{0,1},{1,0},{2,3},{3,2},{4,5},{5,4},{6,7},{7,6},{8,9},{9,8},{10,11... | collective-permute-start | bytes 884744 | tf_op jit(solution)/shard_map/ppermute | solution.py:357
  56.8 11.6 %collective-permute-start.15 = (bf16[2,64,1152]{2,1,0:T(8,128)(2,1)S(1)}, bf16[2,64,1152]{2,1,0:T(8,128)(2,1)S(1)}, u32[]{:S(2)}, u32[]{:S(2)}) collective-permute-start(bf16[2,64,1152]{2,1,0:T(8,128)(2,1)S(1)} %collective-permute-done.13.refs_1_), channel_id=1, source_target_pairs={{0,2},{2,0},{4,6},{6,4},{1,3},{3,1},{5,7},{7,5},{8,10},{10,8},{12,... | collective-permute-start | bytes 884744 | tf_op jit(solution)/shard_map/ppermute | solution.py:357
  62.2 11.3 %collective-permute-start.10 = (bf16[2,2,64,1024]{3,2,1,0:T(8,128)(2,1)S(1)}, bf16[2,2,64,1024]{3,2,1,0:T(8,128)(2,1)S(1)}, u32[]{:S(2)}, u32[]{:S(2)}) collective-permute-start(bf16[2,2,64,1024]{3,2,1,0:T(8,128)(2,1)S(1)} %get-tuple-element.41), channel_id=1, source_target_pairs={{0,2},{2,0},{4,6},{6,4},{1,3},{3,1},{5,7},{7,5},{8,10},{10,8},{12,... | collective-permute-start | bytes 1572872 | tf_op jit(solution)/shard_map/ppermute | solution.py:357
  63.4 5.0 %collective-permute-start.16 = (bf16[2,64,1152]{2,1,0:T(8,128)(2,1)S(1)}, bf16[2,64,1152]{2,1,0:T(8,128)(2,1)S(1)}, u32[]{:S(2)}, u32[]{:S(2)}) collective-permute-start(bf16[2,64,1152]{2,1,0:T(8,128)(2,1)S(1)} %collective-permute-done.14.refs_2_), channel_id=1, source_target_pairs={{0,2},{2,0},{4,6},{6,4},{1,3},{3,1},{5,7},{7,5},{8,10},{10,8},{12,... | collective-permute-start | bytes 884744 | tf_op jit(solution)/shard_map/ppermute | solution.py:357
  66.6 6.7 %collective-permute-start.23 = (bf16[1,2,64,1152]{3,2,0,1:T(8,128)(2,1)S(1)}, bf16[1,2,64,1152]{3,2,0,1:T(8,128)(2,1)S(1)}, u32[]{:S(2)}, u32[]{:S(2)}) collective-permute-start(bf16[1,2,64,1152]{3,2,0,1:T(8,128)(2,1)S(1)} %collective-permute-done.22), channel_id=1, source_target_pairs={{0,1},{1,0},{2,3},{3,2},{4,5},{5,4},{6,7},{7,6},{8,9},{9,8},{10,11... | collective-permute-start | bytes 884744 | tf_op jit(solution)/shard_map/ppermute | solution.py:357
  68.3 7.7 %collective-permute-start.26 = (bf16[2,64,1152]{2,1,0:T(8,128)(2,1)S(1)}, bf16[2,64,1152]{2,1,0:T(8,128)(2,1)S(1)}, u32[]{:S(2)}, u32[]{:S(2)}) collective-permute-start(bf16[2,64,1152]{2,1,0:T(8,128)(2,1)S(1)} %get-tuple-element.58.refs_1_), channel_id=1, source_target_pairs={{0,2},{2,0},{4,6},{6,4},{1,3},{3,1},{5,7},{7,5},{8,10},{10,8},{12,... | collective-permute-start | bytes 884744 | tf_op jit(solution)/shard_map/ppermute | solution.py:357
  72.5 11.8 %collective-permute-start.17 = (bf16[2,2,64,1024]{3,2,1,0:T(8,128)(2,1)S(1)}, bf16[2,2,64,1024]{3,2,1,0:T(8,128)(2,1)S(1)}, u32[]{:S(2)}, u32[]{:S(2)}) collective-permute-start(bf16[2,2,64,1024]{3,2,1,0:T(8,128)(2,1)S(1)} %get-tuple-element.44), channel_id=1, source_target_pairs={{0,2},{2,0},{4,6},{6,4},{1,3},{3,1},{5,7},{7,5},{8,10},{10,8},{12,... | collective-permute-start | bytes 1572872 | tf_op jit(solution)/shard_map/ppermute | solution.py:357
  73.4 2.3 %collective-permute-start.27 = (bf16[2,64,1152]{2,1,0:T(8,128)(2,1)S(1)}, bf16[2,64,1152]{2,1,0:T(8,128)(2,1)S(1)}, u32[]{:S(2)}, u32[]{:S(2)}) collective-permute-start(bf16[2,64,1152]{2,1,0:T(8,128)(2,1)S(1)} %get-tuple-element.56.refs_2_), channel_id=1, source_target_pairs={{0,2},{2,0},{4,6},{6,4},{1,3},{3,1},{5,7},{7,5},{8,10},{10,8},{12,... | collective-permute-start | bytes 884744 | tf_op jit(solution)/shard_map/ppermute | solution.py:357
  73.7 8.8 %collective-permute-start.11 = (bf16[2,64,1024]{2,1,0:T(8,128)(2,1)S(1)}, bf16[2,64,1024]{2,1,0:T(8,128)(2,1)S(1)}, u32[]{:S(2)}, u32[]{:S(2)}) collective-permute-start(bf16[2,64,1024]{2,1,0:T(8,128)(2,1)S(1)} %fusion.3), channel_id=1, source_target_pairs={{0,4},{2,6},{4,0},{6,2},{1,5},{3,7},{5,1},{7,3},{8,12},{10,14},{12... | collective-permute-start | bytes 786440 | tf_op jit(solution)/shard_map/ppermute | solution.py:357
  75.5 10.6 %collective-permute-start.24 = (bf16[2,64,1152]{2,1,0:T(8,128)(2,1)S(1)}, bf16[2,64,1152]{2,1,0:T(8,128)(2,1)S(1)}, u32[]{:S(2)}, u32[]{:S(2)}) collective-permute-start(bf16[2,64,1152]{2,1,0:T(8,128)(2,1)S(1)} %get-tuple-element.59.refs_1_), channel_id=1, source_target_pairs={{0,2},{2,0},{4,6},{6,4},{1,3},{3,1},{5,7},{7,5},{8,10},{10,8},{12,... | collective-permute-start | bytes 884744 | tf_op jit(solution)/shard_map/ppermute | solution.py:357
  75.7 10.4 %collective-permute-start.25 = (bf16[2,64,1152]{2,1,0:T(8,128)(2,1)S(1)}, bf16[2,64,1152]{2,1,0:T(8,128)(2,1)S(1)}, u32[]{:S(2)}, u32[]{:S(2)}) collective-permute-start(bf16[2,64,1152]{2,1,0:T(8,128)(2,1)S(1)} %get-tuple-element.57.refs_2_), channel_id=1, source_target_pairs={{0,2},{2,0},{4,6},{6,4},{1,3},{3,1},{5,7},{7,5},{8,10},{10,8},{12,... | collective-permute-start | bytes 884744 | tf_op jit(solution)/shard_map/ppermute | solution.py:357
  79.9 10.2 %collective-permute-start.31 = (bf16[2,2,64,1024]{3,2,1,0:T(8,128)(2,1)S(1)}, bf16[2,2,64,1024]{3,2,1,0:T(8,128)(2,1)S(1)}, u32[]{:S(2)}, u32[]{:S(2)}) collective-permute-start(bf16[2,2,64,1024]{3,2,1,0:T(8,128)(2,1)S(1)} %get-tuple-element.48), channel_id=1, source_target_pairs={{0,2},{2,0},{4,6},{6,4},{1,3},{3,1},{5,7},{7,5},{8,10},{10,8},{12,... | collective-permute-start | bytes 1572872 | tf_op jit(solution)/shard_map/ppermute | solution.py:357
  82.6 29.4 %collective-permute-start.12 = (bf16[1,64,1024]{2,1,0:T(8,128)(2,1)S(1)}, bf16[1,64,1024]{2,1,0:T(8,128)(2,1)S(1)}, u32[]{:S(2)}, u32[]{:S(2)}) collective-permute-start(bf16[1,64,1024]{2,1,0:T(8,128)(2,1)S(1)} %slice.177), channel_id=1, source_target_pairs={{0,1},{1,0},{2,3},{3,2},{4,5},{5,4},{6,7},{7,6},{8,9},{9,8},{10,11... | collective-permute-start | bytes 393224 | tf_op jit(solution)/shard_map/ppermute | solution.py:357
  84.5 8.2 %collective-permute-start.18 = (bf16[2,64,1024]{2,1,0:T(8,128)(2,1)S(1)}, bf16[2,64,1024]{2,1,0:T(8,128)(2,1)S(1)}, u32[]{:S(2)}, u32[]{:S(2)}) collective-permute-start(bf16[2,64,1024]{2,1,0:T(8,128)(2,1)S(1)} %fusion.4), channel_id=1, source_target_pairs={{0,4},{2,6},{4,0},{6,2},{1,5},{3,7},{5,1},{7,3},{8,12},{10,14},{12... | collective-permute-start | bytes 786440 | tf_op jit(solution)/shard_map/ppermute | solution.py:357
  89.9 2.0 %collective-permute-start.28 = (bf16[2,2,64,1024]{3,2,1,0:T(8,128)(2,1)S(1)}, bf16[2,2,64,1024]{3,2,1,0:T(8,128)(2,1)S(1)}, u32[]{:S(2)}, u32[]{:S(2)}) collective-permute-start(bf16[2,2,64,1024]{3,2,1,0:T(8,128)(2,1)S(1)} %get-tuple-element.51), channel_id=1, source_target_pairs={{0,2},{2,0},{4,6},{6,4},{1,3},{3,1},{5,7},{7,5},{8,10},{10,8},{12,... | collective-permute-start | bytes 1572872 | tf_op jit(solution)/shard_map/ppermute | solution.py:357
  90.3 8.8 %collective-permute-start.32 = (bf16[2,64,1024]{2,1,0:T(8,128)(2,1)S(1)}, bf16[2,64,1024]{2,1,0:T(8,128)(2,1)S(1)}, u32[]{:S(2)}, u32[]{:S(2)}) collective-permute-start(bf16[2,64,1024]{2,1,0:T(8,128)(2,1)S(1)} %fusion.5), channel_id=1, source_target_pairs={{0,4},{2,6},{4,0},{6,2},{1,5},{3,7},{5,1},{7,3},{8,12},{10,14},{12... | collective-permute-start | bytes 786440 | tf_op jit(solution)/shard_map/ppermute | solution.py:357
  92.1 12.8 %collective-permute-start.35 = (bf16[1,2,64,1024]{3,2,1,0:T(8,128)(2,1)S(1)}, bf16[1,2,64,1024]{3,2,1,0:T(8,128)(2,1)S(1)}, u32[]{:S(2)}, u32[]{:S(2)}) collective-permute-start(bf16[1,2,64,1024]{3,2,1,0:T(8,128)(2,1)S(1)} %slice.174), channel_id=1, source_target_pairs={{0,1},{1,0},{2,3},{3,2},{4,5},{5,4},{6,7},{7,6},{8,9},{9,8},{10,11... | collective-permute-start | bytes 786440 | tf_op jit(solution)/shard_map/ppermute | solution.py:357
  92.9 11.3 %collective-permute-start.29 = (bf16[1,64,1024]{2,1,0:T(8,128)(2,1)S(1)}, bf16[1,64,1024]{2,1,0:T(8,128)(2,1)S(1)}, u32[]{:S(2)}, u32[]{:S(2)}) collective-permute-start(bf16[1,64,1024]{2,1,0:T(8,128)(2,1)S(1)} %slice.176), channel_id=1, source_target_pairs={{0,1},{1,0},{2,3},{3,2},{4,5},{5,4},{6,7},{7,6},{8,9},{9,8},{10,11... | collective-permute-start | bytes 393224 | tf_op jit(solution)/shard_map/ppermute | solution.py:357
  99.1 7.0 %collective-permute-start.33 = (bf16[1,64,1024]{2,1,0:T(8,128)(2,1)S(1)}, bf16[1,64,1024]{2,1,0:T(8,128)(2,1)S(1)}, u32[]{:S(2)}, u32[]{:S(2)}) collective-permute-start(bf16[1,64,1024]{2,1,0:T(8,128)(2,1)S(1)} %slice.175), channel_id=1, source_target_pairs={{0,1},{1,0},{2,3},{3,2},{4,5},{5,4},{6,7},{7,6},{8,9},{9,8},{10,11... | collective-permute-start | bytes 393224 | tf_op jit(solution)/shard_map/ppermute | solution.py:357
  104.2 7.8 %collective-permute-start.30 = (bf16[64,1024]{1,0:T(8,128)(2,1)S(1)}, bf16[64,1024]{1,0:T(8,128)(2,1)S(1)}, u32[]{:S(2)}, u32[]{:S(2)}) collective-permute-start(bf16[64,1024]{1,0:T(8,128)(2,1)S(1)} %fusion.17), channel_id=1, source_target_pairs={{0,8},{8,0},{16,24},{24,16},{1,9},{9,1},{17,25},{25,17},{2,10},{10... | collective-permute-start | bytes 393224 | tf_op jit(solution)/shard_map/ppermute | solution.py:357
  105.0 5.0 %collective-permute-start.36 = (bf16[64,1024]{1,0:T(8,128)(2,1)S(1)}, bf16[64,1024]{1,0:T(8,128)(2,1)S(1)}, u32[]{:S(2)}, u32[]{:S(2)}) collective-permute-start(bf16[64,1024]{1,0:T(8,128)(2,1)S(1)} %fusion.19), channel_id=1, source_target_pairs={{0,4},{2,6},{4,0},{6,2},{1,5},{3,7},{5,1},{7,3},{8,12},{10,14},{12... | collective-permute-start | bytes 393224 | tf_op jit(solution)/shard_map/ppermute | solution.py:357
  106.2 8.0 %collective-permute-start.34 = (bf16[64,1024]{1,0:T(8,128)(2,1)S(1)}, bf16[64,1024]{1,0:T(8,128)(2,1)S(1)}, u32[]{:S(2)}, u32[]{:S(2)}) collective-permute-start(bf16[64,1024]{1,0:T(8,128)(2,1)S(1)} %fusion.18), channel_id=1, source_target_pairs={{0,24},{8,16},{16,8},{24,0},{1,25},{9,17},{17,9},{25,1},{2,26},{10... | collective-permute-start | bytes 393224 | tf_op jit(solution)/shard_map/ppermute | solution.py:357
  110.1 9.7 %collective-permute-start.37 = (bf16[64,1024]{1,0:T(8,128)(2,1)S(1)}, bf16[64,1024]{1,0:T(8,128)(2,1)S(1)}, u32[]{:S(2)}, u32[]{:S(2)}) collective-permute-start(bf16[64,1024]{1,0:T(8,128)(2,1)S(1)} %fusion.7), channel_id=1, source_target_pairs={{0,16},{8,24},{16,0},{24,8},{1,17},{9,25},{17,1},{25,9},{2,18},{10... | collective-permute-start | bytes 393224 | tf_op jit(solution)/shard_map/ppermute | solution.py:357
  119.9 5.0 %collective-permute-start.38 = (bf16[1,64,1024]{2,1,0:T(8,128)(2,1)S(1)}, bf16[1,64,1024]{2,1,0:T(8,128)(2,1)S(1)}, u32[]{:S(2)}, u32[]{:S(2)}) collective-permute-start(bf16[1,64,1024]{2,1,0:T(8,128)(2,1)S(1)} %bitcast.89), channel_id=1, source_target_pairs={{0,1},{1,0},{2,3},{3,2},{4,5},{5,4},{6,7},{7,6},{8,9},{9,8},{10,11... | collective-permute-start | bytes 393224 | tf_op jit(solution)/shard_map/ppermute | solution.py:357

commit v9 on v8

--- a/solution.py
+++ b/solution.py
@@ -400,13 +400,10 @@
         value_absorb,
         output_weight,
     )
+    far_near = swap(after(far, tables[0]), "row", n_row, 1)
+    far_keep, far_send = attention_part(False, 2, indices, (far, far_near), cache, tables, weights)
     own_keep, own_send, accepted_latents = attention_part(
-        True, 0, indices, (hidden, near), cache, tables, weights
-    )
-    far = after(far, own_send)
-    far_near = swap(far, "row", n_row, 1)
-    far_keep, far_send = attention_part(
-        False, 2, indices, (far, far_near), cache, tables, weights
+        True, 0, indices, (hidden, after(near, far_send)), cache, tables, weights
     )
 
     def fold(keep, sent):
@@ -431,39 +428,40 @@
         rest, rest_far = col_gather(rest, n_col), col_gather(rest_far, n_col)
         blocks += [rest[:, k] for k in range(rest.shape[1])]
         fars += [rest_far[:, k] for k in range(rest.shape[1])]
-    sends, folds, sums, returns = [], [], [], []
+    sends, cores, sums = [], [], []
     for k, s in enumerate(distances):
         near = swap(blocks[k], "row", n_row, 1)
-        far = fars[k]
-        far_near = swap(far, "row", n_row, 1)
+        far_near = swap(fars[k], "row", n_row, 1)
         if k:
-            far_near = after(far_near, *sends, *folds[: k - 1], *returns[: max(0, k - 2)])
+            far_near = after(far_near, *sends, *cores[: k - 1])
         keep, send = expert_part(
             indices,
             n_col,
             k < 3,
-            (blocks[k], far, near, far_near),
+            (blocks[k], fars[k], near, far_near),
             own_expert,
             router,
             routed_weights,
             () if s else shared_weights,
         )
         sends.append(send)
-        near_sum = keep + swap(send, "row", n_row, 1).astype(jnp.float32)
-        fold = near_sum[1] if k < 3 else near_sum[n_col // 2 :]
-        folds.append(fold.astype(bf16))
-        sums.append(near_sum)
+        cores.append(swap(send, "row", n_row, 1))
+        sums.append(keep + cores[k].astype(jnp.float32))
+    parts = []
+    arrivals = []
+    for k in reversed(range(n_req)):
         if k < 3:
-            returns.append(swap(folds[k], "row", n_row, 2))
-    parts = []
-    for k, near_sum in enumerate(sums):
-        if k < 3:
-            from_far = after(returns[k], *folds[-1:]) if k else returns[k]
-            part = col_scatter(near_sum[0] + from_far.astype(jnp.float32), n_col)[0]
+            from_far = swap(sums[k][1].astype(bf16), "row", n_row, 2)
+            from_far = after(from_far, *(cores[-1:] if k == 2 else arrivals))
+            part = sums[k][0] + from_far.astype(jnp.float32)
+            part, _ = col_scatter(part, n_col, arrivals if k == 2 else ())
+            part = part[0]
         else:
-            part = col_scatter(near_sum, n_col)[0]
+            part, arrivals = col_scatter(sums[k], n_col)
+            part = part[0]
             part = part[0] + swap(part[1].astype(bf16), "row", n_row, 2).astype(jnp.float32)
         parts.append(part.astype(bf16) if k else part)
+    parts.reverse()
     total = parts[0]
     for s, part in zip(distances[1:], parts[1:]):
         total = total + swap(part, "req", n_req, s).astype(jnp.float32)
@@ -481,13 +479,15 @@
     return values
 
 
-def col_scatter(values, n_col):
+def col_scatter(values, n_col, first=()):
     bits = n_col // 2
+    arrived = []
     while bits:
         received = swap(values[bits:].astype(jnp.bfloat16), "col", n_col, bits)
-        values = values[:bits] + received.astype(jnp.float32)
+        arrived.append(after(received, *first))
+        values = values[:bits] + arrived[-1].astype(jnp.float32)
         bits //= 2
-    return values
+    return values, arrived
 
 
 def col_parts(values, n_col):

time: 126 us -> 122 us (0.968)
  waiting for transfers between devices: 59 us -> 52.7 us
  starting transfers between devices: 31.9 us -> 35 us
    ppermute x39, waiting for transfers between devices: 59 us -> 52.7 us  [swap(): return lax.ppermute(values, axis, [(i, i ^ bits) for i in range(size)])]
    ppermute x39, starting transfers between devices: 31.9 us -> 35 us  [swap(): return lax.ppermute(values, axis, [(i, i ^ bits) for i in range(size)])]
  transfers between devices with their start and end apart: 39 -> 39, of which waited for: 21 -> 20; matrix products, arithmetic and copies ran while one was open for 1% -> 1% of each run, Pallas kernels for 19% -> 22%
where the time goes in v9:
time: 122 us
  waiting for transfers between devices  52.7 us (43%)
  starting transfers between devices  35 us (29%)
  Pallas kernels  29.3 us (24%)
  local copies, waits for them, and re-layouts  1.81 us (1%)
  between operations  1.8 us (1%)
  other arithmetic  1.47 us (1%)
    ppermute x39, waiting for transfers between devices, swap(): return lax.ppermute(values, axis, [(i, i ^ bits) for i in range(size)])  52.7 us
    ppermute x39, starting transfers between devices, swap(): return lax.ppermute(values, axis, [(i, i ^ bits) for i in range(size)])  35 us
    pallas_call x4, Pallas kernels, expert_part(): pl.pallas_call(functools.partial(expert_kernel, bool(shared_weights), far...  16.9 us
    pallas_call x2, Pallas kernels, attention_part(): pl.pallas_call(functools.partial(attention_kernel, first, place), out_sha...  8.21 us
  transfers between devices with their start and end apart: 39, of which 20 were waited for; matrix products, arithmetic and copies ran while one was open for 1% of the time, Pallas kernels for 22%

profile of v9, /device:TPU:0, one launch (start us, length us, event | category | flops | bytes accessed | tf_op | source)
XLA Modules:
  0.0 122.1 jit_solution(12768021305629736253)
XLA Ops:
  0.6 3.0 %collective-permute-start.1 = (bf16[64,2048]{1,0:T(8,128)(2,1)}, bf16[64,2048]{1,0:T(8,128)(2,1)S(1)}, u32[]{:S(2)}, u32[]{:S(2)}) collective-permute-start(bf16[64,2048]{1,0:T(8,128)(2,1)} %hidden_ref.1), channel_id=1, source_target_pairs={{0,4},{2,6},{4,0},{6,2},{1,5},{3,7},{5,1},{7,3},{8,12},{10,14},{12... | collective-permute-start | bytes 786440 | tf_op jit(solution)/shard_map/ppermute | solution.py:357
  4.4 0.7 copy-done.14
  5.1 0.7 copy-done.15
  5.8 2.1 %trees.1 = (f32[4,64,64]{2,1,0:T(8,128)S(1)}, f32[4,64,65]{2,1,0:T(8,128)S(1)}, bf16[64,64]{1,0:T(8,128)(2,1)S(1)}, f32[1,16]{1,0:T(1,128)S(1)}) custom-call(s32[3]{0:T(128)S(1)} %pad_add_fusion.row_ref.refs_0_, s32[4]{0:T(128)S(1)} %copy-done.15, s32[1]{0:T(128)S(6)} %copy.24.accepted_ref, s32[4,64]{1,0:T(4,128)S(1)} %copy-done.14), custom_call_target="tpu_custom_call" | custom-call | flops 20000000000 | bytes 1 | tf_op jit(solution)/shard_map/trees/pallas_call | solution.py:110
  7.9 2.2 %collective-permute-done.1.refs_0_ = bf16[64,2048]{1,0:T(8,128)(2,1)S(1)} collective-permute-done((bf16[64,2048]{1,0:T(8,128)(2,1)}, bf16[64,2048]{1,0:T(8,128)(2,1)S(1)}, u32[]{:S(2)}, u32[]{:S(2)}) %collective-permute-start.1) | collective-permute-done | bytes 262176 | tf_op jit(solution)/shard_map/ppermute | solution.py:357
  10.2 0.5 collective-permute-start
  10.7 1.0 collective-permute-done.2.refs_1_
  11.8 3.8 %attention.2 = (f32[64,2048]{1,0:T(8,128)S(1)}, bf16[64,2048]{1,0:T(8,128)(2,1)S(1)}) custom-call(s32[3]{0:T(128)S(1)} %pad_add_fusion.row_ref.refs_0_, bf16[64,2048]{1,0:T(8,128)(2,1)S(1)} %collective-permute-done.1.refs_0_, bf16[64,2048]{1,0:T(8,128)(2,1)S(1)} %collective-permute-done.2.refs_1_, bf16[4,576,384]{2,1,0:T(8,128)(2,1)S(1)} %bitcast.82, ...), custom_call_target="tpu_custom_call" | custom-call | flops 1 | bytes 1 | tf_op jit(solution)/shard_map/attention/pallas_call | solution.py:211
  15.6 0.2 collective-permute-start.4
  15.8 4.4 %attention.3 = (f32[64,2048]{1,0:T(8,128)S(1)}, bf16[64,2048]{1,0:T(8,128)(2,1)S(1)}, bf16[1,64,576]{2,1,0:T(8,128)(2,1)}) custom-call(s32[3]{0:T(128)S(1)} %pad_add_fusion.row_ref.refs_0_, bf16[64,2048]{1,0:T(8,128)(2,1)S(1)} %copy-done.10, bf16[64,2048]{1,0:T(8,128)(2,1)S(1)} %collective-permute-done.refs_1_, bf16[4,576,384]{2,1,0:T(8,128)(2,1)S(1)} %bitcast.83, ...), custom_call_target="tpu_custom_call" | custom-call | flops 1 | bytes 1 | tf_op jit(solution)/shard_map/attention/pallas_call | solution.py:211
  20.2 0.4 collective-permute-start.3
  20.6 1.8 %collective-permute-start.5 = (bf16[64,2048]{1,0:T(8,128)(2,1)S(1)}, bf16[64,2048]{1,0:T(8,128)(2,1)S(1)}, u32[]{:S(2)}, u32[]{:S(2)}) collective-permute-start(bf16[64,2048]{1,0:T(8,128)(2,1)S(1)} %add_convert_fusion.1), channel_id=1, source_target_pairs={{0,4},{2,6},{4,0},{6,2},{1,5},{3,7},{5,1},{7,3},{8,12},{10,14},{12... | collective-permute-start | bytes 786440 | tf_op jit(solution)/shard_map/ppermute | solution.py:357
  22.4 6.6 %collective-permute-done.5 = bf16[64,2048]{1,0:T(8,128)(2,1)S(1)} collective-permute-done((bf16[64,2048]{1,0:T(8,128)(2,1)S(1)}, bf16[64,2048]{1,0:T(8,128)(2,1)S(1)}, u32[]{:S(2)}, u32[]{:S(2)}) %collective-permute-start.5) | collective-permute-done | bytes 262176 | tf_op jit(solution)/shard_map/ppermute | solution.py:357
  29.1 1.8 %collective-permute-start.6 = (bf16[64,2048]{1,0:T(8,128)(2,1)S(1)}, bf16[64,2048]{1,0:T(8,128)(2,1)S(1)}, u32[]{:S(2)}, u32[]{:S(2)}) collective-permute-start(bf16[64,2048]{1,0:T(8,128)(2,1)S(1)} %add_convert_fusion.keep_ref), channel_id=1, source_target_pairs={{0,1},{1,0},{2,3},{3,2},{4,5},{5,4},{6,7},{7,6},{8,9},{9,8},{10,11... | collective-permute-start | bytes 786440 | tf_op jit(solution)/shard_map/ppermute | solution.py:357
  30.9 0.1 fusion.16
  31.1 5.6 %collective-permute-done.6 = bf16[64,2048]{1,0:T(8,128)(2,1)S(1)} collective-permute-done((bf16[64,2048]{1,0:T(8,128)(2,1)S(1)}, bf16[64,2048]{1,0:T(8,128)(2,1)S(1)}, u32[]{:S(2)}, u32[]{:S(2)}) %collective-permute-start.6) | collective-permute-done | bytes 262176 | tf_op jit(solution)/shard_map/ppermute | solution.py:357
  36.7 0.8 join.1
  37.5 1.8 %collective-permute-start.7 = (bf16[2,64,1152]{2,1,0:T(8,128)(2,1)S(1)}, bf16[2,64,1152]{2,1,0:T(8,128)(2,1)S(1)}, u32[]{:S(2)}, u32[]{:S(2)}) collective-permute-start(bf16[2,64,1152]{2,1,0:T(8,128)(2,1)S(1)} %get-tuple-element.42.refs_1_), channel_id=1, source_target_pairs={{0,4},{2,6},{4,0},{6,2},{1,5},{3,7},{5,1},{7,3},{8,12},{10,14},{12... | collective-permute-start | bytes 884744 | tf_op jit(solution)/shard_map/ppermute | solution.py:357
  39.3 3.6 %collective-permute-start.12 = (bf16[1,64,1152]{2,1,0:T(8,128)(2,1)S(1)}, bf16[1,64,1152]{2,1,0:T(8,128)(2,1)S(1)}, u32[]{:S(2)}, u32[]{:S(2)}) collective-permute-start(bf16[1,64,1152]{2,1,0:T(8,128)(2,1)S(1)} %get-tuple-element.46), channel_id=1, source_target_pairs={{0,24},{8,16},{16,8},{24,0},{1,25},{9,17},{17,9},{25,1},{2,26},{10... | collective-permute-start | bytes 442376 | tf_op jit(solution)/shard_map/ppermute | solution.py:357
  43.0 0.8 collective-permute-start.14
  43.7 1.1 collective-permute-done.7.refs_2_
  44.9 3.0 %collective-permute-done.12 = bf16[1,64,1152]{2,1,0:T(8,128)(2,1)S(1)} collective-permute-done((bf16[1,64,1152]{2,1,0:T(8,128)(2,1)S(1)}, bf16[1,64,1152]{2,1,0:T(8,128)(2,1)S(1)}, u32[]{:S(2)}, u32[]{:S(2)}) %collective-permute-start.12) | collective-permute-done | bytes 147488 | tf_op jit(solution)/shard_map/ppermute | solution.py:357
  47.9 5.8 %collective-permute-done.13 = bf16[1,64,1152]{2,1,0:T(8,128)(2,1)S(1)} collective-permute-done((bf16[1,64,1152]{2,1,0:T(8,128)(2,1)S(1)}, bf16[1,64,1152]{2,1,0:T(8,128)(2,1)S(1)}, u32[]{:S(2)}, u32[]{:S(2)}) %collective-permute-start.13) | collective-permute-done | bytes 147488 | tf_op jit(solution)/shard_map/ppermute | solution.py:357
  53.8 0.8 collective-permute-done.14.refs_1_
  54.6 0.5 collective-permute-start.20
  55.1 1.5 %collective-permute-start.16 = (bf16[1,2,64,1152]{3,2,0,1:T(8,128)(2,1)S(1)}, bf16[1,2,64,1152]{3,2,0,1:T(8,128)(2,1)S(1)}, u32[]{:S(2)}, u32[]{:S(2)}) collective-permute-start(bf16[1,2,64,1152]{3,2,0,1:T(8,128)(2,1)S(1)} %maximum_bitcast_fusion), channel_id=1, source_target_pairs={{0,4},{2,6},{4,0},{6,2},{1,5},{3,7},{5,1},{7,3},{8,12},{10,14},{12... | collective-permute-start | bytes 884744 | tf_op jit(solution)/shard_map/ppermute | solution.py:357
  56.7 1.5 %collective-permute-start.15 = (bf16[1,2,64,1152]{3,2,0,1:T(8,128)(2,1)S(1)}, bf16[1,2,64,1152]{3,2,0,1:T(8,128)(2,1)S(1)}, u32[]{:S(2)}, u32[]{:S(2)}) collective-permute-start(bf16[1,2,64,1152]{3,2,0,1:T(8,128)(2,1)S(1)} %maximum_bitcast_fusion), channel_id=1, source_target_pairs={{0,1},{1,0},{2,3},{3,2},{4,5},{5,4},{6,7},{7,6},{8,9},{9,8},{10,11... | collective-permute-start | bytes 884744 | tf_op jit(solution)/shard_map/ppermute | solution.py:357
  58.4 5.2 %experts.4 = (f32[2,2,64,1024]{3,2,1,0:T(8,128)S(1)}, bf16[2,2,64,1024]{3,2,1,0:T(8,128)(2,1)S(1)}) custom-call(s32[3]{0:T(128)S(1)} %pad_add_fusion.row_ref.refs_0_, bf16[2,64,1152]{2,1,0:T(8,128)(2,1)S(1)} %get-tuple-element.42.refs_1_, bf16[2,64,1152]{2,1,0:T(8,128)(2,1)S(1)} %collective-permute-done.7.refs_2_, ...), custom_call_target="tpu_custom_call" | custom-call | flops 1 | bytes 1 | tf_op jit(solution)/shard_map/experts/pallas_call | solution.py:337
  63.5 0.6 collective-permute-start.10
  64.1 0.5 collective-permute-done.20.refs_2_
  64.6 3.6 %collective-permute-done.16 = bf16[1,2,64,1152]{3,2,0,1:T(8,128)(2,1)S(1)} collective-permute-done((bf16[1,2,64,1152]{3,2,0,1:T(8,128)(2,1)S(1)}, bf16[1,2,64,1152]{3,2,0,1:T(8,128)(2,1)S(1)}, u32[]{:S(2)}, u32[]{:S(2)}) %collective-permute-start.16) | collective-permute-done | bytes 294944 | tf_op jit(solution)/shard_map/ppermute | solution.py:357
  68.2 1.5 %collective-permute-start.17 = (bf16[1,2,64,1152]{3,2,0,1:T(8,128)(2,1)S(1)}, bf16[1,2,64,1152]{3,2,0,1:T(8,128)(2,1)S(1)}, u32[]{:S(2)}, u32[]{:S(2)}) collective-permute-start(bf16[1,2,64,1152]{3,2,0,1:T(8,128)(2,1)S(1)} %collective-permute-done.16), channel_id=1, source_target_pairs={{0,1},{1,0},{2,3},{3,2},{4,5},{5,4},{6,7},{7,6},{8,9},{9,8},{10,11... | collective-permute-start | bytes 884744 | tf_op jit(solution)/shard_map/ppermute | solution.py:357
  69.7 4.0 %experts.5 = (f32[2,2,64,1024]{3,2,1,0:T(8,128)S(1)}, bf16[2,2,64,1024]{3,2,1,0:T(8,128)(2,1)S(1)}) custom-call(s32[3]{0:T(128)S(1)} %pad_add_fusion.row_ref.refs_0_, bf16[2,64,1152]{2,1,0:T(8,128)(2,1)S(1)} %collective-permute-done.14.refs_1_, bf16[2,64,1152]{2,1,0:T(8,128)(2,1)S(1)} %collective-permute-done.20.refs_2_, ...), custom_call_target="tpu_custom_call" | custom-call | flops 1 | bytes 1 | tf_op jit(solution)/shard_map/experts/pallas_call | solution.py:337
  73.9 1.0 collective-permute-done.17
  75.1 0.6 collective-permute-start.23
  75.7 0.4 collective-permute-start.19
  76.2 0.1 convert_add_fusion.3
  76.3 0.3 collective-permute-done.24.refs_4_
  76.6 0.4 collective-permute-done.23.refs_3_
  77.0 3.8 %experts.6 = (f32[2,2,64,1024]{3,2,1,0:T(8,128)S(1)}, bf16[2,2,64,1024]{3,2,1,0:T(8,128)(2,1)S(1)}) custom-call(s32[3]{0:T(128)S(1)} %pad_add_fusion.row_ref.refs_0_, bf16[2,64,1152]{2,1,0:T(8,128)(2,1)S(1)} %get-tuple-element.64.refs_1_, bf16[2,64,1152]{2,1,0:T(8,128)(2,1)S(1)} %get-tuple-element.62.refs_2_, ...), custom_call_target="tpu_custom_call" | custom-call | flops 1 | bytes 1 | tf_op jit(solution)/shard_map/experts/pallas_call | solution.py:337
  80.9 0.3 collective-permute-start.32
  81.1 0.1 convert_add_fusion.1
  81.3 0.6 collective-permute-start.29
  81.9 3.8 %experts.7 = (f32[2,2,64,1024]{3,2,1,0:T(8,128)S(1)}, bf16[2,2,64,1024]{3,2,1,0:T(8,128)(2,1)S(1)}) custom-call(s32[3]{0:T(128)S(1)} %pad_add_fusion.row_ref.refs_0_, bf16[2,64,1152]{2,1,0:T(8,128)(2,1)S(1)} %get-tuple-element.65.refs_1_, bf16[2,64,1152]{2,1,0:T(8,128)(2,1)S(1)} %get-tuple-element.63.refs_2_, ...), custom_call_target="tpu_custom_call" | custom-call | flops 1 | bytes 1 | tf_op jit(solution)/shard_map/experts/pallas_call | solution.py:337
  85.9 0.2 convert_add_fusion
  86.1 1.6 %collective-permute-start.33 = (bf16[2,64,1024]{2,1,0:T(8,128)(2,1)S(1)}, bf16[2,64,1024]{2,1,0:T(8,128)(2,1)S(1)}, u32[]{:S(2)}, u32[]{:S(2)}) collective-permute-start(bf16[2,64,1024]{2,1,0:T(8,128)(2,1)S(1)} %fusion.5), channel_id=1, source_target_pairs={{0,4},{2,6},{4,0},{6,2},{1,5},{3,7},{5,1},{7,3},{8,12},{10,14},{12... | collective-permute-start | bytes 786440 | tf_op jit(solution)/shard_map/ppermute | solution.py:357
  87.7 0.1 convert_add_fusion.2
  87.9 1.5 %collective-permute-start.27 = (bf16[1,2,64,1024]{3,2,1,0:T(8,128)(2,1)S(1)}, bf16[1,2,64,1024]{3,2,1,0:T(8,128)(2,1)S(1)}, u32[]{:S(2)}, u32[]{:S(2)}) collective-permute-start(bf16[1,2,64,1024]{3,2,1,0:T(8,128)(2,1)S(1)} %slice.173), channel_id=1, source_target_pairs={{0,1},{1,0},{2,3},{3,2},{4,5},{5,4},{6,7},{7,6},{8,9},{9,8},{10,11... | collective-permute-start | bytes 786440 | tf_op jit(solution)/shard_map/ppermute | solution.py:357
  89.5 1.6 %collective-permute-start.11 = (bf16[2,64,1024]{2,1,0:T(8,128)(2,1)S(1)}, bf16[2,64,1024]{2,1,0:T(8,128)(2,1)S(1)}, u32[]{:S(2)}, u32[]{:S(2)}) collective-permute-start(bf16[2,64,1024]{2,1,0:T(8,128)(2,1)S(1)} %fusion.3), channel_id=1, source_target_pairs={{0,4},{2,6},{4,0},{6,2},{1,5},{3,7},{5,1},{7,3},{8,12},{10,14},{12... | collective-permute-start | bytes 786440 | tf_op jit(solution)/shard_map/ppermute | solution.py:357
  91.1 5.1 %collective-permute-done.33 = bf16[2,64,1024]{2,1,0:T(8,128)(2,1)S(1)} collective-permute-done((bf16[2,64,1024]{2,1,0:T(8,128)(2,1)S(1)}, bf16[2,64,1024]{2,1,0:T(8,128)(2,1)S(1)}, u32[]{:S(2)}, u32[]{:S(2)}) %collective-permute-start.33) | collective-permute-done | bytes 262176 | tf_op jit(solution)/shard_map/ppermute | solution.py:357
  96.3 1.6 %collective-permute-start.34 = (bf16[1,64,1024]{2,1,0:T(8,128)(2,1)S(1)}, bf16[1,64,1024]{2,1,0:T(8,128)(2,1)S(1)}, u32[]{:S(2)}, u32[]{:S(2)}) collective-permute-start(bf16[1,64,1024]{2,1,0:T(8,128)(2,1)S(1)} %slice.174), channel_id=1, source_target_pairs={{0,1},{1,0},{2,3},{3,2},{4,5},{5,4},{6,7},{7,6},{8,9},{9,8},{10,11... | collective-permute-start | bytes 393224 | tf_op jit(solution)/shard_map/ppermute | solution.py:357
  97.9 0.6 collective-permute-start.30
  98.6 3.4 %collective-permute-done.34 = bf16[1,64,1024]{2,1,0:T(8,128)(2,1)S(1)} collective-permute-done((bf16[1,64,1024]{2,1,0:T(8,128)(2,1)S(1)}, bf16[1,64,1024]{2,1,0:T(8,128)(2,1)S(1)}, u32[]{:S(2)}, u32[]{:S(2)}) %collective-permute-start.34) | collective-permute-done | bytes 131104 | tf_op jit(solution)/shard_map/ppermute | solution.py:357
  102.0 1.9 %collective-permute-start.35 = (bf16[64,1024]{1,0:T(8,128)(2,1)S(1)}, bf16[64,1024]{1,0:T(8,128)(2,1)S(1)}, u32[]{:S(2)}, u32[]{:S(2)}) collective-permute-start(bf16[64,1024]{1,0:T(8,128)(2,1)S(1)} %fusion.18), channel_id=1, source_target_pairs={{0,24},{8,16},{16,8},{24,0},{1,25},{9,17},{17,9},{25,1},{2,26},{10... | collective-permute-start | bytes 393224 | tf_op jit(solution)/shard_map/ppermute | solution.py:357
  104.0 1.1 collective-permute-start.36
  105.2 1.6 %collective-permute-start.28 = (bf16[1,64,1024]{2,1,0:T(8,128)(2,1)S(1)}, bf16[1,64,1024]{2,1,0:T(8,128)(2,1)S(1)}, u32[]{:S(2)}, u32[]{:S(2)}) collective-permute-start(bf16[1,64,1024]{2,1,0:T(8,128)(2,1)S(1)} %slice.176), channel_id=1, source_target_pairs={{0,1},{1,0},{2,3},{3,2},{4,5},{5,4},{6,7},{7,6},{8,9},{9,8},{10,11... | collective-permute-start | bytes 393224 | tf_op jit(solution)/shard_map/ppermute | solution.py:357
  106.9 2.1 %collective-permute-done.36 = bf16[64,1024]{1,0:T(8,128)(2,1)S(1)} collective-permute-done((bf16[64,1024]{1,0:T(8,128)(2,1)S(1)}, bf16[64,1024]{1,0:T(8,128)(2,1)S(1)}, u32[]{:S(2)}, u32[]{:S(2)}) %collective-permute-start.36) | collective-permute-done | bytes 131104 | tf_op jit(solution)/shard_map/ppermute | solution.py:357
  109.0 0.4 collective-permute-start.37
  109.5 0.7 collective-permute-done.28
  110.2 2.9 %collective-permute-done.31 = bf16[64,1024]{1,0:T(8,128)(2,1)S(1)} collective-permute-done((bf16[64,1024]{1,0:T(8,128)(2,1)S(1)}, bf16[64,1024]{1,0:T(8,128)(2,1)S(1)}, u32[]{:S(2)}, u32[]{:S(2)}) %collective-permute-start.31) | collective-permute-done | bytes 131104 | tf_op jit(solution)/shard_map/ppermute | solution.py:357
  113.1 2.6 %collective-permute-done.37 = bf16[64,1024]{1,0:T(8,128)(2,1)S(1)} collective-permute-done((bf16[64,1024]{1,0:T(8,128)(2,1)S(1)}, bf16[64,1024]{1,0:T(8,128)(2,1)S(1)}, u32[]{:S(2)}, u32[]{:S(2)}) %collective-permute-start.37) | collective-permute-done | bytes 131104 | tf_op jit(solution)/shard_map/ppermute | solution.py:357
  115.8 1.3 %collective-permute-start.38 = (bf16[1,64,1024]{2,1,0:T(8,128)(2,1)S(1)}, bf16[1,64,1024]{2,1,0:T(8,128)(2,1)S(1)}, u32[]{:S(2)}, u32[]{:S(2)}) collective-permute-start(bf16[1,64,1024]{2,1,0:T(8,128)(2,1)S(1)} %bitcast.89), channel_id=1, source_target_pairs={{0,1},{1,0},{2,3},{3,2},{4,5},{5,4},{6,7},{7,6},{8,9},{9,8},{10,11... | collective-permute-start | bytes 393224 | tf_op jit(solution)/shard_map/ppermute | solution.py:357
  117.1 3.7 %collective-permute-done.38.others_ref = bf16[1,64,1024]{2,1,0:T(8,128)(2,1)S(1)} collective-permute-done((bf16[1,64,1024]{2,1,0:T(8,128)(2,1)S(1)}, bf16[1,64,1024]{2,1,0:T(8,128)(2,1)S(1)}, u32[]{:S(2)}, u32[]{:S(2)}) %collective-permute-start.38) | collective-permute-done | bytes 131104 | tf_op jit(solution)/shard_map/ppermute | solution.py:357
  120.8 1.3 %finish.1 = bf16[64,2048]{1,0:T(8,128)(2,1)} custom-call(s32[3]{0:T(128)S(1)} %pad_add_fusion.row_ref.refs_0_, bf16[64,1024]{1,0:T(8,128)(2,1)S(1)} %fusion.15.own_ref, bf16[1,64,1024]{2,1,0:T(8,128)(2,1)S(1)} %collective-permute-done.38.others_ref), custom_call_target="tpu_custom_call" | custom-call | tf_op jit(solution)/shard_map/finish/pallas_call | solution.py:275
  (94 shorter events, 1.8 us)
Async XLA Ops:
  0.6 9.6 %collective-permute-start.1 = (bf16[64,2048]{1,0:T(8,128)(2,1)}, bf16[64,2048]{1,0:T(8,128)(2,1)S(1)}, u32[]{:S(2)}, u32[]{:S(2)}) collective-permute-start(bf16[64,2048]{1,0:T(8,128)(2,1)} %hidden_ref.1), channel_id=1, source_target_pairs={{0,4},{2,6},{4,0},{6,2},{1,5},{3,7},{5,1},{7,3},{8,12},{10,14},{12... | collective-permute-start | bytes 786440 | tf_op jit(solution)/shard_map/ppermute | solution.py:357
  4.4 0.7 copy-start.14
  5.1 0.7 copy-start.15
  5.7 4.5 %copy-start.10 = (bf16[64,2048]{1,0:T(8,128)(2,1)S(1)}, bf16[64,2048]{1,0:T(8,128)(2,1)}, u32[]{:S(2)}) copy-start(bf16[64,2048]{1,0:T(8,128)(2,1)} %hidden_ref.1) | copy-start | bytes 786436
  5.7 6.0 %copy-start.1 = (bf16[2048,576]{0,1:T(8,128)(2,1)S(1)}, bf16[2048,576]{0,1:T(8,128)(2,1)}, u32[]{:S(2)}) copy-start(bf16[2048,576]{0,1:T(8,128)(2,1)} %param.27) | copy-start | bytes 7077892
  5.7 6.0 %copy-start.2 = (bf16[4,384,576]{1,2,0:T(8,128)(2,1)S(1)}, bf16[4,384,576]{1,2,0:T(8,128)(2,1)}, u32[]{:S(2)}) copy-start(bf16[4,384,576]{1,2,0:T(8,128)(2,1)} %param.20) | copy-start | bytes 5308420
  5.7 6.0 %copy-start.3 = (bf16[2048,384]{1,0:T(8,128)(2,1)S(1)}, bf16[2048,384]{1,0:T(8,128)(2,1)}, u32[]{:S(2)}) copy-start(bf16[2048,384]{1,0:T(8,128)(2,1)} %refs_7_.3) | copy-start | bytes 4718596
  5.7 6.0 %copy-start.4 = (bf16[256,2048]{1,0:T(8,128)(2,1)S(1)}, bf16[256,2048]{1,0:T(8,128)(2,1)}, u32[]{:S(2)}) copy-start(bf16[256,2048]{1,0:T(8,128)(2,1)} %refs_12_.3) | copy-start | bytes 3145732
  5.8 6.0 %copy-start.8 = (bf16[2,128,512]{2,1,0:T(8,128)(2,1)S(1)}, bf16[2,128,512]{2,1,0:T(8,128)(2,1)}, u32[]{:S(2)}) copy-start(bf16[2,128,512]{2,1,0:T(8,128)(2,1)} %refs_10_.4) | copy-start | bytes 786436
  5.8 6.0 %copy-start.9 = (bf16[2,512,128]{2,1,0:T(8,128)(2,1)S(1)}, bf16[2,512,128]{2,1,0:T(8,128)(2,1)}, u32[]{:S(2)}) copy-start(bf16[2,512,128]{2,1,0:T(8,128)(2,1)} %refs_11_.3) | copy-start | bytes 786436
  5.8 6.0 %copy-start.11 = (f32[2048]{0:T(1024)S(1)}, f32[2048]{0:T(1024)}, u32[]{:S(2)}) copy-start(f32[2048]{0:T(1024)} %param.25) | copy-start | bytes 24580
  5.8 6.0 %copy-start.12 = (f32[512]{0:T(512)S(1)}, f32[512]{0:T(512)}, u32[]{:S(2)}) copy-start(f32[512]{0:T(512)} %param.28) | copy-start | bytes 6148
  10.2 1.5 %collective-permute-start.2 = (bf16[64,2048]{1,0:T(8,128)(2,1)S(1)}, bf16[64,2048]{1,0:T(8,128)(2,1)S(1)}, u32[]{:S(2)}, u32[]{:S(2)}) collective-permute-start(bf16[64,2048]{1,0:T(8,128)(2,1)S(1)} %collective-permute-done.1.refs_0_), channel_id=1, source_target_pairs={{0,2},{2,0},{4,6},{6,4},{1,3},{3,1},{5,7},{7,5},{8,10},{10,8},{12,... | collective-permute-start | bytes 786440 | tf_op jit(solution)/shard_map/ppermute | solution.py:357
  10.2 5.6 %collective-permute-start = (bf16[64,2048]{1,0:T(8,128)(2,1)S(1)}, bf16[64,2048]{1,0:T(8,128)(2,1)S(1)}, u32[]{:S(2)}, u32[]{:S(2)}) collective-permute-start(bf16[64,2048]{1,0:T(8,128)(2,1)S(1)} %copy-done.10), channel_id=1, source_target_pairs={{0,2},{2,0},{4,6},{6,4},{1,3},{3,1},{5,7},{7,5},{8,10},{10,8},{12,... | collective-permute-start | bytes 786440 | tf_op jit(solution)/shard_map/ppermute | solution.py:357
  15.6 5.0 %collective-permute-start.4 = (bf16[64,2048]{1,0:T(8,128)(2,1)S(1)}, bf16[64,2048]{1,0:T(8,128)(2,1)S(1)}, u32[]{:S(2)}, u32[]{:S(2)}) collective-permute-start(bf16[64,2048]{1,0:T(8,128)(2,1)S(1)} %get-tuple-element.36), channel_id=1, source_target_pairs={{0,2},{2,0},{4,6},{6,4},{1,3},{3,1},{5,7},{7,5},{8,10},{10,8},{12,... | collective-permute-start | bytes 786440 | tf_op jit(solution)/shard_map/ppermute | solution.py:357
  20.2 10.7 %copy-start.16 = (s32[64,6]{0,1:T(8,128)S(1)}, s32[64,6]{0,1:T(8,128)}, u32[]{:S(2)}) copy-start(s32[64,6]{0,1:T(8,128)} %param.23) | copy-start | bytes 4612
  20.2 16.5 %copy-start.13 = (f32[2048]{0:T(1024)S(1)}, f32[2048]{0:T(1024)}, u32[]{:S(2)}) copy-start(f32[2048]{0:T(1024)} %param.32) | copy-start | bytes 24580
  20.2 2.3 %collective-permute-start.3 = (bf16[64,2048]{1,0:T(8,128)(2,1)S(1)}, bf16[64,2048]{1,0:T(8,128)(2,1)S(1)}, u32[]{:S(2)}, u32[]{:S(2)}) collective-permute-start(bf16[64,2048]{1,0:T(8,128)(2,1)S(1)} %get-tuple-element.39), channel_id=1, source_target_pairs={{0,2},{2,0},{4,6},{6,4},{1,3},{3,1},{5,7},{7,5},{8,10},{10,8},{12,... | collective-permute-start | bytes 786440 | tf_op jit(solution)/shard_map/ppermute | solution.py:357
  20.6 8.4 %collective-permute-start.5 = (bf16[64,2048]{1,0:T(8,128)(2,1)S(1)}, bf16[64,2048]{1,0:T(8,128)(2,1)S(1)}, u32[]{:S(2)}, u32[]{:S(2)}) collective-permute-start(bf16[64,2048]{1,0:T(8,128)(2,1)S(1)} %add_convert_fusion.1), channel_id=1, source_target_pairs={{0,4},{2,6},{4,0},{6,2},{1,5},{3,7},{5,1},{7,3},{8,12},{10,14},{12... | collective-permute-start | bytes 786440 | tf_op jit(solution)/shard_map/ppermute | solution.py:357
  29.1 7.6 %collective-permute-start.6 = (bf16[64,2048]{1,0:T(8,128)(2,1)S(1)}, bf16[64,2048]{1,0:T(8,128)(2,1)S(1)}, u32[]{:S(2)}, u32[]{:S(2)}) collective-permute-start(bf16[64,2048]{1,0:T(8,128)(2,1)S(1)} %add_convert_fusion.keep_ref), channel_id=1, source_target_pairs={{0,1},{1,0},{2,3},{3,2},{4,5},{5,4},{6,7},{7,6},{8,9},{9,8},{10,11... | collective-permute-start | bytes 786440 | tf_op jit(solution)/shard_map/ppermute | solution.py:357
  36.7 21.6 %slice-start = ((s8[5767168]{0:T(1024)(128)(4,1)}), s8[4194304]{0:T(1024)(128)(4,1)S(1)}, s32[]{:S(2)}) async-start(s8[5767168]{0:T(1024)(128)(4,1)} %bitcast.70), calls=%async_computation | async-start | bytes 8388608
  36.7 21.6 %slice-start.1 = ((s8[5767168]{0:T(1024)(128)(4,1)}), s8[1572864]{0:T(1024)(128)(4,1)S(1)}, s32[]{:S(2)}) async-start(s8[5767168]{0:T(1024)(128)(4,1)} %bitcast.70), calls=%async_computation.1 | async-start | bytes 3145728
  36.7 21.6 %copy-start = (bf16[1,704,2048]{2,1,0:T(8,128)(2,1)S(1)}, bf16[1,704,2048]{2,1,0:T(8,128)(2,1)}, u32[]{:S(2)}) copy-start(bf16[1,704,2048]{2,1,0:T(8,128)(2,1)} %param.37) | copy-start | bytes 8650756
  36.7 21.6 %copy-start.5 = (bf16[2,2048,352]{1,2,0:T(8,128)(2,1)S(1)}, bf16[2,2048,352]{1,2,0:T(8,128)(2,1)}, u32[]{:S(2)}) copy-start(bf16[2,2048,352]{1,2,0:T(8,128)(2,1)} %param.34) | copy-start | bytes 8650756
  36.7 21.6 %copy-start.6 = (bf16[352,2048]{1,0:T(8,128)(2,1)S(1)}, bf16[352,2048]{1,0:T(8,128)(2,1)}, u32[]{:S(2)}) copy-start(bf16[352,2048]{1,0:T(8,128)(2,1)} %refs_10_.5) | copy-start | bytes 4325380
  36.7 21.6 %copy-start.7 = (bf16[2048,16]{0,1:T(8,128)(2,1)S(1)}, bf16[2048,16]{0,1:T(8,128)(2,1)}, u32[]{:S(2)}) copy-start(bf16[2048,16]{0,1:T(8,128)(2,1)} %param.33) | copy-start | bytes 196612
  37.5 7.3 %collective-permute-start.7 = (bf16[2,64,1152]{2,1,0:T(8,128)(2,1)S(1)}, bf16[2,64,1152]{2,1,0:T(8,128)(2,1)S(1)}, u32[]{:S(2)}, u32[]{:S(2)}) collective-permute-start(bf16[2,64,1152]{2,1,0:T(8,128)(2,1)S(1)} %get-tuple-element.42.refs_1_), channel_id=1, source_target_pairs={{0,4},{2,6},{4,0},{6,2},{1,5},{3,7},{5,1},{7,3},{8,12},{10,14},{12... | collective-permute-start | bytes 884744 | tf_op jit(solution)/shard_map/ppermute | solution.py:357
  39.3 8.6 %collective-permute-start.12 = (bf16[1,64,1152]{2,1,0:T(8,128)(2,1)S(1)}, bf16[1,64,1152]{2,1,0:T(8,128)(2,1)S(1)}, u32[]{:S(2)}, u32[]{:S(2)}) collective-permute-start(bf16[1,64,1152]{2,1,0:T(8,128)(2,1)S(1)} %get-tuple-element.46), channel_id=1, source_target_pairs={{0,24},{8,16},{16,8},{24,0},{1,25},{9,17},{17,9},{25,1},{2,26},{10... | collective-permute-start | bytes 442376 | tf_op jit(solution)/shard_map/ppermute | solution.py:357
  43.0 10.8 %collective-permute-start.13 = (bf16[1,64,1152]{2,1,0:T(8,128)(2,1)S(1)}, bf16[1,64,1152]{2,1,0:T(8,128)(2,1)S(1)}, u32[]{:S(2)}, u32[]{:S(2)}) collective-permute-start(bf16[1,64,1152]{2,1,0:T(8,128)(2,1)S(1)} %get-tuple-element.46), channel_id=1, source_target_pairs={{0,16},{8,24},{16,0},{24,8},{1,17},{9,25},{17,1},{25,9},{2,18},{10... | collective-permute-start | bytes 442376 | tf_op jit(solution)/shard_map/ppermute | solution.py:357
  43.0 11.7 %collective-permute-start.14 = (bf16[2,64,1152]{2,1,0:T(8,128)(2,1)S(1)}, bf16[2,64,1152]{2,1,0:T(8,128)(2,1)S(1)}, u32[]{:S(2)}, u32[]{:S(2)}) collective-permute-start(bf16[2,64,1152]{2,1,0:T(8,128)(2,1)S(1)} %get-tuple-element.42.refs_1_), channel_id=1, source_target_pairs={{0,8},{8,0},{16,24},{24,16},{1,9},{9,1},{17,25},{25,17},{2,10},{10... | collective-permute-start | bytes 884744 | tf_op jit(solution)/shard_map/ppermute | solution.py:357
  43.7 14.5 %collective-permute-start.8 = (bf16[2,64,1152]{2,1,0:T(8,128)(2,1)S(1)}, bf16[2,64,1152]{2,1,0:T(8,128)(2,1)S(1)}, u32[]{:S(2)}, u32[]{:S(2)}) collective-permute-start(bf16[2,64,1152]{2,1,0:T(8,128)(2,1)S(1)} %get-tuple-element.42.refs_1_), channel_id=1, source_target_pairs={{0,2},{2,0},{4,6},{6,4},{1,3},{3,1},{5,7},{7,5},{8,10},{10,8},{12,... | collective-permute-start | bytes 884744 | tf_op jit(solution)/shard_map/ppermute | solution.py:357
  44.9 13.4 %collective-permute-start.9 = (bf16[2,64,1152]{2,1,0:T(8,128)(2,1)S(1)}, bf16[2,64,1152]{2,1,0:T(8,128)(2,1)S(1)}, u32[]{:S(2)}, u32[]{:S(2)}) collective-permute-start(bf16[2,64,1152]{2,1,0:T(8,128)(2,1)S(1)} %collective-permute-done.7.refs_2_), channel_id=1, source_target_pairs={{0,2},{2,0},{4,6},{6,4},{1,3},{3,1},{5,7},{7,5},{8,10},{10,8},{12,... | collective-permute-start | bytes 884744 | tf_op jit(solution)/shard_map/ppermute | solution.py:357
  54.6 9.9 %collective-permute-start.20 = (bf16[2,64,1152]{2,1,0:T(8,128)(2,1)S(1)}, bf16[2,64,1152]{2,1,0:T(8,128)(2,1)S(1)}, u32[]{:S(2)}, u32[]{:S(2)}) collective-permute-start(bf16[2,64,1152]{2,1,0:T(8,128)(2,1)S(1)} %collective-permute-done.14.refs_1_), channel_id=1, source_target_pairs={{0,4},{2,6},{4,0},{6,2},{1,5},{3,7},{5,1},{7,3},{8,12},{10,14},{12... | collective-permute-start | bytes 884744 | tf_op jit(solution)/shard_map/ppermute | solution.py:357
  55.1 13.0 %collective-permute-start.16 = (bf16[1,2,64,1152]{3,2,0,1:T(8,128)(2,1)S(1)}, bf16[1,2,64,1152]{3,2,0,1:T(8,128)(2,1)S(1)}, u32[]{:S(2)}, u32[]{:S(2)}) collective-permute-start(bf16[1,2,64,1152]{3,2,0,1:T(8,128)(2,1)S(1)} %maximum_bitcast_fusion), channel_id=1, source_target_pairs={{0,4},{2,6},{4,0},{6,2},{1,5},{3,7},{5,1},{7,3},{8,12},{10,14},{12... | collective-permute-start | bytes 884744 | tf_op jit(solution)/shard_map/ppermute | solution.py:357
  56.7 13.0 %collective-permute-start.15 = (bf16[1,2,64,1152]{3,2,0,1:T(8,128)(2,1)S(1)}, bf16[1,2,64,1152]{3,2,0,1:T(8,128)(2,1)S(1)}, u32[]{:S(2)}, u32[]{:S(2)}) collective-permute-start(bf16[1,2,64,1152]{3,2,0,1:T(8,128)(2,1)S(1)} %maximum_bitcast_fusion), channel_id=1, source_target_pairs={{0,1},{1,0},{2,3},{3,2},{4,5},{5,4},{6,7},{7,6},{8,9},{9,8},{10,11... | collective-permute-start | bytes 884744 | tf_op jit(solution)/shard_map/ppermute | solution.py:357
  58.2 11.5 %collective-permute-start.21 = (bf16[2,64,1152]{2,1,0:T(8,128)(2,1)S(1)}, bf16[2,64,1152]{2,1,0:T(8,128)(2,1)S(1)}, u32[]{:S(2)}, u32[]{:S(2)}) collective-permute-start(bf16[2,64,1152]{2,1,0:T(8,128)(2,1)S(1)} %collective-permute-done.14.refs_1_), channel_id=1, source_target_pairs={{0,2},{2,0},{4,6},{6,4},{1,3},{3,1},{5,7},{7,5},{8,10},{10,8},{12,... | collective-permute-start | bytes 884744 | tf_op jit(solution)/shard_map/ppermute | solution.py:357
  63.5 12.2 %collective-permute-start.10 = (bf16[2,2,64,1024]{3,2,1,0:T(8,128)(2,1)S(1)}, bf16[2,2,64,1024]{3,2,1,0:T(8,128)(2,1)S(1)}, u32[]{:S(2)}, u32[]{:S(2)}) collective-permute-start(bf16[2,2,64,1024]{3,2,1,0:T(8,128)(2,1)S(1)} %get-tuple-element.45), channel_id=1, source_target_pairs={{0,2},{2,0},{4,6},{6,4},{1,3},{3,1},{5,7},{7,5},{8,10},{10,8},{12,... | collective-permute-start | bytes 1572872 | tf_op jit(solution)/shard_map/ppermute | solution.py:357
  64.6 5.1 %collective-permute-start.22 = (bf16[2,64,1152]{2,1,0:T(8,128)(2,1)S(1)}, bf16[2,64,1152]{2,1,0:T(8,128)(2,1)S(1)}, u32[]{:S(2)}, u32[]{:S(2)}) collective-permute-start(bf16[2,64,1152]{2,1,0:T(8,128)(2,1)S(1)} %collective-permute-done.20.refs_2_), channel_id=1, source_target_pairs={{0,2},{2,0},{4,6},{6,4},{1,3},{3,1},{5,7},{7,5},{8,10},{10,8},{12,... | collective-permute-start | bytes 884744 | tf_op jit(solution)/shard_map/ppermute | solution.py:357
  68.2 6.7 %collective-permute-start.17 = (bf16[1,2,64,1152]{3,2,0,1:T(8,128)(2,1)S(1)}, bf16[1,2,64,1152]{3,2,0,1:T(8,128)(2,1)S(1)}, u32[]{:S(2)}, u32[]{:S(2)}) collective-permute-start(bf16[1,2,64,1152]{3,2,0,1:T(8,128)(2,1)S(1)} %collective-permute-done.16), channel_id=1, source_target_pairs={{0,1},{1,0},{2,3},{3,2},{4,5},{5,4},{6,7},{7,6},{8,9},{9,8},{10,11... | collective-permute-start | bytes 884744 | tf_op jit(solution)/shard_map/ppermute | solution.py:357
  73.8 7.4 %collective-permute-start.25 = (bf16[2,2,64,1024]{3,2,1,0:T(8,128)(2,1)S(1)}, bf16[2,2,64,1024]{3,2,1,0:T(8,128)(2,1)S(1)}, u32[]{:S(2)}, u32[]{:S(2)}) collective-permute-start(bf16[2,2,64,1024]{3,2,1,0:T(8,128)(2,1)S(1)} %get-tuple-element.49), channel_id=1, source_target_pairs={{0,2},{2,0},{4,6},{6,4},{1,3},{3,1},{5,7},{7,5},{8,10},{10,8},{12,... | collective-permute-start | bytes 1572872 | tf_op jit(solution)/shard_map/ppermute | solution.py:357
  75.0 1.6 %collective-permute-start.24 = (bf16[2,64,1152]{2,1,0:T(8,128)(2,1)S(1)}, bf16[2,64,1152]{2,1,0:T(8,128)(2,1)S(1)}, u32[]{:S(2)}, u32[]{:S(2)}) collective-permute-start(bf16[2,64,1152]{2,1,0:T(8,128)(2,1)S(1)} %get-tuple-element.62.refs_2_), channel_id=1, source_target_pairs={{0,2},{2,0},{4,6},{6,4},{1,3},{3,1},{5,7},{7,5},{8,10},{10,8},{12,... | collective-permute-start | bytes 884744 | tf_op jit(solution)/shard_map/ppermute | solution.py:357
  75.1 1.9 %collective-permute-start.23 = (bf16[2,64,1152]{2,1,0:T(8,128)(2,1)S(1)}, bf16[2,64,1152]{2,1,0:T(8,128)(2,1)S(1)}, u32[]{:S(2)}, u32[]{:S(2)}) collective-permute-start(bf16[2,64,1152]{2,1,0:T(8,128)(2,1)S(1)} %get-tuple-element.64.refs_1_), channel_id=1, source_target_pairs={{0,2},{2,0},{4,6},{6,4},{1,3},{3,1},{5,7},{7,5},{8,10},{10,8},{12,... | collective-permute-start | bytes 884744 | tf_op jit(solution)/shard_map/ppermute | solution.py:357
  75.7 6.3 %collective-permute-start.18 = (bf16[2,64,1152]{2,1,0:T(8,128)(2,1)S(1)}, bf16[2,64,1152]{2,1,0:T(8,128)(2,1)S(1)}, u32[]{:S(2)}, u32[]{:S(2)}) collective-permute-start(bf16[2,64,1152]{2,1,0:T(8,128)(2,1)S(1)} %get-tuple-element.65.refs_1_), channel_id=1, source_target_pairs={{0,2},{2,0},{4,6},{6,4},{1,3},{3,1},{5,7},{7,5},{8,10},{10,8},{12,... | collective-permute-start | bytes 884744 | tf_op jit(solution)/shard_map/ppermute | solution.py:357
  75.7 6.2 %collective-permute-start.19 = (bf16[2,64,1152]{2,1,0:T(8,128)(2,1)S(1)}, bf16[2,64,1152]{2,1,0:T(8,128)(2,1)S(1)}, u32[]{:S(2)}, u32[]{:S(2)}) collective-permute-start(bf16[2,64,1152]{2,1,0:T(8,128)(2,1)S(1)} %get-tuple-element.63.refs_2_), channel_id=1, source_target_pairs={{0,2},{2,0},{4,6},{6,4},{1,3},{3,1},{5,7},{7,5},{8,10},{10,8},{12,... | collective-permute-start | bytes 884744 | tf_op jit(solution)/shard_map/ppermute | solution.py:357
  80.9 5.0 %collective-permute-start.32 = (bf16[2,2,64,1024]{3,2,1,0:T(8,128)(2,1)S(1)}, bf16[2,2,64,1024]{3,2,1,0:T(8,128)(2,1)S(1)}, u32[]{:S(2)}, u32[]{:S(2)}) collective-permute-start(bf16[2,2,64,1024]{3,2,1,0:T(8,128)(2,1)S(1)} %get-tuple-element.51), channel_id=1, source_target_pairs={{0,2},{2,0},{4,6},{6,4},{1,3},{3,1},{5,7},{7,5},{8,10},{10,8},{12,... | collective-permute-start | bytes 1572872 | tf_op jit(solution)/shard_map/ppermute | solution.py:357
  81.3 16.5 %collective-permute-start.29 = (bf16[2,64,1024]{2,1,0:T(8,128)(2,1)S(1)}, bf16[2,64,1024]{2,1,0:T(8,128)(2,1)S(1)}, u32[]{:S(2)}, u32[]{:S(2)}) collective-permute-start(bf16[2,64,1024]{2,1,0:T(8,128)(2,1)S(1)} %fusion.4), channel_id=1, source_target_pairs={{0,4},{2,6},{4,0},{6,2},{1,5},{3,7},{5,1},{7,3},{8,12},{10,14},{12... | collective-permute-start | bytes 786440 | tf_op jit(solution)/shard_map/ppermute | solution.py:357
  85.8 2.0 %collective-permute-start.26 = (bf16[2,2,64,1024]{3,2,1,0:T(8,128)(2,1)S(1)}, bf16[2,2,64,1024]{3,2,1,0:T(8,128)(2,1)S(1)}, u32[]{:S(2)}, u32[]{:S(2)}) collective-permute-start(bf16[2,2,64,1024]{3,2,1,0:T(8,128)(2,1)S(1)} %get-tuple-element.54), channel_id=1, source_target_pairs={{0,2},{2,0},{4,6},{6,4},{1,3},{3,1},{5,7},{7,5},{8,10},{10,8},{12,... | collective-permute-start | bytes 1572872 | tf_op jit(solution)/shard_map/ppermute | solution.py:357
  86.1 10.0 %collective-permute-start.33 = (bf16[2,64,1024]{2,1,0:T(8,128)(2,1)S(1)}, bf16[2,64,1024]{2,1,0:T(8,128)(2,1)S(1)}, u32[]{:S(2)}, u32[]{:S(2)}) collective-permute-start(bf16[2,64,1024]{2,1,0:T(8,128)(2,1)S(1)} %fusion.5), channel_id=1, source_target_pairs={{0,4},{2,6},{4,0},{6,2},{1,5},{3,7},{5,1},{7,3},{8,12},{10,14},{12... | collective-permute-start | bytes 786440 | tf_op jit(solution)/shard_map/ppermute | solution.py:357
  87.9 9.9 %collective-permute-start.27 = (bf16[1,2,64,1024]{3,2,1,0:T(8,128)(2,1)S(1)}, bf16[1,2,64,1024]{3,2,1,0:T(8,128)(2,1)S(1)}, u32[]{:S(2)}, u32[]{:S(2)}) collective-permute-start(bf16[1,2,64,1024]{3,2,1,0:T(8,128)(2,1)S(1)} %slice.173), channel_id=1, source_target_pairs={{0,1},{1,0},{2,3},{3,2},{4,5},{5,4},{6,7},{7,6},{8,9},{9,8},{10,11... | collective-permute-start | bytes 786440 | tf_op jit(solution)/shard_map/ppermute | solution.py:357
  89.5 15.6 %collective-permute-start.11 = (bf16[2,64,1024]{2,1,0:T(8,128)(2,1)S(1)}, bf16[2,64,1024]{2,1,0:T(8,128)(2,1)S(1)}, u32[]{:S(2)}, u32[]{:S(2)}) collective-permute-start(bf16[2,64,1024]{2,1,0:T(8,128)(2,1)S(1)} %fusion.3), channel_id=1, source_target_pairs={{0,4},{2,6},{4,0},{6,2},{1,5},{3,7},{5,1},{7,3},{8,12},{10,14},{12... | collective-permute-start | bytes 786440 | tf_op jit(solution)/shard_map/ppermute | solution.py:357
  96.3 5.8 %collective-permute-start.34 = (bf16[1,64,1024]{2,1,0:T(8,128)(2,1)S(1)}, bf16[1,64,1024]{2,1,0:T(8,128)(2,1)S(1)}, u32[]{:S(2)}, u32[]{:S(2)}) collective-permute-start(bf16[1,64,1024]{2,1,0:T(8,128)(2,1)S(1)} %slice.174), channel_id=1, source_target_pairs={{0,1},{1,0},{2,3},{3,2},{4,5},{5,4},{6,7},{7,6},{8,9},{9,8},{10,11... | collective-permute-start | bytes 393224 | tf_op jit(solution)/shard_map/ppermute | solution.py:357
  97.9 8.8 %collective-permute-start.30 = (bf16[1,64,1024]{2,1,0:T(8,128)(2,1)S(1)}, bf16[1,64,1024]{2,1,0:T(8,128)(2,1)S(1)}, u32[]{:S(2)}, u32[]{:S(2)}) collective-permute-start(bf16[1,64,1024]{2,1,0:T(8,128)(2,1)S(1)} %slice.175), channel_id=1, source_target_pairs={{0,1},{1,0},{2,3},{3,2},{4,5},{5,4},{6,7},{7,6},{8,9},{9,8},{10,11... | collective-permute-start | bytes 393224 | tf_op jit(solution)/shard_map/ppermute | solution.py:357
  102.0 8.2 %collective-permute-start.35 = (bf16[64,1024]{1,0:T(8,128)(2,1)S(1)}, bf16[64,1024]{1,0:T(8,128)(2,1)S(1)}, u32[]{:S(2)}, u32[]{:S(2)}) collective-permute-start(bf16[64,1024]{1,0:T(8,128)(2,1)S(1)} %fusion.18), channel_id=1, source_target_pairs={{0,24},{8,16},{16,8},{24,0},{1,25},{9,17},{17,9},{25,1},{2,26},{10... | collective-permute-start | bytes 393224 | tf_op jit(solution)/shard_map/ppermute | solution.py:357
  104.0 5.0 %collective-permute-start.36 = (bf16[64,1024]{1,0:T(8,128)(2,1)S(1)}, bf16[64,1024]{1,0:T(8,128)(2,1)S(1)}, u32[]{:S(2)}, u32[]{:S(2)}) collective-permute-start(bf16[64,1024]{1,0:T(8,128)(2,1)S(1)} %fusion.19), channel_id=1, source_target_pairs={{0,4},{2,6},{4,0},{6,2},{1,5},{3,7},{5,1},{7,3},{8,12},{10,14},{12... | collective-permute-start | bytes 393224 | tf_op jit(solution)/shard_map/ppermute | solution.py:357
  105.2 5.0 %collective-permute-start.28 = (bf16[1,64,1024]{2,1,0:T(8,128)(2,1)S(1)}, bf16[1,64,1024]{2,1,0:T(8,128)(2,1)S(1)}, u32[]{:S(2)}, u32[]{:S(2)}) collective-permute-start(bf16[1,64,1024]{2,1,0:T(8,128)(2,1)S(1)} %slice.176), channel_id=1, source_target_pairs={{0,1},{1,0},{2,3},{3,2},{4,5},{5,4},{6,7},{7,6},{8,9},{9,8},{10,11... | collective-permute-start | bytes 393224 | tf_op jit(solution)/shard_map/ppermute | solution.py:357
  106.8 6.3 %collective-permute-start.31 = (bf16[64,1024]{1,0:T(8,128)(2,1)S(1)}, bf16[64,1024]{1,0:T(8,128)(2,1)S(1)}, u32[]{:S(2)}, u32[]{:S(2)}) collective-permute-start(bf16[64,1024]{1,0:T(8,128)(2,1)S(1)} %fusion.17), channel_id=1, source_target_pairs={{0,8},{8,0},{16,24},{24,16},{1,9},{9,1},{17,25},{25,17},{2,10},{10... | collective-permute-start | bytes 393224 | tf_op jit(solution)/shard_map/ppermute | solution.py:357
  109.0 6.6 %collective-permute-start.37 = (bf16[64,1024]{1,0:T(8,128)(2,1)S(1)}, bf16[64,1024]{1,0:T(8,128)(2,1)S(1)}, u32[]{:S(2)}, u32[]{:S(2)}) collective-permute-start(bf16[64,1024]{1,0:T(8,128)(2,1)S(1)} %fusion.7), channel_id=1, source_target_pairs={{0,16},{8,24},{16,0},{24,8},{1,17},{9,25},{17,1},{25,9},{2,18},{10... | collective-permute-start | bytes 393224 | tf_op jit(solution)/shard_map/ppermute | solution.py:357
  115.8 5.0 %collective-permute-start.38 = (bf16[1,64,1024]{2,1,0:T(8,128)(2,1)S(1)}, bf16[1,64,1024]{2,1,0:T(8,128)(2,1)S(1)}, u32[]{:S(2)}, u32[]{:S(2)}) collective-permute-start(bf16[1,64,1024]{2,1,0:T(8,128)(2,1)S(1)} %bitcast.89), channel_id=1, source_target_pairs={{0,1},{1,0},{2,3},{3,2},{4,5},{5,4},{6,7},{7,6},{8,9},{9,8},{10,11... | collective-permute-start | bytes 393224 | tf_op jit(solution)/shard_map/ppermute | solution.py:357

commit v10 on v9

--- a/solution.py
+++ b/solution.py
@@ -402,15 +402,14 @@
     )
     far_near = swap(after(far, tables[0]), "row", n_row, 1)
     far_keep, far_send = attention_part(False, 2, indices, (far, far_near), cache, tables, weights)
+    far_core = swap(far_send, "row", n_row, 1)
     own_keep, own_send, accepted_latents = attention_part(
-        True, 0, indices, (hidden, after(near, far_send)), cache, tables, weights
-    )
-
-    def fold(keep, sent):
-        return keep + swap(sent, "row", n_row, 1).astype(jnp.float32)
-
-    from_far = swap(fold(far_keep, far_send).astype(bf16), "row", n_row, 2)
-    partial = fold(own_keep, own_send) + from_far.astype(jnp.float32)
+        True, 0, indices, (hidden, after(near, far_core)), cache, tables, weights
+    )
+
+    from_far = swap((far_keep + far_core.astype(jnp.float32)).astype(bf16), "row", n_row, 2)
+    own_core = swap(own_send, "row", n_row, 1)
+    partial = own_keep + own_core.astype(jnp.float32) + from_far.astype(jnp.float32)
     partial, arrived = col_parts(partial, n_col)
     named = (routes[:, :, None] == jnp.arange(EXTRA, dtype=jnp.int32)).any(axis=1).astype(bf16)
     residual, block, own_part = joined(indices, n_col, hidden, partial, arrived, post_gain[None], named)
@@ -418,26 +417,32 @@
     router = router_weight.T
     routed_weights = (jnp.swapaxes(expert_gate_up[0], 1, 2), expert_down[0])
     shared_weights = (jnp.swapaxes(shared_gate_up, 1, 2), shared_down)
-    distances = [0, 1, *range(n_req - 1, 1, -1)]
-    blocks = [block, swap(block, "req", n_req, 1)]
-    fars = [swap(each, "row", n_row, 2) for each in blocks]
-    rest = [swap(own_part, "req", n_req, s) for s in distances[2:]]
+    distances = [0, *range(n_req - 1, 0, -1)]
+    nearest = swap(block, "req", n_req, 1)
+    blocks, fars = [block], [swap(block, "row", n_row, 2)]
+    rest = [swap(own_part, "req", n_req, s) for s in distances[1:-1]]
+    nearest_far = nearest
     if rest:
-        rest = after(jnp.concatenate(rest, axis=0)[None], fars[0], blocks[1])
+        rest = after(jnp.concatenate(rest, axis=0)[None], fars[0], nearest)
         rest_far = swap(rest, "row", n_row, 2)
+        nearest_far = after(nearest, rest_far)
         rest, rest_far = col_gather(rest, n_col), col_gather(rest_far, n_col)
         blocks += [rest[:, k] for k in range(rest.shape[1])]
         fars += [rest_far[:, k] for k in range(rest.shape[1])]
+    blocks.append(nearest)
+    fars.append(swap(nearest_far, "row", n_row, 2))
     sends, cores, sums = [], [], []
     for k, s in enumerate(distances):
         near = swap(blocks[k], "row", n_row, 1)
+        if k == n_req - 1 and k > 1:
+            fars[k] = after(fars[k], sends[k - 1])
         far_near = swap(fars[k], "row", n_row, 1)
         if k:
             far_near = after(far_near, *sends, *cores[: k - 1])
         keep, send = expert_part(
             indices,
             n_col,
-            k < 3,
+            k != 2,
             (blocks[k], fars[k], near, far_near),
             own_expert,
             router,
@@ -447,21 +452,20 @@
         sends.append(send)
         cores.append(swap(send, "row", n_row, 1))
         sums.append(keep + cores[k].astype(jnp.float32))
+    arrivals = ()
+    if n_req > 2:
+        third, arrivals = col_scatter(sums[2], n_col)
+        third = third[0, 0] + swap(third[0, 1].astype(bf16), "row", n_row, 2).astype(jnp.float32)
     parts = []
-    arrivals = []
-    for k in reversed(range(n_req)):
-        if k < 3:
-            from_far = swap(sums[k][1].astype(bf16), "row", n_row, 2)
-            from_far = after(from_far, *(cores[-1:] if k == 2 else arrivals))
-            part = sums[k][0] + from_far.astype(jnp.float32)
-            part, _ = col_scatter(part, n_col, arrivals if k == 2 else ())
-            part = part[0]
+    for k, near_sum in enumerate(sums):
+        if k == 2:
+            part = third
         else:
-            part, arrivals = col_scatter(sums[k], n_col)
-            part = part[0]
-            part = part[0] + swap(part[1].astype(bf16), "row", n_row, 2).astype(jnp.float32)
+            from_far = swap(near_sum[1].astype(bf16), "row", n_row, 2)
+            from_far = after(from_far, *(cores[2:] if k == 1 else arrivals))
+            part = near_sum[0] + from_far.astype(jnp.float32)
+            part = col_scatter(part, n_col, arrivals if k == 1 else ())[0][0]
         parts.append(part.astype(bf16) if k else part)
-    parts.reverse()
     total = parts[0]
     for s, part in zip(distances[1:], parts[1:]):
         total = total + swap(part, "req", n_req, s).astype(jnp.float32)

time: 122 us -> 122 us (level)
  transfers between devices with their start and end apart: 39 -> 39, of which waited for: 20 -> 22; matrix products, arithmetic and copies ran while one was open for 1% -> 1% of each run, Pallas kernels for 22% -> 19%
where the time goes in v10:
time: 122 us; the launch traced here: 121 us
  waiting for transfers between devices  53.2 us (44%)
  starting transfers between devices  34 us (28%)
  Pallas kernels  29.1 us (24%)
  between operations  1.83 us (2%)
  local copies, waits for them, and re-layouts  1.82 us (1%)
  other arithmetic  1.41 us (1%)
    ppermute x39, waiting for transfers between devices, swap(): return lax.ppermute(values, axis, [(i, i ^ bits) for i in range(size)])  53.2 us
    ppermute x39, starting transfers between devices, swap(): return lax.ppermute(values, axis, [(i, i ^ bits) for i in range(size)])  34 us
    pallas_call x4, Pallas kernels, expert_part(): pl.pallas_call(functools.partial(expert_kernel, bool(shared_weights), far...  16.7 us
    pallas_call x2, Pallas kernels, attention_part(): pl.pallas_call(functools.partial(attention_kernel, first, place), out_sha...  8.2 us
  transfers between devices with their start and end apart: 39, of which 22 were waited for; matrix products, arithmetic and copies ran while one was open for 1% of the time, Pallas kernels for 19%

profile of v10, /device:TPU:0, one launch (start us, length us, event | category | flops | bytes accessed | tf_op | source)
XLA Modules:
  0.0 121.3 jit_solution(15374892994099616525)
XLA Ops:
  0.6 3.0 %collective-permute-start.1 = (bf16[64,2048]{1,0:T(8,128)(2,1)}, bf16[64,2048]{1,0:T(8,128)(2,1)S(1)}, u32[]{:S(2)}, u32[]{:S(2)}) collective-permute-start(bf16[64,2048]{1,0:T(8,128)(2,1)} %hidden_ref.1), channel_id=1, source_target_pairs={{0,4},{2,6},{4,0},{6,2},{1,5},{3,7},{5,1},{7,3},{8,12},{10,14},{12... | collective-permute-start | bytes 786440 | tf_op jit(solution)/shard_map/ppermute | solution.py:357
  4.4 0.7 copy-done.14
  5.1 0.7 copy-done.15
  5.8 2.1 %trees.1 = (f32[4,64,64]{2,1,0:T(8,128)S(1)}, f32[4,64,65]{2,1,0:T(8,128)S(1)}, bf16[64,64]{1,0:T(8,128)(2,1)S(1)}, f32[1,16]{1,0:T(1,128)S(1)}) custom-call(s32[3]{0:T(128)S(1)} %pad_add_fusion.row_ref.refs_0_, s32[4]{0:T(128)S(1)} %copy-done.15, s32[1]{0:T(128)S(6)} %copy.24.accepted_ref, s32[4,64]{1,0:T(4,128)S(1)} %copy-done.14), custom_call_target="tpu_custom_call" | custom-call | flops 20000000000 | bytes 1 | tf_op jit(solution)/shard_map/trees/pallas_call | solution.py:110
  7.9 2.2 %collective-permute-done.1.refs_0_ = bf16[64,2048]{1,0:T(8,128)(2,1)S(1)} collective-permute-done((bf16[64,2048]{1,0:T(8,128)(2,1)}, bf16[64,2048]{1,0:T(8,128)(2,1)S(1)}, u32[]{:S(2)}, u32[]{:S(2)}) %collective-permute-start.1) | collective-permute-done | bytes 262176 | tf_op jit(solution)/shard_map/ppermute | solution.py:357
  10.2 1.5 %collective-permute-done.2.refs_1_ = bf16[64,2048]{1,0:T(8,128)(2,1)S(1)} collective-permute-done((bf16[64,2048]{1,0:T(8,128)(2,1)S(1)}, bf16[64,2048]{1,0:T(8,128)(2,1)S(1)}, u32[]{:S(2)}, u32[]{:S(2)}) %collective-permute-start.2) | collective-permute-done | bytes 262176 | tf_op jit(solution)/shard_map/ppermute | solution.py:357
  11.8 3.8 %attention.2 = (f32[64,2048]{1,0:T(8,128)S(1)}, bf16[64,2048]{1,0:T(8,128)(2,1)S(1)}) custom-call(s32[3]{0:T(128)S(1)} %pad_add_fusion.row_ref.refs_0_, bf16[64,2048]{1,0:T(8,128)(2,1)S(1)} %collective-permute-done.1.refs_0_, bf16[64,2048]{1,0:T(8,128)(2,1)S(1)} %collective-permute-done.2.refs_1_, bf16[4,576,384]{2,1,0:T(8,128)(2,1)S(1)} %bitcast.82, ...), custom_call_target="tpu_custom_call" | custom-call | flops 1 | bytes 1 | tf_op jit(solution)/shard_map/attention/pallas_call | solution.py:211
  15.6 0.2 collective-permute-start.3
  15.8 0.4 collective-permute-start
  16.2 1.0 collective-permute-done.3
  17.3 1.8 %collective-permute-start.5 = (bf16[64,2048]{1,0:T(8,128)(2,1)S(1)}, bf16[64,2048]{1,0:T(8,128)(2,1)S(1)}, u32[]{:S(2)}, u32[]{:S(2)}) collective-permute-start(bf16[64,2048]{1,0:T(8,128)(2,1)S(1)} %add_convert_fusion.1), channel_id=1, source_target_pairs={{0,4},{2,6},{4,0},{6,2},{1,5},{3,7},{5,1},{7,3},{8,12},{10,14},{12... | collective-permute-start | bytes 786440 | tf_op jit(solution)/shard_map/ppermute | solution.py:357
  19.1 4.4 %attention.3 = (f32[64,2048]{1,0:T(8,128)S(1)}, bf16[64,2048]{1,0:T(8,128)(2,1)S(1)}, bf16[1,64,576]{2,1,0:T(8,128)(2,1)}) custom-call(s32[3]{0:T(128)S(1)} %pad_add_fusion.row_ref.refs_0_, bf16[64,2048]{1,0:T(8,128)(2,1)S(1)} %copy-done.10, bf16[64,2048]{1,0:T(8,128)(2,1)S(1)} %collective-permute-done.refs_1_, bf16[4,576,384]{2,1,0:T(8,128)(2,1)S(1)} %bitcast.83, ...), custom_call_target="tpu_custom_call" | custom-call | flops 1 | bytes 1 | tf_op jit(solution)/shard_map/attention/pallas_call | solution.py:211
  23.5 2.2 %collective-permute-done.5 = bf16[64,2048]{1,0:T(8,128)(2,1)S(1)} collective-permute-done((bf16[64,2048]{1,0:T(8,128)(2,1)S(1)}, bf16[64,2048]{1,0:T(8,128)(2,1)S(1)}, u32[]{:S(2)}, u32[]{:S(2)}) %collective-permute-start.5) | collective-permute-done | bytes 262176 | tf_op jit(solution)/shard_map/ppermute | solution.py:357
  25.8 1.8 %collective-permute-start.6 = (bf16[64,2048]{1,0:T(8,128)(2,1)S(1)}, bf16[64,2048]{1,0:T(8,128)(2,1)S(1)}, u32[]{:S(2)}, u32[]{:S(2)}) collective-permute-start(bf16[64,2048]{1,0:T(8,128)(2,1)S(1)} %add_convert_fusion.keep_ref), channel_id=1, source_target_pairs={{0,1},{1,0},{2,3},{3,2},{4,5},{5,4},{6,7},{7,6},{8,9},{9,8},{10,11... | collective-permute-start | bytes 786440 | tf_op jit(solution)/shard_map/ppermute | solution.py:357
  27.7 5.8 %collective-permute-done.6 = bf16[64,2048]{1,0:T(8,128)(2,1)S(1)} collective-permute-done((bf16[64,2048]{1,0:T(8,128)(2,1)S(1)}, bf16[64,2048]{1,0:T(8,128)(2,1)S(1)}, u32[]{:S(2)}, u32[]{:S(2)}) %collective-permute-start.6) | collective-permute-done | bytes 262176 | tf_op jit(solution)/shard_map/ppermute | solution.py:357
  33.6 0.8 join.1
  34.4 1.7 %collective-permute-start.7 = (bf16[2,64,1152]{2,1,0:T(8,128)(2,1)S(1)}, bf16[2,64,1152]{2,1,0:T(8,128)(2,1)S(1)}, u32[]{:S(2)}, u32[]{:S(2)}) collective-permute-start(bf16[2,64,1152]{2,1,0:T(8,128)(2,1)S(1)} %get-tuple-element.44.refs_1_), channel_id=1, source_target_pairs={{0,4},{2,6},{4,0},{6,2},{1,5},{3,7},{5,1},{7,3},{8,12},{10,14},{12... | collective-permute-start | bytes 884744 | tf_op jit(solution)/shard_map/ppermute | solution.py:357
  36.0 2.6 %collective-permute-start.13 = (bf16[1,64,1152]{2,1,0:T(8,128)(2,1)S(1)}, bf16[1,64,1152]{2,1,0:T(8,128)(2,1)S(1)}, u32[]{:S(2)}, u32[]{:S(2)}) collective-permute-start(bf16[1,64,1152]{2,1,0:T(8,128)(2,1)S(1)} %get-tuple-element.48), channel_id=1, source_target_pairs={{0,16},{8,24},{16,0},{24,8},{1,17},{9,25},{17,1},{25,9},{2,18},{10... | collective-permute-start | bytes 442376 | tf_op jit(solution)/shard_map/ppermute | solution.py:357
  38.6 1.3 %collective-permute-start.12 = (bf16[1,64,1152]{2,1,0:T(8,128)(2,1)S(1)}, bf16[1,64,1152]{2,1,0:T(8,128)(2,1)S(1)}, u32[]{:S(2)}, u32[]{:S(2)}) collective-permute-start(bf16[1,64,1152]{2,1,0:T(8,128)(2,1)S(1)} %get-tuple-element.48), channel_id=1, source_target_pairs={{0,24},{8,16},{16,8},{24,0},{1,25},{9,17},{17,9},{25,1},{2,26},{10... | collective-permute-start | bytes 442376 | tf_op jit(solution)/shard_map/ppermute | solution.py:357
  40.0 0.2 collective-permute-start.14
  40.2 1.7 %collective-permute-done.7.refs_2_ = bf16[2,64,1152]{2,1,0:T(8,128)(2,1)S(1)} collective-permute-done((bf16[2,64,1152]{2,1,0:T(8,128)(2,1)S(1)}, bf16[2,64,1152]{2,1,0:T(8,128)(2,1)S(1)}, u32[]{:S(2)}, u32[]{:S(2)}) %collective-permute-start.7) | collective-permute-done | bytes 294944 | tf_op jit(solution)/shard_map/ppermute | solution.py:357
  41.9 6.6 %collective-permute-done.13 = bf16[1,64,1152]{2,1,0:T(8,128)(2,1)S(1)} collective-permute-done((bf16[1,64,1152]{2,1,0:T(8,128)(2,1)S(1)}, bf16[1,64,1152]{2,1,0:T(8,128)(2,1)S(1)}, u32[]{:S(2)}, u32[]{:S(2)}) %collective-permute-start.13) | collective-permute-done | bytes 147488 | tf_op jit(solution)/shard_map/ppermute | solution.py:357
  48.6 3.1 %collective-permute-done.14.refs_1_ = bf16[2,64,1152]{2,1,0:T(8,128)(2,1)S(1)} collective-permute-done((bf16[2,64,1152]{2,1,0:T(8,128)(2,1)S(1)}, bf16[2,64,1152]{2,1,0:T(8,128)(2,1)S(1)}, u32[]{:S(2)}, u32[]{:S(2)}) %collective-permute-start.14) | collective-permute-done | bytes 294944 | tf_op jit(solution)/shard_map/ppermute | solution.py:357
  51.7 0.6 collective-permute-start.16
  52.2 1.4 %collective-permute-start.15 = (bf16[1,2,64,1152]{3,2,0,1:T(8,128)(2,1)S(1)}, bf16[1,2,64,1152]{3,2,0,1:T(8,128)(2,1)S(1)}, u32[]{:S(2)}, u32[]{:S(2)}) collective-permute-start(bf16[1,2,64,1152]{3,2,0,1:T(8,128)(2,1)S(1)} %maximum_bitcast_fusion), channel_id=1, source_target_pairs={{0,1},{1,0},{2,3},{3,2},{4,5},{5,4},{6,7},{7,6},{8,9},{9,8},{10,11... | collective-permute-start | bytes 884744 | tf_op jit(solution)/shard_map/ppermute | solution.py:357
  53.8 5.2 %experts.4 = (f32[2,2,64,1024]{3,2,1,0:T(8,128)S(1)}, bf16[2,2,64,1024]{3,2,1,0:T(8,128)(2,1)S(1)}) custom-call(s32[3]{0:T(128)S(1)} %pad_add_fusion.row_ref.refs_0_, bf16[2,64,1152]{2,1,0:T(8,128)(2,1)S(1)} %get-tuple-element.44.refs_1_, bf16[2,64,1152]{2,1,0:T(8,128)(2,1)S(1)} %collective-permute-done.7.refs_2_, ...), custom_call_target="tpu_custom_call" | custom-call | flops 1 | bytes 1 | tf_op jit(solution)/shard_map/experts/pallas_call | solution.py:337
  59.0 0.4 collective-permute-done.16
  59.4 1.5 %collective-permute-start.17 = (bf16[1,2,64,1152]{3,2,0,1:T(8,128)(2,1)S(1)}, bf16[1,2,64,1152]{3,2,0,1:T(8,128)(2,1)S(1)}, u32[]{:S(2)}, u32[]{:S(2)}) collective-permute-start(bf16[1,2,64,1152]{3,2,0,1:T(8,128)(2,1)S(1)} %collective-permute-done.16), channel_id=1, source_target_pairs={{0,1},{1,0},{2,3},{3,2},{4,5},{5,4},{6,7},{7,6},{8,9},{9,8},{10,11... | collective-permute-start | bytes 884744 | tf_op jit(solution)/shard_map/ppermute | solution.py:357
  60.9 7.5 %collective-permute-done.17 = bf16[1,2,64,1152]{3,2,0,1:T(8,128)(2,1)S(1)} collective-permute-done((bf16[1,2,64,1152]{3,2,0,1:T(8,128)(2,1)S(1)}, bf16[1,2,64,1152]{3,2,0,1:T(8,128)(2,1)S(1)}, u32[]{:S(2)}, u32[]{:S(2)}) %collective-permute-start.17) | collective-permute-done | bytes 294944 | tf_op jit(solution)/shard_map/ppermute | solution.py:357
  68.7 0.6 collective-permute-start.20
  69.3 0.4 collective-permute-start.18
  69.7 0.4 collective-permute-done.21.refs_4_
  70.2 1.5 %collective-permute-start.27 = (bf16[2,64,1152]{2,1,0:T(8,128)(2,1)S(1)}, bf16[2,64,1152]{2,1,0:T(8,128)(2,1)S(1)}, u32[]{:S(2)}, u32[]{:S(2)}) collective-permute-start(bf16[2,64,1152]{2,1,0:T(8,128)(2,1)S(1)} %collective-permute-done.14.refs_1_), channel_id=1, source_target_pairs={{0,4},{2,6},{4,0},{6,2},{1,5},{3,7},{5,1},{7,3},{8,12},{10,14},{12... | collective-permute-start | bytes 884744 | tf_op jit(solution)/shard_map/ppermute | solution.py:357
  71.7 3.8 %experts.5 = (f32[2,2,64,1024]{3,2,1,0:T(8,128)S(1)}, bf16[2,2,64,1024]{3,2,1,0:T(8,128)(2,1)S(1)}) custom-call(s32[3]{0:T(128)S(1)} %pad_add_fusion.row_ref.refs_0_, bf16[2,64,1152]{2,1,0:T(8,128)(2,1)S(1)} %get-tuple-element.68.refs_1_, bf16[2,64,1152]{2,1,0:T(8,128)(2,1)S(1)} %get-tuple-element.66.refs_2_, ...), custom_call_target="tpu_custom_call" | custom-call | flops 1 | bytes 1 | tf_op jit(solution)/shard_map/experts/pallas_call | solution.py:337
  75.6 3.8 %experts.6 = (f32[2,2,64,1024]{3,2,1,0:T(8,128)S(1)}, bf16[2,2,64,1024]{3,2,1,0:T(8,128)(2,1)S(1)}) custom-call(s32[3]{0:T(128)S(1)} %pad_add_fusion.row_ref.refs_0_, bf16[2,64,1152]{2,1,0:T(8,128)(2,1)S(1)} %get-tuple-element.69.refs_1_, bf16[2,64,1152]{2,1,0:T(8,128)(2,1)S(1)} %get-tuple-element.67.refs_2_, ...), custom_call_target="tpu_custom_call" | custom-call | flops 1 | bytes 1 | tf_op jit(solution)/shard_map/experts/pallas_call | solution.py:337
  79.4 0.6 collective-permute-start.22
  80.3 0.5 collective-permute-start.29
  80.8 0.5 collective-permute-start.11
  81.3 0.2 collective-permute-done.22
  81.8 0.6 collective-permute-start.23
  82.3 0.4 collective-permute-done.29.refs_4_
  82.7 3.8 %experts.7 = (f32[2,2,64,1024]{3,2,1,0:T(8,128)S(1)}, bf16[2,2,64,1024]{3,2,1,0:T(8,128)(2,1)S(1)}) custom-call(s32[3]{0:T(128)S(1)} %pad_add_fusion.row_ref.refs_0_, bf16[2,64,1152]{2,1,0:T(8,128)(2,1)S(1)} %collective-permute-done.14.refs_1_, bf16[2,64,1152]{2,1,0:T(8,128)(2,1)S(1)} %collective-permute-done.27.refs_2_, ...), custom_call_target="tpu_custom_call" | custom-call | flops 1 | bytes 1 | tf_op jit(solution)/shard_map/experts/pallas_call | solution.py:337
  86.6 0.4 collective-permute-start.30
  87.2 0.6 collective-permute-start.26
  87.8 2.6 %collective-permute-done.23 = bf16[1,2,64,1024]{3,2,1,0:T(8,128)(2,1)S(1)} collective-permute-done((bf16[1,2,64,1024]{3,2,1,0:T(8,128)(2,1)S(1)}, bf16[1,2,64,1024]{3,2,1,0:T(8,128)(2,1)S(1)}, u32[]{:S(2)}, u32[]{:S(2)}) %collective-permute-start.23) | collective-permute-done | bytes 262176 | tf_op jit(solution)/shard_map/ppermute | solution.py:357
  90.5 0.8 collective-permute-start.33
  91.4 0.6 collective-permute-start.24
  92.0 0.2 convert_add_fusion
  92.2 1.3 %collective-permute-start.35 = (bf16[2,64,1024]{2,1,0:T(8,128)(2,1)S(1)}, bf16[2,64,1024]{2,1,0:T(8,128)(2,1)S(1)}, u32[]{:S(2)}, u32[]{:S(2)}) collective-permute-start(bf16[2,64,1024]{2,1,0:T(8,128)(2,1)S(1)} %fusion.5), channel_id=1, source_target_pairs={{0,4},{2,6},{4,0},{6,2},{1,5},{3,7},{5,1},{7,3},{8,12},{10,14},{12... | collective-permute-start | bytes 786440 | tf_op jit(solution)/shard_map/ppermute | solution.py:357
  93.5 2.9 %collective-permute-done.26 = bf16[2,64,1024]{2,1,0:T(8,128)(2,1)S(1)} collective-permute-done((bf16[2,64,1024]{2,1,0:T(8,128)(2,1)S(1)}, bf16[2,64,1024]{2,1,0:T(8,128)(2,1)S(1)}, u32[]{:S(2)}, u32[]{:S(2)}) %collective-permute-start.26) | collective-permute-done | bytes 262176 | tf_op jit(solution)/shard_map/ppermute | solution.py:357
  96.5 0.9 collective-permute-start.31
  97.4 1.8 %collective-permute-done.33 = bf16[64,1024]{1,0:T(8,128)(2,1)S(1)} collective-permute-done((bf16[64,1024]{1,0:T(8,128)(2,1)S(1)}, bf16[64,1024]{1,0:T(8,128)(2,1)S(1)}, u32[]{:S(2)}, u32[]{:S(2)}) %collective-permute-start.33) | collective-permute-done | bytes 131104 | tf_op jit(solution)/shard_map/ppermute | solution.py:357
  99.3 1.6 %collective-permute-start.34 = (bf16[64,1024]{1,0:T(8,128)(2,1)S(1)}, bf16[64,1024]{1,0:T(8,128)(2,1)S(1)}, u32[]{:S(2)}, u32[]{:S(2)}) collective-permute-start(bf16[64,1024]{1,0:T(8,128)(2,1)S(1)} %fusion.8), channel_id=1, source_target_pairs={{0,16},{8,24},{16,0},{24,8},{1,17},{9,25},{17,1},{25,9},{2,18},{10... | collective-permute-start | bytes 393224 | tf_op jit(solution)/shard_map/ppermute | solution.py:357
  100.8 0.7 collective-permute-done.31
  101.6 2.5 %collective-permute-done.35 = bf16[2,64,1024]{2,1,0:T(8,128)(2,1)S(1)} collective-permute-done((bf16[2,64,1024]{2,1,0:T(8,128)(2,1)S(1)}, bf16[2,64,1024]{2,1,0:T(8,128)(2,1)S(1)}, u32[]{:S(2)}, u32[]{:S(2)}) %collective-permute-start.35) | collective-permute-done | bytes 262176 | tf_op jit(solution)/shard_map/ppermute | solution.py:357
  104.1 1.2 %collective-permute-start.36 = (bf16[1,64,1024]{2,1,0:T(8,128)(2,1)S(1)}, bf16[1,64,1024]{2,1,0:T(8,128)(2,1)S(1)}, u32[]{:S(2)}, u32[]{:S(2)}) collective-permute-start(bf16[1,64,1024]{2,1,0:T(8,128)(2,1)S(1)} %slice.172), channel_id=1, source_target_pairs={{0,1},{1,0},{2,3},{3,2},{4,5},{5,4},{6,7},{7,6},{8,9},{9,8},{10,11... | collective-permute-start | bytes 393224 | tf_op jit(solution)/shard_map/ppermute | solution.py:357
  105.4 3.5 %collective-permute-start.32 = (bf16[64,1024]{1,0:T(8,128)(2,1)S(1)}, bf16[64,1024]{1,0:T(8,128)(2,1)S(1)}, u32[]{:S(2)}, u32[]{:S(2)}) collective-permute-start(bf16[64,1024]{1,0:T(8,128)(2,1)S(1)} %fusion.17), channel_id=1, source_target_pairs={{0,24},{8,16},{16,8},{24,0},{1,25},{9,17},{17,9},{25,1},{2,26},{10... | collective-permute-start | bytes 393224 | tf_op jit(solution)/shard_map/ppermute | solution.py:357
  108.9 0.2 collective-permute-done.36
  109.2 0.4 collective-permute-start.37
  109.6 3.1 %collective-permute-done.32 = bf16[64,1024]{1,0:T(8,128)(2,1)S(1)} collective-permute-done((bf16[64,1024]{1,0:T(8,128)(2,1)S(1)}, bf16[64,1024]{1,0:T(8,128)(2,1)S(1)}, u32[]{:S(2)}, u32[]{:S(2)}) %collective-permute-start.32) | collective-permute-done | bytes 131104 | tf_op jit(solution)/shard_map/ppermute | solution.py:357
  112.7 2.2 %collective-permute-done.37 = bf16[64,1024]{1,0:T(8,128)(2,1)S(1)} collective-permute-done((bf16[64,1024]{1,0:T(8,128)(2,1)S(1)}, bf16[64,1024]{1,0:T(8,128)(2,1)S(1)}, u32[]{:S(2)}, u32[]{:S(2)}) %collective-permute-start.37) | collective-permute-done | bytes 131104 | tf_op jit(solution)/shard_map/ppermute | solution.py:357
  115.0 1.1 collective-permute-start.38
  116.1 4.0 %collective-permute-done.38.others_ref = bf16[1,64,1024]{2,1,0:T(8,128)(2,1)S(1)} collective-permute-done((bf16[1,64,1024]{2,1,0:T(8,128)(2,1)S(1)}, bf16[1,64,1024]{2,1,0:T(8,128)(2,1)S(1)}, u32[]{:S(2)}, u32[]{:S(2)}) %collective-permute-start.38) | collective-permute-done | bytes 131104 | tf_op jit(solution)/shard_map/ppermute | solution.py:357
  120.1 1.3 %finish.1 = bf16[64,2048]{1,0:T(8,128)(2,1)} custom-call(s32[3]{0:T(128)S(1)} %pad_add_fusion.row_ref.refs_0_, bf16[64,1024]{1,0:T(8,128)(2,1)S(1)} %fusion.15.own_ref, bf16[1,64,1024]{2,1,0:T(8,128)(2,1)S(1)} %collective-permute-done.38.others_ref), custom_call_target="tpu_custom_call" | custom-call | tf_op jit(solution)/shard_map/finish/pallas_call | solution.py:275
  (94 shorter events, 2.1 us)
Async XLA Ops:
  0.6 9.6 %collective-permute-start.1 = (bf16[64,2048]{1,0:T(8,128)(2,1)}, bf16[64,2048]{1,0:T(8,128)(2,1)S(1)}, u32[]{:S(2)}, u32[]{:S(2)}) collective-permute-start(bf16[64,2048]{1,0:T(8,128)(2,1)} %hidden_ref.1), channel_id=1, source_target_pairs={{0,4},{2,6},{4,0},{6,2},{1,5},{3,7},{5,1},{7,3},{8,12},{10,14},{12... | collective-permute-start | bytes 786440 | tf_op jit(solution)/shard_map/ppermute | solution.py:357
  4.4 0.7 copy-start.14
  5.1 0.7 copy-start.15
  5.7 6.0 %copy-start.1 = (bf16[2048,576]{0,1:T(8,128)(2,1)S(1)}, bf16[2048,576]{0,1:T(8,128)(2,1)}, u32[]{:S(2)}) copy-start(bf16[2048,576]{0,1:T(8,128)(2,1)} %param.27) | copy-start | bytes 7077892
  5.7 6.0 %copy-start.2 = (bf16[4,384,576]{1,2,0:T(8,128)(2,1)S(1)}, bf16[4,384,576]{1,2,0:T(8,128)(2,1)}, u32[]{:S(2)}) copy-start(bf16[4,384,576]{1,2,0:T(8,128)(2,1)} %param.20) | copy-start | bytes 5308420
  5.7 6.0 %copy-start.3 = (bf16[2048,384]{1,0:T(8,128)(2,1)S(1)}, bf16[2048,384]{1,0:T(8,128)(2,1)}, u32[]{:S(2)}) copy-start(bf16[2048,384]{1,0:T(8,128)(2,1)} %refs_7_.3) | copy-start | bytes 4718596
  5.7 6.0 %copy-start.4 = (bf16[256,2048]{1,0:T(8,128)(2,1)S(1)}, bf16[256,2048]{1,0:T(8,128)(2,1)}, u32[]{:S(2)}) copy-start(bf16[256,2048]{1,0:T(8,128)(2,1)} %refs_12_.3) | copy-start | bytes 3145732
  5.7 6.0 %copy-start.8 = (bf16[2,128,512]{2,1,0:T(8,128)(2,1)S(1)}, bf16[2,128,512]{2,1,0:T(8,128)(2,1)}, u32[]{:S(2)}) copy-start(bf16[2,128,512]{2,1,0:T(8,128)(2,1)} %refs_10_.4) | copy-start | bytes 786436
  5.8 6.0 %copy-start.9 = (bf16[2,512,128]{2,1,0:T(8,128)(2,1)S(1)}, bf16[2,512,128]{2,1,0:T(8,128)(2,1)}, u32[]{:S(2)}) copy-start(bf16[2,512,128]{2,1,0:T(8,128)(2,1)} %refs_11_.3) | copy-start | bytes 786436
  5.8 6.0 %copy-start.11 = (f32[2048]{0:T(1024)S(1)}, f32[2048]{0:T(1024)}, u32[]{:S(2)}) copy-start(f32[2048]{0:T(1024)} %param.25) | copy-start | bytes 24580
  5.8 6.0 %copy-start.12 = (f32[512]{0:T(512)S(1)}, f32[512]{0:T(512)}, u32[]{:S(2)}) copy-start(f32[512]{0:T(512)} %param.28) | copy-start | bytes 6148
  10.2 1.5 %collective-permute-start.2 = (bf16[64,2048]{1,0:T(8,128)(2,1)S(1)}, bf16[64,2048]{1,0:T(8,128)(2,1)S(1)}, u32[]{:S(2)}, u32[]{:S(2)}) collective-permute-start(bf16[64,2048]{1,0:T(8,128)(2,1)S(1)} %collective-permute-done.1.refs_0_), channel_id=1, source_target_pairs={{0,2},{2,0},{4,6},{6,4},{1,3},{3,1},{5,7},{7,5},{8,10},{10,8},{12,... | collective-permute-start | bytes 786440 | tf_op jit(solution)/shard_map/ppermute | solution.py:357
  11.8 4.0 %copy-start.10 = (bf16[64,2048]{1,0:T(8,128)(2,1)S(1)}, bf16[64,2048]{1,0:T(8,128)(2,1)}, u32[]{:S(2)}) copy-start(bf16[64,2048]{1,0:T(8,128)(2,1)} %hidden_ref.1) | copy-start | bytes 786436
  15.6 1.6 %collective-permute-start.3 = (bf16[64,2048]{1,0:T(8,128)(2,1)S(1)}, bf16[64,2048]{1,0:T(8,128)(2,1)S(1)}, u32[]{:S(2)}, u32[]{:S(2)}) collective-permute-start(bf16[64,2048]{1,0:T(8,128)(2,1)S(1)} %get-tuple-element.38), channel_id=1, source_target_pairs={{0,2},{2,0},{4,6},{6,4},{1,3},{3,1},{5,7},{7,5},{8,10},{10,8},{12,... | collective-permute-start | bytes 786440 | tf_op jit(solution)/shard_map/ppermute | solution.py:357
  15.8 3.3 %collective-permute-start = (bf16[64,2048]{1,0:T(8,128)(2,1)S(1)}, bf16[64,2048]{1,0:T(8,128)(2,1)S(1)}, u32[]{:S(2)}, u32[]{:S(2)}) collective-permute-start(bf16[64,2048]{1,0:T(8,128)(2,1)S(1)} %copy-done.10), channel_id=1, source_target_pairs={{0,2},{2,0},{4,6},{6,4},{1,3},{3,1},{5,7},{7,5},{8,10},{10,8},{12,... | collective-permute-start | bytes 786440 | tf_op jit(solution)/shard_map/ppermute | solution.py:357
  17.3 10.3 %copy-start.16 = (s32[64,6]{0,1:T(8,128)S(1)}, s32[64,6]{0,1:T(8,128)}, u32[]{:S(2)}) copy-start(s32[64,6]{0,1:T(8,128)} %param.23) | copy-start | bytes 4612
  17.3 16.3 %copy-start.13 = (f32[2048]{0:T(1024)S(1)}, f32[2048]{0:T(1024)}, u32[]{:S(2)}) copy-start(f32[2048]{0:T(1024)} %param.32) | copy-start | bytes 24580
  17.3 8.4 %collective-permute-start.5 = (bf16[64,2048]{1,0:T(8,128)(2,1)S(1)}, bf16[64,2048]{1,0:T(8,128)(2,1)S(1)}, u32[]{:S(2)}, u32[]{:S(2)}) collective-permute-start(bf16[64,2048]{1,0:T(8,128)(2,1)S(1)} %add_convert_fusion.1), channel_id=1, source_target_pairs={{0,4},{2,6},{4,0},{6,2},{1,5},{3,7},{5,1},{7,3},{8,12},{10,14},{12... | collective-permute-start | bytes 786440 | tf_op jit(solution)/shard_map/ppermute | solution.py:357
  23.5 2.2 %collective-permute-start.4 = (bf16[64,2048]{1,0:T(8,128)(2,1)S(1)}, bf16[64,2048]{1,0:T(8,128)(2,1)S(1)}, u32[]{:S(2)}, u32[]{:S(2)}) collective-permute-start(bf16[64,2048]{1,0:T(8,128)(2,1)S(1)} %get-tuple-element.41), channel_id=1, source_target_pairs={{0,2},{2,0},{4,6},{6,4},{1,3},{3,1},{5,7},{7,5},{8,10},{10,8},{12,... | collective-permute-start | bytes 786440 | tf_op jit(solution)/shard_map/ppermute | solution.py:357
  25.8 7.7 %collective-permute-start.6 = (bf16[64,2048]{1,0:T(8,128)(2,1)S(1)}, bf16[64,2048]{1,0:T(8,128)(2,1)S(1)}, u32[]{:S(2)}, u32[]{:S(2)}) collective-permute-start(bf16[64,2048]{1,0:T(8,128)(2,1)S(1)} %add_convert_fusion.keep_ref), channel_id=1, source_target_pairs={{0,1},{1,0},{2,3},{3,2},{4,5},{5,4},{6,7},{7,6},{8,9},{9,8},{10,11... | collective-permute-start | bytes 786440 | tf_op jit(solution)/shard_map/ppermute | solution.py:357
  33.5 20.2 %slice-start = ((s8[5767168]{0:T(1024)(128)(4,1)}), s8[4194304]{0:T(1024)(128)(4,1)S(1)}, s32[]{:S(2)}) async-start(s8[5767168]{0:T(1024)(128)(4,1)} %bitcast.70), calls=%async_computation | async-start | bytes 8388608
  33.5 20.2 %slice-start.1 = ((s8[5767168]{0:T(1024)(128)(4,1)}), s8[1572864]{0:T(1024)(128)(4,1)S(1)}, s32[]{:S(2)}) async-start(s8[5767168]{0:T(1024)(128)(4,1)} %bitcast.70), calls=%async_computation.1 | async-start | bytes 3145728
  33.5 20.2 %copy-start = (bf16[1,704,2048]{2,1,0:T(8,128)(2,1)S(1)}, bf16[1,704,2048]{2,1,0:T(8,128)(2,1)}, u32[]{:S(2)}) copy-start(bf16[1,704,2048]{2,1,0:T(8,128)(2,1)} %param.37) | copy-start | bytes 8650756
  33.6 20.2 %copy-start.5 = (bf16[2,2048,352]{1,2,0:T(8,128)(2,1)S(1)}, bf16[2,2048,352]{1,2,0:T(8,128)(2,1)}, u32[]{:S(2)}) copy-start(bf16[2,2048,352]{1,2,0:T(8,128)(2,1)} %param.34) | copy-start | bytes 8650756
  33.6 20.2 %copy-start.6 = (bf16[352,2048]{1,0:T(8,128)(2,1)S(1)}, bf16[352,2048]{1,0:T(8,128)(2,1)}, u32[]{:S(2)}) copy-start(bf16[352,2048]{1,0:T(8,128)(2,1)} %refs_10_.5) | copy-start | bytes 4325380
  33.6 20.2 %copy-start.7 = (bf16[2048,16]{0,1:T(8,128)(2,1)S(1)}, bf16[2048,16]{0,1:T(8,128)(2,1)}, u32[]{:S(2)}) copy-start(bf16[2048,16]{0,1:T(8,128)(2,1)} %param.33) | copy-start | bytes 196612
  34.4 7.5 %collective-permute-start.7 = (bf16[2,64,1152]{2,1,0:T(8,128)(2,1)S(1)}, bf16[2,64,1152]{2,1,0:T(8,128)(2,1)S(1)}, u32[]{:S(2)}, u32[]{:S(2)}) collective-permute-start(bf16[2,64,1152]{2,1,0:T(8,128)(2,1)S(1)} %get-tuple-element.44.refs_1_), channel_id=1, source_target_pairs={{0,4},{2,6},{4,0},{6,2},{1,5},{3,7},{5,1},{7,3},{8,12},{10,14},{12... | collective-permute-start | bytes 884744 | tf_op jit(solution)/shard_map/ppermute | solution.py:357
  36.0 12.5 %collective-permute-start.13 = (bf16[1,64,1152]{2,1,0:T(8,128)(2,1)S(1)}, bf16[1,64,1152]{2,1,0:T(8,128)(2,1)S(1)}, u32[]{:S(2)}, u32[]{:S(2)}) collective-permute-start(bf16[1,64,1152]{2,1,0:T(8,128)(2,1)S(1)} %get-tuple-element.48), channel_id=1, source_target_pairs={{0,16},{8,24},{16,0},{24,8},{1,17},{9,25},{17,1},{25,9},{2,18},{10... | collective-permute-start | bytes 442376 | tf_op jit(solution)/shard_map/ppermute | solution.py:357
  38.6 9.9 %collective-permute-start.12 = (bf16[1,64,1152]{2,1,0:T(8,128)(2,1)S(1)}, bf16[1,64,1152]{2,1,0:T(8,128)(2,1)S(1)}, u32[]{:S(2)}, u32[]{:S(2)}) collective-permute-start(bf16[1,64,1152]{2,1,0:T(8,128)(2,1)S(1)} %get-tuple-element.48), channel_id=1, source_target_pairs={{0,24},{8,16},{16,8},{24,0},{1,25},{9,17},{17,9},{25,1},{2,26},{10... | collective-permute-start | bytes 442376 | tf_op jit(solution)/shard_map/ppermute | solution.py:357
  40.0 11.7 %collective-permute-start.14 = (bf16[2,64,1152]{2,1,0:T(8,128)(2,1)S(1)}, bf16[2,64,1152]{2,1,0:T(8,128)(2,1)S(1)}, u32[]{:S(2)}, u32[]{:S(2)}) collective-permute-start(bf16[2,64,1152]{2,1,0:T(8,128)(2,1)S(1)} %get-tuple-element.44.refs_1_), channel_id=1, source_target_pairs={{0,8},{8,0},{16,24},{24,16},{1,9},{9,1},{17,25},{25,17},{2,10},{10... | collective-permute-start | bytes 884744 | tf_op jit(solution)/shard_map/ppermute | solution.py:357
  40.2 13.5 %collective-permute-start.8 = (bf16[2,64,1152]{2,1,0:T(8,128)(2,1)S(1)}, bf16[2,64,1152]{2,1,0:T(8,128)(2,1)S(1)}, u32[]{:S(2)}, u32[]{:S(2)}) collective-permute-start(bf16[2,64,1152]{2,1,0:T(8,128)(2,1)S(1)} %get-tuple-element.44.refs_1_), channel_id=1, source_target_pairs={{0,2},{2,0},{4,6},{6,4},{1,3},{3,1},{5,7},{7,5},{8,10},{10,8},{12,... | collective-permute-start | bytes 884744 | tf_op jit(solution)/shard_map/ppermute | solution.py:357
  41.9 11.8 %collective-permute-start.9 = (bf16[2,64,1152]{2,1,0:T(8,128)(2,1)S(1)}, bf16[2,64,1152]{2,1,0:T(8,128)(2,1)S(1)}, u32[]{:S(2)}, u32[]{:S(2)}) collective-permute-start(bf16[2,64,1152]{2,1,0:T(8,128)(2,1)S(1)} %collective-permute-done.7.refs_2_), channel_id=1, source_target_pairs={{0,2},{2,0},{4,6},{6,4},{1,3},{3,1},{5,7},{7,5},{8,10},{10,8},{12,... | collective-permute-start | bytes 884744 | tf_op jit(solution)/shard_map/ppermute | solution.py:357
  51.7 7.7 %collective-permute-start.16 = (bf16[1,2,64,1152]{3,2,0,1:T(8,128)(2,1)S(1)}, bf16[1,2,64,1152]{3,2,0,1:T(8,128)(2,1)S(1)}, u32[]{:S(2)}, u32[]{:S(2)}) collective-permute-start(bf16[1,2,64,1152]{3,2,0,1:T(8,128)(2,1)S(1)} %maximum_bitcast_fusion), channel_id=1, source_target_pairs={{0,4},{2,6},{4,0},{6,2},{1,5},{3,7},{5,1},{7,3},{8,12},{10,14},{12... | collective-permute-start | bytes 884744 | tf_op jit(solution)/shard_map/ppermute | solution.py:357
  52.2 8.7 %collective-permute-start.15 = (bf16[1,2,64,1152]{3,2,0,1:T(8,128)(2,1)S(1)}, bf16[1,2,64,1152]{3,2,0,1:T(8,128)(2,1)S(1)}, u32[]{:S(2)}, u32[]{:S(2)}) collective-permute-start(bf16[1,2,64,1152]{3,2,0,1:T(8,128)(2,1)S(1)} %maximum_bitcast_fusion), channel_id=1, source_target_pairs={{0,1},{1,0},{2,3},{3,2},{4,5},{5,4},{6,7},{7,6},{8,9},{9,8},{10,11... | collective-permute-start | bytes 884744 | tf_op jit(solution)/shard_map/ppermute | solution.py:357
  59.0 16.6 %collective-permute-start.10 = (bf16[2,2,64,1024]{3,2,1,0:T(8,128)(2,1)S(1)}, bf16[2,2,64,1024]{3,2,1,0:T(8,128)(2,1)S(1)}, u32[]{:S(2)}, u32[]{:S(2)}) collective-permute-start(bf16[2,2,64,1024]{3,2,1,0:T(8,128)(2,1)S(1)} %get-tuple-element.47), channel_id=1, source_target_pairs={{0,2},{2,0},{4,6},{6,4},{1,3},{3,1},{5,7},{7,5},{8,10},{10,8},{12,... | collective-permute-start | bytes 1572872 | tf_op jit(solution)/shard_map/ppermute | solution.py:357
  59.4 9.1 %collective-permute-start.17 = (bf16[1,2,64,1152]{3,2,0,1:T(8,128)(2,1)S(1)}, bf16[1,2,64,1152]{3,2,0,1:T(8,128)(2,1)S(1)}, u32[]{:S(2)}, u32[]{:S(2)}) collective-permute-start(bf16[1,2,64,1152]{3,2,0,1:T(8,128)(2,1)S(1)} %collective-permute-done.16), channel_id=1, source_target_pairs={{0,1},{1,0},{2,3},{3,2},{4,5},{5,4},{6,7},{7,6},{8,9},{9,8},{10,11... | collective-permute-start | bytes 884744 | tf_op jit(solution)/shard_map/ppermute | solution.py:357
  68.5 1.6 %collective-permute-start.21 = (bf16[2,64,1152]{2,1,0:T(8,128)(2,1)S(1)}, bf16[2,64,1152]{2,1,0:T(8,128)(2,1)S(1)}, u32[]{:S(2)}, u32[]{:S(2)}) collective-permute-start(bf16[2,64,1152]{2,1,0:T(8,128)(2,1)S(1)} %get-tuple-element.66.refs_2_), channel_id=1, source_target_pairs={{0,2},{2,0},{4,6},{6,4},{1,3},{3,1},{5,7},{7,5},{8,10},{10,8},{12,... | collective-permute-start | bytes 884744 | tf_op jit(solution)/shard_map/ppermute | solution.py:357
  68.7 3.1 %collective-permute-start.20 = (bf16[2,64,1152]{2,1,0:T(8,128)(2,1)S(1)}, bf16[2,64,1152]{2,1,0:T(8,128)(2,1)S(1)}, u32[]{:S(2)}, u32[]{:S(2)}) collective-permute-start(bf16[2,64,1152]{2,1,0:T(8,128)(2,1)S(1)} %get-tuple-element.68.refs_1_), channel_id=1, source_target_pairs={{0,2},{2,0},{4,6},{6,4},{1,3},{3,1},{5,7},{7,5},{8,10},{10,8},{12,... | collective-permute-start | bytes 884744 | tf_op jit(solution)/shard_map/ppermute | solution.py:357
  69.2 6.4 %collective-permute-start.19 = (bf16[2,64,1152]{2,1,0:T(8,128)(2,1)S(1)}, bf16[2,64,1152]{2,1,0:T(8,128)(2,1)S(1)}, u32[]{:S(2)}, u32[]{:S(2)}) collective-permute-start(bf16[2,64,1152]{2,1,0:T(8,128)(2,1)S(1)} %get-tuple-element.67.refs_2_), channel_id=1, source_target_pairs={{0,2},{2,0},{4,6},{6,4},{1,3},{3,1},{5,7},{7,5},{8,10},{10,8},{12,... | collective-permute-start | bytes 884744 | tf_op jit(solution)/shard_map/ppermute | solution.py:357
  69.3 6.3 %collective-permute-start.18 = (bf16[2,64,1152]{2,1,0:T(8,128)(2,1)S(1)}, bf16[2,64,1152]{2,1,0:T(8,128)(2,1)S(1)}, u32[]{:S(2)}, u32[]{:S(2)}) collective-permute-start(bf16[2,64,1152]{2,1,0:T(8,128)(2,1)S(1)} %get-tuple-element.69.refs_1_), channel_id=1, source_target_pairs={{0,2},{2,0},{4,6},{6,4},{1,3},{3,1},{5,7},{7,5},{8,10},{10,8},{12,... | collective-permute-start | bytes 884744 | tf_op jit(solution)/shard_map/ppermute | solution.py:357
  70.2 10.1 %collective-permute-start.27 = (bf16[2,64,1152]{2,1,0:T(8,128)(2,1)S(1)}, bf16[2,64,1152]{2,1,0:T(8,128)(2,1)S(1)}, u32[]{:S(2)}, u32[]{:S(2)}) collective-permute-start(bf16[2,64,1152]{2,1,0:T(8,128)(2,1)S(1)} %collective-permute-done.14.refs_1_), channel_id=1, source_target_pairs={{0,4},{2,6},{4,0},{6,2},{1,5},{3,7},{5,1},{7,3},{8,12},{10,14},{12... | collective-permute-start | bytes 884744 | tf_op jit(solution)/shard_map/ppermute | solution.py:357
  71.7 11.0 %collective-permute-start.28 = (bf16[2,64,1152]{2,1,0:T(8,128)(2,1)S(1)}, bf16[2,64,1152]{2,1,0:T(8,128)(2,1)S(1)}, u32[]{:S(2)}, u32[]{:S(2)}) collective-permute-start(bf16[2,64,1152]{2,1,0:T(8,128)(2,1)S(1)} %collective-permute-done.14.refs_1_), channel_id=1, source_target_pairs={{0,2},{2,0},{4,6},{6,4},{1,3},{3,1},{5,7},{7,5},{8,10},{10,8},{12,... | collective-permute-start | bytes 884744 | tf_op jit(solution)/shard_map/ppermute | solution.py:357
  79.4 2.1 %collective-permute-start.22 = (bf16[2,2,64,1024]{3,2,1,0:T(8,128)(2,1)S(1)}, bf16[2,2,64,1024]{3,2,1,0:T(8,128)(2,1)S(1)}, u32[]{:S(2)}, u32[]{:S(2)}) collective-permute-start(bf16[2,2,64,1024]{3,2,1,0:T(8,128)(2,1)S(1)} %get-tuple-element.54), channel_id=1, source_target_pairs={{0,2},{2,0},{4,6},{6,4},{1,3},{3,1},{5,7},{7,5},{8,10},{10,8},{12,... | collective-permute-start | bytes 1572872 | tf_op jit(solution)/shard_map/ppermute | solution.py:357
  80.2 2.6 %collective-permute-start.25 = (bf16[2,2,64,1024]{3,2,1,0:T(8,128)(2,1)S(1)}, bf16[2,2,64,1024]{3,2,1,0:T(8,128)(2,1)S(1)}, u32[]{:S(2)}, u32[]{:S(2)}) collective-permute-start(bf16[2,2,64,1024]{3,2,1,0:T(8,128)(2,1)S(1)} %get-tuple-element.51), channel_id=1, source_target_pairs={{0,2},{2,0},{4,6},{6,4},{1,3},{3,1},{5,7},{7,5},{8,10},{10,8},{12,... | collective-permute-start | bytes 1572872 | tf_op jit(solution)/shard_map/ppermute | solution.py:357
  80.3 2.5 %collective-permute-start.29 = (bf16[2,64,1152]{2,1,0:T(8,128)(2,1)S(1)}, bf16[2,64,1152]{2,1,0:T(8,128)(2,1)S(1)}, u32[]{:S(2)}, u32[]{:S(2)}) collective-permute-start(bf16[2,64,1152]{2,1,0:T(8,128)(2,1)S(1)} %collective-permute-done.27.refs_2_), channel_id=1, source_target_pairs={{0,2},{2,0},{4,6},{6,4},{1,3},{3,1},{5,7},{7,5},{8,10},{10,8},{12,... | collective-permute-start | bytes 884744 | tf_op jit(solution)/shard_map/ppermute | solution.py:357
  80.8 9.7 %collective-permute-start.11 = (bf16[2,64,1024]{2,1,0:T(8,128)(2,1)S(1)}, bf16[2,64,1024]{2,1,0:T(8,128)(2,1)S(1)}, u32[]{:S(2)}, u32[]{:S(2)}) collective-permute-start(bf16[2,64,1024]{2,1,0:T(8,128)(2,1)S(1)} %fusion.3), channel_id=1, source_target_pairs={{0,4},{2,6},{4,0},{6,2},{1,5},{3,7},{5,1},{7,3},{8,12},{10,14},{12... | collective-permute-start | bytes 786440 | tf_op jit(solution)/shard_map/ppermute | solution.py:357
  81.8 8.7 %collective-permute-start.23 = (bf16[1,2,64,1024]{3,2,1,0:T(8,128)(2,1)S(1)}, bf16[1,2,64,1024]{3,2,1,0:T(8,128)(2,1)S(1)}, u32[]{:S(2)}, u32[]{:S(2)}) collective-permute-start(bf16[1,2,64,1024]{3,2,1,0:T(8,128)(2,1)S(1)} %slice.171), channel_id=1, source_target_pairs={{0,1},{1,0},{2,3},{3,2},{4,5},{5,4},{6,7},{7,6},{8,9},{9,8},{10,11... | collective-permute-start | bytes 786440 | tf_op jit(solution)/shard_map/ppermute | solution.py:357
  86.6 5.4 %collective-permute-start.30 = (bf16[2,2,64,1024]{3,2,1,0:T(8,128)(2,1)S(1)}, bf16[2,2,64,1024]{3,2,1,0:T(8,128)(2,1)S(1)}, u32[]{:S(2)}, u32[]{:S(2)}) collective-permute-start(bf16[2,2,64,1024]{3,2,1,0:T(8,128)(2,1)S(1)} %get-tuple-element.60), channel_id=1, source_target_pairs={{0,2},{2,0},{4,6},{6,4},{1,3},{3,1},{5,7},{7,5},{8,10},{10,8},{12,... | collective-permute-start | bytes 1572872 | tf_op jit(solution)/shard_map/ppermute | solution.py:357
  87.2 9.2 %collective-permute-start.26 = (bf16[2,64,1024]{2,1,0:T(8,128)(2,1)S(1)}, bf16[2,64,1024]{2,1,0:T(8,128)(2,1)S(1)}, u32[]{:S(2)}, u32[]{:S(2)}) collective-permute-start(bf16[2,64,1024]{2,1,0:T(8,128)(2,1)S(1)} %fusion.4), channel_id=1, source_target_pairs={{0,4},{2,6},{4,0},{6,2},{1,5},{3,7},{5,1},{7,3},{8,12},{10,14},{12... | collective-permute-start | bytes 786440 | tf_op jit(solution)/shard_map/ppermute | solution.py:357
  90.5 8.7 %collective-permute-start.33 = (bf16[64,1024]{1,0:T(8,128)(2,1)S(1)}, bf16[64,1024]{1,0:T(8,128)(2,1)S(1)}, u32[]{:S(2)}, u32[]{:S(2)}) collective-permute-start(bf16[64,1024]{1,0:T(8,128)(2,1)S(1)} %fusion.18), channel_id=1, source_target_pairs={{0,4},{2,6},{4,0},{6,2},{1,5},{3,7},{5,1},{7,3},{8,12},{10,14},{12... | collective-permute-start | bytes 393224 | tf_op jit(solution)/shard_map/ppermute | solution.py:357
  91.4 18.2 %collective-permute-start.24 = (bf16[1,64,1024]{2,1,0:T(8,128)(2,1)S(1)}, bf16[1,64,1024]{2,1,0:T(8,128)(2,1)S(1)}, u32[]{:S(2)}, u32[]{:S(2)}) collective-permute-start(bf16[1,64,1024]{2,1,0:T(8,128)(2,1)S(1)} %slice.174), channel_id=1, source_target_pairs={{0,1},{1,0},{2,3},{3,2},{4,5},{5,4},{6,7},{7,6},{8,9},{9,8},{10,11... | collective-permute-start | bytes 393224 | tf_op jit(solution)/shard_map/ppermute | solution.py:357
  92.2 11.8 %collective-permute-start.35 = (bf16[2,64,1024]{2,1,0:T(8,128)(2,1)S(1)}, bf16[2,64,1024]{2,1,0:T(8,128)(2,1)S(1)}, u32[]{:S(2)}, u32[]{:S(2)}) collective-permute-start(bf16[2,64,1024]{2,1,0:T(8,128)(2,1)S(1)} %fusion.5), channel_id=1, source_target_pairs={{0,4},{2,6},{4,0},{6,2},{1,5},{3,7},{5,1},{7,3},{8,12},{10,14},{12... | collective-permute-start | bytes 786440 | tf_op jit(solution)/shard_map/ppermute | solution.py:357
  96.5 5.0 %collective-permute-start.31 = (bf16[1,64,1024]{2,1,0:T(8,128)(2,1)S(1)}, bf16[1,64,1024]{2,1,0:T(8,128)(2,1)S(1)}, u32[]{:S(2)}, u32[]{:S(2)}) collective-permute-start(bf16[1,64,1024]{2,1,0:T(8,128)(2,1)S(1)} %slice.173), channel_id=1, source_target_pairs={{0,1},{1,0},{2,3},{3,2},{4,5},{5,4},{6,7},{7,6},{8,9},{9,8},{10,11... | collective-permute-start | bytes 393224 | tf_op jit(solution)/shard_map/ppermute | solution.py:357
  99.3 10.4 %collective-permute-start.34 = (bf16[64,1024]{1,0:T(8,128)(2,1)S(1)}, bf16[64,1024]{1,0:T(8,128)(2,1)S(1)}, u32[]{:S(2)}, u32[]{:S(2)}) collective-permute-start(bf16[64,1024]{1,0:T(8,128)(2,1)S(1)} %fusion.8), channel_id=1, source_target_pairs={{0,16},{8,24},{16,0},{24,8},{1,17},{9,25},{17,1},{25,9},{2,18},{10... | collective-permute-start | bytes 393224 | tf_op jit(solution)/shard_map/ppermute | solution.py:357
  104.1 5.0 %collective-permute-start.36 = (bf16[1,64,1024]{2,1,0:T(8,128)(2,1)S(1)}, bf16[1,64,1024]{2,1,0:T(8,128)(2,1)S(1)}, u32[]{:S(2)}, u32[]{:S(2)}) collective-permute-start(bf16[1,64,1024]{2,1,0:T(8,128)(2,1)S(1)} %slice.172), channel_id=1, source_target_pairs={{0,1},{1,0},{2,3},{3,2},{4,5},{5,4},{6,7},{7,6},{8,9},{9,8},{10,11... | collective-permute-start | bytes 393224 | tf_op jit(solution)/shard_map/ppermute | solution.py:357
  105.4 7.3 %collective-permute-start.32 = (bf16[64,1024]{1,0:T(8,128)(2,1)S(1)}, bf16[64,1024]{1,0:T(8,128)(2,1)S(1)}, u32[]{:S(2)}, u32[]{:S(2)}) collective-permute-start(bf16[64,1024]{1,0:T(8,128)(2,1)S(1)} %fusion.17), channel_id=1, source_target_pairs={{0,24},{8,16},{16,8},{24,0},{1,25},{9,17},{17,9},{25,1},{2,26},{10... | collective-permute-start | bytes 393224 | tf_op jit(solution)/shard_map/ppermute | solution.py:357
  109.2 5.7 %collective-permute-start.37 = (bf16[64,1024]{1,0:T(8,128)(2,1)S(1)}, bf16[64,1024]{1,0:T(8,128)(2,1)S(1)}, u32[]{:S(2)}, u32[]{:S(2)}) collective-permute-start(bf16[64,1024]{1,0:T(8,128)(2,1)S(1)} %fusion.19), channel_id=1, source_target_pairs={{0,8},{8,0},{16,24},{24,16},{1,9},{9,1},{17,25},{25,17},{2,10},{10... | collective-permute-start | bytes 393224 | tf_op jit(solution)/shard_map/ppermute | solution.py:357
  115.0 5.0 %collective-permute-start.38 = (bf16[1,64,1024]{2,1,0:T(8,128)(2,1)S(1)}, bf16[1,64,1024]{2,1,0:T(8,128)(2,1)S(1)}, u32[]{:S(2)}, u32[]{:S(2)}) collective-permute-start(bf16[1,64,1024]{2,1,0:T(8,128)(2,1)S(1)} %bitcast.89), channel_id=1, source_target_pairs={{0,1},{1,0},{2,3},{3,2},{4,5},{5,4},{6,7},{7,6},{8,9},{9,8},{10,11... | collective-permute-start | bytes 393224 | tf_op jit(solution)/shard_map/ppermute | solution.py:357

commit v11 on v10

--- a/solution.py
+++ b/solution.py
@@ -462,7 +462,7 @@
             part = third
         else:
             from_far = swap(near_sum[1].astype(bf16), "row", n_row, 2)
-            from_far = after(from_far, *(cores[2:] if k == 1 else arrivals))
+            from_far = after(from_far, *(arrivals if k == 0 else () if k == n_req - 1 else ()))
             part = near_sum[0] + from_far.astype(jnp.float32)
             part = col_scatter(part, n_col, arrivals if k == 1 else ())[0][0]
         parts.append(part.astype(bf16) if k else part)

time: 122 us -> 127 us (1.041)
  starting transfers between devices: 34 us -> 38.1 us
  waiting for transfers between devices: 53.2 us -> 54.8 us
    ppermute x39, starting transfers between devices: 34 us -> 38.1 us  [swap(): return lax.ppermute(values, axis, [(i, i ^ bits) for i in range(size)])]
    ppermute x39, waiting for transfers between devices: 53.2 us -> 54.8 us  [swap(): return lax.ppermute(values, axis, [(i, i ^ bits) for i in range(size)])]
  transfers between devices with their start and end apart: 39 -> 39, of which waited for: 22 -> 21; matrix products, arithmetic and copies ran while one was open for 1% -> 1% of each run, Pallas kernels for 19% -> 18%
where the time goes in v11:
time: 127 us
  waiting for transfers between devices  54.8 us (43%)
  starting transfers between devices  38.1 us (30%)
  Pallas kernels  29.3 us (23%)
  local copies, waits for them, and re-layouts  1.82 us (1%)
  between operations  1.76 us (1%)
  other arithmetic  1.5 us (1%)
    ppermute x39, waiting for transfers between devices, swap(): return lax.ppermute(values, axis, [(i, i ^ bits) for i in range(size)])  54.8 us
    ppermute x39, starting transfers between devices, swap(): return lax.ppermute(values, axis, [(i, i ^ bits) for i in range(size)])  38.1 us
    pallas_call x4, Pallas kernels, expert_part(): pl.pallas_call(functools.partial(expert_kernel, bool(shared_weights), far...  16.9 us
    pallas_call x2, Pallas kernels, attention_part(): pl.pallas_call(functools.partial(attention_kernel, first, place), out_sha...  8.2 us
  transfers between devices with their start and end apart: 39, of which 21 were waited for; matrix products, arithmetic and copies ran while one was open for 1% of the time, Pallas kernels for 18%

profile of v11, /device:TPU:0, one launch (start us, length us, event | category | flops | bytes accessed | tf_op | source)
XLA Modules:
  0.0 127.2 jit_solution(233113653374360839)
XLA Ops:
  0.6 3.0 %collective-permute-start.1 = (bf16[64,2048]{1,0:T(8,128)(2,1)}, bf16[64,2048]{1,0:T(8,128)(2,1)S(1)}, u32[]{:S(2)}, u32[]{:S(2)}) collective-permute-start(bf16[64,2048]{1,0:T(8,128)(2,1)} %hidden_ref.1), channel_id=1, source_target_pairs={{0,4},{2,6},{4,0},{6,2},{1,5},{3,7},{5,1},{7,3},{8,12},{10,14},{12... | collective-permute-start | bytes 786440 | tf_op jit(solution)/shard_map/ppermute | solution.py:357
  4.4 0.7 copy-done.14
  5.1 0.7 copy-done.15
  5.8 2.1 %trees.1 = (f32[4,64,64]{2,1,0:T(8,128)S(1)}, f32[4,64,65]{2,1,0:T(8,128)S(1)}, bf16[64,64]{1,0:T(8,128)(2,1)S(1)}, f32[1,16]{1,0:T(1,128)S(1)}) custom-call(s32[3]{0:T(128)S(1)} %pad_add_fusion.row_ref.refs_0_, s32[4]{0:T(128)S(1)} %copy-done.15, s32[1]{0:T(128)S(6)} %copy.24.accepted_ref, s32[4,64]{1,0:T(4,128)S(1)} %copy-done.14), custom_call_target="tpu_custom_call" | custom-call | flops 20000000000 | bytes 1 | tf_op jit(solution)/shard_map/trees/pallas_call | solution.py:110
  7.9 2.2 %collective-permute-done.1.refs_0_ = bf16[64,2048]{1,0:T(8,128)(2,1)S(1)} collective-permute-done((bf16[64,2048]{1,0:T(8,128)(2,1)}, bf16[64,2048]{1,0:T(8,128)(2,1)S(1)}, u32[]{:S(2)}, u32[]{:S(2)}) %collective-permute-start.1) | collective-permute-done | bytes 262176 | tf_op jit(solution)/shard_map/ppermute | solution.py:357
  10.2 1.5 %collective-permute-done.2.refs_1_ = bf16[64,2048]{1,0:T(8,128)(2,1)S(1)} collective-permute-done((bf16[64,2048]{1,0:T(8,128)(2,1)S(1)}, bf16[64,2048]{1,0:T(8,128)(2,1)S(1)}, u32[]{:S(2)}, u32[]{:S(2)}) %collective-permute-start.2) | collective-permute-done | bytes 262176 | tf_op jit(solution)/shard_map/ppermute | solution.py:357
  11.8 3.8 %attention.2 = (f32[64,2048]{1,0:T(8,128)S(1)}, bf16[64,2048]{1,0:T(8,128)(2,1)S(1)}) custom-call(s32[3]{0:T(128)S(1)} %pad_add_fusion.row_ref.refs_0_, bf16[64,2048]{1,0:T(8,128)(2,1)S(1)} %collective-permute-done.1.refs_0_, bf16[64,2048]{1,0:T(8,128)(2,1)S(1)} %collective-permute-done.2.refs_1_, bf16[4,576,384]{2,1,0:T(8,128)(2,1)S(1)} %bitcast.82, ...), custom_call_target="tpu_custom_call" | custom-call | flops 1 | bytes 1 | tf_op jit(solution)/shard_map/attention/pallas_call | solution.py:211
  15.6 0.2 collective-permute-start.3
  15.8 0.4 collective-permute-start
  16.2 1.0 collective-permute-done.3
  17.3 1.8 %collective-permute-start.5 = (bf16[64,2048]{1,0:T(8,128)(2,1)S(1)}, bf16[64,2048]{1,0:T(8,128)(2,1)S(1)}, u32[]{:S(2)}, u32[]{:S(2)}) collective-permute-start(bf16[64,2048]{1,0:T(8,128)(2,1)S(1)} %add_convert_fusion.1), channel_id=1, source_target_pairs={{0,4},{2,6},{4,0},{6,2},{1,5},{3,7},{5,1},{7,3},{8,12},{10,14},{12... | collective-permute-start | bytes 786440 | tf_op jit(solution)/shard_map/ppermute | solution.py:357
  19.1 4.4 %attention.3 = (f32[64,2048]{1,0:T(8,128)S(1)}, bf16[64,2048]{1,0:T(8,128)(2,1)S(1)}, bf16[1,64,576]{2,1,0:T(8,128)(2,1)}) custom-call(s32[3]{0:T(128)S(1)} %pad_add_fusion.row_ref.refs_0_, bf16[64,2048]{1,0:T(8,128)(2,1)S(1)} %copy-done.10, bf16[64,2048]{1,0:T(8,128)(2,1)S(1)} %collective-permute-done.refs_1_, bf16[4,576,384]{2,1,0:T(8,128)(2,1)S(1)} %bitcast.83, ...), custom_call_target="tpu_custom_call" | custom-call | flops 1 | bytes 1 | tf_op jit(solution)/shard_map/attention/pallas_call | solution.py:211
  23.5 2.2 %collective-permute-done.5 = bf16[64,2048]{1,0:T(8,128)(2,1)S(1)} collective-permute-done((bf16[64,2048]{1,0:T(8,128)(2,1)S(1)}, bf16[64,2048]{1,0:T(8,128)(2,1)S(1)}, u32[]{:S(2)}, u32[]{:S(2)}) %collective-permute-start.5) | collective-permute-done | bytes 262176 | tf_op jit(solution)/shard_map/ppermute | solution.py:357
  25.8 1.8 %collective-permute-start.6 = (bf16[64,2048]{1,0:T(8,128)(2,1)S(1)}, bf16[64,2048]{1,0:T(8,128)(2,1)S(1)}, u32[]{:S(2)}, u32[]{:S(2)}) collective-permute-start(bf16[64,2048]{1,0:T(8,128)(2,1)S(1)} %add_convert_fusion.keep_ref), channel_id=1, source_target_pairs={{0,1},{1,0},{2,3},{3,2},{4,5},{5,4},{6,7},{7,6},{8,9},{9,8},{10,11... | collective-permute-start | bytes 786440 | tf_op jit(solution)/shard_map/ppermute | solution.py:357
  27.7 5.8 %collective-permute-done.6 = bf16[64,2048]{1,0:T(8,128)(2,1)S(1)} collective-permute-done((bf16[64,2048]{1,0:T(8,128)(2,1)S(1)}, bf16[64,2048]{1,0:T(8,128)(2,1)S(1)}, u32[]{:S(2)}, u32[]{:S(2)}) %collective-permute-start.6) | collective-permute-done | bytes 262176 | tf_op jit(solution)/shard_map/ppermute | solution.py:357
  33.5 0.8 join.1
  34.3 3.8 %collective-permute-start.12 = (bf16[1,64,1152]{2,1,0:T(8,128)(2,1)S(1)}, bf16[1,64,1152]{2,1,0:T(8,128)(2,1)S(1)}, u32[]{:S(2)}, u32[]{:S(2)}) collective-permute-start(bf16[1,64,1152]{2,1,0:T(8,128)(2,1)S(1)} %get-tuple-element.46), channel_id=1, source_target_pairs={{0,24},{8,16},{16,8},{24,0},{1,25},{9,17},{17,9},{25,1},{2,26},{10... | collective-permute-start | bytes 442376 | tf_op jit(solution)/shard_map/ppermute | solution.py:357
  38.1 0.7 collective-permute-start.14
  38.8 1.6 %collective-permute-start.7 = (bf16[2,64,1152]{2,1,0:T(8,128)(2,1)S(1)}, bf16[2,64,1152]{2,1,0:T(8,128)(2,1)S(1)}, u32[]{:S(2)}, u32[]{:S(2)}) collective-permute-start(bf16[2,64,1152]{2,1,0:T(8,128)(2,1)S(1)} %get-tuple-element.42.refs_1_), channel_id=1, source_target_pairs={{0,4},{2,6},{4,0},{6,2},{1,5},{3,7},{5,1},{7,3},{8,12},{10,14},{12... | collective-permute-start | bytes 884744 | tf_op jit(solution)/shard_map/ppermute | solution.py:357
  40.4 2.6 %collective-permute-done.12 = bf16[1,64,1152]{2,1,0:T(8,128)(2,1)S(1)} collective-permute-done((bf16[1,64,1152]{2,1,0:T(8,128)(2,1)S(1)}, bf16[1,64,1152]{2,1,0:T(8,128)(2,1)S(1)}, u32[]{:S(2)}, u32[]{:S(2)}) %collective-permute-start.12) | collective-permute-done | bytes 147488 | tf_op jit(solution)/shard_map/ppermute | solution.py:357
  43.0 6.2 %collective-permute-done.13 = bf16[1,64,1152]{2,1,0:T(8,128)(2,1)S(1)} collective-permute-done((bf16[1,64,1152]{2,1,0:T(8,128)(2,1)S(1)}, bf16[1,64,1152]{2,1,0:T(8,128)(2,1)S(1)}, u32[]{:S(2)}, u32[]{:S(2)}) %collective-permute-start.13) | collective-permute-done | bytes 147488 | tf_op jit(solution)/shard_map/ppermute | solution.py:357
  49.3 0.8 collective-permute-done.14.refs_1_
  50.1 1.5 %collective-permute-start.16 = (bf16[1,2,64,1152]{3,2,0,1:T(8,128)(2,1)S(1)}, bf16[1,2,64,1152]{3,2,0,1:T(8,128)(2,1)S(1)}, u32[]{:S(2)}, u32[]{:S(2)}) collective-permute-start(bf16[1,2,64,1152]{3,2,0,1:T(8,128)(2,1)S(1)} %maximum_bitcast_fusion), channel_id=1, source_target_pairs={{0,4},{2,6},{4,0},{6,2},{1,5},{3,7},{5,1},{7,3},{8,12},{10,14},{12... | collective-permute-start | bytes 884744 | tf_op jit(solution)/shard_map/ppermute | solution.py:357
  51.6 1.5 %collective-permute-start.15 = (bf16[1,2,64,1152]{3,2,0,1:T(8,128)(2,1)S(1)}, bf16[1,2,64,1152]{3,2,0,1:T(8,128)(2,1)S(1)}, u32[]{:S(2)}, u32[]{:S(2)}) collective-permute-start(bf16[1,2,64,1152]{3,2,0,1:T(8,128)(2,1)S(1)} %maximum_bitcast_fusion), channel_id=1, source_target_pairs={{0,1},{1,0},{2,3},{3,2},{4,5},{5,4},{6,7},{7,6},{8,9},{9,8},{10,11... | collective-permute-start | bytes 884744 | tf_op jit(solution)/shard_map/ppermute | solution.py:357
  53.1 0.3 collective-permute-start.9
  53.4 3.9 %collective-permute-done.16 = bf16[1,2,64,1152]{3,2,0,1:T(8,128)(2,1)S(1)} collective-permute-done((bf16[1,2,64,1152]{3,2,0,1:T(8,128)(2,1)S(1)}, bf16[1,2,64,1152]{3,2,0,1:T(8,128)(2,1)S(1)}, u32[]{:S(2)}, u32[]{:S(2)}) %collective-permute-start.16) | collective-permute-done | bytes 294944 | tf_op jit(solution)/shard_map/ppermute | solution.py:357
  57.3 1.5 %collective-permute-start.17 = (bf16[1,2,64,1152]{3,2,0,1:T(8,128)(2,1)S(1)}, bf16[1,2,64,1152]{3,2,0,1:T(8,128)(2,1)S(1)}, u32[]{:S(2)}, u32[]{:S(2)}) collective-permute-start(bf16[1,2,64,1152]{3,2,0,1:T(8,128)(2,1)S(1)} %collective-permute-done.16), channel_id=1, source_target_pairs={{0,1},{1,0},{2,3},{3,2},{4,5},{5,4},{6,7},{7,6},{8,9},{9,8},{10,11... | collective-permute-start | bytes 884744 | tf_op jit(solution)/shard_map/ppermute | solution.py:357
  58.8 2.6 %collective-permute-done.15 = bf16[1,2,64,1152]{3,2,0,1:T(8,128)(2,1)S(1)} collective-permute-done((bf16[1,2,64,1152]{3,2,0,1:T(8,128)(2,1)S(1)}, bf16[1,2,64,1152]{3,2,0,1:T(8,128)(2,1)S(1)}, u32[]{:S(2)}, u32[]{:S(2)}) %collective-permute-start.15) | collective-permute-done | bytes 294944 | tf_op jit(solution)/shard_map/ppermute | solution.py:357
  61.4 5.9 %collective-permute-done.17 = bf16[1,2,64,1152]{3,2,0,1:T(8,128)(2,1)S(1)} collective-permute-done((bf16[1,2,64,1152]{3,2,0,1:T(8,128)(2,1)S(1)}, bf16[1,2,64,1152]{3,2,0,1:T(8,128)(2,1)S(1)}, u32[]{:S(2)}, u32[]{:S(2)}) %collective-permute-start.17) | collective-permute-done | bytes 294944 | tf_op jit(solution)/shard_map/ppermute | solution.py:357
  67.6 0.6 collective-permute-start.20
  68.2 5.2 %experts.4 = (f32[2,2,64,1024]{3,2,1,0:T(8,128)S(1)}, bf16[2,2,64,1024]{3,2,1,0:T(8,128)(2,1)S(1)}) custom-call(s32[3]{0:T(128)S(1)} %pad_add_fusion.row_ref.refs_0_, bf16[2,64,1152]{2,1,0:T(8,128)(2,1)S(1)} %get-tuple-element.42.refs_1_, bf16[2,64,1152]{2,1,0:T(8,128)(2,1)S(1)} %collective-permute-done.7.refs_2_, ...), custom_call_target="tpu_custom_call" | custom-call | flops 1 | bytes 1 | tf_op jit(solution)/shard_map/experts/pallas_call | solution.py:337
  73.5 4.0 %experts.5 = (f32[2,2,64,1024]{3,2,1,0:T(8,128)S(1)}, bf16[2,2,64,1024]{3,2,1,0:T(8,128)(2,1)S(1)}) custom-call(s32[3]{0:T(128)S(1)} %pad_add_fusion.row_ref.refs_0_, bf16[2,64,1152]{2,1,0:T(8,128)(2,1)S(1)} %get-tuple-element.64.refs_1_, bf16[2,64,1152]{2,1,0:T(8,128)(2,1)S(1)} %get-tuple-element.62.refs_2_, ...), custom_call_target="tpu_custom_call" | custom-call | flops 1 | bytes 1 | tf_op jit(solution)/shard_map/experts/pallas_call | solution.py:337
  77.5 0.5 collective-permute-start.25
  78.1 0.4 collective-permute-start.18
  78.6 0.5 collective-permute-start.31
  79.1 0.2 convert_add_fusion.3
  79.3 0.7 collective-permute-done.19.refs_4_
  80.0 0.4 collective-permute-done.18.refs_3_
  80.4 3.8 %experts.6 = (f32[2,2,64,1024]{3,2,1,0:T(8,128)S(1)}, bf16[2,2,64,1024]{3,2,1,0:T(8,128)(2,1)S(1)}) custom-call(s32[3]{0:T(128)S(1)} %pad_add_fusion.row_ref.refs_0_, bf16[2,64,1152]{2,1,0:T(8,128)(2,1)S(1)} %get-tuple-element.65.refs_1_, bf16[2,64,1152]{2,1,0:T(8,128)(2,1)S(1)} %get-tuple-element.63.refs_2_, ...), custom_call_target="tpu_custom_call" | custom-call | flops 1 | bytes 1 | tf_op jit(solution)/shard_map/experts/pallas_call | solution.py:337
  84.3 0.4 collective-permute-start.22
  84.7 2.8 %collective-permute-done.31.refs_2_ = bf16[2,64,1152]{2,1,0:T(8,128)(2,1)S(1)} collective-permute-done((bf16[2,64,1152]{2,1,0:T(8,128)(2,1)S(1)}, bf16[2,64,1152]{2,1,0:T(8,128)(2,1)S(1)}, u32[]{:S(2)}, u32[]{:S(2)}) %collective-permute-start.31) | collective-permute-done | bytes 294944 | tf_op jit(solution)/shard_map/ppermute | solution.py:357
  87.8 0.6 collective-permute-start.26
  88.3 0.2 convert_add_fusion.2
  88.6 1.6 %collective-permute-start.23 = (bf16[1,2,64,1024]{3,2,1,0:T(8,128)(2,1)S(1)}, bf16[1,2,64,1024]{3,2,1,0:T(8,128)(2,1)S(1)}, u32[]{:S(2)}, u32[]{:S(2)}) collective-permute-start(bf16[1,2,64,1024]{3,2,1,0:T(8,128)(2,1)S(1)} %slice.171), channel_id=1, source_target_pairs={{0,1},{1,0},{2,3},{3,2},{4,5},{5,4},{6,7},{7,6},{8,9},{9,8},{10,11... | collective-permute-start | bytes 786440 | tf_op jit(solution)/shard_map/ppermute | solution.py:357
  90.2 1.6 %collective-permute-start.11 = (bf16[2,64,1024]{2,1,0:T(8,128)(2,1)S(1)}, bf16[2,64,1024]{2,1,0:T(8,128)(2,1)S(1)}, u32[]{:S(2)}, u32[]{:S(2)}) collective-permute-start(bf16[2,64,1024]{2,1,0:T(8,128)(2,1)S(1)} %fusion.3), channel_id=1, source_target_pairs={{0,4},{2,6},{4,0},{6,2},{1,5},{3,7},{5,1},{7,3},{8,12},{10,14},{12... | collective-permute-start | bytes 786440 | tf_op jit(solution)/shard_map/ppermute | solution.py:357
  91.8 3.8 %experts.7 = (f32[2,2,64,1024]{3,2,1,0:T(8,128)S(1)}, bf16[2,2,64,1024]{3,2,1,0:T(8,128)(2,1)S(1)}) custom-call(s32[3]{0:T(128)S(1)} %pad_add_fusion.row_ref.refs_0_, bf16[2,64,1152]{2,1,0:T(8,128)(2,1)S(1)} %collective-permute-done.14.refs_1_, bf16[2,64,1152]{2,1,0:T(8,128)(2,1)S(1)} %collective-permute-done.31.refs_2_, ...), custom_call_target="tpu_custom_call" | custom-call | flops 1 | bytes 1 | tf_op jit(solution)/shard_map/experts/pallas_call | solution.py:337
  95.7 1.3 collective-permute-done.26
  97.0 1.6 %collective-permute-start.27 = (bf16[1,64,1024]{2,1,0:T(8,128)(2,1)S(1)}, bf16[1,64,1024]{2,1,0:T(8,128)(2,1)S(1)}, u32[]{:S(2)}, u32[]{:S(2)}) collective-permute-start(bf16[1,64,1024]{2,1,0:T(8,128)(2,1)S(1)} %slice.173), channel_id=1, source_target_pairs={{0,1},{1,0},{2,3},{3,2},{4,5},{5,4},{6,7},{7,6},{8,9},{9,8},{10,11... | collective-permute-start | bytes 393224 | tf_op jit(solution)/shard_map/ppermute | solution.py:357
  98.7 0.6 collective-permute-start.29
  99.2 3.3 %collective-permute-done.11 = bf16[2,64,1024]{2,1,0:T(8,128)(2,1)S(1)} collective-permute-done((bf16[2,64,1024]{2,1,0:T(8,128)(2,1)S(1)}, bf16[2,64,1024]{2,1,0:T(8,128)(2,1)S(1)}, u32[]{:S(2)}, u32[]{:S(2)}) %collective-permute-start.11) | collective-permute-done | bytes 262176 | tf_op jit(solution)/shard_map/ppermute | solution.py:357
  102.5 0.2 convert_add_fusion
  102.7 0.6 collective-permute-start.35
  103.4 1.6 %collective-permute-start.24 = (bf16[1,64,1024]{2,1,0:T(8,128)(2,1)S(1)}, bf16[1,64,1024]{2,1,0:T(8,128)(2,1)S(1)}, u32[]{:S(2)}, u32[]{:S(2)}) collective-permute-start(bf16[1,64,1024]{2,1,0:T(8,128)(2,1)S(1)} %slice.174), channel_id=1, source_target_pairs={{0,1},{1,0},{2,3},{3,2},{4,5},{5,4},{6,7},{7,6},{8,9},{9,8},{10,11... | collective-permute-start | bytes 393224 | tf_op jit(solution)/shard_map/ppermute | solution.py:357
  105.0 3.2 %collective-permute-start.28 = (bf16[64,1024]{1,0:T(8,128)(2,1)S(1)}, bf16[64,1024]{1,0:T(8,128)(2,1)S(1)}, u32[]{:S(2)}, u32[]{:S(2)}) collective-permute-start(bf16[64,1024]{1,0:T(8,128)(2,1)S(1)} %fusion.17), channel_id=1, source_target_pairs={{0,24},{8,16},{16,8},{24,0},{1,25},{9,17},{17,9},{25,1},{2,26},{10... | collective-permute-start | bytes 393224 | tf_op jit(solution)/shard_map/ppermute | solution.py:357
  108.2 2.4 %collective-permute-done.35 = bf16[2,64,1024]{2,1,0:T(8,128)(2,1)S(1)} collective-permute-done((bf16[2,64,1024]{2,1,0:T(8,128)(2,1)S(1)}, bf16[2,64,1024]{2,1,0:T(8,128)(2,1)S(1)}, u32[]{:S(2)}, u32[]{:S(2)}) %collective-permute-start.35) | collective-permute-done | bytes 262176 | tf_op jit(solution)/shard_map/ppermute | solution.py:357
  110.7 1.6 %collective-permute-start.36 = (bf16[1,64,1024]{2,1,0:T(8,128)(2,1)S(1)}, bf16[1,64,1024]{2,1,0:T(8,128)(2,1)S(1)}, u32[]{:S(2)}, u32[]{:S(2)}) collective-permute-start(bf16[1,64,1024]{2,1,0:T(8,128)(2,1)S(1)} %slice.172), channel_id=1, source_target_pairs={{0,1},{1,0},{2,3},{3,2},{4,5},{5,4},{6,7},{7,6},{8,9},{9,8},{10,11... | collective-permute-start | bytes 393224 | tf_op jit(solution)/shard_map/ppermute | solution.py:357
  112.3 1.2 collective-permute-start.30
  113.5 2.2 %collective-permute-done.36 = bf16[1,64,1024]{2,1,0:T(8,128)(2,1)S(1)} collective-permute-done((bf16[1,64,1024]{2,1,0:T(8,128)(2,1)S(1)}, bf16[1,64,1024]{2,1,0:T(8,128)(2,1)S(1)}, u32[]{:S(2)}, u32[]{:S(2)}) %collective-permute-start.36) | collective-permute-done | bytes 131104 | tf_op jit(solution)/shard_map/ppermute | solution.py:357
  115.8 1.7 %collective-permute-start.37 = (bf16[64,1024]{1,0:T(8,128)(2,1)S(1)}, bf16[64,1024]{1,0:T(8,128)(2,1)S(1)}, u32[]{:S(2)}, u32[]{:S(2)}) collective-permute-start(bf16[64,1024]{1,0:T(8,128)(2,1)S(1)} %fusion.19), channel_id=1, source_target_pairs={{0,8},{8,0},{16,24},{24,16},{1,9},{9,1},{17,25},{25,17},{2,10},{10... | collective-permute-start | bytes 393224 | tf_op jit(solution)/shard_map/ppermute | solution.py:357
  117.5 1.5 %collective-permute-done.30 = bf16[64,1024]{1,0:T(8,128)(2,1)S(1)} collective-permute-done((bf16[64,1024]{1,0:T(8,128)(2,1)S(1)}, bf16[64,1024]{1,0:T(8,128)(2,1)S(1)}, u32[]{:S(2)}, u32[]{:S(2)}) %collective-permute-start.30) | collective-permute-done | bytes 131104 | tf_op jit(solution)/shard_map/ppermute | solution.py:357
  119.0 1.8 %collective-permute-done.37 = bf16[64,1024]{1,0:T(8,128)(2,1)S(1)} collective-permute-done((bf16[64,1024]{1,0:T(8,128)(2,1)S(1)}, bf16[64,1024]{1,0:T(8,128)(2,1)S(1)}, u32[]{:S(2)}, u32[]{:S(2)}) %collective-permute-start.37) | collective-permute-done | bytes 131104 | tf_op jit(solution)/shard_map/ppermute | solution.py:357
  120.9 1.6 %collective-permute-start.38 = (bf16[1,64,1024]{2,1,0:T(8,128)(2,1)S(1)}, bf16[1,64,1024]{2,1,0:T(8,128)(2,1)S(1)}, u32[]{:S(2)}, u32[]{:S(2)}) collective-permute-start(bf16[1,64,1024]{2,1,0:T(8,128)(2,1)S(1)} %bitcast.89), channel_id=1, source_target_pairs={{0,1},{1,0},{2,3},{3,2},{4,5},{5,4},{6,7},{7,6},{8,9},{9,8},{10,11... | collective-permute-start | bytes 393224 | tf_op jit(solution)/shard_map/ppermute | solution.py:357
  122.4 3.5 %collective-permute-done.38.others_ref = bf16[1,64,1024]{2,1,0:T(8,128)(2,1)S(1)} collective-permute-done((bf16[1,64,1024]{2,1,0:T(8,128)(2,1)S(1)}, bf16[1,64,1024]{2,1,0:T(8,128)(2,1)S(1)}, u32[]{:S(2)}, u32[]{:S(2)}) %collective-permute-start.38) | collective-permute-done | bytes 131104 | tf_op jit(solution)/shard_map/ppermute | solution.py:357
  125.9 1.3 finish.1
  (94 shorter events, 1.8 us)
Async XLA Ops:
  0.6 9.6 %collective-permute-start.1 = (bf16[64,2048]{1,0:T(8,128)(2,1)}, bf16[64,2048]{1,0:T(8,128)(2,1)S(1)}, u32[]{:S(2)}, u32[]{:S(2)}) collective-permute-start(bf16[64,2048]{1,0:T(8,128)(2,1)} %hidden_ref.1), channel_id=1, source_target_pairs={{0,4},{2,6},{4,0},{6,2},{1,5},{3,7},{5,1},{7,3},{8,12},{10,14},{12... | collective-permute-start | bytes 786440 | tf_op jit(solution)/shard_map/ppermute | solution.py:357
  4.4 0.7 copy-start.14
  5.1 0.7 copy-start.15
  5.7 6.0 %copy-start.1 = (bf16[2048,576]{0,1:T(8,128)(2,1)S(1)}, bf16[2048,576]{0,1:T(8,128)(2,1)}, u32[]{:S(2)}) copy-start(bf16[2048,576]{0,1:T(8,128)(2,1)} %param.27) | copy-start | bytes 7077892
  5.7 6.0 %copy-start.2 = (bf16[4,384,576]{1,2,0:T(8,128)(2,1)S(1)}, bf16[4,384,576]{1,2,0:T(8,128)(2,1)}, u32[]{:S(2)}) copy-start(bf16[4,384,576]{1,2,0:T(8,128)(2,1)} %param.20) | copy-start | bytes 5308420
  5.7 6.0 %copy-start.3 = (bf16[2048,384]{1,0:T(8,128)(2,1)S(1)}, bf16[2048,384]{1,0:T(8,128)(2,1)}, u32[]{:S(2)}) copy-start(bf16[2048,384]{1,0:T(8,128)(2,1)} %refs_7_.3) | copy-start | bytes 4718596
  5.7 6.0 %copy-start.4 = (bf16[256,2048]{1,0:T(8,128)(2,1)S(1)}, bf16[256,2048]{1,0:T(8,128)(2,1)}, u32[]{:S(2)}) copy-start(bf16[256,2048]{1,0:T(8,128)(2,1)} %refs_12_.3) | copy-start | bytes 3145732
  5.7 6.0 %copy-start.8 = (bf16[2,128,512]{2,1,0:T(8,128)(2,1)S(1)}, bf16[2,128,512]{2,1,0:T(8,128)(2,1)}, u32[]{:S(2)}) copy-start(bf16[2,128,512]{2,1,0:T(8,128)(2,1)} %refs_10_.4) | copy-start | bytes 786436
  5.8 6.0 %copy-start.9 = (bf16[2,512,128]{2,1,0:T(8,128)(2,1)S(1)}, bf16[2,512,128]{2,1,0:T(8,128)(2,1)}, u32[]{:S(2)}) copy-start(bf16[2,512,128]{2,1,0:T(8,128)(2,1)} %refs_11_.3) | copy-start | bytes 786436
  5.8 6.0 %copy-start.11 = (f32[2048]{0:T(1024)S(1)}, f32[2048]{0:T(1024)}, u32[]{:S(2)}) copy-start(f32[2048]{0:T(1024)} %param.25) | copy-start | bytes 24580
  5.8 6.0 %copy-start.12 = (f32[512]{0:T(512)S(1)}, f32[512]{0:T(512)}, u32[]{:S(2)}) copy-start(f32[512]{0:T(512)} %param.28) | copy-start | bytes 6148
  10.2 1.5 %collective-permute-start.2 = (bf16[64,2048]{1,0:T(8,128)(2,1)S(1)}, bf16[64,2048]{1,0:T(8,128)(2,1)S(1)}, u32[]{:S(2)}, u32[]{:S(2)}) collective-permute-start(bf16[64,2048]{1,0:T(8,128)(2,1)S(1)} %collective-permute-done.1.refs_0_), channel_id=1, source_target_pairs={{0,2},{2,0},{4,6},{6,4},{1,3},{3,1},{5,7},{7,5},{8,10},{10,8},{12,... | collective-permute-start | bytes 786440 | tf_op jit(solution)/shard_map/ppermute | solution.py:357
  11.8 4.0 %copy-start.10 = (bf16[64,2048]{1,0:T(8,128)(2,1)S(1)}, bf16[64,2048]{1,0:T(8,128)(2,1)}, u32[]{:S(2)}) copy-start(bf16[64,2048]{1,0:T(8,128)(2,1)} %hidden_ref.1) | copy-start | bytes 786436
  15.6 1.6 %collective-permute-start.3 = (bf16[64,2048]{1,0:T(8,128)(2,1)S(1)}, bf16[64,2048]{1,0:T(8,128)(2,1)S(1)}, u32[]{:S(2)}, u32[]{:S(2)}) collective-permute-start(bf16[64,2048]{1,0:T(8,128)(2,1)S(1)} %get-tuple-element.36), channel_id=1, source_target_pairs={{0,2},{2,0},{4,6},{6,4},{1,3},{3,1},{5,7},{7,5},{8,10},{10,8},{12,... | collective-permute-start | bytes 786440 | tf_op jit(solution)/shard_map/ppermute | solution.py:357
  15.8 3.3 %collective-permute-start = (bf16[64,2048]{1,0:T(8,128)(2,1)S(1)}, bf16[64,2048]{1,0:T(8,128)(2,1)S(1)}, u32[]{:S(2)}, u32[]{:S(2)}) collective-permute-start(bf16[64,2048]{1,0:T(8,128)(2,1)S(1)} %copy-done.10), channel_id=1, source_target_pairs={{0,2},{2,0},{4,6},{6,4},{1,3},{3,1},{5,7},{7,5},{8,10},{10,8},{12,... | collective-permute-start | bytes 786440 | tf_op jit(solution)/shard_map/ppermute | solution.py:357
  17.3 10.3 %copy-start.16 = (s32[64,6]{0,1:T(8,128)S(1)}, s32[64,6]{0,1:T(8,128)}, u32[]{:S(2)}) copy-start(s32[64,6]{0,1:T(8,128)} %param.23) | copy-start | bytes 4612
  17.3 16.2 %copy-start.13 = (f32[2048]{0:T(1024)S(1)}, f32[2048]{0:T(1024)}, u32[]{:S(2)}) copy-start(f32[2048]{0:T(1024)} %param.32) | copy-start | bytes 24580
  17.3 8.4 %collective-permute-start.5 = (bf16[64,2048]{1,0:T(8,128)(2,1)S(1)}, bf16[64,2048]{1,0:T(8,128)(2,1)S(1)}, u32[]{:S(2)}, u32[]{:S(2)}) collective-permute-start(bf16[64,2048]{1,0:T(8,128)(2,1)S(1)} %add_convert_fusion.1), channel_id=1, source_target_pairs={{0,4},{2,6},{4,0},{6,2},{1,5},{3,7},{5,1},{7,3},{8,12},{10,14},{12... | collective-permute-start | bytes 786440 | tf_op jit(solution)/shard_map/ppermute | solution.py:357
  23.5 2.2 %collective-permute-start.4 = (bf16[64,2048]{1,0:T(8,128)(2,1)S(1)}, bf16[64,2048]{1,0:T(8,128)(2,1)S(1)}, u32[]{:S(2)}, u32[]{:S(2)}) collective-permute-start(bf16[64,2048]{1,0:T(8,128)(2,1)S(1)} %get-tuple-element.39), channel_id=1, source_target_pairs={{0,2},{2,0},{4,6},{6,4},{1,3},{3,1},{5,7},{7,5},{8,10},{10,8},{12,... | collective-permute-start | bytes 786440 | tf_op jit(solution)/shard_map/ppermute | solution.py:357
  25.8 7.7 %collective-permute-start.6 = (bf16[64,2048]{1,0:T(8,128)(2,1)S(1)}, bf16[64,2048]{1,0:T(8,128)(2,1)S(1)}, u32[]{:S(2)}, u32[]{:S(2)}) collective-permute-start(bf16[64,2048]{1,0:T(8,128)(2,1)S(1)} %add_convert_fusion.keep_ref), channel_id=1, source_target_pairs={{0,1},{1,0},{2,3},{3,2},{4,5},{5,4},{6,7},{7,6},{8,9},{9,8},{10,11... | collective-permute-start | bytes 786440 | tf_op jit(solution)/shard_map/ppermute | solution.py:357
  33.5 34.6 %slice-start = ((s8[5767168]{0:T(1024)(128)(4,1)}), s8[4194304]{0:T(1024)(128)(4,1)S(1)}, s32[]{:S(2)}) async-start(s8[5767168]{0:T(1024)(128)(4,1)} %bitcast.70), calls=%async_computation | async-start | bytes 8388608
  33.5 34.6 %slice-start.1 = ((s8[5767168]{0:T(1024)(128)(4,1)}), s8[1572864]{0:T(1024)(128)(4,1)S(1)}, s32[]{:S(2)}) async-start(s8[5767168]{0:T(1024)(128)(4,1)} %bitcast.70), calls=%async_computation.1 | async-start | bytes 3145728
  33.5 34.6 %copy-start.5 = (bf16[2,2048,352]{1,2,0:T(8,128)(2,1)S(1)}, bf16[2,2048,352]{1,2,0:T(8,128)(2,1)}, u32[]{:S(2)}) copy-start(bf16[2,2048,352]{1,2,0:T(8,128)(2,1)} %param.34) | copy-start | bytes 8650756
  34.3 8.6 %collective-permute-start.12 = (bf16[1,64,1152]{2,1,0:T(8,128)(2,1)S(1)}, bf16[1,64,1152]{2,1,0:T(8,128)(2,1)S(1)}, u32[]{:S(2)}, u32[]{:S(2)}) collective-permute-start(bf16[1,64,1152]{2,1,0:T(8,128)(2,1)S(1)} %get-tuple-element.46), channel_id=1, source_target_pairs={{0,24},{8,16},{16,8},{24,0},{1,25},{9,17},{17,9},{25,1},{2,26},{10... | collective-permute-start | bytes 442376 | tf_op jit(solution)/shard_map/ppermute | solution.py:357
  38.1 11.1 %collective-permute-start.13 = (bf16[1,64,1152]{2,1,0:T(8,128)(2,1)S(1)}, bf16[1,64,1152]{2,1,0:T(8,128)(2,1)S(1)}, u32[]{:S(2)}, u32[]{:S(2)}) collective-permute-start(bf16[1,64,1152]{2,1,0:T(8,128)(2,1)S(1)} %get-tuple-element.46), channel_id=1, source_target_pairs={{0,16},{8,24},{16,0},{24,8},{1,17},{9,25},{17,1},{25,9},{2,18},{10... | collective-permute-start | bytes 442376 | tf_op jit(solution)/shard_map/ppermute | solution.py:357
  38.1 12.0 %collective-permute-start.14 = (bf16[2,64,1152]{2,1,0:T(8,128)(2,1)S(1)}, bf16[2,64,1152]{2,1,0:T(8,128)(2,1)S(1)}, u32[]{:S(2)}, u32[]{:S(2)}) collective-permute-start(bf16[2,64,1152]{2,1,0:T(8,128)(2,1)S(1)} %get-tuple-element.42.refs_1_), channel_id=1, source_target_pairs={{0,8},{8,0},{16,24},{24,16},{1,9},{9,1},{17,25},{25,17},{2,10},{10... | collective-permute-start | bytes 884744 | tf_op jit(solution)/shard_map/ppermute | solution.py:357
  38.8 11.3 %collective-permute-start.7 = (bf16[2,64,1152]{2,1,0:T(8,128)(2,1)S(1)}, bf16[2,64,1152]{2,1,0:T(8,128)(2,1)S(1)}, u32[]{:S(2)}, u32[]{:S(2)}) collective-permute-start(bf16[2,64,1152]{2,1,0:T(8,128)(2,1)S(1)} %get-tuple-element.42.refs_1_), channel_id=1, source_target_pairs={{0,4},{2,6},{4,0},{6,2},{1,5},{3,7},{5,1},{7,3},{8,12},{10,14},{12... | collective-permute-start | bytes 884744 | tf_op jit(solution)/shard_map/ppermute | solution.py:357
  49.2 18.9 %copy-start = (bf16[1,704,2048]{2,1,0:T(8,128)(2,1)S(1)}, bf16[1,704,2048]{2,1,0:T(8,128)(2,1)}, u32[]{:S(2)}) copy-start(bf16[1,704,2048]{2,1,0:T(8,128)(2,1)} %param.37) | copy-start | bytes 8650756
  49.3 18.9 %copy-start.6 = (bf16[352,2048]{1,0:T(8,128)(2,1)S(1)}, bf16[352,2048]{1,0:T(8,128)(2,1)}, u32[]{:S(2)}) copy-start(bf16[352,2048]{1,0:T(8,128)(2,1)} %refs_10_.5) | copy-start | bytes 4325380
  49.3 18.9 %copy-start.7 = (bf16[2048,16]{0,1:T(8,128)(2,1)S(1)}, bf16[2048,16]{0,1:T(8,128)(2,1)}, u32[]{:S(2)}) copy-start(bf16[2048,16]{0,1:T(8,128)(2,1)} %param.33) | copy-start | bytes 196612
  50.1 7.3 %collective-permute-start.16 = (bf16[1,2,64,1152]{3,2,0,1:T(8,128)(2,1)S(1)}, bf16[1,2,64,1152]{3,2,0,1:T(8,128)(2,1)S(1)}, u32[]{:S(2)}, u32[]{:S(2)}) collective-permute-start(bf16[1,2,64,1152]{3,2,0,1:T(8,128)(2,1)S(1)} %maximum_bitcast_fusion), channel_id=1, source_target_pairs={{0,4},{2,6},{4,0},{6,2},{1,5},{3,7},{5,1},{7,3},{8,12},{10,14},{12... | collective-permute-start | bytes 884744 | tf_op jit(solution)/shard_map/ppermute | solution.py:357
  51.6 16.5 %collective-permute-start.8 = (bf16[2,64,1152]{2,1,0:T(8,128)(2,1)S(1)}, bf16[2,64,1152]{2,1,0:T(8,128)(2,1)S(1)}, u32[]{:S(2)}, u32[]{:S(2)}) collective-permute-start(bf16[2,64,1152]{2,1,0:T(8,128)(2,1)S(1)} %get-tuple-element.42.refs_1_), channel_id=1, source_target_pairs={{0,2},{2,0},{4,6},{6,4},{1,3},{3,1},{5,7},{7,5},{8,10},{10,8},{12,... | collective-permute-start | bytes 884744 | tf_op jit(solution)/shard_map/ppermute | solution.py:357
  51.6 9.8 %collective-permute-start.15 = (bf16[1,2,64,1152]{3,2,0,1:T(8,128)(2,1)S(1)}, bf16[1,2,64,1152]{3,2,0,1:T(8,128)(2,1)S(1)}, u32[]{:S(2)}, u32[]{:S(2)}) collective-permute-start(bf16[1,2,64,1152]{3,2,0,1:T(8,128)(2,1)S(1)} %maximum_bitcast_fusion), channel_id=1, source_target_pairs={{0,1},{1,0},{2,3},{3,2},{4,5},{5,4},{6,7},{7,6},{8,9},{9,8},{10,11... | collective-permute-start | bytes 884744 | tf_op jit(solution)/shard_map/ppermute | solution.py:357
  53.1 15.0 %collective-permute-start.9 = (bf16[2,64,1152]{2,1,0:T(8,128)(2,1)S(1)}, bf16[2,64,1152]{2,1,0:T(8,128)(2,1)S(1)}, u32[]{:S(2)}, u32[]{:S(2)}) collective-permute-start(bf16[2,64,1152]{2,1,0:T(8,128)(2,1)S(1)} %collective-permute-done.7.refs_2_), channel_id=1, source_target_pairs={{0,2},{2,0},{4,6},{6,4},{1,3},{3,1},{5,7},{7,5},{8,10},{10,8},{12,... | collective-permute-start | bytes 884744 | tf_op jit(solution)/shard_map/ppermute | solution.py:357
  57.3 10.0 %collective-permute-start.17 = (bf16[1,2,64,1152]{3,2,0,1:T(8,128)(2,1)S(1)}, bf16[1,2,64,1152]{3,2,0,1:T(8,128)(2,1)S(1)}, u32[]{:S(2)}, u32[]{:S(2)}) collective-permute-start(bf16[1,2,64,1152]{3,2,0,1:T(8,128)(2,1)S(1)} %collective-permute-done.16), channel_id=1, source_target_pairs={{0,1},{1,0},{2,3},{3,2},{4,5},{5,4},{6,7},{7,6},{8,9},{9,8},{10,11... | collective-permute-start | bytes 884744 | tf_op jit(solution)/shard_map/ppermute | solution.py:357
  67.4 6.0 %collective-permute-start.21 = (bf16[2,64,1152]{2,1,0:T(8,128)(2,1)S(1)}, bf16[2,64,1152]{2,1,0:T(8,128)(2,1)S(1)}, u32[]{:S(2)}, u32[]{:S(2)}) collective-permute-start(bf16[2,64,1152]{2,1,0:T(8,128)(2,1)S(1)} %get-tuple-element.62.refs_2_), channel_id=1, source_target_pairs={{0,2},{2,0},{4,6},{6,4},{1,3},{3,1},{5,7},{7,5},{8,10},{10,8},{12,... | collective-permute-start | bytes 884744 | tf_op jit(solution)/shard_map/ppermute | solution.py:357
  67.6 5.9 %collective-permute-start.20 = (bf16[2,64,1152]{2,1,0:T(8,128)(2,1)S(1)}, bf16[2,64,1152]{2,1,0:T(8,128)(2,1)S(1)}, u32[]{:S(2)}, u32[]{:S(2)}) collective-permute-start(bf16[2,64,1152]{2,1,0:T(8,128)(2,1)S(1)} %get-tuple-element.64.refs_1_), channel_id=1, source_target_pairs={{0,2},{2,0},{4,6},{6,4},{1,3},{3,1},{5,7},{7,5},{8,10},{10,8},{12,... | collective-permute-start | bytes 884744 | tf_op jit(solution)/shard_map/ppermute | solution.py:357
  73.4 5.7 %collective-permute-start.10 = (bf16[2,2,64,1024]{3,2,1,0:T(8,128)(2,1)S(1)}, bf16[2,2,64,1024]{3,2,1,0:T(8,128)(2,1)S(1)}, u32[]{:S(2)}, u32[]{:S(2)}) collective-permute-start(bf16[2,2,64,1024]{3,2,1,0:T(8,128)(2,1)S(1)} %get-tuple-element.45), channel_id=1, source_target_pairs={{0,2},{2,0},{4,6},{6,4},{1,3},{3,1},{5,7},{7,5},{8,10},{10,8},{12,... | collective-permute-start | bytes 1572872 | tf_op jit(solution)/shard_map/ppermute | solution.py:357
  77.5 10.1 %collective-permute-start.25 = (bf16[2,2,64,1024]{3,2,1,0:T(8,128)(2,1)S(1)}, bf16[2,2,64,1024]{3,2,1,0:T(8,128)(2,1)S(1)}, u32[]{:S(2)}, u32[]{:S(2)}) collective-permute-start(bf16[2,2,64,1024]{3,2,1,0:T(8,128)(2,1)S(1)} %get-tuple-element.49), channel_id=1, source_target_pairs={{0,2},{2,0},{4,6},{6,4},{1,3},{3,1},{5,7},{7,5},{8,10},{10,8},{12,... | collective-permute-start | bytes 1572872 | tf_op jit(solution)/shard_map/ppermute | solution.py:357
  78.1 2.0 %collective-permute-start.19 = (bf16[2,64,1152]{2,1,0:T(8,128)(2,1)S(1)}, bf16[2,64,1152]{2,1,0:T(8,128)(2,1)S(1)}, u32[]{:S(2)}, u32[]{:S(2)}) collective-permute-start(bf16[2,64,1152]{2,1,0:T(8,128)(2,1)S(1)} %get-tuple-element.63.refs_2_), channel_id=1, source_target_pairs={{0,2},{2,0},{4,6},{6,4},{1,3},{3,1},{5,7},{7,5},{8,10},{10,8},{12,... | collective-permute-start | bytes 884744 | tf_op jit(solution)/shard_map/ppermute | solution.py:357
  78.1 2.3 %collective-permute-start.18 = (bf16[2,64,1152]{2,1,0:T(8,128)(2,1)S(1)}, bf16[2,64,1152]{2,1,0:T(8,128)(2,1)S(1)}, u32[]{:S(2)}, u32[]{:S(2)}) collective-permute-start(bf16[2,64,1152]{2,1,0:T(8,128)(2,1)S(1)} %get-tuple-element.65.refs_1_), channel_id=1, source_target_pairs={{0,2},{2,0},{4,6},{6,4},{1,3},{3,1},{5,7},{7,5},{8,10},{10,8},{12,... | collective-permute-start | bytes 884744 | tf_op jit(solution)/shard_map/ppermute | solution.py:357
  78.6 9.0 %collective-permute-start.31 = (bf16[2,64,1152]{2,1,0:T(8,128)(2,1)S(1)}, bf16[2,64,1152]{2,1,0:T(8,128)(2,1)S(1)}, u32[]{:S(2)}, u32[]{:S(2)}) collective-permute-start(bf16[2,64,1152]{2,1,0:T(8,128)(2,1)S(1)} %collective-permute-done.14.refs_1_), channel_id=1, source_target_pairs={{0,4},{2,6},{4,0},{6,2},{1,5},{3,7},{5,1},{7,3},{8,12},{10,14},{12... | collective-permute-start | bytes 884744 | tf_op jit(solution)/shard_map/ppermute | solution.py:357
  79.1 12.7 %collective-permute-start.32 = (bf16[2,64,1152]{2,1,0:T(8,128)(2,1)S(1)}, bf16[2,64,1152]{2,1,0:T(8,128)(2,1)S(1)}, u32[]{:S(2)}, u32[]{:S(2)}) collective-permute-start(bf16[2,64,1152]{2,1,0:T(8,128)(2,1)S(1)} %collective-permute-done.14.refs_1_), channel_id=1, source_target_pairs={{0,2},{2,0},{4,6},{6,4},{1,3},{3,1},{5,7},{7,5},{8,10},{10,8},{12,... | collective-permute-start | bytes 884744 | tf_op jit(solution)/shard_map/ppermute | solution.py:357
  84.3 4.1 %collective-permute-start.22 = (bf16[2,2,64,1024]{3,2,1,0:T(8,128)(2,1)S(1)}, bf16[2,2,64,1024]{3,2,1,0:T(8,128)(2,1)S(1)}, u32[]{:S(2)}, u32[]{:S(2)}) collective-permute-start(bf16[2,2,64,1024]{3,2,1,0:T(8,128)(2,1)S(1)} %get-tuple-element.52), channel_id=1, source_target_pairs={{0,2},{2,0},{4,6},{6,4},{1,3},{3,1},{5,7},{7,5},{8,10},{10,8},{12,... | collective-permute-start | bytes 1572872 | tf_op jit(solution)/shard_map/ppermute | solution.py:357
  87.6 4.2 %collective-permute-start.33 = (bf16[2,64,1152]{2,1,0:T(8,128)(2,1)S(1)}, bf16[2,64,1152]{2,1,0:T(8,128)(2,1)S(1)}, u32[]{:S(2)}, u32[]{:S(2)}) collective-permute-start(bf16[2,64,1152]{2,1,0:T(8,128)(2,1)S(1)} %collective-permute-done.31.refs_2_), channel_id=1, source_target_pairs={{0,2},{2,0},{4,6},{6,4},{1,3},{3,1},{5,7},{7,5},{8,10},{10,8},{12,... | collective-permute-start | bytes 884744 | tf_op jit(solution)/shard_map/ppermute | solution.py:357
  87.8 9.2 %collective-permute-start.26 = (bf16[2,64,1024]{2,1,0:T(8,128)(2,1)S(1)}, bf16[2,64,1024]{2,1,0:T(8,128)(2,1)S(1)}, u32[]{:S(2)}, u32[]{:S(2)}) collective-permute-start(bf16[2,64,1024]{2,1,0:T(8,128)(2,1)S(1)} %fusion.4), channel_id=1, source_target_pairs={{0,4},{2,6},{4,0},{6,2},{1,5},{3,7},{5,1},{7,3},{8,12},{10,14},{12... | collective-permute-start | bytes 786440 | tf_op jit(solution)/shard_map/ppermute | solution.py:357
  88.6 10.0 %collective-permute-start.23 = (bf16[1,2,64,1024]{3,2,1,0:T(8,128)(2,1)S(1)}, bf16[1,2,64,1024]{3,2,1,0:T(8,128)(2,1)S(1)}, u32[]{:S(2)}, u32[]{:S(2)}) collective-permute-start(bf16[1,2,64,1024]{3,2,1,0:T(8,128)(2,1)S(1)} %slice.171), channel_id=1, source_target_pairs={{0,1},{1,0},{2,3},{3,2},{4,5},{5,4},{6,7},{7,6},{8,9},{9,8},{10,11... | collective-permute-start | bytes 786440 | tf_op jit(solution)/shard_map/ppermute | solution.py:357
  90.2 12.4 %collective-permute-start.11 = (bf16[2,64,1024]{2,1,0:T(8,128)(2,1)S(1)}, bf16[2,64,1024]{2,1,0:T(8,128)(2,1)S(1)}, u32[]{:S(2)}, u32[]{:S(2)}) collective-permute-start(bf16[2,64,1024]{2,1,0:T(8,128)(2,1)S(1)} %fusion.3), channel_id=1, source_target_pairs={{0,4},{2,6},{4,0},{6,2},{1,5},{3,7},{5,1},{7,3},{8,12},{10,14},{12... | collective-permute-start | bytes 786440 | tf_op jit(solution)/shard_map/ppermute | solution.py:357
  95.6 7.0 %collective-permute-start.34 = (bf16[2,2,64,1024]{3,2,1,0:T(8,128)(2,1)S(1)}, bf16[2,2,64,1024]{3,2,1,0:T(8,128)(2,1)S(1)}, u32[]{:S(2)}, u32[]{:S(2)}) collective-permute-start(bf16[2,2,64,1024]{3,2,1,0:T(8,128)(2,1)S(1)} %get-tuple-element.60), channel_id=1, source_target_pairs={{0,2},{2,0},{4,6},{6,4},{1,3},{3,1},{5,7},{7,5},{8,10},{10,8},{12,... | collective-permute-start | bytes 1572872 | tf_op jit(solution)/shard_map/ppermute | solution.py:357
  97.0 7.9 %collective-permute-start.27 = (bf16[1,64,1024]{2,1,0:T(8,128)(2,1)S(1)}, bf16[1,64,1024]{2,1,0:T(8,128)(2,1)S(1)}, u32[]{:S(2)}, u32[]{:S(2)}) collective-permute-start(bf16[1,64,1024]{2,1,0:T(8,128)(2,1)S(1)} %slice.173), channel_id=1, source_target_pairs={{0,1},{1,0},{2,3},{3,2},{4,5},{5,4},{6,7},{7,6},{8,9},{9,8},{10,11... | collective-permute-start | bytes 393224 | tf_op jit(solution)/shard_map/ppermute | solution.py:357
  98.7 13.6 %collective-permute-start.29 = (bf16[64,1024]{1,0:T(8,128)(2,1)S(1)}, bf16[64,1024]{1,0:T(8,128)(2,1)S(1)}, u32[]{:S(2)}, u32[]{:S(2)}) collective-permute-start(bf16[64,1024]{1,0:T(8,128)(2,1)S(1)} %fusion.18), channel_id=1, source_target_pairs={{0,4},{2,6},{4,0},{6,2},{1,5},{3,7},{5,1},{7,3},{8,12},{10,14},{12... | collective-permute-start | bytes 393224 | tf_op jit(solution)/shard_map/ppermute | solution.py:357
  102.7 7.8 %collective-permute-start.35 = (bf16[2,64,1024]{2,1,0:T(8,128)(2,1)S(1)}, bf16[2,64,1024]{2,1,0:T(8,128)(2,1)S(1)}, u32[]{:S(2)}, u32[]{:S(2)}) collective-permute-start(bf16[2,64,1024]{2,1,0:T(8,128)(2,1)S(1)} %fusion.5), channel_id=1, source_target_pairs={{0,4},{2,6},{4,0},{6,2},{1,5},{3,7},{5,1},{7,3},{8,12},{10,14},{12... | collective-permute-start | bytes 786440 | tf_op jit(solution)/shard_map/ppermute | solution.py:357
  103.4 14.1 %collective-permute-start.24 = (bf16[1,64,1024]{2,1,0:T(8,128)(2,1)S(1)}, bf16[1,64,1024]{2,1,0:T(8,128)(2,1)S(1)}, u32[]{:S(2)}, u32[]{:S(2)}) collective-permute-start(bf16[1,64,1024]{2,1,0:T(8,128)(2,1)S(1)} %slice.174), channel_id=1, source_target_pairs={{0,1},{1,0},{2,3},{3,2},{4,5},{5,4},{6,7},{7,6},{8,9},{9,8},{10,11... | collective-permute-start | bytes 393224 | tf_op jit(solution)/shard_map/ppermute | solution.py:357
  105.0 12.5 %collective-permute-start.28 = (bf16[64,1024]{1,0:T(8,128)(2,1)S(1)}, bf16[64,1024]{1,0:T(8,128)(2,1)S(1)}, u32[]{:S(2)}, u32[]{:S(2)}) collective-permute-start(bf16[64,1024]{1,0:T(8,128)(2,1)S(1)} %fusion.17), channel_id=1, source_target_pairs={{0,24},{8,16},{16,8},{24,0},{1,25},{9,17},{17,9},{25,1},{2,26},{10... | collective-permute-start | bytes 393224 | tf_op jit(solution)/shard_map/ppermute | solution.py:357
  110.7 5.0 %collective-permute-start.36 = (bf16[1,64,1024]{2,1,0:T(8,128)(2,1)S(1)}, bf16[1,64,1024]{2,1,0:T(8,128)(2,1)S(1)}, u32[]{:S(2)}, u32[]{:S(2)}) collective-permute-start(bf16[1,64,1024]{2,1,0:T(8,128)(2,1)S(1)} %slice.172), channel_id=1, source_target_pairs={{0,1},{1,0},{2,3},{3,2},{4,5},{5,4},{6,7},{7,6},{8,9},{9,8},{10,11... | collective-permute-start | bytes 393224 | tf_op jit(solution)/shard_map/ppermute | solution.py:357
  112.3 6.8 %collective-permute-start.30 = (bf16[64,1024]{1,0:T(8,128)(2,1)S(1)}, bf16[64,1024]{1,0:T(8,128)(2,1)S(1)}, u32[]{:S(2)}, u32[]{:S(2)}) collective-permute-start(bf16[64,1024]{1,0:T(8,128)(2,1)S(1)} %fusion.8), channel_id=1, source_target_pairs={{0,16},{8,24},{16,0},{24,8},{1,17},{9,25},{17,1},{25,9},{2,18},{10... | collective-permute-start | bytes 393224 | tf_op jit(solution)/shard_map/ppermute | solution.py:357
  115.8 5.0 %collective-permute-start.37 = (bf16[64,1024]{1,0:T(8,128)(2,1)S(1)}, bf16[64,1024]{1,0:T(8,128)(2,1)S(1)}, u32[]{:S(2)}, u32[]{:S(2)}) collective-permute-start(bf16[64,1024]{1,0:T(8,128)(2,1)S(1)} %fusion.19), channel_id=1, source_target_pairs={{0,8},{8,0},{16,24},{24,16},{1,9},{9,1},{17,25},{25,17},{2,10},{10... | collective-permute-start | bytes 393224 | tf_op jit(solution)/shard_map/ppermute | solution.py:357
  120.9 5.0 %collective-permute-start.38 = (bf16[1,64,1024]{2,1,0:T(8,128)(2,1)S(1)}, bf16[1,64,1024]{2,1,0:T(8,128)(2,1)S(1)}, u32[]{:S(2)}, u32[]{:S(2)}) collective-permute-start(bf16[1,64,1024]{2,1,0:T(8,128)(2,1)S(1)} %bitcast.89), channel_id=1, source_target_pairs={{0,1},{1,0},{2,3},{3,2},{4,5},{5,4},{6,7},{7,6},{8,9},{9,8},{10,11... | collective-permute-start | bytes 393224 | tf_op jit(solution)/shard_map/ppermute | solution.py:357
